TPU v7x, 32 devices: a whole 2x2x4 slice. The times are simulated.
32 devices in a mesh: blk: 32 (over z, y, x, core), col: 1.
Axes of the slice: x: 2, y: 2, z: 4, core: 2. Of those that a mesh axis runs over, the one named last changes fastest.
Arguments:
- kernel: float32 [2048, 1, 2048], P('blk', 'col'), may hold values from -8 to 60
- ritz_block: float32 [2048, 128], P(('blk', 'col')), may hold values from -0.125 to 0.125
- search_block: float32 [2048, 128], P(('blk', 'col')), may hold values from -0.125 to 0.125
- precond_diag: float32 [2048], P(('blk', 'col')), may hold values from 3 to 30
Outputs:
- new_ritz: float32 [2048, 128], P(('blk', 'col'))
- correction: float32 [2048, 128], P(('blk', 'col'))
- residual_norms: float32 [2, 128], replicated
All inputs are finite; a program needn't handle non-finite values.
Results may differ from a plain program's by a relative error of at most 0.0003.
Values sent between devices are 32-bit elements; how exact they have to be, the bound alone decides.
No kernel may reach another device: no remote copies, remote signals or barrier semaphores. Data moves between devices by JAX's collectives and lax.ppermute only.
A program may use at most 64 MiB of HBM per device.

v0:
```python
import jax
import jax.numpy as jnp
from jax import lax
from jax.sharding import PartitionSpec as P

ITERS = 2


highest = lax.Precision.HIGHEST


def inner(former, latter):
    return lax.dot_general(
        former,
        latter,
        (((0,), (0,)), ((), ())),
        precision=highest,
        preferred_element_type=jnp.float32,
    )


def coefficients(blocks, width):
    ritz_ritz, ritz_search, search_search, ritz_image, ritz_wimage, search_wimage = blocks
    metric = jnp.concatenate(
        [
            jnp.concatenate([ritz_ritz, ritz_search], 1),
            jnp.concatenate([ritz_search.T, search_search], 1),
        ],
        0,
    )
    projected = jnp.concatenate(
        [
            jnp.concatenate([ritz_image, ritz_wimage], 1),
            jnp.concatenate([ritz_wimage.T, search_wimage], 1),
        ],
        0,
    )
    lower_metric = jnp.linalg.cholesky(metric)
    halfway = lax.linalg.triangular_solve(
        lower_metric, projected[:, :width], left_side=True, lower=True
    )
    powered = lax.linalg.triangular_solve(
        lower_metric, halfway, left_side=True, lower=True, transpose_a=True
    )
    hermite = jnp.dot(powered.T, jnp.dot(metric, powered, precision=highest), precision=highest)
    lower_hermite = jnp.linalg.cholesky(hermite)
    mixing = lax.linalg.triangular_solve(
        lower_hermite, powered, left_side=False, lower=True, transpose_a=True
    )
    ritz_values = jnp.dot(
        mixing.T, jnp.dot(projected, mixing, precision=highest), precision=highest
    )
    return (mixing, ritz_values)


def update(vectors, images, search, search_images, mixing, ritz_values, precond):
    width = vectors.shape[1]
    upper_part = mixing[:width]
    lower_part = mixing[width:]
    next_ritz = jnp.dot(vectors, upper_part, precision=highest) + jnp.dot(
        search, lower_part, precision=highest
    )
    next_image = jnp.dot(images, upper_part, precision=highest) + jnp.dot(
        search_images, lower_part, precision=highest
    )
    residual = next_image - jnp.dot(next_ritz, ritz_values, precision=highest)
    squares = jnp.sum(residual * residual, axis=0)
    divisor = jnp.maximum(jnp.abs(precond[:, None] - jnp.diagonal(ritz_values)[None, :]), 1.0)
    return (next_ritz, next_image, residual / divisor, squares)


def per_device(kernel, ritz_block, search_block, precond_diag):
    kernel_rows = kernel[:, 0, :]
    width = ritz_block.shape[1]

    def accumulate(segment):
        return jnp.dot(kernel_rows, segment, precision=highest, preferred_element_type=jnp.float32)

    part_ritz = accumulate(lax.all_gather(ritz_block, "blk", axis=0, tiled=True))
    part_search = accumulate(lax.all_gather(search_block, "blk", axis=0, tiled=True))
    joined = jnp.concatenate([part_ritz, part_search], 1)
    summed = lax.psum_scatter(joined, "col", scatter_dimension=0, tiled=True)
    images = summed[:, :width]
    search_images = summed[:, width:]
    vectors = ritz_block
    search = search_block
    norm_rows = []
    pending = None
    ritz_values = None
    for iteration in range(ITERS):
        if iteration > 0:
            partial_value = accumulate(lax.all_gather(search, "blk", axis=0, tiled=True))
            search_images = lax.psum_scatter(partial_value, "col", scatter_dimension=0, tiled=True)
        if iteration == 0:
            local_blocks = (
                inner(vectors, vectors),
                inner(vectors, search),
                inner(search, search),
                inner(vectors, images),
                inner(vectors, search_images),
                inner(search, search_images),
            )
            blocks = lax.psum(
                (
                    local_blocks[0],
                    local_blocks[1],
                    local_blocks[2],
                    local_blocks[3],
                    local_blocks[4],
                    local_blocks[5],
                ),
                ("blk", "col"),
            )
        else:
            gathered_sums = lax.psum(
                (
                    inner(vectors, search),
                    inner(search, search),
                    inner(vectors, search_images),
                    inner(search, search_images),
                    pending,
                ),
                ("blk", "col"),
            )
            identity = jnp.eye(width, dtype=jnp.float32)
            blocks = (
                identity,
                gathered_sums[0],
                gathered_sums[1],
                ritz_values,
                gathered_sums[2],
                gathered_sums[3],
            )
            norm_rows.append(jnp.sqrt(gathered_sums[4]))
        mixing, ritz_values = coefficients(blocks, width)
        vectors, images, search, squares = update(
            vectors, images, search, search_images, mixing, ritz_values, precond_diag
        )
        pending = squares
    norm_rows.append(jnp.sqrt(lax.psum(pending, ("blk", "col"))))
    return (vectors, search, jnp.stack(norm_rows, 0))


def solution(mesh):
    placed = (
        P("blk", "col", None),
        P(("blk", "col"), None),
        P(("blk", "col"), None),
        P(("blk", "col")),
    )
    return jax.shard_map(
        per_device,
        mesh=mesh,
        in_specs=placed,
        out_specs=(P(("blk", "col"), None), P(("blk", "col"), None), P()),
        check_vma=False,
    )
```

profile of v0, /device:TPU:0, one launch (start us, length us, event | category | flops | bytes accessed | tf_op | source)
XLA Modules:
  0.0 677.4 jit_solution(6095994089246775024)
XLA Ops:
  8.0 0.7 all-gather.4.cloned.1.call-update
  8.7 0.9 fusion.84
  9.6 0.9 fusion.85
  10.5 0.9 fusion.86
  11.4 55.8 %all-gather.6.cloned.1.call-done = f32[2048,128]{1,0:T(8,128)} async-done(((f32[64,128]{1,0:T(8,128)}), f32[2048,128]{1,0:T(8,128)}) %all-gather.6.cloned.1.call-update) | async-done | bytes 1048592 | tf_op jit(solution)/shard_map/all_gather | solution.py:80
  67.2 2.3 fusion.2
  69.5 0.9 convolution_bitcast_fusion.2
  70.4 0.9 convolution_bitcast_fusion.3
  71.3 51.4 %all-gather.4.cloned.1.call-done = f32[2048,128]{1,0:T(8,128)} async-done(((f32[64,128]{1,0:T(8,128)}), f32[2048,128]{1,0:T(8,128)}) %all-gather.4.cloned.1.call-update) | async-done | bytes 1048592 | tf_op jit(solution)/shard_map/all_gather | solution.py:79
  122.7 2.1 fusion.4
  124.8 0.9 convolution_bitcast_fusion.4
  126.3 133.0 %all-reduce.9.cloned.1.call-done = (f32[128,128]{0,1:T(8,128)}, f32[128,128]{0,1:T(8,128)}, f32[128,128]{1,0:T(8,128)}, f32[128,128]{1,0:T(8,128)}, f32[128,128]{1,0:T(8,128)}, /*index=5*/f32[128,128]{0,1:T(8,128)}) async-done(((f32[128,128]{0,1:T(8,128)}, f32[128,128]{0,1:T(8,128)}, f32[128,128]{1,0:T(8,128)}, f32[128,128]{1,0:T(8,128)}, f32[128,128]{1,0:T(8,128)}, /*index=5*/f32[128,128]{0,1:T(8,128)}), ...) | async-done | bytes 393232 | tf_op jit(solution)/shard_map/psum | solution.py:103
  259.3 0.9 pad_maximum_fusion
  260.3 0.7 copy-done.4
  261.2 11.7 %cholesky.172 = f32[128,128]{1,0:T(8,128)S(1)} custom-call(f32[128,128]{1,0:T(8,128)S(1)} %cholesky.258), custom_call_target="Cholesky" | custom-call | tf_op jit(solution)/shard_map/jit(cholesky)/cholesky | solution.py:38
  273.0 9.8 %custom-call.27 = f32[1,128,128]{1,2,0:T(8,128)S(1)} custom-call(f32[1,128,128]{2,1,0:T(8,128)S(1)} %get-tuple-element.79), custom_call_target="InvertDiagBlocksLowerTriangular" | custom-call | tf_op jit(solution)/shard_map/jit(cholesky)/cholesky | solution.py:38
  283.3 11.7 %cholesky.189 = f32[128,128]{1,0:T(8,128)S(1)} custom-call(f32[128,128]{1,0:T(8,128)S(1)} %convolution_subtract_fusion.5), custom_call_target="Cholesky" | custom-call | tf_op jit(solution)/shard_map/jit(cholesky)/cholesky | solution.py:38
  295.0 0.7 compare_reduce_fusion.4
  297.2 4.1 while.8
  297.9 1.4 bitcast_dynamic-update-slice_fusion.4
  299.9 1.4 bitcast_dynamic-update-slice_fusion.4
  301.3 19.7 %custom-call.29 = f32[2,128,128]{1,2,0:T(8,128)S(1)} custom-call(f32[2,128,128]{2,1,0:T(8,128)S(1)} %get-tuple-element.37), custom_call_target="InvertDiagBlocksLowerTriangular" | custom-call | tf_op jit(solution)/shard_map/triangular_solve/custom-call.5 | solution.py:42
  321.1 0.7 copy-done.10
  324.5 11.7 %cholesky.204 = f32[128,128]{1,0:T(8,128)S(1)} custom-call(f32[128,128]{1,0:T(8,128)S(1)} %fusion.41), custom_call_target="Cholesky" | custom-call | tf_op jit(solution)/shard_map/jit(cholesky)/cholesky | solution.py:46
  337.6 9.8 %custom-call.30 = f32[1,128,128]{1,2,0:T(8,128)S(1)} custom-call(f32[1,128,128]{2,1,0:T(8,128)S(1)} %fusion.31), custom_call_target="InvertDiagBlocksLowerTriangular" | custom-call | tf_op jit(solution)/shard_map/triangular_solve/custom-call.6 | solution.py:47
  350.3 1.3 gather_fusion
  351.6 0.9 multiply_reduce_fusion.1
  353.2 0.9 fusion.88
  354.1 0.9 fusion.89
  355.0 50.3 %all-gather.8.cloned.1.call-done = f32[2048,128]{1,0:T(8,128)} async-done(((f32[64,128]{1,0:T(8,128)}), f32[2048,128]{1,0:T(8,128)}) %all-gather.8.cloned.1.call-update) | async-done | bytes 1048592 | tf_op jit(solution)/shard_map/all_gather | solution.py:92
  405.3 2.1 fusion
  407.4 0.9 fusion.91
  408.4 0.9 fusion.90
  409.3 128.3 %all-reduce.7.cloned.1.call-done = (f32[128,128]{0,1:T(8,128)}, f32[128,128]{1,0:T(8,128)}, f32[128,128]{1,0:T(8,128)}, f32[128,128]{0,1:T(8,128)}) async-done(((f32[128,128]{0,1:T(8,128)}, f32[128,128]{1,0:T(8,128)}, f32[128,128]{1,0:T(8,128)}, f32[128,128]{0,1:T(8,128)}), (f32[128,128]{0,1:T(8,128)}, f32[128,128]{1,0:T(8,128)}, f32[128,128]{1,0:T(8,128)}, ...) | async-done | bytes 262160 | tf_op jit(solution)/shard_map/psum | solution.py:115
  537.6 0.8 pad_maximum_fusion.2
  538.5 0.7 copy-done.5
  539.5 11.7 %cholesky.217 = f32[128,128]{1,0:T(8,128)S(1)} custom-call(f32[128,128]{1,0:T(8,128)S(1)} %cholesky.261), custom_call_target="Cholesky" | custom-call | tf_op jit(solution)/shard_map/jit(cholesky)/cholesky | solution.py:38
  551.3 9.8 %custom-call.31 = f32[1,128,128]{1,2,0:T(8,128)S(1)} custom-call(f32[1,128,128]{2,1,0:T(8,128)S(1)} %get-tuple-element.75), custom_call_target="InvertDiagBlocksLowerTriangular" | custom-call | tf_op jit(solution)/shard_map/jit(cholesky)/cholesky | solution.py:38
  561.6 11.7 %cholesky.234 = f32[128,128]{1,0:T(8,128)S(1)} custom-call(f32[128,128]{1,0:T(8,128)S(1)} %convolution_subtract_fusion.2), custom_call_target="Cholesky" | custom-call | tf_op jit(solution)/shard_map/jit(cholesky)/cholesky | solution.py:38
  576.0 4.2 while.9
  576.7 1.4 bitcast_dynamic-update-slice_fusion.5
  578.7 1.4 bitcast_dynamic-update-slice_fusion.5
  580.1 19.7 %custom-call.33 = f32[2,128,128]{1,2,0:T(8,128)S(1)} custom-call(f32[2,128,128]{2,1,0:T(8,128)S(1)} %get-tuple-element.39), custom_call_target="InvertDiagBlocksLowerTriangular" | custom-call | tf_op jit(solution)/shard_map/triangular_solve/custom-call.5 | solution.py:42
  603.2 11.7 %cholesky.249 = f32[128,128]{1,0:T(8,128)S(1)} custom-call(f32[128,128]{1,0:T(8,128)S(1)} %fusion.38), custom_call_target="Cholesky" | custom-call | tf_op jit(solution)/shard_map/jit(cholesky)/cholesky | solution.py:46
  616.2 9.8 %custom-call.34 = f32[1,128,128]{1,2,0:T(8,128)S(1)} custom-call(f32[1,128,128]{2,1,0:T(8,128)S(1)} %fusion.32), custom_call_target="InvertDiagBlocksLowerTriangular" | custom-call | tf_op jit(solution)/shard_map/triangular_solve/custom-call.6 | solution.py:47
  628.6 1.2 gather_fusion.1
  630.1 0.8 multiply_reduce_fusion
  630.9 39.2 %all-reduce.1 = (f32[128]{0:T(128)S(1)}, f32[128]{0:T(128)S(1)}) all-reduce(f32[128]{0:T(128)S(1)} %get-tuple-element.82, f32[128]{0:T(128)S(1)} %get-tuple-element.80), channel_id=1, replica_groups=mesh['blk'=32,'col'=1] {'blk','col'}, use_global_device_ids=true, to_apply=%region_19.25 | all-reduce | flops 256 | bytes 2048 | tf_op jit(solution)/shard_map/psum | solution.py:140
  (119 shorter events, 22.4 us)
Async XLA Ops:
  7.2 1.5 copy-start.1
  7.2 60.0 %all-gather.6.cloned.1.call-start = ((), (), s32[]{:S(2)}) async-start(), calls=%async_computation.1 | async-start | bytes 1081344 | tf_op jit(solution)/shard_map/all_gather | solution.py:80
  7.9 114.8 %all-gather.4.cloned.1.call-start = ((), (), s32[]{:S(2)}) async-start(), calls=%async_computation | async-start | bytes 1081344 | tf_op jit(solution)/shard_map/all_gather | solution.py:79
  8.7 250.6 %all-reduce.9.cloned.1.call-start = ((), (), s32[]{:S(2)}) async-start(), calls=%async_computation.4 | async-start | bytes 786432 | tf_op jit(solution)/shard_map/psum | solution.py:103
  8.7 0.9 copy-start.2
  67.2 55.5 %copy-start = (f32[64,1,2048]{2,1,0:T(1,128)S(1)}, f32[64,1,2048]{2,1,0:T(1,128)}, u32[]{:S(2)}) copy-start(f32[64,1,2048]{2,1,0:T(1,128)} %param.12) | copy-start | bytes 1572868
  125.7 279.5 %all-gather.8.cloned.1.call-start = ((), (), s32[]{:S(2)}) async-start(), calls=%async_computation.2 | async-start | bytes 1081344 | tf_op jit(solution)/shard_map/all_gather | solution.py:92
  260.1 0.8 copy-start.4
  260.1 0.9 copy-start.8
  297.1 23.8 %copy-start.6 = (f32[128,128]{1,0:T(8,128)S(1)}, f32[128,128]{1,0:T(8,128)}, u32[]{:S(2)}) copy-start(f32[128,128]{1,0:T(8,128)} %get-tuple-element.66) | copy-start | bytes 196612
  321.0 0.8 copy-start.10
  348.2 0.8 copy-start.11
  350.3 1.3 copy-start.14
  352.5 0.8 copy-start.3
  352.5 185.1 %all-reduce.7.cloned.1.call-start = ((), (), s32[]{:S(2)}) async-start(), calls=%async_computation.3 | async-start | bytes 524288 | tf_op jit(solution)/shard_map/psum | solution.py:115
  538.4 0.8 copy-start.5
  538.4 0.9 copy-start.9
  599.8 0.8 copy-start.7
  626.9 0.8 copy-start.12
  630.1 0.8 copy-start.13
Sparse Core Ops, SparseCore 0:
  10.8 56.3 all-gather.5
  70.1 52.5 all-gather.3
  129.0 130.2 all-reduce.8
  352.6 52.6 all-gather.7
  411.0 126.5 all-reduce.6
where the time goes:
time: 681 us; the launch traced here: 677 us
  waiting for transfers between devices  420 us (62%)
  other arithmetic  156 us (23%)
  blocking collectives  39.2 us (6%)
  matrix products  27.7 us (4%)
  between operations  17.2 us (3%)
  local copies, waits for them, and re-layouts  15.6 us (2%)
    psum x1, waiting for transfers between devices, per_device(): lax.psum((local_blocks[0], local_blocks[1], local_blocks[2], local_blocks...  133 us
    psum x1, waiting for transfers between devices, per_device(): lax.psum((inner(vectors, search), inner(search, search), inner(vectors, s...  128 us
    another operation x13, other arithmetic, coefficients(): lower_metric = jnp.linalg.cholesky(metric)  68.6 us
    all_gather x1, waiting for transfers between devices, per_device(): lax.all_gather(search_block, 'blk', axis=0, tiled=True)  55.8 us
    all_gather x1, waiting for transfers between devices, per_device(): lax.all_gather(ritz_block, 'blk', axis=0, tiled=True)  51.4 us
    all_gather x1, waiting for transfers between devices, per_device(): lax.all_gather(search, 'blk', axis=0, tiled=True)  50.3 us
    another operation x5, other arithmetic, coefficients(): lax.linalg.triangular_solve(lower_metric, halfway, left_side=True, lower=...  39.4 us
    psum x1, blocking collectives, per_device(): norm_rows.append(jnp.sqrt(lax.psum(pending, ('blk', 'col'))))  39.2 us
  transfers between devices with their start and end apart: 5, of which 5 were waited for; matrix products, arithmetic and copies ran while one was open for 1% of the time, Pallas kernels for 0%

commit v1 on v0

v1 whole, which is shorter than its diff:
```python
import jax
import jax.numpy as jnp
from jax import lax
from jax.experimental import pallas as pl
from jax.experimental.pallas import tpu as pltpu
from jax.sharding import PartitionSpec as P

ITERS = 2
F32 = jnp.float32
highest = lax.Precision.HIGHEST
CHUNK = 512


def params():
    return pltpu.CompilerParams(vmem_limit_bytes=56 << 20)


def mm(a, b, ca=1, cb=0):
    return lax.dot_general(
        a, b, (((ca,), (cb,)), ((), ())), precision=highest, preferred_element_type=F32
    )


def inverse_factor(matrix):
    n = matrix.shape[0]
    count = n // 8
    lane = lax.broadcasted_iota(jnp.int32, (8, n), 1)
    sub = lax.broadcasted_iota(jnp.int32, (8, n), 0)
    a = [matrix[8 * v : 8 * v + 8, :] for v in range(count)]

    def wide(x):
        return jnp.broadcast_to(x, (8, n))

    for k in range(0, n, 2):
        r, s = divmod(k, 8)
        row0 = wide(a[r][s : s + 1, :])
        row1 = wide(a[r][s + 1 : s + 2, :])
        p00 = wide(a[r][s : s + 1, k : k + 1])
        p01 = wide(a[r][s : s + 1, k + 1 : k + 2])
        p11 = wide(a[r][s + 1 : s + 2, k + 1 : k + 2])
        scale = 1.0 / (p00 * p11 - p01 * p01)
        q00 = p11 * scale
        q01 = -p01 * scale
        q11 = p00 * scale
        at0 = lane == k
        at1 = lane == k + 1
        g0 = jnp.where(at0, q00, jnp.where(at1, q01, q00 * row0 + q01 * row1))
        g1 = jnp.where(at0, q01, jnp.where(at1, q11, q01 * row0 + q11 * row1))
        inside = at0 | at1
        for v in range(r, count):
            if v == r and s == 6:
                continue
            c0 = wide(a[v][:, k : k + 1])
            c1 = wide(a[v][:, k + 1 : k + 2])
            new = jnp.where(inside, 0.0, a[v]) - c0 * g0 - c1 * g1
            a[v] = jnp.where(sub > s + 1, new, a[v]) if v == r else new
    even = (sub % 2) == 0
    rows = []
    for v in range(count):
        here = sub + 8 * v
        across = jnp.where(even, here + 1, here - 1)
        diag = wide(jnp.sum(jnp.where(lane == here, a[v], 0.0), axis=1, keepdims=True))
        off = wide(jnp.sum(jnp.where(lane == across, a[v], 0.0), axis=1, keepdims=True))
        left = jnp.where(lane < (sub // 2) * 2 + 8 * v, a[v], 0.0)
        unit = jnp.where(lane == here, 1.0, left)
        above = pltpu.roll(unit, 1, 0)
        ratio = off / pltpu.roll(diag, 1, 0)
        norm = lax.rsqrt(jnp.where(even, diag, diag - off * ratio))
        rows.append(jnp.where(even, unit, unit - ratio * above) * norm)
    return jnp.concatenate(rows, 0)


def device_of(me, dz, k, dc, rings):
    z = lax.rem(me // 8 + (dz + rings), rings)
    low = lax.rem(me, 8)
    return z * 8 + jnp.bitwise_xor(low, 2 * k + dc)


def layout_of(rings):
    half = rings // 2
    out = []
    for dc in (0, 1):
        out += [(0, (0, 1), dc), (0, (2, 3), dc)]
        for t in range(1, half):
            out += [(-t, (0, 1), dc), (-t, (2, 3), dc), (t, (0, 1), dc), (t, (2, 3), dc)]
        out += [(-half, (0, 1), dc), (half, (2, 3), dc)]
    return out


def gather(block, n):
    rings = n // 8
    half = rings // 2

    def swap(x, m):
        return lax.ppermute(x, "blk", [(i, i ^ m) for i in range(n)])

    def turn(x, d):
        return lax.ppermute(x, "blk", [(i, ((i // 8 + d) % rings) * 8 + i % 8) for i in range(n)])

    by_x, by_y, by_xy = swap(block, 2), swap(block, 4), swap(block, 6)
    first = jnp.concatenate([block, by_x], 0)
    second = jnp.concatenate([by_y, by_xy], 0)
    near = [first, second]
    up_a, up_b, down_a, down_b = first, second, first, second
    for t in range(1, half):
        up_a, down_b = turn(up_a, 1), turn(down_b, -1)
        up_b, down_a = turn(up_b, 1), turn(down_a, -1)
        near += [up_a, up_b, down_a, down_b]
    near += [turn(up_a, 1), turn(down_b, -1)]
    return near + [swap(x, 1) for x in near]


def assemble(me, pieces, rows, rings, place):
    for piece, (dz, ks, dc) in zip(pieces, layout_of(rings)):
        for slot, k in enumerate(ks):
            place(piece, slot, device_of(me, dz, k, dc, rings))


def first_product(rings, rows, me_ref, kernel_ref, *refs):
    pieces, (y_ref, ky_ref, diag_ref, table) = refs[:-4], refs[-4:]
    width = y_ref.shape[1] // 2
    step = 2 * rows + 8

    def place(piece, slot, device):
        base = slot * step
        at = pl.ds(pl.multiple_of(device * rows, rows), rows)
        y_ref[at, :width] = piece[base : base + rows, :]
        y_ref[at, width:] = piece[base + rows : base + 2 * rows, :]
        table[pl.ds(device, 1), :] = piece[base + 2 * rows : base + 2 * rows + 1, :]

    table[...] = jnp.zeros_like(table)
    assemble(me_ref[0], pieces, rows, rings, place)
    diag_ref[...] = table[...].T
    result = mm(kernel_ref[...], y_ref[...])
    ky_ref[:rows, :] = result[:, :width]
    ky_ref[rows:, :] = result[:, width:]


def metric_factor(y_ref, out_ref):
    total, double = y_ref.shape
    width = double // 2
    chunk = min(CHUNK, total)

    def add(i, acc):
        part = y_ref[pl.ds(pl.multiple_of(i * chunk, chunk), chunk), :]
        return acc + mm(part, part, 0, 0)

    metric = lax.fori_loop(0, total // chunk, add, jnp.zeros((double, double), F32))
    upper = inverse_factor(metric[:width, :width])
    cross = mm(upper, metric[:width, width:])
    lower = inverse_factor(metric[width:, width:] - mm(cross, cross, 0, 0))
    out_ref[:width, :width] = upper
    out_ref[:width, width:] = jnp.zeros((width, width), F32)
    out_ref[width:, :width] = -mm(lower, mm(cross, upper, 0, 0))
    out_ref[width:, width:] = lower


def divided(residual, diag, values):
    eye = lax.broadcasted_iota(jnp.int32, values.shape, 0) == lax.broadcasted_iota(
        jnp.int32, values.shape, 1
    )
    level = jnp.sum(jnp.where(eye, values, 0.0), axis=0, keepdims=True)
    return residual / jnp.maximum(jnp.abs(diag - level), 1.0)


def first_step(y_ref, ky_ref, factor_ref, diag_ref, y2_ref, kx_ref, small_ref, norm_ref):
    total, double = y_ref.shape
    width = double // 2
    rows = diag_ref.shape[0]
    chunk = min(CHUNK, total)

    def add(i, acc):
        at = pl.ds(pl.multiple_of(i * chunk, chunk), chunk)
        return acc + mm(y_ref[at, :], ky_ref[at, :], 0, 0)

    g = lax.fori_loop(0, total // chunk, add, jnp.zeros((double, double), F32))
    factor = factor_ref[...]
    head = g[:width, :]
    side = jnp.concatenate([g[:width, :width], g[:width, width:].T], 0)
    whole = jnp.concatenate(
        [head, jnp.concatenate([g[:width, width:].T, g[width:, width:]], 1)], 0
    )
    z = mm(factor, side)
    small = inverse_factor(mm(z, z, 0, 0))
    mixing = mm(factor, mm(z, small, 1, 1), 0, 0)
    values = mm(mixing, mm(whole, mixing), 0, 0)
    both = jnp.concatenate([mixing, mm(mixing, values)], 1)
    small_ref[...] = values

    def update(i, acc):
        at = pl.ds(pl.multiple_of(i * chunk, chunk), chunk)
        pair = mm(y_ref[at, :], both)
        image = mm(ky_ref[at, :], mixing)
        y2_ref[at, :width] = pair[:, :width]
        kx_ref[at, :] = image
        residual = image - pair[:, width:]
        y2_ref[at, width:] = residual
        return acc + jnp.sum(residual * residual, axis=0, keepdims=True)

    squares = lax.fori_loop(0, total // chunk, update, jnp.zeros((1, width), F32))
    norm_ref[...] = jnp.sqrt(squares)
    for b in range(total // rows):
        at = pl.ds(b * rows, rows)
        y2_ref[at, width:] = divided(y2_ref[at, width:], diag_ref[:rows, b : b + 1], values)


def with_product(rings, rows, me_ref, kernel_ref, y_ref, factor_ref, diag_ref, *refs):
    pieces = refs[:-6]
    y2_ref, kx_ref, small_ref, norm_ref, kw_ref, ky_ref = refs[-6:]
    width = kx_ref.shape[1]

    def place(piece, slot, device):
        base = slot * 2 * rows
        at = pl.ds(pl.multiple_of(device * rows, rows), rows)
        ky_ref[at, :width] = piece[base : base + rows, :]
        ky_ref[at, width:] = piece[base + rows : base + 2 * rows, :]

    assemble(me_ref[0], pieces, rows, rings, place)
    first_step(
        y_ref, ky_ref, factor_ref, diag_ref.at[:rows, :], y2_ref, kx_ref, small_ref, norm_ref
    )
    kw_ref[...] = mm(kernel_ref[...], y2_ref[:, width:])


def second_factor(y2_ref, gram_ref, factor_ref):
    total, double = y2_ref.shape
    width = double // 2
    chunk = min(CHUNK, total)

    def add(i, acc):
        at = pl.ds(pl.multiple_of(i * chunk, chunk), chunk)
        return acc + mm(y2_ref[at, :], y2_ref[at, width:], 0, 0)

    gram = lax.fori_loop(0, total // chunk, add, jnp.zeros((double, width), F32))
    cross = gram[:width]
    gram_ref[...] = cross
    factor_ref[...] = inverse_factor(gram[width:] - mm(cross, cross, 0, 0))


def second_step(
    y2_ref, image_ref, small_ref, cross_ref, factor_ref, own_y2, own_image, own_diag, outs
):
    ritz_ref, search_ref, norm_ref = outs
    total, double = y2_ref.shape
    width = double // 2
    chunk = min(CHUNK, total)

    def add(i, acc):
        at = pl.ds(pl.multiple_of(i * chunk, chunk), chunk)
        return acc + mm(y2_ref[at, :], image_ref[at, width:], 0, 0)

    g = lax.fori_loop(0, total // chunk, add, jnp.zeros((double, width), F32))
    values, cross, factor = small_ref[...], cross_ref[...], factor_ref[...]
    f_t = g[:width].T
    z = mm(factor, f_t - mm(cross, values, 0, 0))
    small = inverse_factor(mm(values, values, 0, 0) + mm(z, z, 0, 0))
    lower = mm(factor, mm(z, small, 1, 1), 0, 0)
    upper = mm(values, small, 1, 1) - mm(cross, lower)
    mixing = jnp.concatenate([upper, lower], 0)
    whole = jnp.concatenate(
        [jnp.concatenate([values, g[:width]], 1), jnp.concatenate([f_t, g[width:]], 1)], 0
    )
    values2 = mm(mixing, mm(whole, mixing), 0, 0)
    turned = mm(mixing, values2)

    def update(i, acc):
        at = pl.ds(pl.multiple_of(i * chunk, chunk), chunk)
        residual = mm(image_ref[at, :], mixing) - mm(y2_ref[at, :], turned)
        return acc + jnp.sum(residual * residual, axis=0, keepdims=True)

    squares = lax.fori_loop(0, total // chunk, update, jnp.zeros((1, width), F32))
    norm_ref[...] = jnp.sqrt(squares)
    own = own_y2()
    ritz = mm(own, mixing)
    ritz_ref[...] = ritz
    residual = mm(own_image(), mixing) - mm(ritz, values2)
    search_ref[...] = divided(residual, own_diag(), values2)


def last_step(rings, rows, me_ref, y2_ref, kx_ref, small_ref, cross_ref, factor_ref, own_ref, *refs):
    pieces = refs[:-4]
    ritz_ref, search_ref, norm_ref, image_ref = refs[-4:]
    width = kx_ref.shape[1]
    me = me_ref[0]

    def place(piece, slot, device):
        at = pl.ds(pl.multiple_of(device * rows, rows), rows)
        image_ref[at, width:] = piece[slot * rows : (slot + 1) * rows, :]

    assemble(me, pieces, rows, rings, place)
    image_ref[:, :width] = kx_ref[...]
    mine = pl.ds(pl.multiple_of(me * rows, rows), rows)
    second_step(
        y2_ref,
        image_ref,
        small_ref,
        cross_ref,
        factor_ref,
        lambda: y2_ref[mine, :],
        lambda: image_ref[mine, :],
        lambda: own_ref[...],
        (ritz_ref, search_ref, norm_ref),
    )


def general_last(y2_ref, image_ref, small_ref, cross_ref, factor_ref, own_y2, own_image, own_diag, *outs):
    second_step(
        y2_ref,
        image_ref,
        small_ref,
        cross_ref,
        factor_ref,
        lambda: own_y2[...],
        lambda: own_image[...],
        lambda: own_diag[...],
        outs,
    )


def shape(*dims):
    return jax.ShapeDtypeStruct(dims, F32)


VMEM = pl.BlockSpec(memory_space=pltpu.VMEM)
SMEM = pl.BlockSpec(memory_space=pltpu.SMEM)


def ringed(n, kernel, ritz, search, diag):
    rows, width = ritz.shape
    rings = n // 8
    total = n * rows
    me = lax.axis_index("blk").astype(jnp.int32).reshape(1)
    lanes = max(128, -(-rows // 128) * 128)
    extra = jnp.zeros((8, width), F32).at[0, :rows].set(diag)
    sent = gather(jnp.concatenate([ritz, search, extra], 0), n)
    y, ky_own, diag_table = pl.pallas_call(
        lambda *refs: first_product(rings, rows, *refs),
        out_shape=(shape(total, 2 * width), shape(2 * rows, width), shape(width, max(n, 128))),
        in_specs=[SMEM, VMEM] + [VMEM] * len(sent),
        out_specs=(VMEM, VMEM, VMEM),
        scratch_shapes=[pltpu.VMEM((max(n, 128), width), F32)],
        compiler_params=params(),
        name="first_product",
    )(me, kernel, *sent)
    images = gather(ky_own, n)
    factor = pl.pallas_call(
        metric_factor,
        out_shape=shape(2 * width, 2 * width),
        in_specs=[VMEM],
        out_specs=VMEM,
        compiler_params=params(),
        name="metric_factor",
    )(y)
    y2, kx, values, norm1, kw_own = pl.pallas_call(
        lambda *refs: with_product(rings, rows, *refs),
        out_shape=(
            shape(total, 2 * width),
            shape(total, width),
            shape(width, width),
            shape(1, width),
            shape(rows, width),
        ),
        in_specs=[SMEM] + [VMEM] * (4 + len(images)),
        out_specs=(VMEM,) * 5,
        scratch_shapes=[pltpu.VMEM((total, 2 * width), F32)],
        compiler_params=params(),
        name="first_step",
    )(me, kernel, y, factor, diag_table, *images)
    images2 = gather(kw_own, n)
    cross, factor2 = pl.pallas_call(
        second_factor,
        out_shape=(shape(width, width), shape(width, width)),
        in_specs=[VMEM],
        out_specs=(VMEM, VMEM),
        compiler_params=params(),
        name="second_factor",
    )(y2)
    new_ritz, correction, norm2 = pl.pallas_call(
        lambda *refs: last_step(rings, rows, *refs),
        out_shape=(shape(rows, width), shape(rows, width), shape(1, width)),
        in_specs=[SMEM] + [VMEM] * (6 + len(images2)),
        out_specs=(VMEM,) * 3,
        scratch_shapes=[pltpu.VMEM((total, 2 * width), F32)],
        compiler_params=params(),
        name="last_step",
    )(me, y2, kx, values, cross, factor2, diag[:, None], *images2)
    return new_ritz, correction, jnp.concatenate([norm1, norm2], 0)


def general(n, cols, kernel, ritz, search, diag):
    rows, width = ritz.shape
    axes = ("blk", "col")
    total = n * cols * rows
    q = lax.axis_index("col")

    def product(part):
        whole = lax.psum_scatter(mm(kernel, part), "col", scatter_dimension=0, tiled=True)
        return whole

    own = jnp.concatenate([ritz, search], 1)
    part = lax.all_gather(own, "blk", axis=0, tiled=True)
    y = lax.all_gather(own, axes, axis=0, tiled=True)
    ky = lax.all_gather(product(part), axes, axis=0, tiled=True)
    table = lax.all_gather(diag, axes, axis=0, tiled=True).reshape(n * cols, rows).T
    factor = pl.pallas_call(
        metric_factor,
        out_shape=shape(2 * width, 2 * width),
        in_specs=[VMEM],
        out_specs=VMEM,
        compiler_params=params(),
        name="metric_factor",
    )(y)
    y2, kx, values, norm1 = pl.pallas_call(
        first_step,
        out_shape=(shape(total, 2 * width), shape(total, width), shape(width, width), shape(1, width)),
        in_specs=[VMEM] * 4,
        out_specs=(VMEM,) * 4,
        compiler_params=params(),
        name="first_step",
    )(y, ky, factor, table)
    held = y2[:, width:].reshape(n, cols, rows, width)
    part2 = lax.dynamic_index_in_dim(held, q, 1, keepdims=False).reshape(n * rows, width)
    kw = lax.all_gather(product(part2), axes, axis=0, tiled=True)
    cross, factor2 = pl.pallas_call(
        second_factor,
        out_shape=(shape(width, width), shape(width, width)),
        in_specs=[VMEM],
        out_specs=(VMEM, VMEM),
        compiler_params=params(),
        name="second_factor",
    )(y2)
    image = jnp.concatenate([kx, kw], 1)
    at = (lax.axis_index("blk") * cols + q) * rows
    new_ritz, correction, norm2 = pl.pallas_call(
        general_last,
        out_shape=(shape(rows, width), shape(rows, width), shape(1, width)),
        in_specs=[VMEM] * 8,
        out_specs=(VMEM,) * 3,
        compiler_params=params(),
        name="last_step",
    )(
        y2,
        image,
        values,
        cross,
        factor2,
        lax.dynamic_slice_in_dim(y2, at, rows, 0),
        lax.dynamic_slice_in_dim(image, at, rows, 0),
        diag[:, None],
    )
    return new_ritz, correction, jnp.concatenate([norm1, norm2], 0)


def solution(mesh):
    n, cols = mesh.shape["blk"], mesh.shape["col"]
    placed = (
        P("blk", "col", None),
        P(("blk", "col"), None),
        P(("blk", "col"), None),
        P(("blk", "col")),
    )

    def per_device(kernel, ritz_block, search_block, precond_diag):
        rows = kernel[:, 0, :]
        if cols == 1 and n % 16 == 0 and ritz_block.shape[0] <= ritz_block.shape[1]:
            return ringed(n, rows, ritz_block, search_block, precond_diag)
        return general(n, cols, rows, ritz_block, search_block, precond_diag)

    return jax.shard_map(
        per_device,
        mesh=mesh,
        in_specs=placed,
        out_specs=(P(("blk", "col"), None), P(("blk", "col"), None), P()),
        check_vma=False,
    )
```

time: 681 us -> 179 us (0.26)
  waiting for transfers between devices: 420 us -> 39.9 us
  other arithmetic: 156 us -> 2.82 us
  Pallas kernels: 0 us -> 89.1 us
  blocking collectives: 39.2 us -> 0 us
  starting transfers between devices: 1.07 us -> 37.7 us
  matrix products: 27.7 us -> 0 us
  between operations: 17.2 us -> 1.35 us
  local copies, waits for them, and re-layouts: 15.6 us -> 7.18 us
    psum x2 -> x0, waiting for transfers between devices: 261 us -> none  [the longest x1 133 us: per_device(): lax.psum((local_blocks[0], local_blocks[1], local_blocks[2], local_blocks...]
    all_gather x3 -> x0, waiting for transfers between devices: 157 us -> none  [the longest x1 55.8 us: per_device(): lax.all_gather(search_block, 'blk', axis=0, tiled=True)]
    another operation x29 -> x0, other arithmetic: 154 us -> none  [the longest x13 68.6 us: coefficients(): lower_metric = jnp.linalg.cholesky(metric)]
    pallas_call x0 -> x5, Pallas kernels: none -> 89.1 us  [the longest x1 24.4 us: ringed(): pl.pallas_call(metric_factor, out_shape=shape(2 * width, 2 * width), in_s...]
    ppermute x0 -> x51, waiting for transfers between devices: none -> 39.9 us  [the longest x18 30.7 us: turn(): lax.ppermute(x, 'blk', [(i, (i // 8 + d) % rings * 8 + i % 8) for i in ra...]
    psum x1 -> x0, blocking collectives: 39.2 us -> none  [per_device(): norm_rows.append(jnp.sqrt(lax.psum(pending, ('blk', 'col'))))]
    ppermute x0 -> x51, starting transfers between devices: none -> 37.7 us  [the longest x18 22.3 us: turn(): lax.ppermute(x, 'blk', [(i, (i // 8 + d) % rings * 8 + i % 8) for i in ra...]
    dot_general x31 -> x0, matrix products: 23 us -> none  [the longest x10 9.08 us: inner(): lax.dot_general(former, latter, (((0,), (0,)), ((), ())), precision=highe...]
  transfers between devices with their start and end apart: 5 -> 51, of which waited for: 5 -> 16; matrix products, arithmetic and copies ran while one was open for 1% -> 3% of each run, Pallas kernels for 0% -> 22%
where the time goes in v1:
time: 179 us; the launch traced here: 178 us
  Pallas kernels  89.1 us (50%)
  waiting for transfers between devices  39.9 us (22%)
  starting transfers between devices  37.7 us (21%)
  local copies, waits for them, and re-layouts  7.18 us (4%)
  other arithmetic  2.82 us (2%)
    ppermute x18, waiting for transfers between devices, turn(): lax.ppermute(x, 'blk', [(i, (i // 8 + d) % rings * 8 + i % 8) for i in ra...  30.7 us
    pallas_call x1, Pallas kernels, ringed(): pl.pallas_call(metric_factor, out_shape=shape(2 * width, 2 * width), in_s...  24.4 us
    pallas_call x1, Pallas kernels, ringed(): pl.pallas_call(lambda *refs: with_product(rings, rows, *refs), out_shape=...  23.8 us
    ppermute x18, starting transfers between devices, turn(): lax.ppermute(x, 'blk', [(i, (i // 8 + d) % rings * 8 + i % 8) for i in ra...  22.3 us
    pallas_call x1, Pallas kernels, ringed(): pl.pallas_call(lambda *refs: last_step(rings, rows, *refs), out_shape=(sh...  22.1 us
    ppermute x33, starting transfers between devices, swap(): return lax.ppermute(x, 'blk', [(i, i ^ m) for i in range(n)])  15.5 us
    pallas_call x1, Pallas kernels, ringed(): pl.pallas_call(second_factor, out_shape=(shape(width, width), shape(width...  14.3 us
    ppermute x33, waiting for transfers between devices, swap(): return lax.ppermute(x, 'blk', [(i, i ^ m) for i in range(n)])  9.18 us
  transfers between devices with their start and end apart: 51, of which 16 were waited for; matrix products, arithmetic and copies ran while one was open for 3% of the time, Pallas kernels for 22%

profile of v1, /device:TPU:0, one launch (start us, length us, event | category | flops | bytes accessed | tf_op | source)
XLA Modules:
  0.0 178.0 jit_solution(1020204614695109590)
XLA Ops:
  0.6 0.7 scatter.4
  1.3 0.8 pad_maximum_fusion.1
  2.1 3.0 %collective-permute-start.1 = (f32[136,128]{1,0:T(8,128)S(1)}, f32[136,128]{1,0:T(8,128)S(1)}, u32[]{:S(2)}, u32[]{:S(2)}) collective-permute-start(f32[136,128]{1,0:T(8,128)S(1)} %pad_maximum_fusion.1), channel_id=1, source_target_pairs={{0,4},{1,5},{2,6},{3,7},{4,0},{5,1},{6,2},{7,3},{8,12},{9,13},{10,... | collective-permute-start | bytes 208904 | tf_op jit(solution)/shard_map/ppermute | solution.py:95
  5.1 1.4 collective-permute-start.2
  6.6 1.3 collective-permute-done.1
  7.9 2.9 %collective-permute-done.2 = f32[136,128]{1,0:T(8,128)S(1)} collective-permute-done((f32[136,128]{1,0:T(8,128)S(1)}, f32[136,128]{1,0:T(8,128)S(1)}, u32[]{:S(2)}, u32[]{:S(2)}) %collective-permute-start.2) | collective-permute-done | bytes 69664 | tf_op jit(solution)/shard_map/ppermute | solution.py:95
  10.8 3.7 %collective-permute-start.6 = (f32[272,128]{1,0:T(8,128)S(1)}, f32[272,128]{1,0:T(8,128)S(1)}, u32[]{:S(2)}, u32[]{:S(2)}) collective-permute-start(f32[272,128]{1,0:T(8,128)S(1)} %constant_dynamic-update-slice_fusion.refs_3_), channel_id=1, source_target_pairs={{0,24},{1,25},{2,26},{3,27},{4,28},{5,29},{6,30},{7,31},{8,0},{9,1... | collective-permute-start | bytes 417800 | tf_op jit(solution)/shard_map/ppermute | solution.py:98
  14.5 0.8 pad_maximum_fusion.refs_2_
  15.4 3.9 %collective-permute-start.5 = (f32[272,128]{1,0:T(8,128)S(1)}, f32[272,128]{1,0:T(8,128)S(1)}, u32[]{:S(2)}, u32[]{:S(2)}) collective-permute-start(f32[272,128]{1,0:T(8,128)S(1)} %pad_maximum_fusion.refs_2_), channel_id=1, source_target_pairs={{0,24},{1,25},{2,26},{3,27},{4,28},{5,29},{6,30},{7,31},{8,0},{9,1... | collective-permute-start | bytes 417800 | tf_op jit(solution)/shard_map/ppermute | solution.py:98
  19.5 3.1 %collective-permute-done.4.refs_5_ = f32[272,128]{1,0:T(8,128)S(1)} collective-permute-done((f32[272,128]{1,0:T(8,128)S(1)}, f32[272,128]{1,0:T(8,128)S(1)}, u32[]{:S(2)}, u32[]{:S(2)}) %collective-permute-start.4) | collective-permute-done | bytes 139296 | tf_op jit(solution)/shard_map/ppermute | solution.py:98
  22.9 2.7 %collective-permute-done.3.refs_4_ = f32[272,128]{1,0:T(8,128)S(1)} collective-permute-done((f32[272,128]{1,0:T(8,128)S(1)}, f32[272,128]{1,0:T(8,128)S(1)}, u32[]{:S(2)}, u32[]{:S(2)}) %collective-permute-start.3) | collective-permute-done | bytes 139296 | tf_op jit(solution)/shard_map/ppermute | solution.py:98
  25.7 1.0 collective-permute-done.5.refs_6_
  26.7 0.5 collective-permute-start.12
  27.2 2.2 %collective-permute-done.8.refs_9_ = f32[272,128]{1,0:T(8,128)S(1)} collective-permute-done((f32[272,128]{1,0:T(8,128)S(1)}, f32[272,128]{1,0:T(8,128)S(1)}, u32[]{:S(2)}, u32[]{:S(2)}) %collective-permute-start.8) | collective-permute-done | bytes 139296 | tf_op jit(solution)/shard_map/ppermute | solution.py:98
  29.9 3.5 %collective-permute-done.7.refs_8_ = f32[272,128]{1,0:T(8,128)S(1)} collective-permute-done((f32[272,128]{1,0:T(8,128)S(1)}, f32[272,128]{1,0:T(8,128)S(1)}, u32[]{:S(2)}, u32[]{:S(2)}) %collective-permute-start.7) | collective-permute-done | bytes 139296 | tf_op jit(solution)/shard_map/ppermute | solution.py:98
  33.5 2.1 %copy.10 = f32[64,1,2048]{2,0,1:T(8,128)} copy(f32[64,1,2048]{2,1,0:T(1,128)} %param.6) | data formatting | bytes 1048576
  36.4 4.5 %first_product.1 = (f32[2048,256]{1,0:T(8,128)}, f32[128,128]{1,0:T(8,128)}, f32[128,128]{1,0:T(8,128)}) custom-call(s32[1]{0:T(128)} %bitcast.refs_0_, f32[64,2048]{1,0:T(8,128)} %bitcast.6, f32[272,128]{1,0:T(8,128)} %copy-done, f32[272,128]{1,0:T(8,128)} %copy-done.1, f32[272,128]{1,0:T(8,128)} %copy-done.8, f32[272,128]{1,0:T(8,128)} %copy-done.7, ...), custom_call_target="tpu_custom_call" | custom-call | tf_op jit(solution)/shard_map/first_product/pallas_call | solution.py:336
  40.9 0.6 collective-permute-start.18
  41.4 2.0 %collective-permute-start.19 = (f32[128,128]{1,0:T(8,128)}, f32[128,128]{1,0:T(8,128)S(1)}, u32[]{:S(2)}, u32[]{:S(2)}) collective-permute-start(f32[128,128]{1,0:T(8,128)} %get-tuple-element.30), channel_id=1, source_target_pairs={{0,6},{1,7},{2,4},{3,5},{4,2},{5,3},{6,0},{7,1},{8,14},{9,15},{10,... | collective-permute-start | bytes 196616 | tf_op jit(solution)/shard_map/ppermute | solution.py:95
  43.4 0.9 collective-permute-start.17
  44.3 0.9 constant_dynamic-update-slice_fusion.3
  45.2 1.1 collective-permute-done.18
  46.4 1.1 collective-permute-done.19
  47.5 0.9 collective-permute-start.23
  48.4 1.2 collective-permute-start.21
  49.6 3.8 %collective-permute-start.22 = (f32[256,128]{1,0:T(8,128)S(1)}, f32[256,128]{1,0:T(8,128)S(1)}, u32[]{:S(2)}, u32[]{:S(2)}) collective-permute-start(f32[256,128]{1,0:T(8,128)S(1)} %constant_dynamic-update-slice_fusion.2.refs_5_), channel_id=1, source_target_pairs={{0,24},{1,25},{2,26},{3,27},{4,28},{5,29},{6,30},{7,31},{8,0},{9,1... | collective-permute-start | bytes 393224 | tf_op jit(solution)/shard_map/ppermute | solution.py:98
  53.4 5.1 %collective-permute-done.23.refs_10_ = f32[256,128]{1,0:T(8,128)S(1)} collective-permute-done((f32[256,128]{1,0:T(8,128)S(1)}, f32[256,128]{1,0:T(8,128)S(1)}, u32[]{:S(2)}, u32[]{:S(2)}) %collective-permute-start.23) | collective-permute-done | bytes 131104 | tf_op jit(solution)/shard_map/ppermute | solution.py:98
  58.6 0.5 collective-permute-start.29
  59.1 1.7 collective-permute-start.24
  60.9 0.5 collective-permute-start.28
  61.4 5.8 %collective-permute-done.25.refs_12_ = f32[256,128]{1,0:T(8,128)S(1)} collective-permute-done((f32[256,128]{1,0:T(8,128)S(1)}, f32[256,128]{1,0:T(8,128)S(1)}, u32[]{:S(2)}, u32[]{:S(2)}) %collective-permute-start.25) | collective-permute-done | bytes 131104 | tf_op jit(solution)/shard_map/ppermute | solution.py:98
  67.3 0.5 collective-permute-start.33
  67.8 24.4 %metric_factor.1.refs_3_ = f32[256,256]{1,0:T(8,128)} custom-call(f32[2048,256]{1,0:T(8,128)} %get-tuple-element.28.y_ref.refs_2_), custom_call_target="tpu_custom_call" | custom-call | tf_op jit(solution)/shard_map/metric_factor/pallas_call | solution.py:346
  93.1 23.8 %first_step.1 = (f32[2048,256]{1,0:T(8,128)}, f32[2048,128]{1,0:T(8,128)}, f32[128,128]{1,0:T(8,128)}, f32[1,128]{1,0:T(1,128)}, f32[64,128]{1,0:T(8,128)}) custom-call(s32[1]{0:T(128)} %bitcast.refs_0_, f32[64,2048]{1,0:T(8,128)} %bitcast.7, f32[2048,256]{1,0:T(8,128)} %get-tuple-element.28.y_ref.refs_2_, f32[256,256]{1,0:T(8,128)} %metric_factor.1.refs_3_, ...), custom_call_target="tpu_custom_call" | custom-call | tf_op jit(solution)/shard_map/first_step/pallas_call | solution.py:354
  116.9 1.7 collective-permute-start.35
  118.8 0.8 constant_dynamic-update-slice_fusion.7
  119.6 1.6 collective-permute-start.34
  121.2 2.7 %collective-permute-done.36 = f32[64,128]{1,0:T(8,128)S(1)} collective-permute-done((f32[64,128]{1,0:T(8,128)}, f32[64,128]{1,0:T(8,128)S(1)}, u32[]{:S(2)}, u32[]{:S(2)}) %collective-permute-start.36) | collective-permute-done | bytes 32800 | tf_op jit(solution)/shard_map/ppermute | solution.py:95
  124.0 1.9 %collective-permute-start.38 = (f32[128,128]{1,0:T(8,128)S(1)}, f32[128,128]{1,0:T(8,128)S(1)}, u32[]{:S(2)}, u32[]{:S(2)}) collective-permute-start(f32[128,128]{1,0:T(8,128)S(1)} %constant_dynamic-update-slice_fusion.8.refs_8_), channel_id=1, source_target_pairs={{0,8},{1,9},{2,10},{3,11},{4,12},{5,13},{6,14},{7,15},{8,16},{9,17... | collective-permute-start | bytes 196616 | tf_op jit(solution)/shard_map/ppermute | solution.py:98
  126.0 3.8 %collective-permute-start.39 = (f32[128,128]{1,0:T(8,128)S(1)}, f32[128,128]{1,0:T(8,128)S(1)}, u32[]{:S(2)}, u32[]{:S(2)}) collective-permute-start(f32[128,128]{1,0:T(8,128)S(1)} %constant_dynamic-update-slice_fusion.6.refs_7_), channel_id=1, source_target_pairs={{0,24},{1,25},{2,26},{3,27},{4,28},{5,29},{6,30},{7,31},{8,0},{9,1... | collective-permute-start | bytes 196616 | tf_op jit(solution)/shard_map/ppermute | solution.py:98
  130.2 0.7 collective-permute-start.42
  130.8 1.9 %collective-permute-done.37.refs_9_ = f32[128,128]{1,0:T(8,128)S(1)} collective-permute-done((f32[128,128]{1,0:T(8,128)S(1)}, f32[128,128]{1,0:T(8,128)S(1)}, u32[]{:S(2)}, u32[]{:S(2)}) %collective-permute-start.37) | collective-permute-done | bytes 65568 | tf_op jit(solution)/shard_map/ppermute | solution.py:98
  133.4 1.0 collective-permute-done.42.refs_14_
  135.0 3.9 %collective-permute-done.41.refs_13_ = f32[128,128]{1,0:T(8,128)S(1)} collective-permute-done((f32[128,128]{1,0:T(8,128)S(1)}, f32[128,128]{1,0:T(8,128)S(1)}, u32[]{:S(2)}, u32[]{:S(2)}) %collective-permute-start.41) | collective-permute-done | bytes 65568 | tf_op jit(solution)/shard_map/ppermute | solution.py:98
  138.9 0.7 copy.7.refs_6_
  139.6 14.3 %second_factor.1 = (f32[128,128]{1,0:T(8,128)}, f32[128,128]{1,0:T(8,128)}) custom-call(f32[2048,256]{1,0:T(8,128)} %get-tuple-element.31.y2_ref.refs_1_), custom_call_target="tpu_custom_call" | custom-call | tf_op jit(solution)/shard_map/second_factor/pallas_call | solution.py:370
  154.6 22.1 %last_step.1 = (f32[64,128]{1,0:T(8,128)}, f32[64,128]{1,0:T(8,128)}, f32[1,128]{1,0:T(1,128)}) custom-call(s32[1]{0:T(128)} %bitcast.refs_0_, f32[2048,256]{1,0:T(8,128)} %get-tuple-element.31.y2_ref.refs_1_, f32[2048,128]{1,0:T(8,128)} %get-tuple-element.32.refs_2_, f32[128,128]{1,0:T(8,128)} %get-tuple-element.33.refs_3_, ...), custom_call_target="tpu_custom_call" | custom-call | tf_op jit(solution)/shard_map/last_step/pallas_call | solution.py:378
  176.8 1.2 pad_maximum_fusion.2
  (175 shorter events, 5.4 us)
Async XLA Ops:
  2.1 5.8 %collective-permute-start.1 = (f32[136,128]{1,0:T(8,128)S(1)}, f32[136,128]{1,0:T(8,128)S(1)}, u32[]{:S(2)}, u32[]{:S(2)}) collective-permute-start(f32[136,128]{1,0:T(8,128)S(1)} %pad_maximum_fusion.1), channel_id=1, source_target_pairs={{0,4},{1,5},{2,6},{3,7},{4,0},{5,1},{6,2},{7,3},{8,12},{9,13},{10,... | collective-permute-start | bytes 208904 | tf_op jit(solution)/shard_map/ppermute | solution.py:95
  5.1 5.8 %collective-permute-start.2 = (f32[136,128]{1,0:T(8,128)S(1)}, f32[136,128]{1,0:T(8,128)S(1)}, u32[]{:S(2)}, u32[]{:S(2)}) collective-permute-start(f32[136,128]{1,0:T(8,128)S(1)} %pad_maximum_fusion.1), channel_id=1, source_target_pairs={{0,6},{1,7},{2,4},{3,5},{4,2},{5,3},{6,0},{7,1},{8,14},{9,15},{10,... | collective-permute-start | bytes 208904 | tf_op jit(solution)/shard_map/ppermute | solution.py:95
  6.5 8.0 %collective-permute-start = (f32[136,128]{1,0:T(8,128)S(1)}, f32[136,128]{1,0:T(8,128)S(1)}, u32[]{:S(2)}, u32[]{:S(2)}) collective-permute-start(f32[136,128]{1,0:T(8,128)S(1)} %pad_maximum_fusion.1), channel_id=1, source_target_pairs={{0,2},{1,3},{2,0},{3,1},{4,6},{5,7},{6,4},{7,5},{8,10},{9,11},{10,... | collective-permute-start | bytes 208904 | tf_op jit(solution)/shard_map/ppermute | solution.py:95
  10.8 8.5 %collective-permute-start.6 = (f32[272,128]{1,0:T(8,128)S(1)}, f32[272,128]{1,0:T(8,128)S(1)}, u32[]{:S(2)}, u32[]{:S(2)}) collective-permute-start(f32[272,128]{1,0:T(8,128)S(1)} %constant_dynamic-update-slice_fusion.refs_3_), channel_id=1, source_target_pairs={{0,24},{1,25},{2,26},{3,27},{4,28},{5,29},{6,30},{7,31},{8,0},{9,1... | collective-permute-start | bytes 417800 | tf_op jit(solution)/shard_map/ppermute | solution.py:98
  14.5 8.1 %collective-permute-start.4 = (f32[272,128]{1,0:T(8,128)S(1)}, f32[272,128]{1,0:T(8,128)S(1)}, u32[]{:S(2)}, u32[]{:S(2)}) collective-permute-start(f32[272,128]{1,0:T(8,128)S(1)} %constant_dynamic-update-slice_fusion.refs_3_), channel_id=1, source_target_pairs={{0,8},{1,9},{2,10},{3,11},{4,12},{5,13},{6,14},{7,15},{8,16},{9,17... | collective-permute-start | bytes 417800 | tf_op jit(solution)/shard_map/ppermute | solution.py:98
  15.3 10.3 %collective-permute-start.3 = (f32[272,128]{1,0:T(8,128)S(1)}, f32[272,128]{1,0:T(8,128)S(1)}, u32[]{:S(2)}, u32[]{:S(2)}) collective-permute-start(f32[272,128]{1,0:T(8,128)S(1)} %pad_maximum_fusion.refs_2_), channel_id=1, source_target_pairs={{0,8},{1,9},{2,10},{3,11},{4,12},{5,13},{6,14},{7,15},{8,16},{9,17... | collective-permute-start | bytes 417800 | tf_op jit(solution)/shard_map/ppermute | solution.py:98
  15.4 10.2 %collective-permute-start.10 = (f32[272,128]{1,0:T(8,128)S(1)}, f32[272,128]{1,0:T(8,128)S(1)}, u32[]{:S(2)}, u32[]{:S(2)}) collective-permute-start(f32[272,128]{1,0:T(8,128)S(1)} %constant_dynamic-update-slice_fusion.refs_3_), channel_id=1, source_target_pairs={{0,1},{1,0},{2,3},{3,2},{4,5},{5,4},{6,7},{7,6},{8,9},{9,8},{10,11... | collective-permute-start | bytes 417800 | tf_op jit(solution)/shard_map/ppermute | solution.py:95
  15.4 11.3 %collective-permute-start.5 = (f32[272,128]{1,0:T(8,128)S(1)}, f32[272,128]{1,0:T(8,128)S(1)}, u32[]{:S(2)}, u32[]{:S(2)}) collective-permute-start(f32[272,128]{1,0:T(8,128)S(1)} %pad_maximum_fusion.refs_2_), channel_id=1, source_target_pairs={{0,24},{1,25},{2,26},{3,27},{4,28},{5,29},{6,30},{7,31},{8,0},{9,1... | collective-permute-start | bytes 417800 | tf_op jit(solution)/shard_map/ppermute | solution.py:98
  19.3 7.4 %collective-permute-start.9 = (f32[272,128]{1,0:T(8,128)S(1)}, f32[272,128]{1,0:T(8,128)S(1)}, u32[]{:S(2)}, u32[]{:S(2)}) collective-permute-start(f32[272,128]{1,0:T(8,128)S(1)} %pad_maximum_fusion.refs_2_), channel_id=1, source_target_pairs={{0,1},{1,0},{2,3},{3,2},{4,5},{5,4},{6,7},{7,6},{8,9},{9,8},{10,11... | collective-permute-start | bytes 417800 | tf_op jit(solution)/shard_map/ppermute | solution.py:95
  22.6 6.8 %collective-permute-start.8 = (f32[272,128]{1,0:T(8,128)S(1)}, f32[272,128]{1,0:T(8,128)S(1)}, u32[]{:S(2)}, u32[]{:S(2)}) collective-permute-start(f32[272,128]{1,0:T(8,128)S(1)} %collective-permute-done.6.refs_7_), channel_id=1, source_target_pairs={{0,24},{1,25},{2,26},{3,27},{4,28},{5,29},{6,30},{7,31},{8,0},{9,1... | collective-permute-start | bytes 417800 | tf_op jit(solution)/shard_map/ppermute | solution.py:98
  25.6 3.9 %collective-permute-start.14 = (f32[272,128]{1,0:T(8,128)S(1)}, f32[272,128]{1,0:T(8,128)S(1)}, u32[]{:S(2)}, u32[]{:S(2)}) collective-permute-start(f32[272,128]{1,0:T(8,128)S(1)} %collective-permute-done.6.refs_7_), channel_id=1, source_target_pairs={{0,1},{1,0},{2,3},{3,2},{4,5},{5,4},{6,7},{7,6},{8,9},{9,8},{10,11... | collective-permute-start | bytes 417800 | tf_op jit(solution)/shard_map/ppermute | solution.py:95
  25.6 7.9 %collective-permute-start.7 = (f32[272,128]{1,0:T(8,128)S(1)}, f32[272,128]{1,0:T(8,128)S(1)}, u32[]{:S(2)}, u32[]{:S(2)}) collective-permute-start(f32[272,128]{1,0:T(8,128)S(1)} %collective-permute-done.3.refs_4_), channel_id=1, source_target_pairs={{0,8},{1,9},{2,10},{3,11},{4,12},{5,13},{6,14},{7,15},{8,16},{9,17... | collective-permute-start | bytes 417800 | tf_op jit(solution)/shard_map/ppermute | solution.py:98
  26.7 8.8 %collective-permute-start.11 = (f32[272,128]{1,0:T(8,128)S(1)}, f32[272,128]{1,0:T(8,128)S(1)}, u32[]{:S(2)}, u32[]{:S(2)}) collective-permute-start(f32[272,128]{1,0:T(8,128)S(1)} %collective-permute-done.3.refs_4_), channel_id=1, source_target_pairs={{0,1},{1,0},{2,3},{3,2},{4,5},{5,4},{6,7},{7,6},{8,9},{9,8},{10,11... | collective-permute-start | bytes 417800 | tf_op jit(solution)/shard_map/ppermute | solution.py:95
  26.7 8.8 %collective-permute-start.12 = (f32[272,128]{1,0:T(8,128)S(1)}, f32[272,128]{1,0:T(8,128)S(1)}, u32[]{:S(2)}, u32[]{:S(2)}) collective-permute-start(f32[272,128]{1,0:T(8,128)S(1)} %collective-permute-done.4.refs_5_), channel_id=1, source_target_pairs={{0,1},{1,0},{2,3},{3,2},{4,5},{5,4},{6,7},{7,6},{8,9},{9,8},{10,11... | collective-permute-start | bytes 417800 | tf_op jit(solution)/shard_map/ppermute | solution.py:95
  29.4 6.1 %collective-permute-start.13 = (f32[272,128]{1,0:T(8,128)S(1)}, f32[272,128]{1,0:T(8,128)S(1)}, u32[]{:S(2)}, u32[]{:S(2)}) collective-permute-start(f32[272,128]{1,0:T(8,128)S(1)} %collective-permute-done.5.refs_6_), channel_id=1, source_target_pairs={{0,1},{1,0},{2,3},{3,2},{4,5},{5,4},{6,7},{7,6},{8,9},{9,8},{10,11... | collective-permute-start | bytes 417800 | tf_op jit(solution)/shard_map/ppermute | solution.py:95
  29.4 6.1 %collective-permute-start.16 = (f32[272,128]{1,0:T(8,128)S(1)}, f32[272,128]{1,0:T(8,128)S(1)}, u32[]{:S(2)}, u32[]{:S(2)}) collective-permute-start(f32[272,128]{1,0:T(8,128)S(1)} %collective-permute-done.8.refs_9_), channel_id=1, source_target_pairs={{0,1},{1,0},{2,3},{3,2},{4,5},{5,4},{6,7},{7,6},{8,9},{9,8},{10,11... | collective-permute-start | bytes 417800 | tf_op jit(solution)/shard_map/ppermute | solution.py:95
  40.9 5.5 %collective-permute-start.18 = (f32[128,128]{1,0:T(8,128)}, f32[128,128]{1,0:T(8,128)S(1)}, u32[]{:S(2)}, u32[]{:S(2)}) collective-permute-start(f32[128,128]{1,0:T(8,128)} %get-tuple-element.30), channel_id=1, source_target_pairs={{0,4},{1,5},{2,6},{3,7},{4,0},{5,1},{6,2},{7,3},{8,12},{9,13},{10,... | collective-permute-start | bytes 196616 | tf_op jit(solution)/shard_map/ppermute | solution.py:95
  41.4 6.0 %collective-permute-start.19 = (f32[128,128]{1,0:T(8,128)}, f32[128,128]{1,0:T(8,128)S(1)}, u32[]{:S(2)}, u32[]{:S(2)}) collective-permute-start(f32[128,128]{1,0:T(8,128)} %get-tuple-element.30), channel_id=1, source_target_pairs={{0,6},{1,7},{2,4},{3,5},{4,2},{5,3},{6,0},{7,1},{8,14},{9,15},{10,... | collective-permute-start | bytes 196616 | tf_op jit(solution)/shard_map/ppermute | solution.py:95
  43.4 6.1 %collective-permute-start.17 = (f32[128,128]{1,0:T(8,128)}, f32[128,128]{1,0:T(8,128)S(1)}, u32[]{:S(2)}, u32[]{:S(2)}) collective-permute-start(f32[128,128]{1,0:T(8,128)} %get-tuple-element.30), channel_id=1, source_target_pairs={{0,2},{1,3},{2,0},{3,1},{4,6},{5,7},{6,4},{7,5},{8,10},{9,11},{10,... | collective-permute-start | bytes 196616 | tf_op jit(solution)/shard_map/ppermute | solution.py:95
  47.5 11.0 %collective-permute-start.23 = (f32[256,128]{1,0:T(8,128)S(1)}, f32[256,128]{1,0:T(8,128)S(1)}, u32[]{:S(2)}, u32[]{:S(2)}) collective-permute-start(f32[256,128]{1,0:T(8,128)S(1)} %constant_dynamic-update-slice_fusion.4.refs_6_), channel_id=1, source_target_pairs={{0,24},{1,25},{2,26},{3,27},{4,28},{5,29},{6,30},{7,31},{8,0},{9,1... | collective-permute-start | bytes 393224 | tf_op jit(solution)/shard_map/ppermute | solution.py:98
  48.4 10.1 %collective-permute-start.21 = (f32[256,128]{1,0:T(8,128)S(1)}, f32[256,128]{1,0:T(8,128)S(1)}, u32[]{:S(2)}, u32[]{:S(2)}) collective-permute-start(f32[256,128]{1,0:T(8,128)S(1)} %constant_dynamic-update-slice_fusion.4.refs_6_), channel_id=1, source_target_pairs={{0,8},{1,9},{2,10},{3,11},{4,12},{5,13},{6,14},{7,15},{8,16},{9,17... | collective-permute-start | bytes 393224 | tf_op jit(solution)/shard_map/ppermute | solution.py:98
  49.5 9.0 %collective-permute-start.27 = (f32[256,128]{1,0:T(8,128)S(1)}, f32[256,128]{1,0:T(8,128)S(1)}, u32[]{:S(2)}, u32[]{:S(2)}) collective-permute-start(f32[256,128]{1,0:T(8,128)S(1)} %constant_dynamic-update-slice_fusion.4.refs_6_), channel_id=1, source_target_pairs={{0,1},{1,0},{2,3},{3,2},{4,5},{5,4},{6,7},{7,6},{8,9},{9,8},{10,11... | collective-permute-start | bytes 393224 | tf_op jit(solution)/shard_map/ppermute | solution.py:95
  49.6 9.5 %collective-permute-start.20 = (f32[256,128]{1,0:T(8,128)S(1)}, f32[256,128]{1,0:T(8,128)S(1)}, u32[]{:S(2)}, u32[]{:S(2)}) collective-permute-start(f32[256,128]{1,0:T(8,128)S(1)} %constant_dynamic-update-slice_fusion.2.refs_5_), channel_id=1, source_target_pairs={{0,8},{1,9},{2,10},{3,11},{4,12},{5,13},{6,14},{7,15},{8,16},{9,17... | collective-permute-start | bytes 393224 | tf_op jit(solution)/shard_map/ppermute | solution.py:98
  49.6 11.3 %collective-permute-start.22 = (f32[256,128]{1,0:T(8,128)S(1)}, f32[256,128]{1,0:T(8,128)S(1)}, u32[]{:S(2)}, u32[]{:S(2)}) collective-permute-start(f32[256,128]{1,0:T(8,128)S(1)} %constant_dynamic-update-slice_fusion.2.refs_5_), channel_id=1, source_target_pairs={{0,24},{1,25},{2,26},{3,27},{4,28},{5,29},{6,30},{7,31},{8,0},{9,1... | collective-permute-start | bytes 393224 | tf_op jit(solution)/shard_map/ppermute | solution.py:98
  58.5 8.7 %collective-permute-start.25 = (f32[256,128]{1,0:T(8,128)S(1)}, f32[256,128]{1,0:T(8,128)S(1)}, u32[]{:S(2)}, u32[]{:S(2)}) collective-permute-start(f32[256,128]{1,0:T(8,128)S(1)} %collective-permute-done.23.refs_10_), channel_id=1, source_target_pairs={{0,24},{1,25},{2,26},{3,27},{4,28},{5,29},{6,30},{7,31},{8,0},{9,1... | collective-permute-start | bytes 393224 | tf_op jit(solution)/shard_map/ppermute | solution.py:98
  58.6 8.6 %collective-permute-start.29 = (f32[256,128]{1,0:T(8,128)S(1)}, f32[256,128]{1,0:T(8,128)S(1)}, u32[]{:S(2)}, u32[]{:S(2)}) collective-permute-start(f32[256,128]{1,0:T(8,128)S(1)} %collective-permute-done.21.refs_8_), channel_id=1, source_target_pairs={{0,1},{1,0},{2,3},{3,2},{4,5},{5,4},{6,7},{7,6},{8,9},{9,8},{10,11... | collective-permute-start | bytes 393224 | tf_op jit(solution)/shard_map/ppermute | solution.py:95
  59.1 8.6 %collective-permute-start.24 = (f32[256,128]{1,0:T(8,128)S(1)}, f32[256,128]{1,0:T(8,128)S(1)}, u32[]{:S(2)}, u32[]{:S(2)}) collective-permute-start(f32[256,128]{1,0:T(8,128)S(1)} %collective-permute-done.20.refs_7_), channel_id=1, source_target_pairs={{0,8},{1,9},{2,10},{3,11},{4,12},{5,13},{6,14},{7,15},{8,16},{9,17... | collective-permute-start | bytes 393224 | tf_op jit(solution)/shard_map/ppermute | solution.py:98
  60.9 31.3 %collective-permute-start.31 = (f32[256,128]{1,0:T(8,128)S(1)}, f32[256,128]{1,0:T(8,128)S(1)}, u32[]{:S(2)}, u32[]{:S(2)}) collective-permute-start(f32[256,128]{1,0:T(8,128)S(1)} %collective-permute-done.23.refs_10_), channel_id=1, source_target_pairs={{0,1},{1,0},{2,3},{3,2},{4,5},{5,4},{6,7},{7,6},{8,9},{9,8},{10,11... | collective-permute-start | bytes 393224 | tf_op jit(solution)/shard_map/ppermute | solution.py:95
  60.9 31.3 %collective-permute-start.28 = (f32[256,128]{1,0:T(8,128)S(1)}, f32[256,128]{1,0:T(8,128)S(1)}, u32[]{:S(2)}, u32[]{:S(2)}) collective-permute-start(f32[256,128]{1,0:T(8,128)S(1)} %collective-permute-done.20.refs_7_), channel_id=1, source_target_pairs={{0,1},{1,0},{2,3},{3,2},{4,5},{5,4},{6,7},{7,6},{8,9},{9,8},{10,11... | collective-permute-start | bytes 393224 | tf_op jit(solution)/shard_map/ppermute | solution.py:95
  67.2 25.0 %collective-permute-start.30 = (f32[256,128]{1,0:T(8,128)S(1)}, f32[256,128]{1,0:T(8,128)S(1)}, u32[]{:S(2)}, u32[]{:S(2)}) collective-permute-start(f32[256,128]{1,0:T(8,128)S(1)} %collective-permute-done.22.refs_9_), channel_id=1, source_target_pairs={{0,1},{1,0},{2,3},{3,2},{4,5},{5,4},{6,7},{7,6},{8,9},{9,8},{10,11... | collective-permute-start | bytes 393224 | tf_op jit(solution)/shard_map/ppermute | solution.py:95
  67.3 25.0 %collective-permute-start.33 = (f32[256,128]{1,0:T(8,128)S(1)}, f32[256,128]{1,0:T(8,128)S(1)}, u32[]{:S(2)}, u32[]{:S(2)}) collective-permute-start(f32[256,128]{1,0:T(8,128)S(1)} %collective-permute-done.25.refs_12_), channel_id=1, source_target_pairs={{0,1},{1,0},{2,3},{3,2},{4,5},{5,4},{6,7},{7,6},{8,9},{9,8},{10,11... | collective-permute-start | bytes 393224 | tf_op jit(solution)/shard_map/ppermute | solution.py:95
  67.8 24.6 %collective-permute-start.32 = (f32[256,128]{1,0:T(8,128)S(1)}, f32[256,128]{1,0:T(8,128)S(1)}, u32[]{:S(2)}, u32[]{:S(2)}) collective-permute-start(f32[256,128]{1,0:T(8,128)S(1)} %collective-permute-done.24.refs_11_), channel_id=1, source_target_pairs={{0,1},{1,0},{2,3},{3,2},{4,5},{5,4},{6,7},{7,6},{8,9},{9,8},{10,11... | collective-permute-start | bytes 393224 | tf_op jit(solution)/shard_map/ppermute | solution.py:95
  116.9 4.3 %collective-permute-start.35 = (f32[64,128]{1,0:T(8,128)}, f32[64,128]{1,0:T(8,128)S(1)}, u32[]{:S(2)}, u32[]{:S(2)}) collective-permute-start(f32[64,128]{1,0:T(8,128)} %get-tuple-element.36), channel_id=1, source_target_pairs={{0,4},{1,5},{2,6},{3,7},{4,0},{5,1},{6,2},{7,3},{8,12},{9,13},{10,... | collective-permute-start | bytes 98312 | tf_op jit(solution)/shard_map/ppermute | solution.py:95
  118.6 5.3 %collective-permute-start.36 = (f32[64,128]{1,0:T(8,128)}, f32[64,128]{1,0:T(8,128)S(1)}, u32[]{:S(2)}, u32[]{:S(2)}) collective-permute-start(f32[64,128]{1,0:T(8,128)} %get-tuple-element.36), channel_id=1, source_target_pairs={{0,6},{1,7},{2,4},{3,5},{4,2},{5,3},{6,0},{7,1},{8,14},{9,15},{10,... | collective-permute-start | bytes 98312 | tf_op jit(solution)/shard_map/ppermute | solution.py:95
  119.6 6.3 %collective-permute-start.34 = (f32[64,128]{1,0:T(8,128)}, f32[64,128]{1,0:T(8,128)S(1)}, u32[]{:S(2)}, u32[]{:S(2)}) collective-permute-start(f32[64,128]{1,0:T(8,128)} %get-tuple-element.36), channel_id=1, source_target_pairs={{0,2},{1,3},{2,0},{3,1},{4,6},{5,7},{6,4},{7,5},{8,10},{9,11},{10,... | collective-permute-start | bytes 98312 | tf_op jit(solution)/shard_map/ppermute | solution.py:95
  123.9 5.9 %collective-permute-start.40 = (f32[128,128]{1,0:T(8,128)S(1)}, f32[128,128]{1,0:T(8,128)S(1)}, u32[]{:S(2)}, u32[]{:S(2)}) collective-permute-start(f32[128,128]{1,0:T(8,128)S(1)} %constant_dynamic-update-slice_fusion.8.refs_8_), channel_id=1, source_target_pairs={{0,24},{1,25},{2,26},{3,27},{4,28},{5,29},{6,30},{7,31},{8,0},{9,1... | collective-permute-start | bytes 196616 | tf_op jit(solution)/shard_map/ppermute | solution.py:98
  124.0 6.2 %collective-permute-start.38 = (f32[128,128]{1,0:T(8,128)S(1)}, f32[128,128]{1,0:T(8,128)S(1)}, u32[]{:S(2)}, u32[]{:S(2)}) collective-permute-start(f32[128,128]{1,0:T(8,128)S(1)} %constant_dynamic-update-slice_fusion.8.refs_8_), channel_id=1, source_target_pairs={{0,8},{1,9},{2,10},{3,11},{4,12},{5,13},{6,14},{7,15},{8,16},{9,17... | collective-permute-start | bytes 196616 | tf_op jit(solution)/shard_map/ppermute | solution.py:98
  125.9 4.9 %collective-permute-start.44 = (f32[128,128]{1,0:T(8,128)S(1)}, f32[128,128]{1,0:T(8,128)S(1)}, u32[]{:S(2)}, u32[]{:S(2)}) collective-permute-start(f32[128,128]{1,0:T(8,128)S(1)} %constant_dynamic-update-slice_fusion.8.refs_8_), channel_id=1, source_target_pairs={{0,1},{1,0},{2,3},{3,2},{4,5},{5,4},{6,7},{7,6},{8,9},{9,8},{10,11... | collective-permute-start | bytes 196616 | tf_op jit(solution)/shard_map/ppermute | solution.py:95
  126.0 6.8 %collective-permute-start.37 = (f32[128,128]{1,0:T(8,128)S(1)}, f32[128,128]{1,0:T(8,128)S(1)}, u32[]{:S(2)}, u32[]{:S(2)}) collective-permute-start(f32[128,128]{1,0:T(8,128)S(1)} %constant_dynamic-update-slice_fusion.6.refs_7_), channel_id=1, source_target_pairs={{0,8},{1,9},{2,10},{3,11},{4,12},{5,13},{6,14},{7,15},{8,16},{9,17... | collective-permute-start | bytes 196616 | tf_op jit(solution)/shard_map/ppermute | solution.py:98
  126.0 6.8 %collective-permute-start.39 = (f32[128,128]{1,0:T(8,128)S(1)}, f32[128,128]{1,0:T(8,128)S(1)}, u32[]{:S(2)}, u32[]{:S(2)}) collective-permute-start(f32[128,128]{1,0:T(8,128)S(1)} %constant_dynamic-update-slice_fusion.6.refs_7_), channel_id=1, source_target_pairs={{0,24},{1,25},{2,26},{3,27},{4,28},{5,29},{6,30},{7,31},{8,0},{9,1... | collective-permute-start | bytes 196616 | tf_op jit(solution)/shard_map/ppermute | solution.py:98
  130.2 4.3 %collective-permute-start.42 = (f32[128,128]{1,0:T(8,128)S(1)}, f32[128,128]{1,0:T(8,128)S(1)}, u32[]{:S(2)}, u32[]{:S(2)}) collective-permute-start(f32[128,128]{1,0:T(8,128)S(1)} %collective-permute-done.40.refs_12_), channel_id=1, source_target_pairs={{0,24},{1,25},{2,26},{3,27},{4,28},{5,29},{6,30},{7,31},{8,0},{9,1... | collective-permute-start | bytes 196616 | tf_op jit(solution)/shard_map/ppermute | solution.py:98
  130.8 3.6 %collective-permute-start.46 = (f32[128,128]{1,0:T(8,128)S(1)}, f32[128,128]{1,0:T(8,128)S(1)}, u32[]{:S(2)}, u32[]{:S(2)}) collective-permute-start(f32[128,128]{1,0:T(8,128)S(1)} %collective-permute-done.38.refs_10_), channel_id=1, source_target_pairs={{0,1},{1,0},{2,3},{3,2},{4,5},{5,4},{6,7},{7,6},{8,9},{9,8},{10,11... | collective-permute-start | bytes 196616 | tf_op jit(solution)/shard_map/ppermute | solution.py:95
  132.8 6.1 %collective-permute-start.41 = (f32[128,128]{1,0:T(8,128)S(1)}, f32[128,128]{1,0:T(8,128)S(1)}, u32[]{:S(2)}, u32[]{:S(2)}) collective-permute-start(f32[128,128]{1,0:T(8,128)S(1)} %collective-permute-done.37.refs_9_), channel_id=1, source_target_pairs={{0,8},{1,9},{2,10},{3,11},{4,12},{5,13},{6,14},{7,15},{8,16},{9,17... | collective-permute-start | bytes 196616 | tf_op jit(solution)/shard_map/ppermute | solution.py:98
  132.8 21.1 %collective-permute-start.48 = (f32[128,128]{1,0:T(8,128)S(1)}, f32[128,128]{1,0:T(8,128)S(1)}, u32[]{:S(2)}, u32[]{:S(2)}) collective-permute-start(f32[128,128]{1,0:T(8,128)S(1)} %collective-permute-done.40.refs_12_), channel_id=1, source_target_pairs={{0,1},{1,0},{2,3},{3,2},{4,5},{5,4},{6,7},{7,6},{8,9},{9,8},{10,11... | collective-permute-start | bytes 196616 | tf_op jit(solution)/shard_map/ppermute | solution.py:95
  132.9 21.0 %collective-permute-start.45 = (f32[128,128]{1,0:T(8,128)S(1)}, f32[128,128]{1,0:T(8,128)S(1)}, u32[]{:S(2)}, u32[]{:S(2)}) collective-permute-start(f32[128,128]{1,0:T(8,128)S(1)} %collective-permute-done.37.refs_9_), channel_id=1, source_target_pairs={{0,1},{1,0},{2,3},{3,2},{4,5},{5,4},{6,7},{7,6},{8,9},{9,8},{10,11... | collective-permute-start | bytes 196616 | tf_op jit(solution)/shard_map/ppermute | solution.py:95
  134.4 19.5 %collective-permute-start.47 = (f32[128,128]{1,0:T(8,128)S(1)}, f32[128,128]{1,0:T(8,128)S(1)}, u32[]{:S(2)}, u32[]{:S(2)}) collective-permute-start(f32[128,128]{1,0:T(8,128)S(1)} %collective-permute-done.39.refs_11_), channel_id=1, source_target_pairs={{0,1},{1,0},{2,3},{3,2},{4,5},{5,4},{6,7},{7,6},{8,9},{9,8},{10,11... | collective-permute-start | bytes 196616 | tf_op jit(solution)/shard_map/ppermute | solution.py:95
  134.5 19.5 %collective-permute-start.50 = (f32[128,128]{1,0:T(8,128)S(1)}, f32[128,128]{1,0:T(8,128)S(1)}, u32[]{:S(2)}, u32[]{:S(2)}) collective-permute-start(f32[128,128]{1,0:T(8,128)S(1)} %collective-permute-done.42.refs_14_), channel_id=1, source_target_pairs={{0,1},{1,0},{2,3},{3,2},{4,5},{5,4},{6,7},{7,6},{8,9},{9,8},{10,11... | collective-permute-start | bytes 196616 | tf_op jit(solution)/shard_map/ppermute | solution.py:95
  138.9 15.1 %collective-permute-start.49 = (f32[128,128]{1,0:T(8,128)S(1)}, f32[128,128]{1,0:T(8,128)S(1)}, u32[]{:S(2)}, u32[]{:S(2)}) collective-permute-start(f32[128,128]{1,0:T(8,128)S(1)} %collective-permute-done.41.refs_13_), channel_id=1, source_target_pairs={{0,1},{1,0},{2,3},{3,2},{4,5},{5,4},{6,7},{7,6},{8,9},{9,8},{10,11... | collective-permute-start | bytes 196616 | tf_op jit(solution)/shard_map/ppermute | solution.py:95
  (53 other events, 821.2 us)

commit v2 on v1

--- a/solution.py
+++ b/solution.py
@@ -7,6 +7,7 @@
 
 ITERS = 2
 F32 = jnp.float32
+BF16 = jnp.bfloat16
 highest = lax.Precision.HIGHEST
 CHUNK = 512
 
@@ -21,52 +22,112 @@
     )
 
 
-def inverse_factor(matrix):
+def halves(x):
+    top = x.astype(BF16)
+    return top, (x - top.astype(F32)).astype(BF16)
+
+
+def mm3(a, b, ca=1, cb=0):
+    a1, a2 = halves(a)
+    b1, b2 = halves(b)
+    return lax.dot_general(
+        jnp.concatenate([a1, a1, a2], ca),
+        jnp.concatenate([b1, b2, b1], cb),
+        (((ca,), (cb,)), ((), ())),
+        preferred_element_type=F32,
+    )
+
+
+def total_of(xs, ys):
+    out = xs[0] * ys[0]
+    for x, y in zip(xs[1:], ys[1:]):
+        out = out + x * y
+    return out
+
+
+def solved(entry, columns):
+    size = len(columns[0])
+    if size == 2:
+        x, y, z = entry(0, 0), entry(0, 1), entry(1, 1)
+        scale = 1.0 / (x * z - y * y)
+        q00, q01, q11 = z * scale, -(y * scale), x * scale
+        return [[q00 * c[0] + q01 * c[1], q01 * c[0] + q11 * c[1]] for c in columns]
+    h = size // 2
+    side = [[entry(i, h + j) for i in range(h)] for j in range(h)]
+    done = solved(entry, side + [c[:h] for c in columns])
+    ties, upper = done[:h], done[h:]
+    rest = {
+        (i, j): entry(h + i, h + j) - total_of(side[i], ties[j])
+        for j in range(h)
+        for i in range(j + 1)
+    }
+    lower = solved(
+        lambda i, j: rest[i, j],
+        [[c[h + j] - total_of(ties[j], c[:h]) for j in range(h)] for c in columns],
+    )
+    return [
+        [u[i] - total_of([ties[j][i] for j in range(h)], g) for i in range(h)] + g
+        for u, g in zip(upper, lower)
+    ]
+
+
+def inverse_factor(matrix, panel=32, step=8):
     n = matrix.shape[0]
-    count = n // 8
     lane = lax.broadcasted_iota(jnp.int32, (8, n), 1)
     sub = lax.broadcasted_iota(jnp.int32, (8, n), 0)
-    a = [matrix[8 * v : 8 * v + 8, :] for v in range(count)]
-
-    def wide(x):
-        return jnp.broadcast_to(x, (8, n))
-
-    for k in range(0, n, 2):
-        r, s = divmod(k, 8)
-        row0 = wide(a[r][s : s + 1, :])
-        row1 = wide(a[r][s + 1 : s + 2, :])
-        p00 = wide(a[r][s : s + 1, k : k + 1])
-        p01 = wide(a[r][s : s + 1, k + 1 : k + 2])
-        p11 = wide(a[r][s + 1 : s + 2, k + 1 : k + 2])
-        scale = 1.0 / (p00 * p11 - p01 * p01)
-        q00 = p11 * scale
-        q01 = -p01 * scale
-        q11 = p00 * scale
-        at0 = lane == k
-        at1 = lane == k + 1
-        g0 = jnp.where(at0, q00, jnp.where(at1, q01, q00 * row0 + q01 * row1))
-        g1 = jnp.where(at0, q01, jnp.where(at1, q11, q01 * row0 + q11 * row1))
-        inside = at0 | at1
-        for v in range(r, count):
-            if v == r and s == 6:
-                continue
-            c0 = wide(a[v][:, k : k + 1])
-            c1 = wide(a[v][:, k + 1 : k + 2])
-            new = jnp.where(inside, 0.0, a[v]) - c0 * g0 - c1 * g1
-            a[v] = jnp.where(sub > s + 1, new, a[v]) if v == r else new
-    even = (sub % 2) == 0
+    a = [matrix[8 * v : 8 * v + 8, :] for v in range(n // 8)]
+
+    def along(x, j):
+        return jnp.broadcast_to(x[:, j : j + 1], (8, n))
+
+    def down(x, i):
+        return jnp.broadcast_to(x[i : i + 1, :], (8, n))
+
     rows = []
-    for v in range(count):
-        here = sub + 8 * v
-        across = jnp.where(even, here + 1, here - 1)
-        diag = wide(jnp.sum(jnp.where(lane == here, a[v], 0.0), axis=1, keepdims=True))
-        off = wide(jnp.sum(jnp.where(lane == across, a[v], 0.0), axis=1, keepdims=True))
-        left = jnp.where(lane < (sub // 2) * 2 + 8 * v, a[v], 0.0)
-        unit = jnp.where(lane == here, 1.0, left)
-        above = pltpu.roll(unit, 1, 0)
-        ratio = off / pltpu.roll(diag, 1, 0)
-        norm = lax.rsqrt(jnp.where(even, diag, diag - off * ratio))
-        rows.append(jnp.where(even, unit, unit - ratio * above) * norm)
+    for first in range(0, n, panel):
+        last = (first + panel) // 8
+        multipliers = []
+        for k in range(first, first + panel, step):
+            r = k // 8
+            own = [along(a[r], k + j) for j in range(step)]
+            pivot = {(i, j): down(own[j], i) for j in range(step) for i in range(j + 1)}
+            inside = (lane >= k) & (lane < k + step)
+            right = [
+                jnp.where(lane == k + i, 1.0, jnp.where(inside, 0.0, down(a[r], i)))
+                for i in range(step)
+            ]
+            g = solved(lambda i, j: pivot[i, j], [right])[0]
+            finished, factor, norms = [], {}, []
+            for i in range(step):
+                y, d = right[i], pivot[i, i]
+                for j in range(i):
+                    e = pivot[j, i]
+                    for m in range(j):
+                        e = e - factor[i, m] * factor[j, m]
+                    factor[i, j] = e * norms[j]
+                for j in range(i):
+                    d = d - factor[i, j] * factor[i, j]
+                    y = y - factor[i, j] * finished[j]
+                norms.append(lax.rsqrt(d))
+                finished.append(y * norms[i])
+            row, held = finished[0], g[0]
+            for i in range(1, step):
+                row = jnp.where(sub == i, finished[i], row)
+                held = jnp.where(sub == i, g[i], held)
+            rows.append(jnp.where(lane <= sub + k, row, 0.0))
+            multipliers.append(
+                jnp.where((lane >= k + step) & (lane < first + panel), 0.0, held)
+            )
+            for v in range(r + 1, last):
+                other = [along(a[v], k + j) for j in range(step)]
+                a[v] = jnp.where(inside, 0.0, a[v]) - total_of(other, g)
+        if last < n // 8:
+            change = mm(
+                jnp.concatenate(a[first // 8 : last], 0), jnp.concatenate(multipliers, 0), 0, 0
+            )
+            inside = (lane >= first) & (lane < first + panel)
+            for v in range(last, n // 8):
+                a[v] = jnp.where(inside, 0.0, a[v]) - change[8 * v : 8 * v + 8]
     return jnp.concatenate(rows, 0)
 
 
@@ -78,36 +139,38 @@
 
 def layout_of(rings):
     half = rings // 2
-    out = []
-    for dc in (0, 1):
-        out += [(0, (0, 1), dc), (0, (2, 3), dc)]
-        for t in range(1, half):
-            out += [(-t, (0, 1), dc), (-t, (2, 3), dc), (t, (0, 1), dc), (t, (2, 3), dc)]
-        out += [(-half, (0, 1), dc), (half, (2, 3), dc)]
-    return out
-
-
-def gather(block, n):
+    chips = [(0, (0, 1, 2, 3))]
+    for t in range(1, half):
+        chips += [(-t, (0, 1, 2, 3)), (t, (0, 1, 2, 3))]
+    chips += [(-half, (0, 1)), (half, (2, 3))]
+    return [chip + (dc,) for dc in (0, 1) for chip in chips]
+
+
+def gather(block, n, tag):
     rings = n // 8
     half = rings // 2
 
-    def swap(x, m):
-        return lax.ppermute(x, "blk", [(i, i ^ m) for i in range(n)])
-
-    def turn(x, d):
-        return lax.ppermute(x, "blk", [(i, ((i // 8 + d) % rings) * 8 + i % 8) for i in range(n)])
-
-    by_x, by_y, by_xy = swap(block, 2), swap(block, 4), swap(block, 6)
-    first = jnp.concatenate([block, by_x], 0)
-    second = jnp.concatenate([by_y, by_xy], 0)
-    near = [first, second]
-    up_a, up_b, down_a, down_b = first, second, first, second
+    def send(x, pairs, name):
+        with jax.named_scope(tag + name):
+            return lax.ppermute(x, "blk", pairs)
+
+    def swap(x, m, name):
+        return send(x, [(i, i ^ m) for i in range(n)], name)
+
+    def turn(x, d, name):
+        pairs = [(i, ((i // 8 + d) % rings) * 8 + i % 8) for i in range(n)]
+        return send(x, pairs, name)
+
+    parts = [block, swap(block, 2, "_x"), swap(block, 4, "_y"), swap(block, 6, "_xy")]
+    own = jnp.concatenate(parts, 0)
+    near, up, down = [own], own, own
     for t in range(1, half):
-        up_a, down_b = turn(up_a, 1), turn(down_b, -1)
-        up_b, down_a = turn(up_b, 1), turn(down_a, -1)
-        near += [up_a, up_b, down_a, down_b]
-    near += [turn(up_a, 1), turn(down_b, -1)]
-    return near + [swap(x, 1) for x in near]
+        up, down = turn(up, 1, "_up"), turn(down, -1, "_down")
+        near += [up, down]
+    middle = own.shape[0] // 2
+    near.append(turn(up[:middle], 1, "_lastup"))
+    near.append(turn(down[middle:], -1, "_lastdown"))
+    return near + [swap(x, 1, f"_core{i}") for i, x in enumerate(near)]
 
 
 def assemble(me, pieces, rows, rings, place):
@@ -131,24 +194,30 @@
     table[...] = jnp.zeros_like(table)
     assemble(me_ref[0], pieces, rows, rings, place)
     diag_ref[...] = table[...].T
-    result = mm(kernel_ref[...], y_ref[...])
+    result = mm3(kernel_ref[...], y_ref[...])
     ky_ref[:rows, :] = result[:, :width]
     ky_ref[rows:, :] = result[:, width:]
 
 
-def metric_factor(y_ref, out_ref):
+def metric_head(y_ref, metric_ref, upper_ref):
     total, double = y_ref.shape
     width = double // 2
     chunk = min(CHUNK, total)
 
     def add(i, acc):
         part = y_ref[pl.ds(pl.multiple_of(i * chunk, chunk), chunk), :]
-        return acc + mm(part, part, 0, 0)
+        return acc + mm3(part, part, 0, 0)
 
     metric = lax.fori_loop(0, total // chunk, add, jnp.zeros((double, double), F32))
-    upper = inverse_factor(metric[:width, :width])
-    cross = mm(upper, metric[:width, width:])
-    lower = inverse_factor(metric[width:, width:] - mm(cross, cross, 0, 0))
+    metric_ref[...] = metric
+    upper_ref[...] = inverse_factor(metric[:width, :width])
+
+
+def metric_tail(metric_ref, upper_ref, out_ref):
+    width = upper_ref.shape[0]
+    upper = upper_ref[...]
+    cross = mm(upper, metric_ref[:width, width:])
+    lower = inverse_factor(metric_ref[width:, width:] - mm(cross, cross, 0, 0))
     out_ref[:width, :width] = upper
     out_ref[:width, width:] = jnp.zeros((width, width), F32)
     out_ref[width:, :width] = -mm(lower, mm(cross, upper, 0, 0))
@@ -171,7 +240,7 @@
 
     def add(i, acc):
         at = pl.ds(pl.multiple_of(i * chunk, chunk), chunk)
-        return acc + mm(y_ref[at, :], ky_ref[at, :], 0, 0)
+        return acc + mm3(y_ref[at, :], ky_ref[at, :], 0, 0)
 
     g = lax.fori_loop(0, total // chunk, add, jnp.zeros((double, double), F32))
     factor = factor_ref[...]
@@ -189,8 +258,8 @@
 
     def update(i, acc):
         at = pl.ds(pl.multiple_of(i * chunk, chunk), chunk)
-        pair = mm(y_ref[at, :], both)
-        image = mm(ky_ref[at, :], mixing)
+        pair = mm3(y_ref[at, :], both)
+        image = mm3(ky_ref[at, :], mixing)
         y2_ref[at, :width] = pair[:, :width]
         kx_ref[at, :] = image
         residual = image - pair[:, width:]
@@ -219,7 +288,7 @@
     first_step(
         y_ref, ky_ref, factor_ref, diag_ref.at[:rows, :], y2_ref, kx_ref, small_ref, norm_ref
     )
-    kw_ref[...] = mm(kernel_ref[...], y2_ref[:, width:])
+    kw_ref[...] = mm3(kernel_ref[...], y2_ref[:, width:])
 
 
 def second_factor(y2_ref, gram_ref, factor_ref):
@@ -229,7 +298,7 @@
 
     def add(i, acc):
         at = pl.ds(pl.multiple_of(i * chunk, chunk), chunk)
-        return acc + mm(y2_ref[at, :], y2_ref[at, width:], 0, 0)
+        return acc + mm3(y2_ref[at, :], y2_ref[at, width:], 0, 0)
 
     gram = lax.fori_loop(0, total // chunk, add, jnp.zeros((double, width), F32))
     cross = gram[:width]
@@ -247,7 +316,7 @@
 
     def add(i, acc):
         at = pl.ds(pl.multiple_of(i * chunk, chunk), chunk)
-        return acc + mm(y2_ref[at, :], image_ref[at, width:], 0, 0)
+        return acc + mm3(y2_ref[at, :], image_ref[at, width:], 0, 0)
 
     g = lax.fori_loop(0, total // chunk, add, jnp.zeros((double, width), F32))
     values, cross, factor = small_ref[...], cross_ref[...], factor_ref[...]
@@ -265,7 +334,7 @@
 
     def update(i, acc):
         at = pl.ds(pl.multiple_of(i * chunk, chunk), chunk)
-        residual = mm(image_ref[at, :], mixing) - mm(y2_ref[at, :], turned)
+        residual = mm3(image_ref[at, :], mixing) - mm3(y2_ref[at, :], turned)
         return acc + jnp.sum(residual * residual, axis=0, keepdims=True)
 
     squares = lax.fori_loop(0, total // chunk, update, jnp.zeros((1, width), F32))
@@ -317,12 +386,40 @@
     )
 
 
+def cost(us):
+    return pl.CostEstimate(flops=int(us * 1e9), bytes_accessed=0, transcendentals=0)
+
+
 def shape(*dims):
     return jax.ShapeDtypeStruct(dims, F32)
 
 
 VMEM = pl.BlockSpec(memory_space=pltpu.VMEM)
 SMEM = pl.BlockSpec(memory_space=pltpu.SMEM)
+
+
+def metric_factor(y):
+    width = y.shape[1] // 2
+    with jax.named_scope("metric_head"):
+        metric, upper = pl.pallas_call(
+            metric_head,
+            out_shape=(shape(2 * width, 2 * width), shape(width, width)),
+            in_specs=[VMEM],
+            out_specs=(VMEM, VMEM),
+            compiler_params=params(),
+            cost_estimate=cost(7),
+            name="metric_head",
+        )(y)
+    with jax.named_scope("metric_tail"):
+        return pl.pallas_call(
+            metric_tail,
+            out_shape=shape(2 * width, 2 * width),
+            in_specs=[VMEM, VMEM],
+            out_specs=VMEM,
+            compiler_params=params(),
+            cost_estimate=cost(7),
+            name="metric_tail",
+        )(metric, upper)
 
 
 def ringed(n, kernel, ritz, search, diag):
@@ -332,7 +429,7 @@
     me = lax.axis_index("blk").astype(jnp.int32).reshape(1)
     lanes = max(128, -(-rows // 128) * 128)
     extra = jnp.zeros((8, width), F32).at[0, :rows].set(diag)
-    sent = gather(jnp.concatenate([ritz, search, extra], 0), n)
+    sent = gather(jnp.concatenate([ritz, search, extra], 0), n, "ag1")
     y, ky_own, diag_table = pl.pallas_call(
         lambda *refs: first_product(rings, rows, *refs),
         out_shape=(shape(total, 2 * width), shape(2 * rows, width), shape(width, max(n, 128))),
@@ -342,15 +439,8 @@
         compiler_params=params(),
         name="first_product",
     )(me, kernel, *sent)
-    images = gather(ky_own, n)
-    factor = pl.pallas_call(
-        metric_factor,
-        out_shape=shape(2 * width, 2 * width),
-        in_specs=[VMEM],
-        out_specs=VMEM,
-        compiler_params=params(),
-        name="metric_factor",
-    )(y)
+    images = gather(ky_own, n, "ag2")
+    factor = metric_factor(y)
     y2, kx, values, norm1, kw_own = pl.pallas_call(
         lambda *refs: with_product(rings, rows, *refs),
         out_shape=(
@@ -366,7 +456,7 @@
         compiler_params=params(),
         name="first_step",
     )(me, kernel, y, factor, diag_table, *images)
-    images2 = gather(kw_own, n)
+    images2 = gather(kw_own, n, "ag3")
     cross, factor2 = pl.pallas_call(
         second_factor,
         out_shape=(shape(width, width), shape(width, width)),
@@ -402,14 +492,7 @@
     y = lax.all_gather(own, axes, axis=0, tiled=True)
     ky = lax.all_gather(product(part), axes, axis=0, tiled=True)
     table = lax.all_gather(diag, axes, axis=0, tiled=True).reshape(n * cols, rows).T
-    factor = pl.pallas_call(
-        metric_factor,
-        out_shape=shape(2 * width, 2 * width),
-        in_specs=[VMEM],
-        out_specs=VMEM,
-        compiler_params=params(),
-        name="metric_factor",
-    )(y)
+    factor = metric_factor(y)
     y2, kx, values, norm1 = pl.pallas_call(
         first_step,
         out_shape=(shape(total, 2 * width), shape(total, width), shape(width, width), shape(1, width)),

time: 179 us -> 151 us (0.84)
  Pallas kernels: 89.1 us -> 59.3 us
  waiting for transfers between devices: 39.9 us -> 42.3 us
  local copies, waits for them, and re-layouts: 7.18 us -> 9.28 us
    pallas_call x1 -> x2, Pallas kernels: 24.4 us -> 15.7 us  [the longest x1 8.68 us: metric_factor(): pl.pallas_call(metric_head, out_shape=(shape(2 * width, 2 * width), shape...]
    pallas_call x1, Pallas kernels: 23.8 us -> 16.1 us  [ringed(): pl.pallas_call(lambda *refs: with_product(rings, rows, *refs), out_shape=...]
    pallas_call x1, Pallas kernels: 22.1 us -> 14.9 us  [ringed(): pl.pallas_call(lambda *refs: last_step(rings, rows, *refs), out_shape=(sh...]
    pallas_call x1, Pallas kernels: 14.3 us -> 8.84 us  [ringed(): pl.pallas_call(second_factor, out_shape=(shape(width, width), shape(width...]
    ppermute x51 -> x36, waiting for transfers between devices: 39.9 us -> 42.3 us  [send(): return lax.ppermute(x, 'blk', pairs)]
    unnamed x106 -> x75, local copies, waits for them, and re-layouts: 5.79 us -> 7.85 us
    ppermute x51 -> x36, starting transfers between devices: 37.7 us -> 36.2 us  [send(): return lax.ppermute(x, 'blk', pairs)]
  transfers between devices with their start and end apart: 51 -> 36, of which waited for: 16 -> 16; matrix products, arithmetic and copies ran while one was open for 3% -> 3% of each run, Pallas kernels for 22% -> 16%
where the time goes in v2:
time: 151 us; the launch traced here: 150 us
  Pallas kernels  59.3 us (39%)
  waiting for transfers between devices  42.3 us (28%)
  starting transfers between devices  36.2 us (24%)
  local copies, waits for them, and re-layouts  9.28 us (6%)
  other arithmetic  2.02 us (1%)
    ppermute x36, waiting for transfers between devices, send(): return lax.ppermute(x, 'blk', pairs)  42.3 us
    ppermute x36, starting transfers between devices, send(): return lax.ppermute(x, 'blk', pairs)  36.2 us
    pallas_call x1, Pallas kernels, ringed(): pl.pallas_call(lambda *refs: with_product(rings, rows, *refs), out_shape=...  16.1 us
    pallas_call x1, Pallas kernels, ringed(): pl.pallas_call(lambda *refs: last_step(rings, rows, *refs), out_shape=(sh...  14.9 us
    pallas_call x1, Pallas kernels, ringed(): pl.pallas_call(second_factor, out_shape=(shape(width, width), shape(width...  8.84 us
    pallas_call x1, Pallas kernels, metric_factor(): pl.pallas_call(metric_head, out_shape=(shape(2 * width, 2 * width), shape...  8.68 us
    unnamed x75, local copies, waits for them, and re-layouts  7.85 us
    pallas_call x1, Pallas kernels, metric_factor(): pl.pallas_call(metric_tail, out_shape=shape(2 * width, 2 * width), in_spe...  7.02 us
  transfers between devices with their start and end apart: 36, of which 16 were waited for; matrix products, arithmetic and copies ran while one was open for 3% of the time, Pallas kernels for 16%

profile of v2, /device:TPU:0, one launch (start us, length us, event | category | flops | bytes accessed | tf_op | source)
XLA Modules:
  0.0 150.2 jit_solution(13284697745464986940)
XLA Ops:
  0.6 0.8 constant_dynamic-update-slice_fusion.5
  1.4 0.8 constant_dynamic-update-slice_fusion.4
  2.2 0.7 fusion
  2.8 0.8 pad_maximum_fusion
  3.6 3.0 %collective-permute-start = (f32[136,128]{1,0:T(8,128)S(1)}, f32[136,128]{1,0:T(8,128)S(1)}, u32[]{:S(2)}, u32[]{:S(2)}) collective-permute-start(f32[136,128]{1,0:T(8,128)S(1)} %pad_maximum_fusion), channel_id=1, source_target_pairs={{0,2},{1,3},{2,0},{3,1},{4,6},{5,7},{6,4},{7,5},{8,10},{9,11},{10,... | collective-permute-start | bytes 208904 | tf_op jit(solution)/shard_map/ag1_x/ppermute | solution.py:155
  6.6 1.5 %collective-permute-start.1 = (f32[136,128]{1,0:T(8,128)S(1)}, f32[136,128]{1,0:T(8,128)S(1)}, u32[]{:S(2)}, u32[]{:S(2)}) collective-permute-start(f32[136,128]{1,0:T(8,128)S(1)} %pad_maximum_fusion), channel_id=1, source_target_pairs={{0,4},{1,5},{2,6},{3,7},{4,0},{5,1},{6,2},{7,3},{8,12},{9,13},{10,... | collective-permute-start | bytes 208904 | tf_op jit(solution)/shard_map/ag1_y/ppermute | solution.py:155
  8.1 0.9 collective-permute-done
  9.0 1.9 %collective-permute-done.1 = f32[136,128]{1,0:T(8,128)S(1)} collective-permute-done((f32[136,128]{1,0:T(8,128)S(1)}, f32[136,128]{1,0:T(8,128)S(1)}, u32[]{:S(2)}, u32[]{:S(2)}) %collective-permute-start.1) | collective-permute-done | bytes 69664 | tf_op jit(solution)/shard_map/ag1_y/ppermute | solution.py:155
  10.9 2.4 %collective-permute-done.2 = f32[136,128]{1,0:T(8,128)S(1)} collective-permute-done((f32[136,128]{1,0:T(8,128)S(1)}, f32[136,128]{1,0:T(8,128)S(1)}, u32[]{:S(2)}, u32[]{:S(2)}) %collective-permute-start.2) | collective-permute-done | bytes 69664 | tf_op jit(solution)/shard_map/ag1_xy/ppermute | solution.py:155
  13.3 1.6 %collective-permute-start.3 = (f32[544,128]{1,0:T(8,128)S(1)}, f32[544,128]{1,0:T(8,128)S(1)}, u32[]{:S(2)}, u32[]{:S(2)}) collective-permute-start(f32[544,128]{1,0:T(8,128)S(1)} %constant_dynamic-update-slice_fusion.refs_2_), channel_id=1, source_target_pairs={{0,8},{1,9},{2,10},{3,11},{4,12},{5,13},{6,14},{7,15},{8,16},{9,17... | collective-permute-start | bytes 835592 | tf_op jit(solution)/shard_map/ag1_up/ppermute | solution.py:155
  14.9 2.2 %collective-permute-start.4 = (f32[544,128]{1,0:T(8,128)S(1)}, f32[544,128]{1,0:T(8,128)S(1)}, u32[]{:S(2)}, u32[]{:S(2)}) collective-permute-start(f32[544,128]{1,0:T(8,128)S(1)} %constant_dynamic-update-slice_fusion.refs_2_), channel_id=1, source_target_pairs={{0,24},{1,25},{2,26},{3,27},{4,28},{5,29},{6,30},{7,31},{8,0},{9,1... | collective-permute-start | bytes 835592 | tf_op jit(solution)/shard_map/ag1_down/ppermute | solution.py:155
  17.2 7.5 %collective-permute-done.3.refs_3_ = f32[544,128]{1,0:T(8,128)S(1)} collective-permute-done((f32[544,128]{1,0:T(8,128)S(1)}, f32[544,128]{1,0:T(8,128)S(1)}, u32[]{:S(2)}, u32[]{:S(2)}) %collective-permute-start.3) | collective-permute-done | bytes 278560 | tf_op jit(solution)/shard_map/ag1_up/ppermute | solution.py:155
  24.7 1.7 %collective-permute-start.5 = (f32[272,128]{1,0:T(8,128)S(1)}, f32[272,128]{1,0:T(8,128)S(1)}, u32[]{:S(2)}, u32[]{:S(2)}) collective-permute-start(f32[272,128]{1,0:T(8,128)S(1)} %slice.40), channel_id=1, source_target_pairs={{0,8},{1,9},{2,10},{3,11},{4,12},{5,13},{6,14},{7,15},{8,16},{9,17... | collective-permute-start | bytes 417800 | tf_op jit(solution)/shard_map/ag1_lastup/ppermute | solution.py:155
  26.4 2.4 %collective-permute-done.4.refs_4_ = f32[544,128]{1,0:T(8,128)S(1)} collective-permute-done((f32[544,128]{1,0:T(8,128)S(1)}, f32[544,128]{1,0:T(8,128)S(1)}, u32[]{:S(2)}, u32[]{:S(2)}) %collective-permute-start.4) | collective-permute-done | bytes 278560 | tf_op jit(solution)/shard_map/ag1_down/ppermute | solution.py:155
  28.8 2.4 %collective-permute-start.6 = (f32[272,128]{1,0:T(8,128)S(1)}, f32[272,128]{1,0:T(8,128)S(1)}, u32[]{:S(2)}, u32[]{:S(2)}) collective-permute-start(f32[272,128]{1,0:T(8,128)S(1)} %slice.41), channel_id=1, source_target_pairs={{0,24},{1,25},{2,26},{3,27},{4,28},{5,29},{6,30},{7,31},{8,0},{9,1... | collective-permute-start | bytes 417800 | tf_op jit(solution)/shard_map/ag1_lastdown/ppermute | solution.py:155
  31.8 2.5 %collective-permute-done.5.refs_5_ = f32[272,128]{1,0:T(8,128)S(1)} collective-permute-done((f32[272,128]{1,0:T(8,128)S(1)}, f32[272,128]{1,0:T(8,128)S(1)}, u32[]{:S(2)}, u32[]{:S(2)}) %collective-permute-start.5) | collective-permute-done | bytes 139296 | tf_op jit(solution)/shard_map/ag1_lastup/ppermute | solution.py:155
  34.3 1.2 collective-permute-done.6.refs_6_
  35.4 2.1 %copy.10 = f32[64,1,2048]{2,0,1:T(8,128)} copy(f32[64,1,2048]{2,1,0:T(1,128)} %param.6) | data formatting | bytes 1048576
  38.5 3.7 %first_product.1 = (f32[2048,256]{1,0:T(8,128)}, f32[128,128]{1,0:T(8,128)}, f32[128,128]{1,0:T(8,128)}) custom-call(s32[1]{0:T(128)} %bitcast.refs_0_, f32[64,2048]{1,0:T(8,128)} %bitcast.6, f32[544,128]{1,0:T(8,128)} %copy-done.5, f32[544,128]{1,0:T(8,128)} %copy-done, f32[544,128]{1,0:T(8,128)} %copy-done.1, f32[272,128]{1,0:T(8,128)} %copy-done.15, ...), custom_call_target="tpu_custom_call" | custom-call | tf_op jit(solution)/shard_map/first_product/pallas_call | solution.py:433
  42.2 0.9 collective-permute-start.12
  43.1 0.6 collective-permute-start.13
  43.7 2.0 %collective-permute-start.14 = (f32[128,128]{1,0:T(8,128)}, f32[128,128]{1,0:T(8,128)S(1)}, u32[]{:S(2)}, u32[]{:S(2)}) collective-permute-start(f32[128,128]{1,0:T(8,128)} %get-tuple-element.34), channel_id=1, source_target_pairs={{0,6},{1,7},{2,4},{3,5},{4,2},{5,3},{6,0},{7,1},{8,14},{9,15},{10,... | collective-permute-start | bytes 196616 | tf_op jit(solution)/shard_map/ag2_xy/ppermute | solution.py:155
  45.7 0.9 constant_dynamic-update-slice_fusion.9
  46.9 1.4 collective-permute-done.13
  48.3 0.8 collective-permute-done.14
  49.1 1.2 collective-permute-start.15
  50.3 2.6 %collective-permute-start.16 = (f32[512,128]{1,0:T(8,128)S(1)}, f32[512,128]{1,0:T(8,128)S(1)}, u32[]{:S(2)}, u32[]{:S(2)}) collective-permute-start(f32[512,128]{1,0:T(8,128)S(1)} %constant_dynamic-update-slice_fusion.6.refs_5_), channel_id=1, source_target_pairs={{0,24},{1,25},{2,26},{3,27},{4,28},{5,29},{6,30},{7,31},{8,0},{9,1... | collective-permute-start | bytes 786440 | tf_op jit(solution)/shard_map/ag2_down/ppermute | solution.py:155
  53.0 7.2 %collective-permute-done.15.refs_6_ = f32[512,128]{1,0:T(8,128)S(1)} collective-permute-done((f32[512,128]{1,0:T(8,128)S(1)}, f32[512,128]{1,0:T(8,128)S(1)}, u32[]{:S(2)}, u32[]{:S(2)}) %collective-permute-start.15) | collective-permute-done | bytes 262176 | tf_op jit(solution)/shard_map/ag2_up/ppermute | solution.py:155
  60.2 3.6 %collective-permute-done.16.refs_7_ = f32[512,128]{1,0:T(8,128)S(1)} collective-permute-done((f32[512,128]{1,0:T(8,128)S(1)}, f32[512,128]{1,0:T(8,128)S(1)}, u32[]{:S(2)}, u32[]{:S(2)}) %collective-permute-start.16) | collective-permute-done | bytes 262176 | tf_op jit(solution)/shard_map/ag2_down/ppermute | solution.py:155
  63.9 2.4 %collective-permute-start.18 = (f32[256,128]{1,0:T(8,128)S(1)}, f32[256,128]{1,0:T(8,128)S(1)}, u32[]{:S(2)}, u32[]{:S(2)}) collective-permute-start(f32[256,128]{1,0:T(8,128)S(1)} %slice.43), channel_id=1, source_target_pairs={{0,24},{1,25},{2,26},{3,27},{4,28},{5,29},{6,30},{7,31},{8,0},{9,1... | collective-permute-start | bytes 393224 | tf_op jit(solution)/shard_map/ag2_lastdown/ppermute | solution.py:155
  66.3 8.7 %metric_head.1 = (f32[256,256]{1,0:T(8,128)}, f32[128,128]{1,0:T(8,128)}) custom-call(f32[2048,256]{1,0:T(8,128)} %get-tuple-element.30.y_ref.refs_2_), custom_call_target="tpu_custom_call" | custom-call | flops 7000000000 | tf_op jit(solution)/shard_map/metric_head/metric_head/pallas_call | solution.py:404
  76.1 7.0 %metric_tail.1.refs_3_ = f32[256,256]{1,0:T(8,128)} custom-call(f32[256,256]{1,0:T(8,128)} %get-tuple-element.31.metric_ref, f32[128,128]{1,0:T(8,128)} %get-tuple-element.32.upper_ref), custom_call_target="tpu_custom_call" | custom-call | flops 7000000000 | tf_op jit(solution)/shard_map/metric_tail/metric_tail/pallas_call | solution.py:414
  83.2 0.6 copy-done.11
  84.2 16.1 %first_step.1 = (f32[2048,256]{1,0:T(8,128)}, f32[2048,128]{1,0:T(8,128)}, f32[128,128]{1,0:T(8,128)}, f32[1,128]{1,0:T(1,128)}, f32[64,128]{1,0:T(8,128)}) custom-call(s32[1]{0:T(128)} %bitcast.refs_0_, f32[64,2048]{1,0:T(8,128)} %bitcast.7, f32[2048,256]{1,0:T(8,128)} %get-tuple-element.30.y_ref.refs_2_, f32[256,256]{1,0:T(8,128)} %metric_tail.1.refs_3_, ...), custom_call_target="tpu_custom_call" | custom-call | tf_op jit(solution)/shard_map/first_step/pallas_call | solution.py:444
  100.3 1.5 %collective-permute-start.24 = (f32[64,128]{1,0:T(8,128)}, f32[64,128]{1,0:T(8,128)S(1)}, u32[]{:S(2)}, u32[]{:S(2)}) collective-permute-start(f32[64,128]{1,0:T(8,128)} %get-tuple-element.40), channel_id=1, source_target_pairs={{0,2},{1,3},{2,0},{3,1},{4,6},{5,7},{6,4},{7,5},{8,10},{9,11},{10,... | collective-permute-start | bytes 98312 | tf_op jit(solution)/shard_map/ag3_x/ppermute | solution.py:155
  101.8 0.8 constant_dynamic-update-slice_fusion.13
  102.6 1.4 collective-permute-start.25
  104.0 0.6 collective-permute-start.26
  104.6 2.1 %collective-permute-done.25 = f32[64,128]{1,0:T(8,128)S(1)} collective-permute-done((f32[64,128]{1,0:T(8,128)}, f32[64,128]{1,0:T(8,128)S(1)}, u32[]{:S(2)}, u32[]{:S(2)}) %collective-permute-start.25) | collective-permute-done | bytes 32800 | tf_op jit(solution)/shard_map/ag3_y/ppermute | solution.py:155
  106.7 2.3 %collective-permute-done.26 = f32[64,128]{1,0:T(8,128)S(1)} collective-permute-done((f32[64,128]{1,0:T(8,128)}, f32[64,128]{1,0:T(8,128)S(1)}, u32[]{:S(2)}, u32[]{:S(2)}) %collective-permute-start.26) | collective-permute-done | bytes 32800 | tf_op jit(solution)/shard_map/ag3_xy/ppermute | solution.py:155
  109.0 3.8 %collective-permute-start.28 = (f32[256,128]{1,0:T(8,128)S(1)}, f32[256,128]{1,0:T(8,128)S(1)}, u32[]{:S(2)}, u32[]{:S(2)}) collective-permute-start(f32[256,128]{1,0:T(8,128)S(1)} %constant_dynamic-update-slice_fusion.10.refs_7_), channel_id=1, source_target_pairs={{0,24},{1,25},{2,26},{3,27},{4,28},{5,29},{6,30},{7,31},{8,0},{9,1... | collective-permute-start | bytes 393224 | tf_op jit(solution)/shard_map/ag3_down/ppermute | solution.py:155
  112.8 3.5 %collective-permute-done.27.refs_8_ = f32[256,128]{1,0:T(8,128)S(1)} collective-permute-done((f32[256,128]{1,0:T(8,128)S(1)}, f32[256,128]{1,0:T(8,128)S(1)}, u32[]{:S(2)}, u32[]{:S(2)}) %collective-permute-start.27) | collective-permute-done | bytes 131104 | tf_op jit(solution)/shard_map/ag3_up/ppermute | solution.py:155
  117.1 3.7 %collective-permute-start.30 = (f32[128,128]{1,0:T(8,128)S(1)}, f32[128,128]{1,0:T(8,128)S(1)}, u32[]{:S(2)}, u32[]{:S(2)}) collective-permute-start(f32[128,128]{1,0:T(8,128)S(1)} %slice.45), channel_id=1, source_target_pairs={{0,24},{1,25},{2,26},{3,27},{4,28},{5,29},{6,30},{7,31},{8,0},{9,1... | collective-permute-start | bytes 196616 | tf_op jit(solution)/shard_map/ag3_lastdown/ppermute | solution.py:155
  120.8 2.3 %collective-permute-done.29.refs_10_ = f32[128,128]{1,0:T(8,128)S(1)} collective-permute-done((f32[128,128]{1,0:T(8,128)S(1)}, f32[128,128]{1,0:T(8,128)S(1)}, u32[]{:S(2)}, u32[]{:S(2)}) %collective-permute-start.29) | collective-permute-done | bytes 65568 | tf_op jit(solution)/shard_map/ag3_lastup/ppermute | solution.py:155
  123.6 0.7 copy.7.refs_6_
  124.3 8.8 %second_factor.1 = (f32[128,128]{1,0:T(8,128)}, f32[128,128]{1,0:T(8,128)}) custom-call(f32[2048,256]{1,0:T(8,128)} %get-tuple-element.35.y2_ref.refs_1_), custom_call_target="tpu_custom_call" | custom-call | tf_op jit(solution)/shard_map/second_factor/pallas_call | solution.py:460
  134.0 14.9 %last_step.1 = (f32[64,128]{1,0:T(8,128)}, f32[64,128]{1,0:T(8,128)}, f32[1,128]{1,0:T(1,128)}) custom-call(s32[1]{0:T(128)} %bitcast.refs_0_, f32[2048,256]{1,0:T(8,128)} %get-tuple-element.35.y2_ref.refs_1_, f32[2048,128]{1,0:T(8,128)} %get-tuple-element.36.refs_2_, f32[128,128]{1,0:T(8,128)} %get-tuple-element.37.refs_3_, ...), custom_call_target="tpu_custom_call" | custom-call | tf_op jit(solution)/shard_map/last_step/pallas_call | solution.py:468
  148.9 1.2 pad_maximum_fusion.1
  (118 shorter events, 5.3 us)
Async XLA Ops:
  3.6 5.4 %collective-permute-start = (f32[136,128]{1,0:T(8,128)S(1)}, f32[136,128]{1,0:T(8,128)S(1)}, u32[]{:S(2)}, u32[]{:S(2)}) collective-permute-start(f32[136,128]{1,0:T(8,128)S(1)} %pad_maximum_fusion), channel_id=1, source_target_pairs={{0,2},{1,3},{2,0},{3,1},{4,6},{5,7},{6,4},{7,5},{8,10},{9,11},{10,... | collective-permute-start | bytes 208904 | tf_op jit(solution)/shard_map/ag1_x/ppermute | solution.py:155
  6.6 4.3 %collective-permute-start.1 = (f32[136,128]{1,0:T(8,128)S(1)}, f32[136,128]{1,0:T(8,128)S(1)}, u32[]{:S(2)}, u32[]{:S(2)}) collective-permute-start(f32[136,128]{1,0:T(8,128)S(1)} %pad_maximum_fusion), channel_id=1, source_target_pairs={{0,4},{1,5},{2,6},{3,7},{4,0},{5,1},{6,2},{7,3},{8,12},{9,13},{10,... | collective-permute-start | bytes 208904 | tf_op jit(solution)/shard_map/ag1_y/ppermute | solution.py:155
  8.1 5.2 %collective-permute-start.2 = (f32[136,128]{1,0:T(8,128)S(1)}, f32[136,128]{1,0:T(8,128)S(1)}, u32[]{:S(2)}, u32[]{:S(2)}) collective-permute-start(f32[136,128]{1,0:T(8,128)S(1)} %pad_maximum_fusion), channel_id=1, source_target_pairs={{0,6},{1,7},{2,4},{3,5},{4,2},{5,3},{6,0},{7,1},{8,14},{9,15},{10,... | collective-permute-start | bytes 208904 | tf_op jit(solution)/shard_map/ag1_xy/ppermute | solution.py:155
  13.3 24.3 %copy-start.5 = (f32[544,128]{1,0:T(8,128)}, f32[544,128]{1,0:T(8,128)S(1)}, u32[]{:S(2)}) copy-start(f32[544,128]{1,0:T(8,128)S(1)} %constant_dynamic-update-slice_fusion.refs_2_) | copy-start | bytes 835588
  13.3 11.4 %collective-permute-start.3 = (f32[544,128]{1,0:T(8,128)S(1)}, f32[544,128]{1,0:T(8,128)S(1)}, u32[]{:S(2)}, u32[]{:S(2)}) collective-permute-start(f32[544,128]{1,0:T(8,128)S(1)} %constant_dynamic-update-slice_fusion.refs_2_), channel_id=1, source_target_pairs={{0,8},{1,9},{2,10},{3,11},{4,12},{5,13},{6,14},{7,15},{8,16},{9,17... | collective-permute-start | bytes 835592 | tf_op jit(solution)/shard_map/ag1_up/ppermute | solution.py:155
  14.9 13.9 %collective-permute-start.4 = (f32[544,128]{1,0:T(8,128)S(1)}, f32[544,128]{1,0:T(8,128)S(1)}, u32[]{:S(2)}, u32[]{:S(2)}) collective-permute-start(f32[544,128]{1,0:T(8,128)S(1)} %constant_dynamic-update-slice_fusion.refs_2_), channel_id=1, source_target_pairs={{0,24},{1,25},{2,26},{3,27},{4,28},{5,29},{6,30},{7,31},{8,0},{9,1... | collective-permute-start | bytes 835592 | tf_op jit(solution)/shard_map/ag1_down/ppermute | solution.py:155
  17.2 20.3 %collective-permute-start.7 = (f32[544,128]{1,0:T(8,128)S(1)}, f32[544,128]{1,0:T(8,128)S(1)}, u32[]{:S(2)}, u32[]{:S(2)}) collective-permute-start(f32[544,128]{1,0:T(8,128)S(1)} %constant_dynamic-update-slice_fusion.refs_2_), channel_id=1, source_target_pairs={{0,1},{1,0},{2,3},{3,2},{4,5},{5,4},{6,7},{7,6},{8,9},{9,8},{10,11... | collective-permute-start | bytes 835592 | tf_op jit(solution)/shard_map/ag1_core0/ppermute | solution.py:155
  24.7 12.9 %copy-start = (f32[544,128]{1,0:T(8,128)}, f32[544,128]{1,0:T(8,128)S(1)}, u32[]{:S(2)}) copy-start(f32[544,128]{1,0:T(8,128)S(1)} %collective-permute-done.3.refs_3_) | copy-start | bytes 835588
  24.7 9.6 %collective-permute-start.5 = (f32[272,128]{1,0:T(8,128)S(1)}, f32[272,128]{1,0:T(8,128)S(1)}, u32[]{:S(2)}, u32[]{:S(2)}) collective-permute-start(f32[272,128]{1,0:T(8,128)S(1)} %slice.40), channel_id=1, source_target_pairs={{0,8},{1,9},{2,10},{3,11},{4,12},{5,13},{6,14},{7,15},{8,16},{9,17... | collective-permute-start | bytes 417800 | tf_op jit(solution)/shard_map/ag1_lastup/ppermute | solution.py:155
  28.8 6.6 %collective-permute-start.6 = (f32[272,128]{1,0:T(8,128)S(1)}, f32[272,128]{1,0:T(8,128)S(1)}, u32[]{:S(2)}, u32[]{:S(2)}) collective-permute-start(f32[272,128]{1,0:T(8,128)S(1)} %slice.41), channel_id=1, source_target_pairs={{0,24},{1,25},{2,26},{3,27},{4,28},{5,29},{6,30},{7,31},{8,0},{9,1... | collective-permute-start | bytes 417800 | tf_op jit(solution)/shard_map/ag1_lastdown/ppermute | solution.py:155
  31.2 6.3 %collective-permute-start.8 = (f32[544,128]{1,0:T(8,128)S(1)}, f32[544,128]{1,0:T(8,128)S(1)}, u32[]{:S(2)}, u32[]{:S(2)}) collective-permute-start(f32[544,128]{1,0:T(8,128)S(1)} %collective-permute-done.3.refs_3_), channel_id=1, source_target_pairs={{0,1},{1,0},{2,3},{3,2},{4,5},{5,4},{6,7},{7,6},{8,9},{9,8},{10,11... | collective-permute-start | bytes 835592 | tf_op jit(solution)/shard_map/ag1_core1/ppermute | solution.py:155
  31.2 6.3 %collective-permute-start.9 = (f32[544,128]{1,0:T(8,128)S(1)}, f32[544,128]{1,0:T(8,128)S(1)}, u32[]{:S(2)}, u32[]{:S(2)}) collective-permute-start(f32[544,128]{1,0:T(8,128)S(1)} %collective-permute-done.4.refs_4_), channel_id=1, source_target_pairs={{0,1},{1,0},{2,3},{3,2},{4,5},{5,4},{6,7},{7,6},{8,9},{9,8},{10,11... | collective-permute-start | bytes 835592 | tf_op jit(solution)/shard_map/ag1_core2/ppermute | solution.py:155
  34.3 3.2 %collective-permute-start.10 = (f32[272,128]{1,0:T(8,128)S(1)}, f32[272,128]{1,0:T(8,128)S(1)}, u32[]{:S(2)}, u32[]{:S(2)}) collective-permute-start(f32[272,128]{1,0:T(8,128)S(1)} %collective-permute-done.5.refs_5_), channel_id=1, source_target_pairs={{0,1},{1,0},{2,3},{3,2},{4,5},{5,4},{6,7},{7,6},{8,9},{9,8},{10,11... | collective-permute-start | bytes 417800 | tf_op jit(solution)/shard_map/ag1_core3/ppermute | solution.py:155
  35.4 2.1 %collective-permute-start.11 = (f32[272,128]{1,0:T(8,128)S(1)}, f32[272,128]{1,0:T(8,128)S(1)}, u32[]{:S(2)}, u32[]{:S(2)}) collective-permute-start(f32[272,128]{1,0:T(8,128)S(1)} %collective-permute-done.6.refs_6_), channel_id=1, source_target_pairs={{0,1},{1,0},{2,3},{3,2},{4,5},{5,4},{6,7},{7,6},{8,9},{9,8},{10,11... | collective-permute-start | bytes 417800 | tf_op jit(solution)/shard_map/ag1_core4/ppermute | solution.py:155
  42.2 4.7 %collective-permute-start.12 = (f32[128,128]{1,0:T(8,128)}, f32[128,128]{1,0:T(8,128)S(1)}, u32[]{:S(2)}, u32[]{:S(2)}) collective-permute-start(f32[128,128]{1,0:T(8,128)} %get-tuple-element.34), channel_id=1, source_target_pairs={{0,2},{1,3},{2,0},{3,1},{4,6},{5,7},{6,4},{7,5},{8,10},{9,11},{10,... | collective-permute-start | bytes 196616 | tf_op jit(solution)/shard_map/ag2_x/ppermute | solution.py:155
  43.1 5.2 %collective-permute-start.13 = (f32[128,128]{1,0:T(8,128)}, f32[128,128]{1,0:T(8,128)S(1)}, u32[]{:S(2)}, u32[]{:S(2)}) collective-permute-start(f32[128,128]{1,0:T(8,128)} %get-tuple-element.34), channel_id=1, source_target_pairs={{0,4},{1,5},{2,6},{3,7},{4,0},{5,1},{6,2},{7,3},{8,12},{9,13},{10,... | collective-permute-start | bytes 196616 | tf_op jit(solution)/shard_map/ag2_y/ppermute | solution.py:155
  43.7 5.4 %collective-permute-start.14 = (f32[128,128]{1,0:T(8,128)}, f32[128,128]{1,0:T(8,128)S(1)}, u32[]{:S(2)}, u32[]{:S(2)}) collective-permute-start(f32[128,128]{1,0:T(8,128)} %get-tuple-element.34), channel_id=1, source_target_pairs={{0,6},{1,7},{2,4},{3,5},{4,2},{5,3},{6,0},{7,1},{8,14},{9,15},{10,... | collective-permute-start | bytes 196616 | tf_op jit(solution)/shard_map/ag2_xy/ppermute | solution.py:155
  49.1 25.9 %copy-start.4 = (f32[512,128]{1,0:T(8,128)}, f32[512,128]{1,0:T(8,128)S(1)}, u32[]{:S(2)}) copy-start(f32[512,128]{1,0:T(8,128)S(1)} %constant_dynamic-update-slice_fusion.6.refs_5_) | copy-start | bytes 786436
  49.1 11.0 %collective-permute-start.15 = (f32[512,128]{1,0:T(8,128)S(1)}, f32[512,128]{1,0:T(8,128)S(1)}, u32[]{:S(2)}, u32[]{:S(2)}) collective-permute-start(f32[512,128]{1,0:T(8,128)S(1)} %constant_dynamic-update-slice_fusion.6.refs_5_), channel_id=1, source_target_pairs={{0,8},{1,9},{2,10},{3,11},{4,12},{5,13},{6,14},{7,15},{8,16},{9,17... | collective-permute-start | bytes 786440 | tf_op jit(solution)/shard_map/ag2_up/ppermute | solution.py:155
  50.3 13.5 %collective-permute-start.16 = (f32[512,128]{1,0:T(8,128)S(1)}, f32[512,128]{1,0:T(8,128)S(1)}, u32[]{:S(2)}, u32[]{:S(2)}) collective-permute-start(f32[512,128]{1,0:T(8,128)S(1)} %constant_dynamic-update-slice_fusion.6.refs_5_), channel_id=1, source_target_pairs={{0,24},{1,25},{2,26},{3,27},{4,28},{5,29},{6,30},{7,31},{8,0},{9,1... | collective-permute-start | bytes 786440 | tf_op jit(solution)/shard_map/ag2_down/ppermute | solution.py:155
  60.1 14.9 %copy-start.2 = (f32[512,128]{1,0:T(8,128)}, f32[512,128]{1,0:T(8,128)S(1)}, u32[]{:S(2)}) copy-start(f32[512,128]{1,0:T(8,128)S(1)} %collective-permute-done.15.refs_6_) | copy-start | bytes 786436
  60.1 15.5 %collective-permute-start.17 = (f32[256,128]{1,0:T(8,128)S(1)}, f32[256,128]{1,0:T(8,128)S(1)}, u32[]{:S(2)}, u32[]{:S(2)}) collective-permute-start(f32[256,128]{1,0:T(8,128)S(1)} %slice.42), channel_id=1, source_target_pairs={{0,8},{1,9},{2,10},{3,11},{4,12},{5,13},{6,14},{7,15},{8,16},{9,17... | collective-permute-start | bytes 393224 | tf_op jit(solution)/shard_map/ag2_lastup/ppermute | solution.py:155
  63.8 11.7 %copy-start.3 = (f32[512,128]{1,0:T(8,128)}, f32[512,128]{1,0:T(8,128)S(1)}, u32[]{:S(2)}) copy-start(f32[512,128]{1,0:T(8,128)S(1)} %collective-permute-done.16.refs_7_) | copy-start | bytes 786436
  63.9 12.2 %collective-permute-start.18 = (f32[256,128]{1,0:T(8,128)S(1)}, f32[256,128]{1,0:T(8,128)S(1)}, u32[]{:S(2)}, u32[]{:S(2)}) collective-permute-start(f32[256,128]{1,0:T(8,128)S(1)} %slice.43), channel_id=1, source_target_pairs={{0,24},{1,25},{2,26},{3,27},{4,28},{5,29},{6,30},{7,31},{8,0},{9,1... | collective-permute-start | bytes 393224 | tf_op jit(solution)/shard_map/ag2_lastdown/ppermute | solution.py:155
  75.0 8.2 %collective-permute-start.19 = (f32[512,128]{1,0:T(8,128)S(1)}, f32[512,128]{1,0:T(8,128)S(1)}, u32[]{:S(2)}, u32[]{:S(2)}) collective-permute-start(f32[512,128]{1,0:T(8,128)S(1)} %constant_dynamic-update-slice_fusion.6.refs_5_), channel_id=1, source_target_pairs={{0,1},{1,0},{2,3},{3,2},{4,5},{5,4},{6,7},{7,6},{8,9},{9,8},{10,11... | collective-permute-start | bytes 786440 | tf_op jit(solution)/shard_map/ag2_core0/ppermute | solution.py:155
  75.0 8.2 %collective-permute-start.20 = (f32[512,128]{1,0:T(8,128)S(1)}, f32[512,128]{1,0:T(8,128)S(1)}, u32[]{:S(2)}, u32[]{:S(2)}) collective-permute-start(f32[512,128]{1,0:T(8,128)S(1)} %collective-permute-done.15.refs_6_), channel_id=1, source_target_pairs={{0,1},{1,0},{2,3},{3,2},{4,5},{5,4},{6,7},{7,6},{8,9},{9,8},{10,11... | collective-permute-start | bytes 786440 | tf_op jit(solution)/shard_map/ag2_core1/ppermute | solution.py:155
  75.5 7.7 %collective-permute-start.21 = (f32[512,128]{1,0:T(8,128)S(1)}, f32[512,128]{1,0:T(8,128)S(1)}, u32[]{:S(2)}, u32[]{:S(2)}) collective-permute-start(f32[512,128]{1,0:T(8,128)S(1)} %collective-permute-done.16.refs_7_), channel_id=1, source_target_pairs={{0,1},{1,0},{2,3},{3,2},{4,5},{5,4},{6,7},{7,6},{8,9},{9,8},{10,11... | collective-permute-start | bytes 786440 | tf_op jit(solution)/shard_map/ag2_core2/ppermute | solution.py:155
  75.6 7.6 %collective-permute-start.22 = (f32[256,128]{1,0:T(8,128)S(1)}, f32[256,128]{1,0:T(8,128)S(1)}, u32[]{:S(2)}, u32[]{:S(2)}) collective-permute-start(f32[256,128]{1,0:T(8,128)S(1)} %collective-permute-done.17.refs_8_), channel_id=1, source_target_pairs={{0,1},{1,0},{2,3},{3,2},{4,5},{5,4},{6,7},{7,6},{8,9},{9,8},{10,11... | collective-permute-start | bytes 393224 | tf_op jit(solution)/shard_map/ag2_core3/ppermute | solution.py:155
  76.0 7.2 %collective-permute-start.23 = (f32[256,128]{1,0:T(8,128)S(1)}, f32[256,128]{1,0:T(8,128)S(1)}, u32[]{:S(2)}, u32[]{:S(2)}) collective-permute-start(f32[256,128]{1,0:T(8,128)S(1)} %collective-permute-done.18.refs_9_), channel_id=1, source_target_pairs={{0,1},{1,0},{2,3},{3,2},{4,5},{5,4},{6,7},{7,6},{8,9},{9,8},{10,11... | collective-permute-start | bytes 393224 | tf_op jit(solution)/shard_map/ag2_core4/ppermute | solution.py:155
  84.2 39.5 %copy-start.30 = (f32[64]{0:T(128)S(1)}, f32[64]{0:T(128)}, u32[]{:S(2)}) copy-start(f32[64]{0:T(128)} %param.9) | copy-start | bytes 772
  100.3 4.3 %collective-permute-start.24 = (f32[64,128]{1,0:T(8,128)}, f32[64,128]{1,0:T(8,128)S(1)}, u32[]{:S(2)}, u32[]{:S(2)}) collective-permute-start(f32[64,128]{1,0:T(8,128)} %get-tuple-element.40), channel_id=1, source_target_pairs={{0,2},{1,3},{2,0},{3,1},{4,6},{5,7},{6,4},{7,5},{8,10},{9,11},{10,... | collective-permute-start | bytes 98312 | tf_op jit(solution)/shard_map/ag3_x/ppermute | solution.py:155
  102.6 4.1 %collective-permute-start.25 = (f32[64,128]{1,0:T(8,128)}, f32[64,128]{1,0:T(8,128)S(1)}, u32[]{:S(2)}, u32[]{:S(2)}) collective-permute-start(f32[64,128]{1,0:T(8,128)} %get-tuple-element.40), channel_id=1, source_target_pairs={{0,4},{1,5},{2,6},{3,7},{4,0},{5,1},{6,2},{7,3},{8,12},{9,13},{10,... | collective-permute-start | bytes 98312 | tf_op jit(solution)/shard_map/ag3_y/ppermute | solution.py:155
  104.0 5.0 %collective-permute-start.26 = (f32[64,128]{1,0:T(8,128)}, f32[64,128]{1,0:T(8,128)S(1)}, u32[]{:S(2)}, u32[]{:S(2)}) collective-permute-start(f32[64,128]{1,0:T(8,128)} %get-tuple-element.40), channel_id=1, source_target_pairs={{0,6},{1,7},{2,4},{3,5},{4,2},{5,3},{6,0},{7,1},{8,14},{9,15},{10,... | collective-permute-start | bytes 98312 | tf_op jit(solution)/shard_map/ag3_xy/ppermute | solution.py:155
  109.0 24.3 %copy-start.14 = (f32[256,128]{1,0:T(8,128)}, f32[256,128]{1,0:T(8,128)S(1)}, u32[]{:S(2)}) copy-start(f32[256,128]{1,0:T(8,128)S(1)} %constant_dynamic-update-slice_fusion.10.refs_7_) | copy-start | bytes 393220
  109.0 7.3 %collective-permute-start.27 = (f32[256,128]{1,0:T(8,128)S(1)}, f32[256,128]{1,0:T(8,128)S(1)}, u32[]{:S(2)}, u32[]{:S(2)}) collective-permute-start(f32[256,128]{1,0:T(8,128)S(1)} %constant_dynamic-update-slice_fusion.10.refs_7_), channel_id=1, source_target_pairs={{0,8},{1,9},{2,10},{3,11},{4,12},{5,13},{6,14},{7,15},{8,16},{9,17... | collective-permute-start | bytes 393224 | tf_op jit(solution)/shard_map/ag3_up/ppermute | solution.py:155
  109.0 7.5 %collective-permute-start.28 = (f32[256,128]{1,0:T(8,128)S(1)}, f32[256,128]{1,0:T(8,128)S(1)}, u32[]{:S(2)}, u32[]{:S(2)}) collective-permute-start(f32[256,128]{1,0:T(8,128)S(1)} %constant_dynamic-update-slice_fusion.10.refs_7_), channel_id=1, source_target_pairs={{0,24},{1,25},{2,26},{3,27},{4,28},{5,29},{6,30},{7,31},{8,0},{9,1... | collective-permute-start | bytes 393224 | tf_op jit(solution)/shard_map/ag3_down/ppermute | solution.py:155
  112.8 20.4 %collective-permute-start.31 = (f32[256,128]{1,0:T(8,128)S(1)}, f32[256,128]{1,0:T(8,128)S(1)}, u32[]{:S(2)}, u32[]{:S(2)}) collective-permute-start(f32[256,128]{1,0:T(8,128)S(1)} %constant_dynamic-update-slice_fusion.10.refs_7_), channel_id=1, source_target_pairs={{0,1},{1,0},{2,3},{3,2},{4,5},{5,4},{6,7},{7,6},{8,9},{9,8},{10,11... | collective-permute-start | bytes 393224 | tf_op jit(solution)/shard_map/ag3_core0/ppermute | solution.py:155
  116.3 16.9 %copy-start.6 = (f32[256,128]{1,0:T(8,128)}, f32[256,128]{1,0:T(8,128)S(1)}, u32[]{:S(2)}) copy-start(f32[256,128]{1,0:T(8,128)S(1)} %collective-permute-done.27.refs_8_) | copy-start | bytes 393220
  116.4 6.8 %collective-permute-start.29 = (f32[128,128]{1,0:T(8,128)S(1)}, f32[128,128]{1,0:T(8,128)S(1)}, u32[]{:S(2)}, u32[]{:S(2)}) collective-permute-start(f32[128,128]{1,0:T(8,128)S(1)} %slice.44), channel_id=1, source_target_pairs={{0,8},{1,9},{2,10},{3,11},{4,12},{5,13},{6,14},{7,15},{8,16},{9,17... | collective-permute-start | bytes 196616 | tf_op jit(solution)/shard_map/ag3_lastup/ppermute | solution.py:155
  116.4 16.8 %collective-permute-start.32 = (f32[256,128]{1,0:T(8,128)S(1)}, f32[256,128]{1,0:T(8,128)S(1)}, u32[]{:S(2)}, u32[]{:S(2)}) collective-permute-start(f32[256,128]{1,0:T(8,128)S(1)} %collective-permute-done.27.refs_8_), channel_id=1, source_target_pairs={{0,1},{1,0},{2,3},{3,2},{4,5},{5,4},{6,7},{7,6},{8,9},{9,8},{10,11... | collective-permute-start | bytes 393224 | tf_op jit(solution)/shard_map/ag3_core1/ppermute | solution.py:155
  116.5 16.8 %copy-start.7 = (f32[256,128]{1,0:T(8,128)}, f32[256,128]{1,0:T(8,128)S(1)}, u32[]{:S(2)}) copy-start(f32[256,128]{1,0:T(8,128)S(1)} %collective-permute-done.28.refs_9_) | copy-start | bytes 393220
  116.5 16.7 %collective-permute-start.33 = (f32[256,128]{1,0:T(8,128)S(1)}, f32[256,128]{1,0:T(8,128)S(1)}, u32[]{:S(2)}, u32[]{:S(2)}) collective-permute-start(f32[256,128]{1,0:T(8,128)S(1)} %collective-permute-done.28.refs_9_), channel_id=1, source_target_pairs={{0,1},{1,0},{2,3},{3,2},{4,5},{5,4},{6,7},{7,6},{8,9},{9,8},{10,11... | collective-permute-start | bytes 393224 | tf_op jit(solution)/shard_map/ag3_core2/ppermute | solution.py:155
  117.1 6.0 %collective-permute-start.30 = (f32[128,128]{1,0:T(8,128)S(1)}, f32[128,128]{1,0:T(8,128)S(1)}, u32[]{:S(2)}, u32[]{:S(2)}) collective-permute-start(f32[128,128]{1,0:T(8,128)S(1)} %slice.45), channel_id=1, source_target_pairs={{0,24},{1,25},{2,26},{3,27},{4,28},{5,29},{6,30},{7,31},{8,0},{9,1... | collective-permute-start | bytes 196616 | tf_op jit(solution)/shard_map/ag3_lastdown/ppermute | solution.py:155
  123.1 10.2 %copy-start.26 = (f32[128,128]{1,0:T(8,128)}, f32[128,128]{1,0:T(8,128)S(1)}, u32[]{:S(2)}) copy-start(f32[128,128]{1,0:T(8,128)S(1)} %collective-permute-done.29.refs_10_) | copy-start | bytes 196612
  123.1 10.1 %collective-permute-start.34 = (f32[128,128]{1,0:T(8,128)S(1)}, f32[128,128]{1,0:T(8,128)S(1)}, u32[]{:S(2)}, u32[]{:S(2)}) collective-permute-start(f32[128,128]{1,0:T(8,128)S(1)} %collective-permute-done.29.refs_10_), channel_id=1, source_target_pairs={{0,1},{1,0},{2,3},{3,2},{4,5},{5,4},{6,7},{7,6},{8,9},{9,8},{10,11... | collective-permute-start | bytes 196616 | tf_op jit(solution)/shard_map/ag3_core3/ppermute | solution.py:155
  123.1 10.2 %copy-start.27 = (f32[128,128]{1,0:T(8,128)}, f32[128,128]{1,0:T(8,128)S(1)}, u32[]{:S(2)}) copy-start(f32[128,128]{1,0:T(8,128)S(1)} %collective-permute-done.30.refs_11_) | copy-start | bytes 196612
  123.1 10.1 %collective-permute-start.35 = (f32[128,128]{1,0:T(8,128)S(1)}, f32[128,128]{1,0:T(8,128)S(1)}, u32[]{:S(2)}, u32[]{:S(2)}) collective-permute-start(f32[128,128]{1,0:T(8,128)S(1)} %collective-permute-done.30.refs_11_), channel_id=1, source_target_pairs={{0,1},{1,0},{2,3},{3,2},{4,5},{5,4},{6,7},{7,6},{8,9},{9,8},{10,11... | collective-permute-start | bytes 196616 | tf_op jit(solution)/shard_map/ag3_core4/ppermute | solution.py:155
  134.0 14.9 %copy-start.31 = (f32[1,128]{1,0:T(1,128)S(1)}, f32[1,128]{1,0:T(1,128)}, u32[]{:S(2)}) copy-start(f32[1,128]{1,0:T(1,128)} %get-tuple-element.43) | copy-start | bytes 1540
  (20 other events, 40.5 us)

commit v3 on v2

--- a/solution.py
+++ b/solution.py
@@ -12,8 +12,8 @@
 CHUNK = 512
 
 
-def params():
-    return pltpu.CompilerParams(vmem_limit_bytes=56 << 20)
+def params(mebibytes=56):
+    return pltpu.CompilerParams(vmem_limit_bytes=mebibytes << 20)
 
 
 def mm(a, b, ca=1, cb=0):
@@ -131,72 +131,69 @@
     return jnp.concatenate(rows, 0)
 
 
-def device_of(me, dz, k, dc, rings):
-    z = lax.rem(me // 8 + (dz + rings), rings)
-    low = lax.rem(me, 8)
-    return z * 8 + jnp.bitwise_xor(low, 2 * k + dc)
-
-
 def layout_of(rings):
-    half = rings // 2
-    chips = [(0, (0, 1, 2, 3))]
-    for t in range(1, half):
-        chips += [(-t, (0, 1, 2, 3)), (t, (0, 1, 2, 3))]
-    chips += [(-half, (0, 1)), (half, (2, 3))]
-    return [chip + (dc,) for dc in (0, 1) for chip in chips]
+    far = [8 * z for z in range(1, rings)]
+    chips = [[0, 2, 4, 6], far] + [[d ^ m for d in far] for m in (2, 4, 6)]
+    return chips + [[d ^ 1 for d in piece] for piece in chips]
+
+
+def pack_blocks(*refs):
+    parts, out_ref = refs[:-1], refs[-1]
+    at = 0
+    for part in parts:
+        out_ref[at : at + part.shape[0], :] = part[...]
+        at += part.shape[0]
+
+
+def packed(parts, name):
+    rows = sum(part.shape[0] for part in parts)
+    with jax.named_scope(name):
+        return pl.pallas_call(
+            pack_blocks,
+            out_shape=shape(rows, parts[0].shape[1]),
+            in_specs=[VMEM] * len(parts),
+            out_specs=VMEM,
+            compiler_params=params(2),
+            cost_estimate=cost(0.5),
+            name=name,
+        )(*parts)
 
 
 def gather(block, n, tag):
-    rings = n // 8
-    half = rings // 2
-
-    def send(x, pairs, name):
+    def swap(x, m, name):
         with jax.named_scope(tag + name):
-            return lax.ppermute(x, "blk", pairs)
-
-    def swap(x, m, name):
-        return send(x, [(i, i ^ m) for i in range(n)], name)
-
-    def turn(x, d, name):
-        pairs = [(i, ((i // 8 + d) % rings) * 8 + i % 8) for i in range(n)]
-        return send(x, pairs, name)
-
-    parts = [block, swap(block, 2, "_x"), swap(block, 4, "_y"), swap(block, 6, "_xy")]
-    own = jnp.concatenate(parts, 0)
-    near, up, down = [own], own, own
-    for t in range(1, half):
-        up, down = turn(up, 1, "_up"), turn(down, -1, "_down")
-        near += [up, down]
-    middle = own.shape[0] // 2
-    near.append(turn(up[:middle], 1, "_lastup"))
-    near.append(turn(down[middle:], -1, "_lastdown"))
-    return near + [swap(x, 1, f"_core{i}") for i, x in enumerate(near)]
-
-
-def assemble(me, pieces, rows, rings, place):
-    for piece, (dz, ks, dc) in zip(pieces, layout_of(rings)):
-        for slot, k in enumerate(ks):
-            place(piece, slot, device_of(me, dz, k, dc, rings))
-
-
-def first_product(rings, rows, me_ref, kernel_ref, *refs):
-    pieces, (y_ref, ky_ref, diag_ref, table) = refs[:-4], refs[-4:]
+            return lax.ppermute(x, "blk", [(i, i ^ m) for i in range(n)])
+
+    far = [swap(block, 8 * z, f"_z{z}") for z in range(n // 8 - 1, 0, -1)][::-1]
+    near = [block] + [swap(block, 2 * k, f"_n{k}") for k in (3, 1, 2)]
+    near = [near[0], near[2], near[3], near[1]]
+    column = packed(far, tag + "_column")
+    corner = swap(column, 6, "_c3")
+    chips = [packed(near, tag + "_near"), column, swap(column, 2, "_c1"), swap(column, 4, "_c2"), corner]
+    return chips + [swap(x, 1, f"_core{i}") for i, x in enumerate(chips)]
+
+
+def assemble(me, pieces, rings, place):
+    for piece, distances in zip(pieces, layout_of(rings)):
+        for slot, distance in enumerate(distances):
+            place(piece, slot, jnp.bitwise_xor(me, distance))
+
+
+def first_product(rings, rows, me_ref, kernel_ref, diag_ref, *refs):
+    pieces, (y_ref, ky_ref) = refs[:-2], refs[-2:]
     width = y_ref.shape[1] // 2
-    step = 2 * rows + 8
 
     def place(piece, slot, device):
-        base = slot * step
+        base = slot * 2 * rows
         at = pl.ds(pl.multiple_of(device * rows, rows), rows)
         y_ref[at, :width] = piece[base : base + rows, :]
         y_ref[at, width:] = piece[base + rows : base + 2 * rows, :]
-        table[pl.ds(device, 1), :] = piece[base + 2 * rows : base + 2 * rows + 1, :]
-
-    table[...] = jnp.zeros_like(table)
-    assemble(me_ref[0], pieces, rows, rings, place)
-    diag_ref[...] = table[...].T
+
+    assemble(me_ref[0], pieces, rings, place)
     result = mm3(kernel_ref[...], y_ref[...])
     ky_ref[:rows, :] = result[:, :width]
-    ky_ref[rows:, :] = result[:, width:]
+    ky_ref[rows : 2 * rows, :] = result[:, width:]
+    ky_ref[2 * rows :, :] = jnp.broadcast_to(diag_ref[...], (8, width))
 
 
 def metric_head(y_ref, metric_ref, upper_ref):
@@ -273,18 +270,22 @@
         y2_ref[at, width:] = divided(y2_ref[at, width:], diag_ref[:rows, b : b + 1], values)
 
 
-def with_product(rings, rows, me_ref, kernel_ref, y_ref, factor_ref, diag_ref, *refs):
-    pieces = refs[:-6]
-    y2_ref, kx_ref, small_ref, norm_ref, kw_ref, ky_ref = refs[-6:]
+def with_product(rings, rows, me_ref, kernel_ref, y_ref, factor_ref, *refs):
+    pieces = refs[:-8]
+    y2_ref, kx_ref, small_ref, norm_ref, kw_ref, ky_ref, table, diag_ref = refs[-8:]
     width = kx_ref.shape[1]
+    step = 2 * rows + 8
 
     def place(piece, slot, device):
-        base = slot * 2 * rows
+        base = slot * step
         at = pl.ds(pl.multiple_of(device * rows, rows), rows)
         ky_ref[at, :width] = piece[base : base + rows, :]
         ky_ref[at, width:] = piece[base + rows : base + 2 * rows, :]
-
-    assemble(me_ref[0], pieces, rows, rings, place)
+        table[pl.ds(device, 1), :] = piece[base + 2 * rows : base + 2 * rows + 1, :]
+
+    table[...] = jnp.zeros_like(table)
+    assemble(me_ref[0], pieces, rings, place)
+    diag_ref[...] = table[...].T
     first_step(
         y_ref, ky_ref, factor_ref, diag_ref.at[:rows, :], y2_ref, kx_ref, small_ref, norm_ref
     )
@@ -356,7 +357,7 @@
         at = pl.ds(pl.multiple_of(device * rows, rows), rows)
         image_ref[at, width:] = piece[slot * rows : (slot + 1) * rows, :]
 
-    assemble(me, pieces, rows, rings, place)
+    assemble(me, pieces, rings, place)
     image_ref[:, :width] = kx_ref[...]
     mine = pl.ds(pl.multiple_of(me * rows, rows), rows)
     second_step(
@@ -398,7 +399,7 @@
 SMEM = pl.BlockSpec(memory_space=pltpu.SMEM)
 
 
-def metric_factor(y):
+def metric_factor(y, mebibytes):
     width = y.shape[1] // 2
     with jax.named_scope("metric_head"):
         metric, upper = pl.pallas_call(
@@ -406,7 +407,7 @@
             out_shape=(shape(2 * width, 2 * width), shape(width, width)),
             in_specs=[VMEM],
             out_specs=(VMEM, VMEM),
-            compiler_params=params(),
+            compiler_params=params(mebibytes),
             cost_estimate=cost(7),
             name="metric_head",
         )(y)
@@ -416,31 +417,44 @@
             out_shape=shape(2 * width, 2 * width),
             in_specs=[VMEM, VMEM],
             out_specs=VMEM,
-            compiler_params=params(),
+            compiler_params=params(mebibytes),
             cost_estimate=cost(7),
             name="metric_tail",
         )(metric, upper)
 
 
-def ringed(n, kernel, ritz, search, diag):
+def second_metric(y2, mebibytes):
+    width = y2.shape[1] // 2
+    with jax.named_scope("second_factor"):
+        return pl.pallas_call(
+            second_factor,
+            out_shape=(shape(width, width), shape(width, width)),
+            in_specs=[VMEM],
+            out_specs=(VMEM, VMEM),
+            compiler_params=params(mebibytes),
+            cost_estimate=cost(9),
+            name="second_factor",
+        )(y2)
+
+
+def cubed(n, kernel, ritz, search, diag):
     rows, width = ritz.shape
     rings = n // 8
     total = n * rows
+    lanes = max(n, 128)
     me = lax.axis_index("blk").astype(jnp.int32).reshape(1)
-    lanes = max(128, -(-rows // 128) * 128)
-    extra = jnp.zeros((8, width), F32).at[0, :rows].set(diag)
-    sent = gather(jnp.concatenate([ritz, search, extra], 0), n, "ag1")
-    y, ky_own, diag_table = pl.pallas_call(
+    along = jnp.zeros((1, width), F32).at[0, :rows].set(diag)
+    sent = gather(jnp.concatenate([ritz, search], 0), n, "ag1")
+    y, ky_own = pl.pallas_call(
         lambda *refs: first_product(rings, rows, *refs),
-        out_shape=(shape(total, 2 * width), shape(2 * rows, width), shape(width, max(n, 128))),
-        in_specs=[SMEM, VMEM] + [VMEM] * len(sent),
-        out_specs=(VMEM, VMEM, VMEM),
-        scratch_shapes=[pltpu.VMEM((max(n, 128), width), F32)],
-        compiler_params=params(),
+        out_shape=(shape(total, 2 * width), shape(2 * rows + 8, width)),
+        in_specs=[SMEM, VMEM, VMEM] + [VMEM] * len(sent),
+        out_specs=(VMEM, VMEM),
+        compiler_params=params(16),
         name="first_product",
-    )(me, kernel, *sent)
+    )(me, kernel, along, *sent)
     images = gather(ky_own, n, "ag2")
-    factor = metric_factor(y)
+    factor = metric_factor(y, 12)
     y2, kx, values, norm1, kw_own = pl.pallas_call(
         lambda *refs: with_product(rings, rows, *refs),
         out_shape=(
@@ -450,28 +464,25 @@
             shape(1, width),
             shape(rows, width),
         ),
-        in_specs=[SMEM] + [VMEM] * (4 + len(images)),
+        in_specs=[SMEM] + [VMEM] * (3 + len(images)),
         out_specs=(VMEM,) * 5,
-        scratch_shapes=[pltpu.VMEM((total, 2 * width), F32)],
-        compiler_params=params(),
+        scratch_shapes=[
+            pltpu.VMEM((total, 2 * width), F32),
+            pltpu.VMEM((lanes, width), F32),
+            pltpu.VMEM((width, lanes), F32),
+        ],
+        compiler_params=params(24),
         name="first_step",
-    )(me, kernel, y, factor, diag_table, *images)
+    )(me, kernel, y, factor, *images)
     images2 = gather(kw_own, n, "ag3")
-    cross, factor2 = pl.pallas_call(
-        second_factor,
-        out_shape=(shape(width, width), shape(width, width)),
-        in_specs=[VMEM],
-        out_specs=(VMEM, VMEM),
-        compiler_params=params(),
-        name="second_factor",
-    )(y2)
+    cross, factor2 = second_metric(y2, 12)
     new_ritz, correction, norm2 = pl.pallas_call(
         lambda *refs: last_step(rings, rows, *refs),
         out_shape=(shape(rows, width), shape(rows, width), shape(1, width)),
         in_specs=[SMEM] + [VMEM] * (6 + len(images2)),
         out_specs=(VMEM,) * 3,
         scratch_shapes=[pltpu.VMEM((total, 2 * width), F32)],
-        compiler_params=params(),
+        compiler_params=params(24),
         name="last_step",
     )(me, y2, kx, values, cross, factor2, diag[:, None], *images2)
     return new_ritz, correction, jnp.concatenate([norm1, norm2], 0)
@@ -492,7 +503,7 @@
     y = lax.all_gather(own, axes, axis=0, tiled=True)
     ky = lax.all_gather(product(part), axes, axis=0, tiled=True)
     table = lax.all_gather(diag, axes, axis=0, tiled=True).reshape(n * cols, rows).T
-    factor = metric_factor(y)
+    factor = metric_factor(y, 56)
     y2, kx, values, norm1 = pl.pallas_call(
         first_step,
         out_shape=(shape(total, 2 * width), shape(total, width), shape(width, width), shape(1, width)),
@@ -504,14 +515,7 @@
     held = y2[:, width:].reshape(n, cols, rows, width)
     part2 = lax.dynamic_index_in_dim(held, q, 1, keepdims=False).reshape(n * rows, width)
     kw = lax.all_gather(product(part2), axes, axis=0, tiled=True)
-    cross, factor2 = pl.pallas_call(
-        second_factor,
-        out_shape=(shape(width, width), shape(width, width)),
-        in_specs=[VMEM],
-        out_specs=(VMEM, VMEM),
-        compiler_params=params(),
-        name="second_factor",
-    )(y2)
+    cross, factor2 = second_metric(y2, 56)
     image = jnp.concatenate([kx, kw], 1)
     at = (lax.axis_index("blk") * cols + q) * rows
     new_ritz, correction, norm2 = pl.pallas_call(
@@ -545,8 +549,8 @@
 
     def per_device(kernel, ritz_block, search_block, precond_diag):
         rows = kernel[:, 0, :]
-        if cols == 1 and n % 16 == 0 and ritz_block.shape[0] <= ritz_block.shape[1]:
-            return ringed(n, rows, ritz_block, search_block, precond_diag)
+        if cols == 1 and n >= 16 and n & (n - 1) == 0 and ritz_block.shape[0] <= ritz_block.shape[1]:
+            return cubed(n, rows, ritz_block, search_block, precond_diag)
         return general(n, cols, rows, ritz_block, search_block, precond_diag)
 
     return jax.shard_map(

time: 151 us -> 116 us (0.77)
  waiting for transfers between devices: 42.3 us -> 20.5 us
  Pallas kernels: 59.3 us -> 47.6 us
  local copies, waits for them, and re-layouts: 9.28 us -> 3.22 us
  starting transfers between devices: 36.2 us -> 41.3 us
    ppermute x36 -> x42, waiting for transfers between devices: 42.3 us -> 20.5 us  [swap(): return lax.ppermute(x, 'blk', [(i, i ^ m) for i in range(n)])]
    pallas_call x4 -> x10, Pallas kernels: 43.6 us -> 35.7 us  [the longest x1 13.9 us: cubed(): pl.pallas_call(lambda *refs: last_step(rings, rows, *refs), out_shape=(sh...]
    unnamed x75 -> x10, local copies, waits for them, and re-layouts: 7.85 us -> 2.36 us
    ppermute x36 -> x42, starting transfers between devices: 36.2 us -> 41.3 us  [swap(): return lax.ppermute(x, 'blk', [(i, i ^ m) for i in range(n)])]
    pallas_call x1, Pallas kernels: 8.68 us -> 6.45 us  [metric_factor(): pl.pallas_call(metric_head, out_shape=(shape(2 * width, 2 * width), shape...]
    pallas_call x1, Pallas kernels: 7.02 us -> 5.37 us  [metric_factor(): pl.pallas_call(metric_tail, out_shape=shape(2 * width, 2 * width), in_spe...]
  transfers between devices with their start and end apart: 36 -> 42, of which waited for: 16 -> 12; matrix products, arithmetic and copies ran while one was open for 3% -> 1% of each run, Pallas kernels for 16% -> 17%
where the time goes in v3:
time: 116 us; the launch traced here: 115 us
  Pallas kernels  47.6 us (41%)
  starting transfers between devices  41.3 us (36%)
  waiting for transfers between devices  20.5 us (18%)
  local copies, waits for them, and re-layouts  3.22 us (3%)
  other arithmetic  1.86 us (2%)
    ppermute x42, starting transfers between devices, swap(): return lax.ppermute(x, 'blk', [(i, i ^ m) for i in range(n)])  41.3 us
    ppermute x42, waiting for transfers between devices, swap(): return lax.ppermute(x, 'blk', [(i, i ^ m) for i in range(n)])  20.5 us
    pallas_call x1, Pallas kernels, cubed(): pl.pallas_call(lambda *refs: last_step(rings, rows, *refs), out_shape=(sh...  13.9 us
    pallas_call x1, Pallas kernels, cubed(): pl.pallas_call(lambda *refs: with_product(rings, rows, *refs), out_shape=...  13.5 us
    pallas_call x1, Pallas kernels, second_metric(): pl.pallas_call(second_factor, out_shape=(shape(width, width), shape(width...  6.62 us
    pallas_call x1, Pallas kernels, metric_factor(): pl.pallas_call(metric_head, out_shape=(shape(2 * width, 2 * width), shape...  6.45 us
    pallas_call x1, Pallas kernels, metric_factor(): pl.pallas_call(metric_tail, out_shape=shape(2 * width, 2 * width), in_spe...  5.37 us
    unnamed x10, local copies, waits for them, and re-layouts  2.36 us
  transfers between devices with their start and end apart: 42, of which 12 were waited for; matrix products, arithmetic and copies ran while one was open for 1% of the time, Pallas kernels for 17%

profile of v3, /device:TPU:0, one launch (start us, length us, event | category | flops | bytes accessed | tf_op | source)
XLA Modules:
  0.0 115.3 jit_solution(10937608793515438962)
XLA Ops:
  0.6 0.8 constant_dynamic-update-slice_fusion.1
  1.5 0.8 constant_dynamic-update-slice_fusion.refs_0_
  2.2 3.1 %collective-permute-start.3 = (f32[128,128]{1,0:T(8,128)S(1)}, f32[128,128]{1,0:T(8,128)S(1)}, u32[]{:S(2)}, u32[]{:S(2)}) collective-permute-start(f32[128,128]{1,0:T(8,128)S(1)} %constant_dynamic-update-slice_fusion.refs_0_), channel_id=1, source_target_pairs={{0,8},{1,9},{2,10},{3,11},{4,12},{5,13},{6,14},{7,15},{8,0},{9,1},... | collective-permute-start | bytes 196616 | tf_op jit(solution)/shard_map/ag1_z1/ppermute | solution.py:165
  5.3 2.6 %collective-permute-start.4 = (f32[128,128]{1,0:T(8,128)S(1)}, f32[128,128]{1,0:T(8,128)S(1)}, u32[]{:S(2)}, u32[]{:S(2)}) collective-permute-start(f32[128,128]{1,0:T(8,128)S(1)} %constant_dynamic-update-slice_fusion.refs_0_), channel_id=1, source_target_pairs={{0,16},{1,17},{2,18},{3,19},{4,20},{5,21},{6,22},{7,23},{8,24},{9,... | collective-permute-start | bytes 196616 | tf_op jit(solution)/shard_map/ag1_z2/ppermute | solution.py:165
  7.9 1.7 %collective-permute-start = (f32[128,128]{1,0:T(8,128)S(1)}, f32[128,128]{1,0:T(8,128)S(1)}, u32[]{:S(2)}, u32[]{:S(2)}) collective-permute-start(f32[128,128]{1,0:T(8,128)S(1)} %constant_dynamic-update-slice_fusion.refs_0_), channel_id=1, source_target_pairs={{0,2},{1,3},{2,0},{3,1},{4,6},{5,7},{6,4},{7,5},{8,10},{9,11},{10,... | collective-permute-start | bytes 196616 | tf_op jit(solution)/shard_map/ag1_n1/ppermute | solution.py:165
  9.6 3.0 %collective-permute-done.4.refs_1_ = f32[128,128]{1,0:T(8,128)S(1)} collective-permute-done((f32[128,128]{1,0:T(8,128)S(1)}, f32[128,128]{1,0:T(8,128)S(1)}, u32[]{:S(2)}, u32[]{:S(2)}) %collective-permute-start.4) | collective-permute-done | bytes 65568 | tf_op jit(solution)/shard_map/ag1_z2/ppermute | solution.py:165
  12.5 1.4 %collective-permute-done.5.refs_2_ = f32[128,128]{1,0:T(8,128)S(1)} collective-permute-done((f32[128,128]{1,0:T(8,128)S(1)}, f32[128,128]{1,0:T(8,128)S(1)}, u32[]{:S(2)}, u32[]{:S(2)}) %collective-permute-start.5) | collective-permute-done | bytes 65568 | tf_op jit(solution)/shard_map/ag1_z3/ppermute | solution.py:165
  14.0 1.6 %collective-permute-start.6 = (f32[384,128]{1,0:T(8,128)S(1)}, f32[384,128]{1,0:T(8,128)S(1)}, u32[]{:S(2)}, u32[]{:S(2)}) collective-permute-start(f32[384,128]{1,0:T(8,128)S(1)} %ag1_column.1.refs_4_), channel_id=1, source_target_pairs={{0,2},{1,3},{2,0},{3,1},{4,6},{5,7},{6,4},{7,5},{8,10},{9,11},{10,... | collective-permute-start | bytes 589832 | tf_op jit(solution)/shard_map/ag1_c1/ppermute | solution.py:165
  15.5 1.5 %collective-permute-start.7 = (f32[384,128]{1,0:T(8,128)S(1)}, f32[384,128]{1,0:T(8,128)S(1)}, u32[]{:S(2)}, u32[]{:S(2)}) collective-permute-start(f32[384,128]{1,0:T(8,128)S(1)} %ag1_column.1.refs_4_), channel_id=1, source_target_pairs={{0,4},{1,5},{2,6},{3,7},{4,0},{5,1},{6,2},{7,3},{8,12},{9,13},{10,... | collective-permute-start | bytes 589832 | tf_op jit(solution)/shard_map/ag1_c2/ppermute | solution.py:165
  17.5 1.5 %collective-permute-start.1 = (f32[128,128]{1,0:T(8,128)S(1)}, f32[128,128]{1,0:T(8,128)S(1)}, u32[]{:S(2)}, u32[]{:S(2)}) collective-permute-start(f32[128,128]{1,0:T(8,128)S(1)} %constant_dynamic-update-slice_fusion.refs_0_), channel_id=1, source_target_pairs={{0,4},{1,5},{2,6},{3,7},{4,0},{5,1},{6,2},{7,3},{8,12},{9,13},{10,... | collective-permute-start | bytes 196616 | tf_op jit(solution)/shard_map/ag1_n2/ppermute | solution.py:165
  19.0 1.4 %collective-permute-start.2 = (f32[128,128]{1,0:T(8,128)S(1)}, f32[128,128]{1,0:T(8,128)S(1)}, u32[]{:S(2)}, u32[]{:S(2)}) collective-permute-start(f32[128,128]{1,0:T(8,128)S(1)} %constant_dynamic-update-slice_fusion.refs_0_), channel_id=1, source_target_pairs={{0,6},{1,7},{2,4},{3,5},{4,2},{5,3},{6,0},{7,1},{8,14},{9,15},{10,... | collective-permute-start | bytes 196616 | tf_op jit(solution)/shard_map/ag1_n3/ppermute | solution.py:165
  20.5 6.8 %collective-permute-done.1.refs_2_ = f32[128,128]{1,0:T(8,128)S(1)} collective-permute-done((f32[128,128]{1,0:T(8,128)S(1)}, f32[128,128]{1,0:T(8,128)S(1)}, u32[]{:S(2)}, u32[]{:S(2)}) %collective-permute-start.1) | collective-permute-done | bytes 65568 | tf_op jit(solution)/shard_map/ag1_n2/ppermute | solution.py:165
  27.6 0.6 compare_reduce_fusion
  29.3 0.6 fusion
  30.7 0.8 first_product.1
  31.5 1.1 collective-permute-start.17
  32.6 1.2 %collective-permute-start.18 = (f32[136,128]{1,0:T(8,128)S(1)}, f32[136,128]{1,0:T(8,128)S(1)}, u32[]{:S(2)}, u32[]{:S(2)}) collective-permute-start(f32[136,128]{1,0:T(8,128)S(1)} %get-tuple-element.32.refs_0_), channel_id=1, source_target_pairs={{0,16},{1,17},{2,18},{3,19},{4,20},{5,21},{6,22},{7,23},{8,24},{9,... | collective-permute-start | bytes 208904 | tf_op jit(solution)/shard_map/ag2_z2/ppermute | solution.py:165
  33.7 2.2 %collective-permute-start.19 = (f32[136,128]{1,0:T(8,128)S(1)}, f32[136,128]{1,0:T(8,128)S(1)}, u32[]{:S(2)}, u32[]{:S(2)}) collective-permute-start(f32[136,128]{1,0:T(8,128)S(1)} %get-tuple-element.32.refs_0_), channel_id=1, source_target_pairs={{0,24},{1,25},{2,26},{3,27},{4,28},{5,29},{6,30},{7,31},{8,16},{9,... | collective-permute-start | bytes 208904 | tf_op jit(solution)/shard_map/ag2_z3/ppermute | solution.py:165
  36.0 0.8 collective-permute-start.14
  36.8 1.2 %collective-permute-start.15 = (f32[136,128]{1,0:T(8,128)S(1)}, f32[136,128]{1,0:T(8,128)S(1)}, u32[]{:S(2)}, u32[]{:S(2)}) collective-permute-start(f32[136,128]{1,0:T(8,128)S(1)} %get-tuple-element.32.refs_0_), channel_id=1, source_target_pairs={{0,4},{1,5},{2,6},{3,7},{4,0},{5,1},{6,2},{7,3},{8,12},{9,13},{10,... | collective-permute-start | bytes 208904 | tf_op jit(solution)/shard_map/ag2_n2/ppermute | solution.py:165
  38.0 1.4 %collective-permute-start.16 = (f32[136,128]{1,0:T(8,128)S(1)}, f32[136,128]{1,0:T(8,128)S(1)}, u32[]{:S(2)}, u32[]{:S(2)}) collective-permute-start(f32[136,128]{1,0:T(8,128)S(1)} %get-tuple-element.32.refs_0_), channel_id=1, source_target_pairs={{0,6},{1,7},{2,4},{3,5},{4,2},{5,3},{6,0},{7,1},{8,14},{9,15},{10,... | collective-permute-start | bytes 208904 | tf_op jit(solution)/shard_map/ag2_n3/ppermute | solution.py:165
  39.5 1.7 %collective-permute-done.18.refs_1_ = f32[136,128]{1,0:T(8,128)S(1)} collective-permute-done((f32[136,128]{1,0:T(8,128)S(1)}, f32[136,128]{1,0:T(8,128)S(1)}, u32[]{:S(2)}, u32[]{:S(2)}) %collective-permute-start.18) | collective-permute-done | bytes 69664 | tf_op jit(solution)/shard_map/ag2_z2/ppermute | solution.py:165
  41.2 0.6 collective-permute-start.20
  41.8 1.5 %collective-permute-start.21 = (f32[408,128]{1,0:T(8,128)S(1)}, f32[408,128]{1,0:T(8,128)S(1)}, u32[]{:S(2)}, u32[]{:S(2)}) collective-permute-start(f32[408,128]{1,0:T(8,128)S(1)} %ag2_column.1.refs_5_), channel_id=1, source_target_pairs={{0,4},{1,5},{2,6},{3,7},{4,0},{5,1},{6,2},{7,3},{8,12},{9,13},{10,... | collective-permute-start | bytes 626696 | tf_op jit(solution)/shard_map/ag2_c2/ppermute | solution.py:165
  43.3 1.4 %collective-permute-start.22 = (f32[408,128]{1,0:T(8,128)S(1)}, f32[408,128]{1,0:T(8,128)S(1)}, u32[]{:S(2)}, u32[]{:S(2)}) collective-permute-start(f32[408,128]{1,0:T(8,128)S(1)} %ag2_column.1.refs_5_), channel_id=1, source_target_pairs={{0,6},{1,7},{2,4},{3,5},{4,2},{5,3},{6,0},{7,1},{8,14},{9,15},{10,... | collective-permute-start | bytes 626696 | tf_op jit(solution)/shard_map/ag2_c3/ppermute | solution.py:165
  44.8 6.5 %metric_head.1 = (f32[256,256]{1,0:T(8,128)S(1)}, f32[128,128]{1,0:T(8,128)S(1)}) custom-call(f32[2048,256]{1,0:T(8,128)S(1)} %get-tuple-element.29.y_ref.refs_2_), custom_call_target="tpu_custom_call" | custom-call | flops 7000000000 | tf_op jit(solution)/shard_map/metric_head/metric_head/pallas_call | solution.py:405
  51.4 0.5 collective-permute-start.23
  52.5 5.4 %metric_tail.1.refs_3_ = f32[256,256]{1,0:T(8,128)S(1)} custom-call(f32[256,256]{1,0:T(8,128)S(1)} %get-tuple-element.30.metric_ref, f32[128,128]{1,0:T(8,128)S(1)} %get-tuple-element.31.upper_ref), custom_call_target="tpu_custom_call" | custom-call | flops 7000000000 | tf_op jit(solution)/shard_map/metric_tail/metric_tail/pallas_call | solution.py:415
  58.0 13.5 %first_step.1 = (f32[2048,256]{1,0:T(8,128)S(1)}, f32[2048,128]{1,0:T(8,128)S(1)}, f32[128,128]{1,0:T(8,128)S(1)}, f32[1,128]{1,0:T(1,128)S(1)}, f32[64,128]{1,0:T(8,128)}) custom-call(s32[1]{0:T(128)} %bitcast.refs_0_, f32[64,2048]{1,0:T(8,128)S(1)} %bitcast.8, f32[2048,256]{1,0:T(8,128)S(1)} %get-tuple-element.29.y_ref.refs_2_, ...), custom_call_target="tpu_custom_call" | custom-call | tf_op jit(solution)/shard_map/first_step/pallas_call | solution.py:458
  71.5 2.3 %collective-permute-start.31 = (f32[64,128]{1,0:T(8,128)}, f32[64,128]{1,0:T(8,128)S(1)}, u32[]{:S(2)}, u32[]{:S(2)}) collective-permute-start(f32[64,128]{1,0:T(8,128)} %get-tuple-element.38.refs_0_), channel_id=1, source_target_pairs={{0,8},{1,9},{2,10},{3,11},{4,12},{5,13},{6,14},{7,15},{8,0},{9,1},... | collective-permute-start | bytes 98312 | tf_op jit(solution)/shard_map/ag3_z1/ppermute | solution.py:165
  73.8 1.1 collective-permute-start.32
  74.9 1.5 %collective-permute-start.33 = (f32[64,128]{1,0:T(8,128)}, f32[64,128]{1,0:T(8,128)S(1)}, u32[]{:S(2)}, u32[]{:S(2)}) collective-permute-start(f32[64,128]{1,0:T(8,128)} %get-tuple-element.38.refs_0_), channel_id=1, source_target_pairs={{0,24},{1,25},{2,26},{3,27},{4,28},{5,29},{6,30},{7,31},{8,16},{9,... | collective-permute-start | bytes 98312 | tf_op jit(solution)/shard_map/ag3_z3/ppermute | solution.py:165
  76.4 1.3 %collective-permute-start.28 = (f32[64,128]{1,0:T(8,128)}, f32[64,128]{1,0:T(8,128)S(1)}, u32[]{:S(2)}, u32[]{:S(2)}) collective-permute-start(f32[64,128]{1,0:T(8,128)} %get-tuple-element.38.refs_0_), channel_id=1, source_target_pairs={{0,2},{1,3},{2,0},{3,1},{4,6},{5,7},{6,4},{7,5},{8,10},{9,11},{10,... | collective-permute-start | bytes 98312 | tf_op jit(solution)/shard_map/ag3_n1/ppermute | solution.py:165
  77.7 1.7 %collective-permute-done.32.refs_1_ = f32[64,128]{1,0:T(8,128)S(1)} collective-permute-done((f32[64,128]{1,0:T(8,128)}, f32[64,128]{1,0:T(8,128)S(1)}, u32[]{:S(2)}, u32[]{:S(2)}) %collective-permute-start.32) | collective-permute-done | bytes 32800 | tf_op jit(solution)/shard_map/ag3_z2/ppermute | solution.py:165
  79.4 1.5 %collective-permute-done.33.refs_2_ = f32[64,128]{1,0:T(8,128)S(1)} collective-permute-done((f32[64,128]{1,0:T(8,128)}, f32[64,128]{1,0:T(8,128)S(1)}, u32[]{:S(2)}, u32[]{:S(2)}) %collective-permute-start.33) | collective-permute-done | bytes 32800 | tf_op jit(solution)/shard_map/ag3_z3/ppermute | solution.py:165
  80.9 1.4 %collective-permute-start.34 = (f32[192,128]{1,0:T(8,128)S(1)}, f32[192,128]{1,0:T(8,128)S(1)}, u32[]{:S(2)}, u32[]{:S(2)}) collective-permute-start(f32[192,128]{1,0:T(8,128)S(1)} %ag3_column.1.refs_8_), channel_id=1, source_target_pairs={{0,2},{1,3},{2,0},{3,1},{4,6},{5,7},{6,4},{7,5},{8,10},{9,11},{10,... | collective-permute-start | bytes 294920 | tf_op jit(solution)/shard_map/ag3_c1/ppermute | solution.py:165
  82.3 1.5 %collective-permute-start.35 = (f32[192,128]{1,0:T(8,128)S(1)}, f32[192,128]{1,0:T(8,128)S(1)}, u32[]{:S(2)}, u32[]{:S(2)}) collective-permute-start(f32[192,128]{1,0:T(8,128)S(1)} %ag3_column.1.refs_8_), channel_id=1, source_target_pairs={{0,4},{1,5},{2,6},{3,7},{4,0},{5,1},{6,2},{7,3},{8,12},{9,13},{10,... | collective-permute-start | bytes 294920 | tf_op jit(solution)/shard_map/ag3_c2/ppermute | solution.py:165
  83.8 0.7 collective-permute-start.36
  84.4 1.3 %collective-permute-start.29 = (f32[64,128]{1,0:T(8,128)}, f32[64,128]{1,0:T(8,128)}, u32[]{:S(2)}, u32[]{:S(2)}) collective-permute-start(f32[64,128]{1,0:T(8,128)} %get-tuple-element.38.refs_0_), channel_id=1, source_target_pairs={{0,4},{1,5},{2,6},{3,7},{4,0},{5,1},{6,2},{7,3},{8,12},{9,13},{10,... | collective-permute-start | bytes 98312 | tf_op jit(solution)/shard_map/ag3_n2/ppermute | solution.py:165
  85.8 0.6 copy-done
  86.4 1.4 %collective-permute-start.30 = (f32[64,128]{1,0:T(8,128)}, f32[64,128]{1,0:T(8,128)}, u32[]{:S(2)}, u32[]{:S(2)}) collective-permute-start(f32[64,128]{1,0:T(8,128)} %get-tuple-element.38.refs_0_), channel_id=1, source_target_pairs={{0,6},{1,7},{2,4},{3,5},{4,2},{5,3},{6,0},{7,1},{8,14},{9,15},{10,... | collective-permute-start | bytes 98312 | tf_op jit(solution)/shard_map/ag3_n3/ppermute | solution.py:165
  87.9 1.8 %collective-permute-done.29.refs_2_ = f32[64,128]{1,0:T(8,128)} collective-permute-done((f32[64,128]{1,0:T(8,128)}, f32[64,128]{1,0:T(8,128)}, u32[]{:S(2)}, u32[]{:S(2)}) %collective-permute-start.29) | collective-permute-done | bytes 32800 | tf_op jit(solution)/shard_map/ag3_n2/ppermute | solution.py:165
  89.7 1.8 %collective-permute-done.30.refs_3_ = f32[64,128]{1,0:T(8,128)} collective-permute-done((f32[64,128]{1,0:T(8,128)}, f32[64,128]{1,0:T(8,128)}, u32[]{:S(2)}, u32[]{:S(2)}) %collective-permute-start.30) | collective-permute-done | bytes 32800 | tf_op jit(solution)/shard_map/ag3_n3/ppermute | solution.py:165
  91.5 0.8 copy-done.1
  92.3 0.8 ag3_near.1.refs_7_
  94.2 6.6 %second_factor.1 = (f32[128,128]{1,0:T(8,128)S(1)}, f32[128,128]{1,0:T(8,128)S(1)}) custom-call(f32[2048,256]{1,0:T(8,128)S(1)} %get-tuple-element.33.y2_ref.refs_1_), custom_call_target="tpu_custom_call" | custom-call | flops 8999999488 | tf_op jit(solution)/shard_map/second_factor/second_factor/pallas_call | solution.py:429
  100.9 13.9 %last_step.1 = (f32[64,128]{1,0:T(8,128)}, f32[64,128]{1,0:T(8,128)}, f32[1,128]{1,0:T(1,128)S(1)}) custom-call(s32[1]{0:T(128)} %bitcast.refs_0_, f32[2048,256]{1,0:T(8,128)S(1)} %get-tuple-element.33.y2_ref.refs_1_, f32[2048,128]{1,0:T(8,128)S(1)} %get-tuple-element.34.refs_2_, f32[128,128]{1,0:T(8,128)S(1)} %get-tuple-element.35.refs_3_, ...), custom_call_target="tpu_custom_call" | custom-call | tf_op jit(solution)/shard_map/last_step/pallas_call | solution.py:479
  114.7 0.6 pad_maximum_fusion
  (64 shorter events, 4.5 us)
Async XLA Ops:
  0.6 26.8 %copy-start.2 = (f32[64,1,2048]{2,1,0:T(1,128)S(1)}, f32[64,1,2048]{2,1,0:T(1,128)}, u32[]{:S(2)}) copy-start(f32[64,1,2048]{2,1,0:T(1,128)} %param.6) | copy-start | bytes 1572868
  2.2 27.1 %copy-start.3 = (f32[64]{0:T(128)S(1)}, f32[64]{0:T(128)}, u32[]{:S(2)}) copy-start(f32[64]{0:T(128)} %param.9) | copy-start | bytes 772
  2.2 7.4 %collective-permute-start.3 = (f32[128,128]{1,0:T(8,128)S(1)}, f32[128,128]{1,0:T(8,128)S(1)}, u32[]{:S(2)}, u32[]{:S(2)}) collective-permute-start(f32[128,128]{1,0:T(8,128)S(1)} %constant_dynamic-update-slice_fusion.refs_0_), channel_id=1, source_target_pairs={{0,8},{1,9},{2,10},{3,11},{4,12},{5,13},{6,14},{7,15},{8,0},{9,1},... | collective-permute-start | bytes 196616 | tf_op jit(solution)/shard_map/ag1_z1/ppermute | solution.py:165
  5.3 7.3 %collective-permute-start.4 = (f32[128,128]{1,0:T(8,128)S(1)}, f32[128,128]{1,0:T(8,128)S(1)}, u32[]{:S(2)}, u32[]{:S(2)}) collective-permute-start(f32[128,128]{1,0:T(8,128)S(1)} %constant_dynamic-update-slice_fusion.refs_0_), channel_id=1, source_target_pairs={{0,16},{1,17},{2,18},{3,19},{4,20},{5,21},{6,22},{7,23},{8,24},{9,... | collective-permute-start | bytes 196616 | tf_op jit(solution)/shard_map/ag1_z2/ppermute | solution.py:165
  7.9 6.1 %collective-permute-start.5 = (f32[128,128]{1,0:T(8,128)S(1)}, f32[128,128]{1,0:T(8,128)S(1)}, u32[]{:S(2)}, u32[]{:S(2)}) collective-permute-start(f32[128,128]{1,0:T(8,128)S(1)} %constant_dynamic-update-slice_fusion.refs_0_), channel_id=1, source_target_pairs={{0,24},{1,25},{2,26},{3,27},{4,28},{5,29},{6,30},{7,31},{8,16},{9,... | collective-permute-start | bytes 196616 | tf_op jit(solution)/shard_map/ag1_z3/ppermute | solution.py:165
  7.9 11.2 %collective-permute-start = (f32[128,128]{1,0:T(8,128)S(1)}, f32[128,128]{1,0:T(8,128)S(1)}, u32[]{:S(2)}, u32[]{:S(2)}) collective-permute-start(f32[128,128]{1,0:T(8,128)S(1)} %constant_dynamic-update-slice_fusion.refs_0_), channel_id=1, source_target_pairs={{0,2},{1,3},{2,0},{3,1},{4,6},{5,7},{6,4},{7,5},{8,10},{9,11},{10,... | collective-permute-start | bytes 196616 | tf_op jit(solution)/shard_map/ag1_n1/ppermute | solution.py:165
  14.0 14.7 %collective-permute-start.6 = (f32[384,128]{1,0:T(8,128)S(1)}, f32[384,128]{1,0:T(8,128)S(1)}, u32[]{:S(2)}, u32[]{:S(2)}) collective-permute-start(f32[384,128]{1,0:T(8,128)S(1)} %ag1_column.1.refs_4_), channel_id=1, source_target_pairs={{0,2},{1,3},{2,0},{3,1},{4,6},{5,7},{6,4},{7,5},{8,10},{9,11},{10,... | collective-permute-start | bytes 589832 | tf_op jit(solution)/shard_map/ag1_c1/ppermute | solution.py:165
  15.5 13.2 %collective-permute-start.7 = (f32[384,128]{1,0:T(8,128)S(1)}, f32[384,128]{1,0:T(8,128)S(1)}, u32[]{:S(2)}, u32[]{:S(2)}) collective-permute-start(f32[384,128]{1,0:T(8,128)S(1)} %ag1_column.1.refs_4_), channel_id=1, source_target_pairs={{0,4},{1,5},{2,6},{3,7},{4,0},{5,1},{6,2},{7,3},{8,12},{9,13},{10,... | collective-permute-start | bytes 589832 | tf_op jit(solution)/shard_map/ag1_c2/ppermute | solution.py:165
  17.0 12.2 %collective-permute-start.8 = (f32[384,128]{1,0:T(8,128)S(1)}, f32[384,128]{1,0:T(8,128)S(1)}, u32[]{:S(2)}, u32[]{:S(2)}) collective-permute-start(f32[384,128]{1,0:T(8,128)S(1)} %ag1_column.1.refs_4_), channel_id=1, source_target_pairs={{0,6},{1,7},{2,4},{3,5},{4,2},{5,3},{6,0},{7,1},{8,14},{9,15},{10,... | collective-permute-start | bytes 589832 | tf_op jit(solution)/shard_map/ag1_c3/ppermute | solution.py:165
  17.5 9.8 %collective-permute-start.1 = (f32[128,128]{1,0:T(8,128)S(1)}, f32[128,128]{1,0:T(8,128)S(1)}, u32[]{:S(2)}, u32[]{:S(2)}) collective-permute-start(f32[128,128]{1,0:T(8,128)S(1)} %constant_dynamic-update-slice_fusion.refs_0_), channel_id=1, source_target_pairs={{0,4},{1,5},{2,6},{3,7},{4,0},{5,1},{6,2},{7,3},{8,12},{9,13},{10,... | collective-permute-start | bytes 196616 | tf_op jit(solution)/shard_map/ag1_n2/ppermute | solution.py:165
  19.0 8.2 %collective-permute-start.2 = (f32[128,128]{1,0:T(8,128)S(1)}, f32[128,128]{1,0:T(8,128)S(1)}, u32[]{:S(2)}, u32[]{:S(2)}) collective-permute-start(f32[128,128]{1,0:T(8,128)S(1)} %constant_dynamic-update-slice_fusion.refs_0_), channel_id=1, source_target_pairs={{0,6},{1,7},{2,4},{3,5},{4,2},{5,3},{6,0},{7,1},{8,14},{9,15},{10,... | collective-permute-start | bytes 196616 | tf_op jit(solution)/shard_map/ag1_n3/ppermute | solution.py:165
  27.3 2.7 %collective-permute-start.9 = (f32[512,128]{1,0:T(8,128)S(1)}, f32[512,128]{1,0:T(8,128)S(1)}, u32[]{:S(2)}, u32[]{:S(2)}) collective-permute-start(f32[512,128]{1,0:T(8,128)S(1)} %ag1_near.1.refs_3_), channel_id=1, source_target_pairs={{0,1},{1,0},{2,3},{3,2},{4,5},{5,4},{6,7},{7,6},{8,9},{9,8},{10,11... | collective-permute-start | bytes 786440 | tf_op jit(solution)/shard_map/ag1_core0/ppermute | solution.py:165
  28.2 1.7 %collective-permute-start.10 = (f32[384,128]{1,0:T(8,128)S(1)}, f32[384,128]{1,0:T(8,128)S(1)}, u32[]{:S(2)}, u32[]{:S(2)}) collective-permute-start(f32[384,128]{1,0:T(8,128)S(1)} %ag1_column.1.refs_4_), channel_id=1, source_target_pairs={{0,1},{1,0},{2,3},{3,2},{4,5},{5,4},{6,7},{7,6},{8,9},{9,8},{10,11... | collective-permute-start | bytes 589832 | tf_op jit(solution)/shard_map/ag1_core1/ppermute | solution.py:165
  28.7 1.4 %collective-permute-start.11 = (f32[384,128]{1,0:T(8,128)S(1)}, f32[384,128]{1,0:T(8,128)S(1)}, u32[]{:S(2)}, u32[]{:S(2)}) collective-permute-start(f32[384,128]{1,0:T(8,128)S(1)} %collective-permute-done.6.refs_5_), channel_id=1, source_target_pairs={{0,1},{1,0},{2,3},{3,2},{4,5},{5,4},{6,7},{7,6},{8,9},{9,8},{10,11... | collective-permute-start | bytes 589832 | tf_op jit(solution)/shard_map/ag1_core2/ppermute | solution.py:165
  28.7 1.7 %collective-permute-start.12 = (f32[384,128]{1,0:T(8,128)S(1)}, f32[384,128]{1,0:T(8,128)S(1)}, u32[]{:S(2)}, u32[]{:S(2)}) collective-permute-start(f32[384,128]{1,0:T(8,128)S(1)} %collective-permute-done.7.refs_6_), channel_id=1, source_target_pairs={{0,1},{1,0},{2,3},{3,2},{4,5},{5,4},{6,7},{7,6},{8,9},{9,8},{10,11... | collective-permute-start | bytes 589832 | tf_op jit(solution)/shard_map/ag1_core3/ppermute | solution.py:165
  29.2 1.5 %collective-permute-start.13 = (f32[384,128]{1,0:T(8,128)S(1)}, f32[384,128]{1,0:T(8,128)S(1)}, u32[]{:S(2)}, u32[]{:S(2)}) collective-permute-start(f32[384,128]{1,0:T(8,128)S(1)} %collective-permute-done.8.refs_7_), channel_id=1, source_target_pairs={{0,1},{1,0},{2,3},{3,2},{4,5},{5,4},{6,7},{7,6},{8,9},{9,8},{10,11... | collective-permute-start | bytes 589832 | tf_op jit(solution)/shard_map/ag1_core4/ppermute | solution.py:165
  31.5 6.5 %collective-permute-start.17 = (f32[136,128]{1,0:T(8,128)S(1)}, f32[136,128]{1,0:T(8,128)S(1)}, u32[]{:S(2)}, u32[]{:S(2)}) collective-permute-start(f32[136,128]{1,0:T(8,128)S(1)} %get-tuple-element.32.refs_0_), channel_id=1, source_target_pairs={{0,8},{1,9},{2,10},{3,11},{4,12},{5,13},{6,14},{7,15},{8,0},{9,1},... | collective-permute-start | bytes 208904 | tf_op jit(solution)/shard_map/ag2_z1/ppermute | solution.py:165
  32.6 8.6 %collective-permute-start.18 = (f32[136,128]{1,0:T(8,128)S(1)}, f32[136,128]{1,0:T(8,128)S(1)}, u32[]{:S(2)}, u32[]{:S(2)}) collective-permute-start(f32[136,128]{1,0:T(8,128)S(1)} %get-tuple-element.32.refs_0_), channel_id=1, source_target_pairs={{0,16},{1,17},{2,18},{3,19},{4,20},{5,21},{6,22},{7,23},{8,24},{9,... | collective-permute-start | bytes 208904 | tf_op jit(solution)/shard_map/ag2_z2/ppermute | solution.py:165
  33.7 7.4 %collective-permute-start.19 = (f32[136,128]{1,0:T(8,128)S(1)}, f32[136,128]{1,0:T(8,128)S(1)}, u32[]{:S(2)}, u32[]{:S(2)}) collective-permute-start(f32[136,128]{1,0:T(8,128)S(1)} %get-tuple-element.32.refs_0_), channel_id=1, source_target_pairs={{0,24},{1,25},{2,26},{3,27},{4,28},{5,29},{6,30},{7,31},{8,16},{9,... | collective-permute-start | bytes 208904 | tf_op jit(solution)/shard_map/ag2_z3/ppermute | solution.py:165
  36.0 7.4 %collective-permute-start.14 = (f32[136,128]{1,0:T(8,128)S(1)}, f32[136,128]{1,0:T(8,128)S(1)}, u32[]{:S(2)}, u32[]{:S(2)}) collective-permute-start(f32[136,128]{1,0:T(8,128)S(1)} %get-tuple-element.32.refs_0_), channel_id=1, source_target_pairs={{0,2},{1,3},{2,0},{3,1},{4,6},{5,7},{6,4},{7,5},{8,10},{9,11},{10,... | collective-permute-start | bytes 208904 | tf_op jit(solution)/shard_map/ag2_n1/ppermute | solution.py:165
  36.8 14.4 %collective-permute-start.15 = (f32[136,128]{1,0:T(8,128)S(1)}, f32[136,128]{1,0:T(8,128)S(1)}, u32[]{:S(2)}, u32[]{:S(2)}) collective-permute-start(f32[136,128]{1,0:T(8,128)S(1)} %get-tuple-element.32.refs_0_), channel_id=1, source_target_pairs={{0,4},{1,5},{2,6},{3,7},{4,0},{5,1},{6,2},{7,3},{8,12},{9,13},{10,... | collective-permute-start | bytes 208904 | tf_op jit(solution)/shard_map/ag2_n2/ppermute | solution.py:165
  38.0 13.3 %collective-permute-start.16 = (f32[136,128]{1,0:T(8,128)S(1)}, f32[136,128]{1,0:T(8,128)S(1)}, u32[]{:S(2)}, u32[]{:S(2)}) collective-permute-start(f32[136,128]{1,0:T(8,128)S(1)} %get-tuple-element.32.refs_0_), channel_id=1, source_target_pairs={{0,6},{1,7},{2,4},{3,5},{4,2},{5,3},{6,0},{7,1},{8,14},{9,15},{10,... | collective-permute-start | bytes 208904 | tf_op jit(solution)/shard_map/ag2_n3/ppermute | solution.py:165
  41.2 10.7 %collective-permute-start.20 = (f32[408,128]{1,0:T(8,128)S(1)}, f32[408,128]{1,0:T(8,128)S(1)}, u32[]{:S(2)}, u32[]{:S(2)}) collective-permute-start(f32[408,128]{1,0:T(8,128)S(1)} %ag2_column.1.refs_5_), channel_id=1, source_target_pairs={{0,2},{1,3},{2,0},{3,1},{4,6},{5,7},{6,4},{7,5},{8,10},{9,11},{10,... | collective-permute-start | bytes 626696 | tf_op jit(solution)/shard_map/ag2_c1/ppermute | solution.py:165
  41.8 10.2 %collective-permute-start.21 = (f32[408,128]{1,0:T(8,128)S(1)}, f32[408,128]{1,0:T(8,128)S(1)}, u32[]{:S(2)}, u32[]{:S(2)}) collective-permute-start(f32[408,128]{1,0:T(8,128)S(1)} %ag2_column.1.refs_5_), channel_id=1, source_target_pairs={{0,4},{1,5},{2,6},{3,7},{4,0},{5,1},{6,2},{7,3},{8,12},{9,13},{10,... | collective-permute-start | bytes 626696 | tf_op jit(solution)/shard_map/ag2_c2/ppermute | solution.py:165
  43.3 9.2 %collective-permute-start.22 = (f32[408,128]{1,0:T(8,128)S(1)}, f32[408,128]{1,0:T(8,128)S(1)}, u32[]{:S(2)}, u32[]{:S(2)}) collective-permute-start(f32[408,128]{1,0:T(8,128)S(1)} %ag2_column.1.refs_5_), channel_id=1, source_target_pairs={{0,6},{1,7},{2,4},{3,5},{4,2},{5,3},{6,0},{7,1},{8,14},{9,15},{10,... | collective-permute-start | bytes 626696 | tf_op jit(solution)/shard_map/ag2_c3/ppermute | solution.py:165
  51.2 6.7 %collective-permute-start.24 = (f32[408,128]{1,0:T(8,128)S(1)}, f32[408,128]{1,0:T(8,128)S(1)}, u32[]{:S(2)}, u32[]{:S(2)}) collective-permute-start(f32[408,128]{1,0:T(8,128)S(1)} %ag2_column.1.refs_5_), channel_id=1, source_target_pairs={{0,1},{1,0},{2,3},{3,2},{4,5},{5,4},{6,7},{7,6},{8,9},{9,8},{10,11... | collective-permute-start | bytes 626696 | tf_op jit(solution)/shard_map/ag2_core1/ppermute | solution.py:165
  51.4 6.6 %collective-permute-start.23 = (f32[544,128]{1,0:T(8,128)S(1)}, f32[544,128]{1,0:T(8,128)S(1)}, u32[]{:S(2)}, u32[]{:S(2)}) collective-permute-start(f32[544,128]{1,0:T(8,128)S(1)} %ag2_near.1.refs_4_), channel_id=1, source_target_pairs={{0,1},{1,0},{2,3},{3,2},{4,5},{5,4},{6,7},{7,6},{8,9},{9,8},{10,11... | collective-permute-start | bytes 835592 | tf_op jit(solution)/shard_map/ag2_core0/ppermute | solution.py:165
  51.9 6.0 %collective-permute-start.25 = (f32[408,128]{1,0:T(8,128)S(1)}, f32[408,128]{1,0:T(8,128)S(1)}, u32[]{:S(2)}, u32[]{:S(2)}) collective-permute-start(f32[408,128]{1,0:T(8,128)S(1)} %collective-permute-done.20.refs_6_), channel_id=1, source_target_pairs={{0,1},{1,0},{2,3},{3,2},{4,5},{5,4},{6,7},{7,6},{8,9},{9,8},{10,11... | collective-permute-start | bytes 626696 | tf_op jit(solution)/shard_map/ag2_core2/ppermute | solution.py:165
  52.0 5.9 %collective-permute-start.26 = (f32[408,128]{1,0:T(8,128)S(1)}, f32[408,128]{1,0:T(8,128)S(1)}, u32[]{:S(2)}, u32[]{:S(2)}) collective-permute-start(f32[408,128]{1,0:T(8,128)S(1)} %collective-permute-done.21.refs_7_), channel_id=1, source_target_pairs={{0,1},{1,0},{2,3},{3,2},{4,5},{5,4},{6,7},{7,6},{8,9},{9,8},{10,11... | collective-permute-start | bytes 626696 | tf_op jit(solution)/shard_map/ag2_core3/ppermute | solution.py:165
  52.5 5.4 %collective-permute-start.27 = (f32[408,128]{1,0:T(8,128)S(1)}, f32[408,128]{1,0:T(8,128)S(1)}, u32[]{:S(2)}, u32[]{:S(2)}) collective-permute-start(f32[408,128]{1,0:T(8,128)S(1)} %collective-permute-done.22.refs_8_), channel_id=1, source_target_pairs={{0,1},{1,0},{2,3},{3,2},{4,5},{5,4},{6,7},{7,6},{8,9},{9,8},{10,11... | collective-permute-start | bytes 626696 | tf_op jit(solution)/shard_map/ag2_core4/ppermute | solution.py:165
  71.5 6.2 %collective-permute-start.31 = (f32[64,128]{1,0:T(8,128)}, f32[64,128]{1,0:T(8,128)S(1)}, u32[]{:S(2)}, u32[]{:S(2)}) collective-permute-start(f32[64,128]{1,0:T(8,128)} %get-tuple-element.38.refs_0_), channel_id=1, source_target_pairs={{0,8},{1,9},{2,10},{3,11},{4,12},{5,13},{6,14},{7,15},{8,0},{9,1},... | collective-permute-start | bytes 98312 | tf_op jit(solution)/shard_map/ag3_z1/ppermute | solution.py:165
  73.8 5.6 %collective-permute-start.32 = (f32[64,128]{1,0:T(8,128)}, f32[64,128]{1,0:T(8,128)S(1)}, u32[]{:S(2)}, u32[]{:S(2)}) collective-permute-start(f32[64,128]{1,0:T(8,128)} %get-tuple-element.38.refs_0_), channel_id=1, source_target_pairs={{0,16},{1,17},{2,18},{3,19},{4,20},{5,21},{6,22},{7,23},{8,24},{9,... | collective-permute-start | bytes 98312 | tf_op jit(solution)/shard_map/ag3_z2/ppermute | solution.py:165
  74.9 5.9 %collective-permute-start.33 = (f32[64,128]{1,0:T(8,128)}, f32[64,128]{1,0:T(8,128)S(1)}, u32[]{:S(2)}, u32[]{:S(2)}) collective-permute-start(f32[64,128]{1,0:T(8,128)} %get-tuple-element.38.refs_0_), channel_id=1, source_target_pairs={{0,24},{1,25},{2,26},{3,27},{4,28},{5,29},{6,30},{7,31},{8,16},{9,... | collective-permute-start | bytes 98312 | tf_op jit(solution)/shard_map/ag3_z3/ppermute | solution.py:165
  76.4 9.4 %collective-permute-start.28 = (f32[64,128]{1,0:T(8,128)}, f32[64,128]{1,0:T(8,128)S(1)}, u32[]{:S(2)}, u32[]{:S(2)}) collective-permute-start(f32[64,128]{1,0:T(8,128)} %get-tuple-element.38.refs_0_), channel_id=1, source_target_pairs={{0,2},{1,3},{2,0},{3,1},{4,6},{5,7},{6,4},{7,5},{8,10},{9,11},{10,... | collective-permute-start | bytes 98312 | tf_op jit(solution)/shard_map/ag3_n1/ppermute | solution.py:165
  80.9 12.3 %collective-permute-start.34 = (f32[192,128]{1,0:T(8,128)S(1)}, f32[192,128]{1,0:T(8,128)S(1)}, u32[]{:S(2)}, u32[]{:S(2)}) collective-permute-start(f32[192,128]{1,0:T(8,128)S(1)} %ag3_column.1.refs_8_), channel_id=1, source_target_pairs={{0,2},{1,3},{2,0},{3,1},{4,6},{5,7},{6,4},{7,5},{8,10},{9,11},{10,... | collective-permute-start | bytes 294920 | tf_op jit(solution)/shard_map/ag3_c1/ppermute | solution.py:165
  82.3 11.4 %collective-permute-start.35 = (f32[192,128]{1,0:T(8,128)S(1)}, f32[192,128]{1,0:T(8,128)S(1)}, u32[]{:S(2)}, u32[]{:S(2)}) collective-permute-start(f32[192,128]{1,0:T(8,128)S(1)} %ag3_column.1.refs_8_), channel_id=1, source_target_pairs={{0,4},{1,5},{2,6},{3,7},{4,0},{5,1},{6,2},{7,3},{8,12},{9,13},{10,... | collective-permute-start | bytes 294920 | tf_op jit(solution)/shard_map/ag3_c2/ppermute | solution.py:165
  83.8 10.0 %collective-permute-start.36 = (f32[192,128]{1,0:T(8,128)S(1)}, f32[192,128]{1,0:T(8,128)}, u32[]{:S(2)}, u32[]{:S(2)}) collective-permute-start(f32[192,128]{1,0:T(8,128)S(1)} %ag3_column.1.refs_8_), channel_id=1, source_target_pairs={{0,6},{1,7},{2,4},{3,5},{4,2},{5,3},{6,0},{7,1},{8,14},{9,15},{10,... | collective-permute-start | bytes 294920 | tf_op jit(solution)/shard_map/ag3_c3/ppermute | solution.py:165
  84.4 5.3 %collective-permute-start.29 = (f32[64,128]{1,0:T(8,128)}, f32[64,128]{1,0:T(8,128)}, u32[]{:S(2)}, u32[]{:S(2)}) collective-permute-start(f32[64,128]{1,0:T(8,128)} %get-tuple-element.38.refs_0_), channel_id=1, source_target_pairs={{0,4},{1,5},{2,6},{3,7},{4,0},{5,1},{6,2},{7,3},{8,12},{9,13},{10,... | collective-permute-start | bytes 98312 | tf_op jit(solution)/shard_map/ag3_n2/ppermute | solution.py:165
  85.8 0.6 copy-start
  86.4 5.1 %collective-permute-start.30 = (f32[64,128]{1,0:T(8,128)}, f32[64,128]{1,0:T(8,128)}, u32[]{:S(2)}, u32[]{:S(2)}) collective-permute-start(f32[64,128]{1,0:T(8,128)} %get-tuple-element.38.refs_0_), channel_id=1, source_target_pairs={{0,6},{1,7},{2,4},{3,5},{4,2},{5,3},{6,0},{7,1},{8,14},{9,15},{10,... | collective-permute-start | bytes 98312 | tf_op jit(solution)/shard_map/ag3_n3/ppermute | solution.py:165
  89.7 11.1 %collective-permute-start.38 = (f32[192,128]{1,0:T(8,128)S(1)}, f32[192,128]{1,0:T(8,128)S(1)}, u32[]{:S(2)}, u32[]{:S(2)}) collective-permute-start(f32[192,128]{1,0:T(8,128)S(1)} %ag3_column.1.refs_8_), channel_id=1, source_target_pairs={{0,1},{1,0},{2,3},{3,2},{4,5},{5,4},{6,7},{7,6},{8,9},{9,8},{10,11... | collective-permute-start | bytes 294920 | tf_op jit(solution)/shard_map/ag3_core1/ppermute | solution.py:165
  91.5 0.8 copy-start.1
  93.1 7.7 %collective-permute-start.37 = (f32[256,128]{1,0:T(8,128)S(1)}, f32[256,128]{1,0:T(8,128)S(1)}, u32[]{:S(2)}, u32[]{:S(2)}) collective-permute-start(f32[256,128]{1,0:T(8,128)S(1)} %ag3_near.1.refs_7_), channel_id=1, source_target_pairs={{0,1},{1,0},{2,3},{3,2},{4,5},{5,4},{6,7},{7,6},{8,9},{9,8},{10,11... | collective-permute-start | bytes 393224 | tf_op jit(solution)/shard_map/ag3_core0/ppermute | solution.py:165
  93.2 7.7 %collective-permute-start.39 = (f32[192,128]{1,0:T(8,128)S(1)}, f32[192,128]{1,0:T(8,128)S(1)}, u32[]{:S(2)}, u32[]{:S(2)}) collective-permute-start(f32[192,128]{1,0:T(8,128)S(1)} %collective-permute-done.34.refs_9_), channel_id=1, source_target_pairs={{0,1},{1,0},{2,3},{3,2},{4,5},{5,4},{6,7},{7,6},{8,9},{9,8},{10,11... | collective-permute-start | bytes 294920 | tf_op jit(solution)/shard_map/ag3_core2/ppermute | solution.py:165
  93.7 7.2 %collective-permute-start.40 = (f32[192,128]{1,0:T(8,128)S(1)}, f32[192,128]{1,0:T(8,128)S(1)}, u32[]{:S(2)}, u32[]{:S(2)}) collective-permute-start(f32[192,128]{1,0:T(8,128)S(1)} %collective-permute-done.35.refs_10_), channel_id=1, source_target_pairs={{0,1},{1,0},{2,3},{3,2},{4,5},{5,4},{6,7},{7,6},{8,9},{9,8},{10,11... | collective-permute-start | bytes 294920 | tf_op jit(solution)/shard_map/ag3_core3/ppermute | solution.py:165
  93.8 7.1 %collective-permute-start.41 = (f32[192,128]{1,0:T(8,128)}, f32[192,128]{1,0:T(8,128)S(1)}, u32[]{:S(2)}, u32[]{:S(2)}) collective-permute-start(f32[192,128]{1,0:T(8,128)} %collective-permute-done.36.refs_11_), channel_id=1, source_target_pairs={{0,1},{1,0},{2,3},{3,2},{4,5},{5,4},{6,7},{7,6},{8,9},{9,8},{10,11... | collective-permute-start | bytes 294920 | tf_op jit(solution)/shard_map/ag3_core4/ppermute | solution.py:165

commit v4 on v3

--- a/solution.py
+++ b/solution.py
@@ -4,6 +4,7 @@
 from jax.experimental import pallas as pl
 from jax.experimental.pallas import tpu as pltpu
 from jax.sharding import PartitionSpec as P
+
 
 ITERS = 2
 F32 = jnp.float32
@@ -132,8 +133,8 @@
 
 
 def layout_of(rings):
-    far = [8 * z for z in range(1, rings)]
-    chips = [[0, 2, 4, 6], far] + [[d ^ m for d in far] for m in (2, 4, 6)]
+    column = [8 * z for z in range(rings)]
+    chips = [[d ^ m for d in column] for m in (0, 2, 4, 6)]
     return chips + [[d ^ 1 for d in piece] for piece in chips]
 
 
@@ -145,32 +146,25 @@
         at += part.shape[0]
 
 
-def packed(parts, name):
+def packed(parts):
     rows = sum(part.shape[0] for part in parts)
-    with jax.named_scope(name):
-        return pl.pallas_call(
-            pack_blocks,
-            out_shape=shape(rows, parts[0].shape[1]),
-            in_specs=[VMEM] * len(parts),
-            out_specs=VMEM,
-            compiler_params=params(2),
-            cost_estimate=cost(0.5),
-            name=name,
-        )(*parts)
-
-
-def gather(block, n, tag):
-    def swap(x, m, name):
-        with jax.named_scope(tag + name):
-            return lax.ppermute(x, "blk", [(i, i ^ m) for i in range(n)])
-
-    far = [swap(block, 8 * z, f"_z{z}") for z in range(n // 8 - 1, 0, -1)][::-1]
-    near = [block] + [swap(block, 2 * k, f"_n{k}") for k in (3, 1, 2)]
-    near = [near[0], near[2], near[3], near[1]]
-    column = packed(far, tag + "_column")
-    corner = swap(column, 6, "_c3")
-    chips = [packed(near, tag + "_near"), column, swap(column, 2, "_c1"), swap(column, 4, "_c2"), corner]
-    return chips + [swap(x, 1, f"_core{i}") for i, x in enumerate(chips)]
+    return pl.pallas_call(
+        pack_blocks,
+        out_shape=shape(rows, parts[0].shape[1]),
+        in_specs=[VMEM] * len(parts),
+        out_specs=VMEM,
+        compiler_params=params(2),
+        cost_estimate=cost(0.5),
+    )(*parts)
+
+
+def gather(block, n):
+    def swap(x, m):
+        return lax.ppermute(x, "blk", [(i, i ^ m) for i in range(n)])
+
+    column = packed([block] + [swap(block, 8 * z) for z in range(1, n // 8)])
+    chips = [column] + [swap(column, 2 * k) for k in (1, 2, 3)]
+    return chips + [swap(x, 1) for x in chips]
 
 
 def assemble(me, pieces, rings, place):
@@ -193,7 +187,8 @@
     result = mm3(kernel_ref[...], y_ref[...])
     ky_ref[:rows, :] = result[:, :width]
     ky_ref[rows : 2 * rows, :] = result[:, width:]
-    ky_ref[2 * rows :, :] = jnp.broadcast_to(diag_ref[...], (8, width))
+    ky_ref[2 * rows :, :] = jnp.zeros((8, width), F32)
+    ky_ref[2 * rows : 2 * rows + 1, :rows] = diag_ref[...]
 
 
 def metric_head(y_ref, metric_ref, upper_ref):
@@ -308,7 +303,7 @@
 
 
 def second_step(
-    y2_ref, image_ref, small_ref, cross_ref, factor_ref, own_y2, own_image, own_diag, outs
+    y2_ref, image_ref, small_ref, cross_ref, factor_ref, first_ref, own_y2, own_image, own_diag, outs
 ):
     ritz_ref, search_ref, norm_ref = outs
     total, double = y2_ref.shape
@@ -339,7 +334,8 @@
         return acc + jnp.sum(residual * residual, axis=0, keepdims=True)
 
     squares = lax.fori_loop(0, total // chunk, update, jnp.zeros((1, width), F32))
-    norm_ref[...] = jnp.sqrt(squares)
+    norm_ref[:1, :] = first_ref[...]
+    norm_ref[1:, :] = jnp.sqrt(squares)
     own = own_y2()
     ritz = mm(own, mixing)
     ritz_ref[...] = ritz
@@ -347,7 +343,7 @@
     search_ref[...] = divided(residual, own_diag(), values2)
 
 
-def last_step(rings, rows, me_ref, y2_ref, kx_ref, small_ref, cross_ref, factor_ref, own_ref, *refs):
+def last_step(rings, rows, me_ref, y2_ref, kx_ref, small_ref, cross_ref, factor_ref, first_ref, diag_ref, *refs):
     pieces = refs[:-4]
     ritz_ref, search_ref, norm_ref, image_ref = refs[-4:]
     width = kx_ref.shape[1]
@@ -366,20 +362,24 @@
         small_ref,
         cross_ref,
         factor_ref,
+        first_ref,
         lambda: y2_ref[mine, :],
         lambda: image_ref[mine, :],
-        lambda: own_ref[...],
+        lambda: jnp.broadcast_to(diag_ref[...], (8, rows)).T[:, :1],
         (ritz_ref, search_ref, norm_ref),
     )
 
 
-def general_last(y2_ref, image_ref, small_ref, cross_ref, factor_ref, own_y2, own_image, own_diag, *outs):
+def general_last(
+    y2_ref, image_ref, small_ref, cross_ref, factor_ref, first_ref, own_y2, own_image, own_diag, *outs
+):
     second_step(
         y2_ref,
         image_ref,
         small_ref,
         cross_ref,
         factor_ref,
+        first_ref,
         lambda: own_y2[...],
         lambda: own_image[...],
         lambda: own_diag[...],
@@ -401,40 +401,37 @@
 
 def metric_factor(y, mebibytes):
     width = y.shape[1] // 2
-    with jax.named_scope("metric_head"):
-        metric, upper = pl.pallas_call(
-            metric_head,
-            out_shape=(shape(2 * width, 2 * width), shape(width, width)),
-            in_specs=[VMEM],
-            out_specs=(VMEM, VMEM),
-            compiler_params=params(mebibytes),
-            cost_estimate=cost(7),
-            name="metric_head",
-        )(y)
-    with jax.named_scope("metric_tail"):
-        return pl.pallas_call(
-            metric_tail,
-            out_shape=shape(2 * width, 2 * width),
-            in_specs=[VMEM, VMEM],
-            out_specs=VMEM,
-            compiler_params=params(mebibytes),
-            cost_estimate=cost(7),
-            name="metric_tail",
-        )(metric, upper)
+    metric, upper = pl.pallas_call(
+        metric_head,
+        out_shape=(shape(2 * width, 2 * width), shape(width, width)),
+        in_specs=[VMEM],
+        out_specs=(VMEM, VMEM),
+        compiler_params=params(mebibytes),
+        cost_estimate=cost(7),
+        name="metric_head",
+    )(y)
+    return pl.pallas_call(
+        metric_tail,
+        out_shape=shape(2 * width, 2 * width),
+        in_specs=[VMEM, VMEM],
+        out_specs=VMEM,
+        compiler_params=params(mebibytes),
+        cost_estimate=cost(7),
+        name="metric_tail",
+    )(metric, upper)
 
 
 def second_metric(y2, mebibytes):
     width = y2.shape[1] // 2
-    with jax.named_scope("second_factor"):
-        return pl.pallas_call(
-            second_factor,
-            out_shape=(shape(width, width), shape(width, width)),
-            in_specs=[VMEM],
-            out_specs=(VMEM, VMEM),
-            compiler_params=params(mebibytes),
-            cost_estimate=cost(9),
-            name="second_factor",
-        )(y2)
+    return pl.pallas_call(
+        second_factor,
+        out_shape=(shape(width, width), shape(width, width)),
+        in_specs=[VMEM],
+        out_specs=(VMEM, VMEM),
+        compiler_params=params(mebibytes),
+        cost_estimate=cost(9),
+        name="second_factor",
+    )(y2)
 
 
 def cubed(n, kernel, ritz, search, diag):
@@ -443,8 +440,8 @@
     total = n * rows
     lanes = max(n, 128)
     me = lax.axis_index("blk").astype(jnp.int32).reshape(1)
-    along = jnp.zeros((1, width), F32).at[0, :rows].set(diag)
-    sent = gather(jnp.concatenate([ritz, search], 0), n, "ag1")
+    along = diag.reshape(1, rows)
+    sent = gather(packed([ritz, search]), n)
     y, ky_own = pl.pallas_call(
         lambda *refs: first_product(rings, rows, *refs),
         out_shape=(shape(total, 2 * width), shape(2 * rows + 8, width)),
@@ -453,7 +450,7 @@
         compiler_params=params(16),
         name="first_product",
     )(me, kernel, along, *sent)
-    images = gather(ky_own, n, "ag2")
+    images = gather(ky_own, n)
     factor = metric_factor(y, 12)
     y2, kx, values, norm1, kw_own = pl.pallas_call(
         lambda *refs: with_product(rings, rows, *refs),
@@ -474,18 +471,17 @@
         compiler_params=params(24),
         name="first_step",
     )(me, kernel, y, factor, *images)
-    images2 = gather(kw_own, n, "ag3")
+    images2 = gather(kw_own, n)
     cross, factor2 = second_metric(y2, 12)
-    new_ritz, correction, norm2 = pl.pallas_call(
+    return pl.pallas_call(
         lambda *refs: last_step(rings, rows, *refs),
-        out_shape=(shape(rows, width), shape(rows, width), shape(1, width)),
-        in_specs=[SMEM] + [VMEM] * (6 + len(images2)),
+        out_shape=(shape(rows, width), shape(rows, width), shape(ITERS, width)),
+        in_specs=[SMEM] + [VMEM] * (7 + len(images2)),
         out_specs=(VMEM,) * 3,
         scratch_shapes=[pltpu.VMEM((total, 2 * width), F32)],
         compiler_params=params(24),
         name="last_step",
-    )(me, y2, kx, values, cross, factor2, diag[:, None], *images2)
-    return new_ritz, correction, jnp.concatenate([norm1, norm2], 0)
+    )(me, y2, kx, values, cross, factor2, norm1, along, *images2)
 
 
 def general(n, cols, kernel, ritz, search, diag):
@@ -518,10 +514,10 @@
     cross, factor2 = second_metric(y2, 56)
     image = jnp.concatenate([kx, kw], 1)
     at = (lax.axis_index("blk") * cols + q) * rows
-    new_ritz, correction, norm2 = pl.pallas_call(
+    return pl.pallas_call(
         general_last,
-        out_shape=(shape(rows, width), shape(rows, width), shape(1, width)),
-        in_specs=[VMEM] * 8,
+        out_shape=(shape(rows, width), shape(rows, width), shape(ITERS, width)),
+        in_specs=[VMEM] * 9,
         out_specs=(VMEM,) * 3,
         compiler_params=params(),
         name="last_step",
@@ -531,11 +527,11 @@
         values,
         cross,
         factor2,
+        norm1,
         lax.dynamic_slice_in_dim(y2, at, rows, 0),
         lax.dynamic_slice_in_dim(image, at, rows, 0),
         diag[:, None],
     )
-    return new_ritz, correction, jnp.concatenate([norm1, norm2], 0)
 
 
 def solution(mesh):
@@ -547,9 +543,11 @@
         P(("blk", "col")),
     )
 
+    cubes = cols == 1 and n >= 16 and n & (n - 1) == 0
+
     def per_device(kernel, ritz_block, search_block, precond_diag):
         rows = kernel[:, 0, :]
-        if cols == 1 and n >= 16 and n & (n - 1) == 0 and ritz_block.shape[0] <= ritz_block.shape[1]:
+        if cubes:
             return cubed(n, rows, ritz_block, search_block, precond_diag)
         return general(n, cols, rows, ritz_block, search_block, precond_diag)
 

time: 116 us -> 110 us (0.948)
  waiting for transfers between devices: 20.5 us -> 35.4 us
  starting transfers between devices: 41.3 us -> 26.7 us
  Pallas kernels: 47.6 us -> 45.3 us
  other arithmetic: 1.86 us -> 0 us
  local copies, waits for them, and re-layouts: 3.22 us -> 1.68 us
    ppermute x42 -> x30, waiting for transfers between devices: 20.5 us -> 35.4 us  [swap(): return lax.ppermute(x, 'blk', [(i, i ^ m) for i in range(n)])]
    ppermute x42 -> x30, starting transfers between devices: 41.3 us -> 26.7 us  [swap(): return lax.ppermute(x, 'blk', [(i, i ^ m) for i in range(n)])]
    another operation x2 -> x0, other arithmetic: 1.29 us -> none
    unnamed x10 -> x9, local copies, waits for them, and re-layouts: 2.36 us -> 1.68 us
  transfers between devices with their start and end apart: 42 -> 30, of which waited for: 12 -> 17; matrix products, arithmetic and copies ran while one was open for 1% -> 0% of each run, Pallas kernels for 17% -> 17%
where the time goes in v4:
time: 110 us
  Pallas kernels  45.3 us (41%)
  waiting for transfers between devices  35.4 us (32%)
  starting transfers between devices  26.7 us (24%)
  local copies, waits for them, and re-layouts  1.68 us (2%)
    ppermute x30, waiting for transfers between devices, swap(): return lax.ppermute(x, 'blk', [(i, i ^ m) for i in range(n)])  35.4 us
    ppermute x30, starting transfers between devices, swap(): return lax.ppermute(x, 'blk', [(i, i ^ m) for i in range(n)])  26.7 us
    pallas_call x1, Pallas kernels, cubed(): pl.pallas_call(lambda *refs: last_step(rings, rows, *refs), out_shape=(sh...  13.1 us
    pallas_call x1, Pallas kernels, cubed(): pl.pallas_call(lambda *refs: with_product(rings, rows, *refs), out_shape=...  12.9 us
    pallas_call x1, Pallas kernels, second_metric(): pl.pallas_call(second_factor, out_shape=(shape(width, width), shape(width...  6.63 us
    pallas_call x1, Pallas kernels, metric_factor(): pl.pallas_call(metric_head, out_shape=(shape(2 * width, 2 * width), shape...  6.48 us
    pallas_call x1, Pallas kernels, metric_factor(): pl.pallas_call(metric_tail, out_shape=shape(2 * width, 2 * width), in_spe...  5.37 us
  transfers between devices with their start and end apart: 30, of which 17 were waited for; matrix products, arithmetic and copies ran while one was open for 0% of the time, Pallas kernels for 17%

profile of v4, /device:TPU:0, one launch (start us, length us, event | category | flops | bytes accessed | tf_op | source)
XLA Modules:
  0.0 109.8 jit_solution(17299405406872880308)
XLA Ops:
  0.6 0.7 copy-done.1
  1.4 0.8 copy-done.2
  2.2 5.1 %collective-permute-start.2 = (f32[128,128]{1,0:T(8,128)S(1)}, f32[128,128]{1,0:T(8,128)S(1)}, u32[]{:S(2)}, u32[]{:S(2)}) collective-permute-start(f32[128,128]{1,0:T(8,128)S(1)} %shard_map.67.refs_0_), channel_id=1, source_target_pairs={{0,24},{1,25},{2,26},{3,27},{4,28},{5,29},{6,30},{7,31},{8,16},{9,... | collective-permute-start | bytes 196616 | tf_op jit(solution)/shard_map/ppermute | solution.py:163
  7.3 0.6 collective-permute-start
  7.9 1.8 %collective-permute-done.2.refs_3_ = f32[128,128]{1,0:T(8,128)S(1)} collective-permute-done((f32[128,128]{1,0:T(8,128)S(1)}, f32[128,128]{1,0:T(8,128)S(1)}, u32[]{:S(2)}, u32[]{:S(2)}) %collective-permute-start.2) | collective-permute-done | bytes 65568 | tf_op jit(solution)/shard_map/ppermute | solution.py:163
  9.8 3.1 %collective-permute-done.1.refs_2_ = f32[128,128]{1,0:T(8,128)S(1)} collective-permute-done((f32[128,128]{1,0:T(8,128)S(1)}, f32[128,128]{1,0:T(8,128)S(1)}, u32[]{:S(2)}, u32[]{:S(2)}) %collective-permute-start.1) | collective-permute-done | bytes 65568 | tf_op jit(solution)/shard_map/ppermute | solution.py:163
  12.9 2.5 %collective-permute-start.5 = (f32[512,128]{1,0:T(8,128)S(1)}, f32[512,128]{1,0:T(8,128)S(1)}, u32[]{:S(2)}, u32[]{:S(2)}) collective-permute-start(f32[512,128]{1,0:T(8,128)S(1)} %shard_map.68.refs_3_), channel_id=1, source_target_pairs={{0,6},{1,7},{2,4},{3,5},{4,2},{5,3},{6,0},{7,1},{8,14},{9,15},{10,... | collective-permute-start | bytes 786440 | tf_op jit(solution)/shard_map/ppermute | solution.py:163
  15.4 0.5 collective-permute-start.4
  16.0 0.5 collective-permute-start.3
  16.5 6.6 %collective-permute-done.5.refs_6_ = f32[512,128]{1,0:T(8,128)S(1)} collective-permute-done((f32[512,128]{1,0:T(8,128)S(1)}, f32[512,128]{1,0:T(8,128)S(1)}, u32[]{:S(2)}, u32[]{:S(2)}) %collective-permute-start.5) | collective-permute-done | bytes 262176 | tf_op jit(solution)/shard_map/ppermute | solution.py:163
  23.1 4.3 %collective-permute-done.4.refs_5_ = f32[512,128]{1,0:T(8,128)S(1)} collective-permute-done((f32[512,128]{1,0:T(8,128)S(1)}, f32[512,128]{1,0:T(8,128)S(1)}, u32[]{:S(2)}, u32[]{:S(2)}) %collective-permute-start.4) | collective-permute-done | bytes 262176 | tf_op jit(solution)/shard_map/ppermute | solution.py:163
  27.4 0.0 collective-permute-start.8
  27.4 0.2 collective-permute-done.3.refs_4_
  27.6 0.3 collective-permute-start.7
  27.9 0.2 copy.9
  28.1 0.8 collective-permute-done.8.refs_9_
  28.9 0.4 collective-permute-done.7.refs_8_
  29.3 0.8 first_product.1
  30.1 1.7 %collective-permute-start.12 = (f32[136,128]{1,0:T(8,128)S(1)}, f32[136,128]{1,0:T(8,128)S(1)}, u32[]{:S(2)}, u32[]{:S(2)}) collective-permute-start(f32[136,128]{1,0:T(8,128)S(1)} %get-tuple-element.17.refs_0_), channel_id=1, source_target_pairs={{0,24},{1,25},{2,26},{3,27},{4,28},{5,29},{6,30},{7,31},{8,16},{9,... | collective-permute-start | bytes 208904 | tf_op jit(solution)/shard_map/ppermute | solution.py:163
  31.8 2.8 %collective-permute-start.10 = (f32[136,128]{1,0:T(8,128)S(1)}, f32[136,128]{1,0:T(8,128)S(1)}, u32[]{:S(2)}, u32[]{:S(2)}) collective-permute-start(f32[136,128]{1,0:T(8,128)S(1)} %get-tuple-element.17.refs_0_), channel_id=1, source_target_pairs={{0,8},{1,9},{2,10},{3,11},{4,12},{5,13},{6,14},{7,15},{8,0},{9,1},... | collective-permute-start | bytes 208904 | tf_op jit(solution)/shard_map/ppermute | solution.py:163
  34.6 2.5 %collective-permute-done.12.refs_3_ = f32[136,128]{1,0:T(8,128)S(1)} collective-permute-done((f32[136,128]{1,0:T(8,128)S(1)}, f32[136,128]{1,0:T(8,128)S(1)}, u32[]{:S(2)}, u32[]{:S(2)}) %collective-permute-start.12) | collective-permute-done | bytes 69664 | tf_op jit(solution)/shard_map/ppermute | solution.py:163
  37.1 2.1 %collective-permute-done.11.refs_2_ = f32[136,128]{1,0:T(8,128)S(1)} collective-permute-done((f32[136,128]{1,0:T(8,128)S(1)}, f32[136,128]{1,0:T(8,128)S(1)}, u32[]{:S(2)}, u32[]{:S(2)}) %collective-permute-start.11) | collective-permute-done | bytes 69664 | tf_op jit(solution)/shard_map/ppermute | solution.py:163
  39.2 1.8 %collective-permute-start.15 = (f32[544,128]{1,0:T(8,128)S(1)}, f32[544,128]{1,0:T(8,128)S(1)}, u32[]{:S(2)}, u32[]{:S(2)}) collective-permute-start(f32[544,128]{1,0:T(8,128)S(1)} %shard_map.69.refs_4_), channel_id=1, source_target_pairs={{0,6},{1,7},{2,4},{3,5},{4,2},{5,3},{6,0},{7,1},{8,14},{9,15},{10,... | collective-permute-start | bytes 835592 | tf_op jit(solution)/shard_map/ppermute | solution.py:163
  41.0 1.3 %collective-permute-start.14 = (f32[544,128]{1,0:T(8,128)S(1)}, f32[544,128]{1,0:T(8,128)S(1)}, u32[]{:S(2)}, u32[]{:S(2)}) collective-permute-start(f32[544,128]{1,0:T(8,128)S(1)} %shard_map.69.refs_4_), channel_id=1, source_target_pairs={{0,4},{1,5},{2,6},{3,7},{4,0},{5,1},{6,2},{7,3},{8,12},{9,13},{10,... | collective-permute-start | bytes 835592 | tf_op jit(solution)/shard_map/ppermute | solution.py:163
  42.4 0.4 collective-permute-start.13
  42.8 6.5 %metric_head.1 = (f32[256,256]{1,0:T(8,128)S(1)}, f32[128,128]{1,0:T(8,128)S(1)}) custom-call(f32[2048,256]{1,0:T(8,128)S(1)} %get-tuple-element.14.y_ref.refs_2_), custom_call_target="tpu_custom_call" | custom-call | flops 7000000000 | tf_op jit(solution)/shard_map/metric_head/pallas_call | solution.py:404
  49.3 0.1 collective-permute-start.16
  49.4 0.4 collective-permute-done.15.refs_7_
  49.8 0.1 collective-permute-start.19
  49.9 4.9 %collective-permute-done.14.refs_6_ = f32[544,128]{1,0:T(8,128)S(1)} collective-permute-done((f32[544,128]{1,0:T(8,128)S(1)}, f32[544,128]{1,0:T(8,128)S(1)}, u32[]{:S(2)}, u32[]{:S(2)}) %collective-permute-start.14) | collective-permute-done | bytes 278560 | tf_op jit(solution)/shard_map/ppermute | solution.py:163
  54.7 0.0 collective-permute-start.18
  54.8 0.2 collective-permute-done.13.refs_5_
  55.0 0.3 collective-permute-start.17
  55.3 5.4 %metric_tail.1.refs_3_ = f32[256,256]{1,0:T(8,128)S(1)} custom-call(f32[256,256]{1,0:T(8,128)S(1)} %get-tuple-element.15.metric_ref, f32[128,128]{1,0:T(8,128)S(1)} %get-tuple-element.16.upper_ref), custom_call_target="tpu_custom_call" | custom-call | flops 7000000000 | tf_op jit(solution)/shard_map/metric_tail/pallas_call | solution.py:413
  60.7 12.9 %first_step.1 = (f32[2048,256]{1,0:T(8,128)S(1)}, f32[2048,128]{1,0:T(8,128)S(1)}, f32[128,128]{1,0:T(8,128)S(1)}, f32[1,128]{1,0:T(1,128)S(1)}, f32[64,128]{1,0:T(8,128)S(1)}) custom-call(s32[1]{0:T(128)} %bitcast.refs_0_, f32[64,2048]{1,0:T(8,128)S(1)} %bitcast.6, f32[2048,256]{1,0:T(8,128)S(1)} %get-tuple-element.14.y_ref.refs_2_, ...), custom_call_target="tpu_custom_call" | custom-call | tf_op jit(solution)/shard_map/first_step/pallas_call | solution.py:455
  73.6 1.7 %collective-permute-start.22 = (f32[64,128]{1,0:T(8,128)S(1)}, f32[64,128]{1,0:T(8,128)S(1)}, u32[]{:S(2)}, u32[]{:S(2)}) collective-permute-start(f32[64,128]{1,0:T(8,128)S(1)} %get-tuple-element.24.refs_0_), channel_id=1, source_target_pairs={{0,24},{1,25},{2,26},{3,27},{4,28},{5,29},{6,30},{7,31},{8,16},{9,... | collective-permute-start | bytes 98312 | tf_op jit(solution)/shard_map/ppermute | solution.py:163
  75.2 2.8 %collective-permute-start.20 = (f32[64,128]{1,0:T(8,128)S(1)}, f32[64,128]{1,0:T(8,128)S(1)}, u32[]{:S(2)}, u32[]{:S(2)}) collective-permute-start(f32[64,128]{1,0:T(8,128)S(1)} %get-tuple-element.24.refs_0_), channel_id=1, source_target_pairs={{0,8},{1,9},{2,10},{3,11},{4,12},{5,13},{6,14},{7,15},{8,0},{9,1},... | collective-permute-start | bytes 98312 | tf_op jit(solution)/shard_map/ppermute | solution.py:163
  78.0 1.4 %collective-permute-done.22.refs_3_ = f32[64,128]{1,0:T(8,128)S(1)} collective-permute-done((f32[64,128]{1,0:T(8,128)S(1)}, f32[64,128]{1,0:T(8,128)S(1)}, u32[]{:S(2)}, u32[]{:S(2)}) %collective-permute-start.22) | collective-permute-done | bytes 32800 | tf_op jit(solution)/shard_map/ppermute | solution.py:163
  79.4 1.0 collective-permute-done.21.refs_2_
  80.3 0.2 collective-permute-done.20.refs_1_
  80.5 1.7 %collective-permute-start.25 = (f32[256,128]{1,0:T(8,128)S(1)}, f32[256,128]{1,0:T(8,128)S(1)}, u32[]{:S(2)}, u32[]{:S(2)}) collective-permute-start(f32[256,128]{1,0:T(8,128)S(1)} %shard_map.70.refs_8_), channel_id=1, source_target_pairs={{0,6},{1,7},{2,4},{3,5},{4,2},{5,3},{6,0},{7,1},{8,14},{9,15},{10,... | collective-permute-start | bytes 393224 | tf_op jit(solution)/shard_map/ppermute | solution.py:163
  82.2 1.3 %collective-permute-start.24 = (f32[256,128]{1,0:T(8,128)S(1)}, f32[256,128]{1,0:T(8,128)S(1)}, u32[]{:S(2)}, u32[]{:S(2)}) collective-permute-start(f32[256,128]{1,0:T(8,128)S(1)} %shard_map.70.refs_8_), channel_id=1, source_target_pairs={{0,4},{1,5},{2,6},{3,7},{4,0},{5,1},{6,2},{7,3},{8,12},{9,13},{10,... | collective-permute-start | bytes 393224 | tf_op jit(solution)/shard_map/ppermute | solution.py:163
  83.5 0.6 collective-permute-start.23
  84.1 3.8 %collective-permute-done.25.refs_11_ = f32[256,128]{1,0:T(8,128)S(1)} collective-permute-done((f32[256,128]{1,0:T(8,128)S(1)}, f32[256,128]{1,0:T(8,128)S(1)}, u32[]{:S(2)}, u32[]{:S(2)}) %collective-permute-start.25) | collective-permute-done | bytes 131104 | tf_op jit(solution)/shard_map/ppermute | solution.py:163
  87.9 1.7 %collective-permute-done.24.refs_10_ = f32[256,128]{1,0:T(8,128)S(1)} collective-permute-done((f32[256,128]{1,0:T(8,128)S(1)}, f32[256,128]{1,0:T(8,128)S(1)}, u32[]{:S(2)}, u32[]{:S(2)}) %collective-permute-start.24) | collective-permute-done | bytes 131104 | tf_op jit(solution)/shard_map/ppermute | solution.py:163
  89.6 0.5 collective-permute-start.27
  90.1 6.6 %second_factor.1 = (f32[128,128]{1,0:T(8,128)S(1)}, f32[128,128]{1,0:T(8,128)S(1)}) custom-call(f32[2048,256]{1,0:T(8,128)S(1)} %get-tuple-element.18.y2_ref.refs_1_), custom_call_target="tpu_custom_call" | custom-call | flops 8999999488 | tf_op jit(solution)/shard_map/second_factor/pallas_call | solution.py:426
  96.7 13.1 %last_step.1 = (f32[64,128]{1,0:T(8,128)}, f32[64,128]{1,0:T(8,128)}, f32[2,128]{1,0:T(2,128)}) custom-call(s32[1]{0:T(128)} %bitcast.refs_0_, f32[2048,256]{1,0:T(8,128)S(1)} %get-tuple-element.18.y2_ref.refs_1_, f32[2048,128]{1,0:T(8,128)S(1)} %get-tuple-element.19.refs_2_, f32[128,128]{1,0:T(8,128)S(1)} %get-tuple-element.20.refs_3_, ...), custom_call_target="tpu_custom_call" | custom-call | tf_op jit(solution)/shard_map/last_step/pallas_call | solution.py:476
  (31 shorter events, 0.1 us)
Async XLA Ops:
  0.6 0.8 copy-start.1
  1.4 0.8 copy-start.2
  2.1 25.8 %copy-start.3 = (f32[64,1,2048]{2,1,0:T(1,128)S(1)}, f32[64,1,2048]{2,1,0:T(1,128)}, u32[]{:S(2)}) copy-start(f32[64,1,2048]{2,1,0:T(1,128)} %param.4) | copy-start | bytes 1572868
  2.2 27.2 %copy-start = (f32[64]{0:T(128)S(1)}, f32[64]{0:T(128)}, u32[]{:S(2)}) copy-start(f32[64]{0:T(128)} %param.7) | copy-start | bytes 772
  2.2 7.6 %collective-permute-start.2 = (f32[128,128]{1,0:T(8,128)S(1)}, f32[128,128]{1,0:T(8,128)S(1)}, u32[]{:S(2)}, u32[]{:S(2)}) collective-permute-start(f32[128,128]{1,0:T(8,128)S(1)} %shard_map.67.refs_0_), channel_id=1, source_target_pairs={{0,24},{1,25},{2,26},{3,27},{4,28},{5,29},{6,30},{7,31},{8,16},{9,... | collective-permute-start | bytes 196616 | tf_op jit(solution)/shard_map/ppermute | solution.py:163
  7.3 5.6 %collective-permute-start.1 = (f32[128,128]{1,0:T(8,128)S(1)}, f32[128,128]{1,0:T(8,128)S(1)}, u32[]{:S(2)}, u32[]{:S(2)}) collective-permute-start(f32[128,128]{1,0:T(8,128)S(1)} %shard_map.67.refs_0_), channel_id=1, source_target_pairs={{0,16},{1,17},{2,18},{3,19},{4,20},{5,21},{6,22},{7,23},{8,24},{9,... | collective-permute-start | bytes 196616 | tf_op jit(solution)/shard_map/ppermute | solution.py:163
  7.3 5.6 %collective-permute-start = (f32[128,128]{1,0:T(8,128)S(1)}, f32[128,128]{1,0:T(8,128)S(1)}, u32[]{:S(2)}, u32[]{:S(2)}) collective-permute-start(f32[128,128]{1,0:T(8,128)S(1)} %shard_map.67.refs_0_), channel_id=1, source_target_pairs={{0,8},{1,9},{2,10},{3,11},{4,12},{5,13},{6,14},{7,15},{8,0},{9,1},... | collective-permute-start | bytes 196616 | tf_op jit(solution)/shard_map/ppermute | solution.py:163
  12.9 10.2 %collective-permute-start.5 = (f32[512,128]{1,0:T(8,128)S(1)}, f32[512,128]{1,0:T(8,128)S(1)}, u32[]{:S(2)}, u32[]{:S(2)}) collective-permute-start(f32[512,128]{1,0:T(8,128)S(1)} %shard_map.68.refs_3_), channel_id=1, source_target_pairs={{0,6},{1,7},{2,4},{3,5},{4,2},{5,3},{6,0},{7,1},{8,14},{9,15},{10,... | collective-permute-start | bytes 786440 | tf_op jit(solution)/shard_map/ppermute | solution.py:163
  15.4 11.9 %collective-permute-start.4 = (f32[512,128]{1,0:T(8,128)S(1)}, f32[512,128]{1,0:T(8,128)S(1)}, u32[]{:S(2)}, u32[]{:S(2)}) collective-permute-start(f32[512,128]{1,0:T(8,128)S(1)} %shard_map.68.refs_3_), channel_id=1, source_target_pairs={{0,4},{1,5},{2,6},{3,7},{4,0},{5,1},{6,2},{7,3},{8,12},{9,13},{10,... | collective-permute-start | bytes 786440 | tf_op jit(solution)/shard_map/ppermute | solution.py:163
  16.0 11.7 %collective-permute-start.3 = (f32[512,128]{1,0:T(8,128)S(1)}, f32[512,128]{1,0:T(8,128)S(1)}, u32[]{:S(2)}, u32[]{:S(2)}) collective-permute-start(f32[512,128]{1,0:T(8,128)S(1)} %shard_map.68.refs_3_), channel_id=1, source_target_pairs={{0,2},{1,3},{2,0},{3,1},{4,6},{5,7},{6,4},{7,5},{8,10},{9,11},{10,... | collective-permute-start | bytes 786440 | tf_op jit(solution)/shard_map/ppermute | solution.py:163
  16.5 11.6 %collective-permute-start.6 = (f32[512,128]{1,0:T(8,128)S(1)}, f32[512,128]{1,0:T(8,128)S(1)}, u32[]{:S(2)}, u32[]{:S(2)}) collective-permute-start(f32[512,128]{1,0:T(8,128)S(1)} %shard_map.68.refs_3_), channel_id=1, source_target_pairs={{0,1},{1,0},{2,3},{3,2},{4,5},{5,4},{6,7},{7,6},{8,9},{9,8},{10,11... | collective-permute-start | bytes 786440 | tf_op jit(solution)/shard_map/ppermute | solution.py:163
  23.1 5.0 %collective-permute-start.9 = (f32[512,128]{1,0:T(8,128)S(1)}, f32[512,128]{1,0:T(8,128)S(1)}, u32[]{:S(2)}, u32[]{:S(2)}) collective-permute-start(f32[512,128]{1,0:T(8,128)S(1)} %collective-permute-done.5.refs_6_), channel_id=1, source_target_pairs={{0,1},{1,0},{2,3},{3,2},{4,5},{5,4},{6,7},{7,6},{8,9},{9,8},{10,11... | collective-permute-start | bytes 786440 | tf_op jit(solution)/shard_map/ppermute | solution.py:163
  27.4 1.5 %collective-permute-start.8 = (f32[512,128]{1,0:T(8,128)S(1)}, f32[512,128]{1,0:T(8,128)S(1)}, u32[]{:S(2)}, u32[]{:S(2)}) collective-permute-start(f32[512,128]{1,0:T(8,128)S(1)} %collective-permute-done.4.refs_5_), channel_id=1, source_target_pairs={{0,1},{1,0},{2,3},{3,2},{4,5},{5,4},{6,7},{7,6},{8,9},{9,8},{10,11... | collective-permute-start | bytes 786440 | tf_op jit(solution)/shard_map/ppermute | solution.py:163
  27.6 1.7 %collective-permute-start.7 = (f32[512,128]{1,0:T(8,128)S(1)}, f32[512,128]{1,0:T(8,128)S(1)}, u32[]{:S(2)}, u32[]{:S(2)}) collective-permute-start(f32[512,128]{1,0:T(8,128)S(1)} %collective-permute-done.3.refs_4_), channel_id=1, source_target_pairs={{0,1},{1,0},{2,3},{3,2},{4,5},{5,4},{6,7},{7,6},{8,9},{9,8},{10,11... | collective-permute-start | bytes 786440 | tf_op jit(solution)/shard_map/ppermute | solution.py:163
  30.1 6.9 %collective-permute-start.12 = (f32[136,128]{1,0:T(8,128)S(1)}, f32[136,128]{1,0:T(8,128)S(1)}, u32[]{:S(2)}, u32[]{:S(2)}) collective-permute-start(f32[136,128]{1,0:T(8,128)S(1)} %get-tuple-element.17.refs_0_), channel_id=1, source_target_pairs={{0,24},{1,25},{2,26},{3,27},{4,28},{5,29},{6,30},{7,31},{8,16},{9,... | collective-permute-start | bytes 208904 | tf_op jit(solution)/shard_map/ppermute | solution.py:163
  31.8 7.4 %collective-permute-start.11 = (f32[136,128]{1,0:T(8,128)S(1)}, f32[136,128]{1,0:T(8,128)S(1)}, u32[]{:S(2)}, u32[]{:S(2)}) collective-permute-start(f32[136,128]{1,0:T(8,128)S(1)} %get-tuple-element.17.refs_0_), channel_id=1, source_target_pairs={{0,16},{1,17},{2,18},{3,19},{4,20},{5,21},{6,22},{7,23},{8,24},{9,... | collective-permute-start | bytes 208904 | tf_op jit(solution)/shard_map/ppermute | solution.py:163
  31.8 7.4 %collective-permute-start.10 = (f32[136,128]{1,0:T(8,128)S(1)}, f32[136,128]{1,0:T(8,128)S(1)}, u32[]{:S(2)}, u32[]{:S(2)}) collective-permute-start(f32[136,128]{1,0:T(8,128)S(1)} %get-tuple-element.17.refs_0_), channel_id=1, source_target_pairs={{0,8},{1,9},{2,10},{3,11},{4,12},{5,13},{6,14},{7,15},{8,0},{9,1},... | collective-permute-start | bytes 208904 | tf_op jit(solution)/shard_map/ppermute | solution.py:163
  39.2 10.5 %collective-permute-start.15 = (f32[544,128]{1,0:T(8,128)S(1)}, f32[544,128]{1,0:T(8,128)S(1)}, u32[]{:S(2)}, u32[]{:S(2)}) collective-permute-start(f32[544,128]{1,0:T(8,128)S(1)} %shard_map.69.refs_4_), channel_id=1, source_target_pairs={{0,6},{1,7},{2,4},{3,5},{4,2},{5,3},{6,0},{7,1},{8,14},{9,15},{10,... | collective-permute-start | bytes 835592 | tf_op jit(solution)/shard_map/ppermute | solution.py:163
  41.0 13.7 %collective-permute-start.14 = (f32[544,128]{1,0:T(8,128)S(1)}, f32[544,128]{1,0:T(8,128)S(1)}, u32[]{:S(2)}, u32[]{:S(2)}) collective-permute-start(f32[544,128]{1,0:T(8,128)S(1)} %shard_map.69.refs_4_), channel_id=1, source_target_pairs={{0,4},{1,5},{2,6},{3,7},{4,0},{5,1},{6,2},{7,3},{8,12},{9,13},{10,... | collective-permute-start | bytes 835592 | tf_op jit(solution)/shard_map/ppermute | solution.py:163
  42.4 12.6 %collective-permute-start.13 = (f32[544,128]{1,0:T(8,128)S(1)}, f32[544,128]{1,0:T(8,128)S(1)}, u32[]{:S(2)}, u32[]{:S(2)}) collective-permute-start(f32[544,128]{1,0:T(8,128)S(1)} %shard_map.69.refs_4_), channel_id=1, source_target_pairs={{0,2},{1,3},{2,0},{3,1},{4,6},{5,7},{6,4},{7,5},{8,10},{9,11},{10,... | collective-permute-start | bytes 835592 | tf_op jit(solution)/shard_map/ppermute | solution.py:163
  49.3 11.4 %collective-permute-start.16 = (f32[544,128]{1,0:T(8,128)S(1)}, f32[544,128]{1,0:T(8,128)S(1)}, u32[]{:S(2)}, u32[]{:S(2)}) collective-permute-start(f32[544,128]{1,0:T(8,128)S(1)} %shard_map.69.refs_4_), channel_id=1, source_target_pairs={{0,1},{1,0},{2,3},{3,2},{4,5},{5,4},{6,7},{7,6},{8,9},{9,8},{10,11... | collective-permute-start | bytes 835592 | tf_op jit(solution)/shard_map/ppermute | solution.py:163
  49.8 10.9 %collective-permute-start.19 = (f32[544,128]{1,0:T(8,128)S(1)}, f32[544,128]{1,0:T(8,128)S(1)}, u32[]{:S(2)}, u32[]{:S(2)}) collective-permute-start(f32[544,128]{1,0:T(8,128)S(1)} %collective-permute-done.15.refs_7_), channel_id=1, source_target_pairs={{0,1},{1,0},{2,3},{3,2},{4,5},{5,4},{6,7},{7,6},{8,9},{9,8},{10,11... | collective-permute-start | bytes 835592 | tf_op jit(solution)/shard_map/ppermute | solution.py:163
  54.7 5.9 %collective-permute-start.18 = (f32[544,128]{1,0:T(8,128)S(1)}, f32[544,128]{1,0:T(8,128)S(1)}, u32[]{:S(2)}, u32[]{:S(2)}) collective-permute-start(f32[544,128]{1,0:T(8,128)S(1)} %collective-permute-done.14.refs_6_), channel_id=1, source_target_pairs={{0,1},{1,0},{2,3},{3,2},{4,5},{5,4},{6,7},{7,6},{8,9},{9,8},{10,11... | collective-permute-start | bytes 835592 | tf_op jit(solution)/shard_map/ppermute | solution.py:163
  55.0 5.7 %collective-permute-start.17 = (f32[544,128]{1,0:T(8,128)S(1)}, f32[544,128]{1,0:T(8,128)S(1)}, u32[]{:S(2)}, u32[]{:S(2)}) collective-permute-start(f32[544,128]{1,0:T(8,128)S(1)} %collective-permute-done.13.refs_5_), channel_id=1, source_target_pairs={{0,1},{1,0},{2,3},{3,2},{4,5},{5,4},{6,7},{7,6},{8,9},{9,8},{10,11... | collective-permute-start | bytes 835592 | tf_op jit(solution)/shard_map/ppermute | solution.py:163
  73.6 5.8 %collective-permute-start.22 = (f32[64,128]{1,0:T(8,128)S(1)}, f32[64,128]{1,0:T(8,128)S(1)}, u32[]{:S(2)}, u32[]{:S(2)}) collective-permute-start(f32[64,128]{1,0:T(8,128)S(1)} %get-tuple-element.24.refs_0_), channel_id=1, source_target_pairs={{0,24},{1,25},{2,26},{3,27},{4,28},{5,29},{6,30},{7,31},{8,16},{9,... | collective-permute-start | bytes 98312 | tf_op jit(solution)/shard_map/ppermute | solution.py:163
  75.2 5.1 %collective-permute-start.21 = (f32[64,128]{1,0:T(8,128)S(1)}, f32[64,128]{1,0:T(8,128)S(1)}, u32[]{:S(2)}, u32[]{:S(2)}) collective-permute-start(f32[64,128]{1,0:T(8,128)S(1)} %get-tuple-element.24.refs_0_), channel_id=1, source_target_pairs={{0,16},{1,17},{2,18},{3,19},{4,20},{5,21},{6,22},{7,23},{8,24},{9,... | collective-permute-start | bytes 98312 | tf_op jit(solution)/shard_map/ppermute | solution.py:163
  75.2 5.3 %collective-permute-start.20 = (f32[64,128]{1,0:T(8,128)S(1)}, f32[64,128]{1,0:T(8,128)S(1)}, u32[]{:S(2)}, u32[]{:S(2)}) collective-permute-start(f32[64,128]{1,0:T(8,128)S(1)} %get-tuple-element.24.refs_0_), channel_id=1, source_target_pairs={{0,8},{1,9},{2,10},{3,11},{4,12},{5,13},{6,14},{7,15},{8,0},{9,1},... | collective-permute-start | bytes 98312 | tf_op jit(solution)/shard_map/ppermute | solution.py:163
  80.5 7.3 %collective-permute-start.25 = (f32[256,128]{1,0:T(8,128)S(1)}, f32[256,128]{1,0:T(8,128)S(1)}, u32[]{:S(2)}, u32[]{:S(2)}) collective-permute-start(f32[256,128]{1,0:T(8,128)S(1)} %shard_map.70.refs_8_), channel_id=1, source_target_pairs={{0,6},{1,7},{2,4},{3,5},{4,2},{5,3},{6,0},{7,1},{8,14},{9,15},{10,... | collective-permute-start | bytes 393224 | tf_op jit(solution)/shard_map/ppermute | solution.py:163
  82.2 7.4 %collective-permute-start.24 = (f32[256,128]{1,0:T(8,128)S(1)}, f32[256,128]{1,0:T(8,128)S(1)}, u32[]{:S(2)}, u32[]{:S(2)}) collective-permute-start(f32[256,128]{1,0:T(8,128)S(1)} %shard_map.70.refs_8_), channel_id=1, source_target_pairs={{0,4},{1,5},{2,6},{3,7},{4,0},{5,1},{6,2},{7,3},{8,12},{9,13},{10,... | collective-permute-start | bytes 393224 | tf_op jit(solution)/shard_map/ppermute | solution.py:163
  83.5 6.1 %collective-permute-start.23 = (f32[256,128]{1,0:T(8,128)S(1)}, f32[256,128]{1,0:T(8,128)S(1)}, u32[]{:S(2)}, u32[]{:S(2)}) collective-permute-start(f32[256,128]{1,0:T(8,128)S(1)} %shard_map.70.refs_8_), channel_id=1, source_target_pairs={{0,2},{1,3},{2,0},{3,1},{4,6},{5,7},{6,4},{7,5},{8,10},{9,11},{10,... | collective-permute-start | bytes 393224 | tf_op jit(solution)/shard_map/ppermute | solution.py:163
  84.1 12.6 %collective-permute-start.26 = (f32[256,128]{1,0:T(8,128)S(1)}, f32[256,128]{1,0:T(8,128)S(1)}, u32[]{:S(2)}, u32[]{:S(2)}) collective-permute-start(f32[256,128]{1,0:T(8,128)S(1)} %shard_map.70.refs_8_), channel_id=1, source_target_pairs={{0,1},{1,0},{2,3},{3,2},{4,5},{5,4},{6,7},{7,6},{8,9},{9,8},{10,11... | collective-permute-start | bytes 393224 | tf_op jit(solution)/shard_map/ppermute | solution.py:163
  87.9 8.8 %collective-permute-start.29 = (f32[256,128]{1,0:T(8,128)S(1)}, f32[256,128]{1,0:T(8,128)S(1)}, u32[]{:S(2)}, u32[]{:S(2)}) collective-permute-start(f32[256,128]{1,0:T(8,128)S(1)} %collective-permute-done.25.refs_11_), channel_id=1, source_target_pairs={{0,1},{1,0},{2,3},{3,2},{4,5},{5,4},{6,7},{7,6},{8,9},{9,8},{10,11... | collective-permute-start | bytes 393224 | tf_op jit(solution)/shard_map/ppermute | solution.py:163
  89.6 7.2 %collective-permute-start.28 = (f32[256,128]{1,0:T(8,128)S(1)}, f32[256,128]{1,0:T(8,128)S(1)}, u32[]{:S(2)}, u32[]{:S(2)}) collective-permute-start(f32[256,128]{1,0:T(8,128)S(1)} %collective-permute-done.24.refs_10_), channel_id=1, source_target_pairs={{0,1},{1,0},{2,3},{3,2},{4,5},{5,4},{6,7},{7,6},{8,9},{9,8},{10,11... | collective-permute-start | bytes 393224 | tf_op jit(solution)/shard_map/ppermute | solution.py:163
  89.6 7.2 %collective-permute-start.27 = (f32[256,128]{1,0:T(8,128)S(1)}, f32[256,128]{1,0:T(8,128)S(1)}, u32[]{:S(2)}, u32[]{:S(2)}) collective-permute-start(f32[256,128]{1,0:T(8,128)S(1)} %collective-permute-done.23.refs_9_), channel_id=1, source_target_pairs={{0,1},{1,0},{2,3},{3,2},{4,5},{5,4},{6,7},{7,6},{8,9},{9,8},{10,11... | collective-permute-start | bytes 393224 | tf_op jit(solution)/shard_map/ppermute | solution.py:163

commit v5 on v4

--- a/solution.py
+++ b/solution.py
@@ -28,34 +28,47 @@
     return top, (x - top.astype(F32)).astype(BF16)
 
 
+def stacked(b, cb=0):
+    b1, b2 = halves(b)
+    return jnp.concatenate([b1, b2, b1], cb)
+
+
 def mm3(a, b, ca=1, cb=0):
+    return with_stacked(a, stacked(b, cb), ca, cb)
+
+
+def with_stacked(a, b3, ca=1, cb=0):
     a1, a2 = halves(a)
-    b1, b2 = halves(b)
     return lax.dot_general(
         jnp.concatenate([a1, a1, a2], ca),
-        jnp.concatenate([b1, b2, b1], cb),
+        b3,
         (((ca,), (cb,)), ((), ())),
         preferred_element_type=F32,
     )
 
 
+def pair_sum(terms):
+    terms = list(terms)
+    while len(terms) > 1:
+        terms = [sum(terms[i + 1 : i + 2], terms[i]) for i in range(0, len(terms), 2)]
+    return terms[0]
+
+
 def total_of(xs, ys):
-    out = xs[0] * ys[0]
-    for x, y in zip(xs[1:], ys[1:]):
-        out = out + x * y
-    return out
-
-
-def solved(entry, columns):
+    return pair_sum(x * y for x, y in zip(xs, ys))
+
+
+def solved(entry, columns, leaf):
     size = len(columns[0])
     if size == 2:
         x, y, z = entry(0, 0), entry(0, 1), entry(1, 1)
         scale = 1.0 / (x * z - y * y)
         q00, q01, q11 = z * scale, -(y * scale), x * scale
+        leaf(x, y, z, columns[-1])
         return [[q00 * c[0] + q01 * c[1], q01 * c[0] + q11 * c[1]] for c in columns]
     h = size // 2
     side = [[entry(i, h + j) for i in range(h)] for j in range(h)]
-    done = solved(entry, side + [c[:h] for c in columns])
+    done = solved(entry, side + [c[:h] for c in columns], leaf)
     ties, upper = done[:h], done[h:]
     rest = {
         (i, j): entry(h + i, h + j) - total_of(side[i], ties[j])
@@ -65,6 +78,7 @@
     lower = solved(
         lambda i, j: rest[i, j],
         [[c[h + j] - total_of(ties[j], c[:h]) for j in range(h)] for c in columns],
+        leaf,
     )
     return [
         [u[i] - total_of([ties[j][i] for j in range(h)], g) for i in range(h)] + g
@@ -72,11 +86,12 @@
     ]
 
 
-def inverse_factor(matrix, panel=32, step=8):
-    n = matrix.shape[0]
+def inverse_factor(matrix, panel=32):
+    n, step = matrix.shape[0], 8
     lane = lax.broadcasted_iota(jnp.int32, (8, n), 1)
     sub = lax.broadcasted_iota(jnp.int32, (8, n), 0)
     a = [matrix[8 * v : 8 * v + 8, :] for v in range(n // 8)]
+    zero = a[0] * 0.0
 
     def along(x, j):
         return jnp.broadcast_to(x[:, j : j + 1], (8, n))
@@ -90,27 +105,19 @@
         multipliers = []
         for k in range(first, first + panel, step):
             r = k // 8
-            own = [along(a[r], k + j) for j in range(step)]
+            own = [along(a[r], k + j) + zero for j in range(step)]
             pivot = {(i, j): down(own[j], i) for j in range(step) for i in range(j + 1)}
             inside = (lane >= k) & (lane < k + step)
-            right = [
-                jnp.where(lane == k + i, 1.0, jnp.where(inside, 0.0, down(a[r], i)))
-                for i in range(step)
-            ]
-            g = solved(lambda i, j: pivot[i, j], [right])[0]
-            finished, factor, norms = [], {}, []
-            for i in range(step):
-                y, d = right[i], pivot[i, i]
-                for j in range(i):
-                    e = pivot[j, i]
-                    for m in range(j):
-                        e = e - factor[i, m] * factor[j, m]
-                    factor[i, j] = e * norms[j]
-                for j in range(i):
-                    d = d - factor[i, j] * factor[i, j]
-                    y = y - factor[i, j] * finished[j]
-                norms.append(lax.rsqrt(d))
-                finished.append(y * norms[i])
+            base = jnp.where(inside, jnp.where(lane - k == sub, 1.0, 0.0), a[r])
+            finished = []
+
+            def leaf(x, y, z, e):
+                scale = lax.rsqrt(x)
+                ratio = y * (scale * scale)
+                finished.append(e[0] * scale)
+                finished.append((e[1] - ratio * e[0]) * lax.rsqrt(z - y * ratio))
+
+            g = solved(lambda i, j: pivot[i, j], [[down(base, i) for i in range(step)]], leaf)[0]
             row, held = finished[0], g[0]
             for i in range(1, step):
                 row = jnp.where(sub == i, finished[i], row)
@@ -132,9 +139,14 @@
     return jnp.concatenate(rows, 0)
 
 
-def layout_of(rings):
+def layout_of(rings, early):
     column = [8 * z for z in range(rings)]
-    chips = [[d ^ m for d in column] for m in (0, 2, 4, 6)]
+    if early:
+        first = [[0, 2, 4, 6], column[1:]]
+        column = column[1:]
+    else:
+        first = [column]
+    chips = first + [[d ^ m for d in column] for m in (2, 4, 6)]
     return chips + [[d ^ 1 for d in piece] for piece in chips]
 
 
@@ -144,6 +156,31 @@
     for part in parts:
         out_ref[at : at + part.shape[0], :] = part[...]
         at += part.shape[0]
+
+
+def join_blocks(a_ref, b_ref, out_ref, sems):
+    rows = a_ref.shape[0]
+    copies = [
+        pltpu.make_async_copy(a_ref, out_ref.at[:rows, :], sems.at[0]),
+        pltpu.make_async_copy(b_ref, out_ref.at[rows:, :], sems.at[1]),
+    ]
+    for copy in copies:
+        copy.start()
+    for copy in copies:
+        copy.wait()
+
+
+def joined(a, b):
+    return pl.pallas_call(
+        join_blocks,
+        out_shape=shape(2 * a.shape[0], a.shape[1]),
+        in_specs=[pl.BlockSpec(memory_space=pltpu.HBM)] * 2,
+        out_specs=VMEM,
+        scratch_shapes=[pltpu.SemaphoreType.DMA((2,))],
+        compiler_params=params(2),
+        cost_estimate=cost(1),
+        name="own",
+    )(a, b)
 
 
 def packed(parts):
@@ -158,17 +195,24 @@
     )(*parts)
 
 
-def gather(block, n):
+def gather(block, n, early):
     def swap(x, m):
         return lax.ppermute(x, "blk", [(i, i ^ m) for i in range(n)])
 
-    column = packed([block] + [swap(block, 8 * z) for z in range(1, n // 8)])
-    chips = [column] + [swap(column, 2 * k) for k in (1, 2, 3)]
+    column = [swap(block, 8 * z) for z in range(1, n // 8)]
+    if early:
+        near = packed([block] + [swap(block, 2 * k) for k in (1, 2, 3)])
+        column = packed(column)
+        chips = [near, column]
+    else:
+        column = packed([block] + column)
+        chips = [column]
+    chips += [swap(column, 2 * k) for k in (1, 2, 3)]
     return chips + [swap(x, 1) for x in chips]
 
 
-def assemble(me, pieces, rings, place):
-    for piece, distances in zip(pieces, layout_of(rings)):
+def assemble(me, pieces, rings, early, place):
+    for piece, distances in zip(pieces, layout_of(rings, early)):
         for slot, distance in enumerate(distances):
             place(piece, slot, jnp.bitwise_xor(me, distance))
 
@@ -183,7 +227,7 @@
         y_ref[at, :width] = piece[base : base + rows, :]
         y_ref[at, width:] = piece[base + rows : base + 2 * rows, :]
 
-    assemble(me_ref[0], pieces, rings, place)
+    assemble(me_ref[0], pieces, rings, True, place)
     result = mm3(kernel_ref[...], y_ref[...])
     ky_ref[:rows, :] = result[:, :width]
     ky_ref[rows : 2 * rows, :] = result[:, width:]
@@ -197,10 +241,17 @@
     chunk = min(CHUNK, total)
 
     def add(i, acc):
-        part = y_ref[pl.ds(pl.multiple_of(i * chunk, chunk), chunk), :]
-        return acc + mm3(part, part, 0, 0)
-
-    metric = lax.fori_loop(0, total // chunk, add, jnp.zeros((double, double), F32))
+        top, rest = halves(y_ref[pl.ds(pl.multiple_of(i * chunk, chunk), chunk), :])
+        product = lax.dot_general(
+            top,
+            jnp.concatenate([top, rest], 1),
+            (((0,), (0,)), ((), ())),
+            preferred_element_type=F32,
+        )
+        return acc + product
+
+    sums = lax.fori_loop(0, total // chunk, add, jnp.zeros((double, 2 * double), F32))
+    metric = sums[:, :double] + (sums[:, double:] + sums[:, double:].T)
     metric_ref[...] = metric
     upper_ref[...] = inverse_factor(metric[:width, :width])
 
@@ -236,22 +287,23 @@
 
     g = lax.fori_loop(0, total // chunk, add, jnp.zeros((double, double), F32))
     factor = factor_ref[...]
-    head = g[:width, :]
-    side = jnp.concatenate([g[:width, :width], g[:width, width:].T], 0)
-    whole = jnp.concatenate(
-        [head, jnp.concatenate([g[:width, width:].T, g[width:, width:]], 1)], 0
-    )
-    z = mm(factor, side)
-    small = inverse_factor(mm(z, z, 0, 0))
-    mixing = mm(factor, mm(z, small, 1, 1), 0, 0)
-    values = mm(mixing, mm(whole, mixing), 0, 0)
-    both = jnp.concatenate([mixing, mm(mixing, values)], 1)
+    tie = g[:width, width:].T
+    side = jnp.concatenate([g[:width, :width], tie], 0)
+    whole = jnp.concatenate([g[:width, :], jnp.concatenate([tie, g[width:, width:]], 1)], 0)
+    z = mm3(factor, side)
+    small = inverse_factor(mm3(z, z, 0, 0))
+    raw = mm3(factor, z, 0, 0)
+    held = mm3(jnp.concatenate([raw, mm3(whole, raw)], 0), small, 1, 1)
+    mixing = held[:double]
+    values = mm3(mixing, held[double:], 0, 0)
+    both = stacked(jnp.concatenate([mixing, mm3(mixing, values)], 1))
+    mixing = stacked(mixing)
     small_ref[...] = values
 
     def update(i, acc):
         at = pl.ds(pl.multiple_of(i * chunk, chunk), chunk)
-        pair = mm3(y_ref[at, :], both)
-        image = mm3(ky_ref[at, :], mixing)
+        pair = with_stacked(y_ref[at, :], both)
+        image = with_stacked(ky_ref[at, :], mixing)
         y2_ref[at, :width] = pair[:, :width]
         kx_ref[at, :] = image
         residual = image - pair[:, width:]
@@ -279,7 +331,7 @@
         table[pl.ds(device, 1), :] = piece[base + 2 * rows : base + 2 * rows + 1, :]
 
     table[...] = jnp.zeros_like(table)
-    assemble(me_ref[0], pieces, rings, place)
+    assemble(me_ref[0], pieces, rings, True, place)
     diag_ref[...] = table[...].T
     first_step(
         y_ref, ky_ref, factor_ref, diag_ref.at[:rows, :], y2_ref, kx_ref, small_ref, norm_ref
@@ -287,24 +339,26 @@
     kw_ref[...] = mm3(kernel_ref[...], y2_ref[:, width:])
 
 
-def second_factor(y2_ref, gram_ref, factor_ref):
+def second_factor(y2_ref, small_ref, tie_ref, factor_ref, known_ref, square_ref):
     total, double = y2_ref.shape
     width = double // 2
     chunk = min(CHUNK, total)
 
     def add(i, acc):
         at = pl.ds(pl.multiple_of(i * chunk, chunk), chunk)
-        return acc + mm3(y2_ref[at, :], y2_ref[at, width:], 0, 0)
-
-    gram = lax.fori_loop(0, total // chunk, add, jnp.zeros((double, width), F32))
-    cross = gram[:width]
-    gram_ref[...] = cross
-    factor_ref[...] = inverse_factor(gram[width:] - mm(cross, cross, 0, 0))
-
-
-def second_step(
-    y2_ref, image_ref, small_ref, cross_ref, factor_ref, first_ref, own_y2, own_image, own_diag, outs
-):
+        return acc + mm3(y2_ref[at, width:], y2_ref[at, :], 0, 0)
+
+    gram = lax.fori_loop(0, total // chunk, add, jnp.zeros((width, double), F32))
+    tie = gram[:, :width]
+    values = small_ref[...]
+    factor = inverse_factor(gram[:, width:] - mm(tie, tie, 1, 1))
+    tie_ref[...] = tie
+    factor_ref[...] = factor
+    known_ref[...] = mm(factor, mm(tie, values))
+    square_ref[...] = mm(values, values, 0, 0)
+
+
+def second_step(y2_ref, image_ref, known, first_ref, own_y2, own_image, own_diag, outs):
     ritz_ref, search_ref, norm_ref = outs
     total, double = y2_ref.shape
     width = double // 2
@@ -312,39 +366,36 @@
 
     def add(i, acc):
         at = pl.ds(pl.multiple_of(i * chunk, chunk), chunk)
-        return acc + mm3(y2_ref[at, :], image_ref[at, width:], 0, 0)
-
-    g = lax.fori_loop(0, total // chunk, add, jnp.zeros((double, width), F32))
-    values, cross, factor = small_ref[...], cross_ref[...], factor_ref[...]
-    f_t = g[:width].T
-    z = mm(factor, f_t - mm(cross, values, 0, 0))
-    small = inverse_factor(mm(values, values, 0, 0) + mm(z, z, 0, 0))
-    lower = mm(factor, mm(z, small, 1, 1), 0, 0)
-    upper = mm(values, small, 1, 1) - mm(cross, lower)
-    mixing = jnp.concatenate([upper, lower], 0)
-    whole = jnp.concatenate(
-        [jnp.concatenate([values, g[:width]], 1), jnp.concatenate([f_t, g[width:]], 1)], 0
-    )
-    values2 = mm(mixing, mm(whole, mixing), 0, 0)
-    turned = mm(mixing, values2)
+        return acc + mm3(image_ref[at, width:], y2_ref[at, :], 0, 0)
+
+    g = lax.fori_loop(0, total // chunk, add, jnp.zeros((width, double), F32))
+    values, tie, factor, done, square = [ref[...] for ref in known]
+    z = mm3(factor, g[:, :width]) - done
+    small = inverse_factor(square + mm3(z, z, 0, 0))
+    lower = mm3(factor, z, 0, 0)
+    raw = jnp.concatenate([values - mm3(tie, lower, 0, 0), lower], 0)
+    whole = jnp.concatenate([jnp.concatenate([values, g[:, :width].T], 1), g], 0)
+    held = mm3(jnp.concatenate([raw, mm3(whole, raw)], 0), small, 1, 1)
+    mixing = held[:double]
+    values2 = mm3(mixing, held[double:], 0, 0)
+    weights = stacked(jnp.concatenate([mixing, -mm3(mixing, values2)], 0))
 
     def update(i, acc):
         at = pl.ds(pl.multiple_of(i * chunk, chunk), chunk)
-        residual = mm3(image_ref[at, :], mixing) - mm3(y2_ref[at, :], turned)
+        residual = with_stacked(jnp.concatenate([image_ref[at, :], y2_ref[at, :]], 1), weights)
         return acc + jnp.sum(residual * residual, axis=0, keepdims=True)
 
     squares = lax.fori_loop(0, total // chunk, update, jnp.zeros((1, width), F32))
     norm_ref[:1, :] = first_ref[...]
     norm_ref[1:, :] = jnp.sqrt(squares)
     own = own_y2()
-    ritz = mm(own, mixing)
-    ritz_ref[...] = ritz
-    residual = mm(own_image(), mixing) - mm(ritz, values2)
+    ritz_ref[...] = mm3(own, mixing)
+    residual = with_stacked(jnp.concatenate([own_image(), own], 1), weights)
     search_ref[...] = divided(residual, own_diag(), values2)
 
 
-def last_step(rings, rows, me_ref, y2_ref, kx_ref, small_ref, cross_ref, factor_ref, first_ref, diag_ref, *refs):
-    pieces = refs[:-4]
+def last_step(rings, rows, me_ref, y2_ref, kx_ref, first_ref, diag_ref, *refs):
+    known, pieces = refs[:5], refs[5:-4]
     ritz_ref, search_ref, norm_ref, image_ref = refs[-4:]
     width = kx_ref.shape[1]
     me = me_ref[0]
@@ -353,15 +404,13 @@
         at = pl.ds(pl.multiple_of(device * rows, rows), rows)
         image_ref[at, width:] = piece[slot * rows : (slot + 1) * rows, :]
 
-    assemble(me, pieces, rings, place)
+    assemble(me, pieces, rings, False, place)
     image_ref[:, :width] = kx_ref[...]
     mine = pl.ds(pl.multiple_of(me * rows, rows), rows)
     second_step(
         y2_ref,
         image_ref,
-        small_ref,
-        cross_ref,
-        factor_ref,
+        known,
         first_ref,
         lambda: y2_ref[mine, :],
         lambda: image_ref[mine, :],
@@ -370,15 +419,12 @@
     )
 
 
-def general_last(
-    y2_ref, image_ref, small_ref, cross_ref, factor_ref, first_ref, own_y2, own_image, own_diag, *outs
-):
+def general_last(y2_ref, image_ref, first_ref, own_y2, own_image, own_diag, *refs):
+    known, outs = refs[:5], refs[5:]
     second_step(
         y2_ref,
         image_ref,
-        small_ref,
-        cross_ref,
-        factor_ref,
+        known,
         first_ref,
         lambda: own_y2[...],
         lambda: own_image[...],
@@ -421,17 +467,17 @@
     )(metric, upper)
 
 
-def second_metric(y2, mebibytes):
+def second_metric(y2, values, mebibytes):
     width = y2.shape[1] // 2
     return pl.pallas_call(
         second_factor,
-        out_shape=(shape(width, width), shape(width, width)),
-        in_specs=[VMEM],
-        out_specs=(VMEM, VMEM),
+        out_shape=(shape(width, width),) * 4,
+        in_specs=[VMEM] * 2,
+        out_specs=(VMEM,) * 4,
         compiler_params=params(mebibytes),
         cost_estimate=cost(9),
         name="second_factor",
-    )(y2)
+    )(y2, values)
 
 
 def cubed(n, kernel, ritz, search, diag):
@@ -441,7 +487,7 @@
     lanes = max(n, 128)
     me = lax.axis_index("blk").astype(jnp.int32).reshape(1)
     along = diag.reshape(1, rows)
-    sent = gather(packed([ritz, search]), n)
+    sent = gather(joined(ritz, search), n, True)
     y, ky_own = pl.pallas_call(
         lambda *refs: first_product(rings, rows, *refs),
         out_shape=(shape(total, 2 * width), shape(2 * rows + 8, width)),
@@ -450,7 +496,7 @@
         compiler_params=params(16),
         name="first_product",
     )(me, kernel, along, *sent)
-    images = gather(ky_own, n)
+    images = gather(ky_own, n, True)
     factor = metric_factor(y, 12)
     y2, kx, values, norm1, kw_own = pl.pallas_call(
         lambda *refs: with_product(rings, rows, *refs),
@@ -471,17 +517,17 @@
         compiler_params=params(24),
         name="first_step",
     )(me, kernel, y, factor, *images)
-    images2 = gather(kw_own, n)
-    cross, factor2 = second_metric(y2, 12)
+    images2 = gather(kw_own, n, False)
+    known = second_metric(y2, values, 12)
     return pl.pallas_call(
         lambda *refs: last_step(rings, rows, *refs),
         out_shape=(shape(rows, width), shape(rows, width), shape(ITERS, width)),
-        in_specs=[SMEM] + [VMEM] * (7 + len(images2)),
+        in_specs=[SMEM] + [VMEM] * (9 + len(images2)),
         out_specs=(VMEM,) * 3,
         scratch_shapes=[pltpu.VMEM((total, 2 * width), F32)],
         compiler_params=params(24),
         name="last_step",
-    )(me, y2, kx, values, cross, factor2, norm1, along, *images2)
+    )(me, y2, kx, norm1, along, values, *known, *images2)
 
 
 def general(n, cols, kernel, ritz, search, diag):
@@ -511,26 +557,25 @@
     held = y2[:, width:].reshape(n, cols, rows, width)
     part2 = lax.dynamic_index_in_dim(held, q, 1, keepdims=False).reshape(n * rows, width)
     kw = lax.all_gather(product(part2), axes, axis=0, tiled=True)
-    cross, factor2 = second_metric(y2, 56)
+    known = second_metric(y2, values, 56)
     image = jnp.concatenate([kx, kw], 1)
     at = (lax.axis_index("blk") * cols + q) * rows
     return pl.pallas_call(
         general_last,
         out_shape=(shape(rows, width), shape(rows, width), shape(ITERS, width)),
-        in_specs=[VMEM] * 9,
+        in_specs=[VMEM] * 11,
         out_specs=(VMEM,) * 3,
         compiler_params=params(),
         name="last_step",
     )(
         y2,
         image,
-        values,
-        cross,
-        factor2,
         norm1,
         lax.dynamic_slice_in_dim(y2, at, rows, 0),
         lax.dynamic_slice_in_dim(image, at, rows, 0),
         diag[:, None],
+        values,
+        *known,
     )
 
 

time: 110 us -> 96.9 us (0.88)
  waiting for transfers between devices: 35.4 us -> 21.9 us
  starting transfers between devices: 26.7 us -> 37.8 us
  Pallas kernels: 45.3 us -> 34.3 us
    ppermute x30 -> x38, waiting for transfers between devices: 35.4 us -> 21.9 us  [swap(): return lax.ppermute(x, 'blk', [(i, i ^ m) for i in range(n)])]
    ppermute x30 -> x38, starting transfers between devices: 26.7 us -> 37.8 us  [swap(): return lax.ppermute(x, 'blk', [(i, i ^ m) for i in range(n)])]
    pallas_call x1, Pallas kernels: 13.1 us -> 9.12 us  [cubed(): pl.pallas_call(lambda *refs: last_step(rings, rows, *refs), out_shape=(sh...]
    pallas_call x1, Pallas kernels: 12.9 us -> 9.96 us  [cubed(): pl.pallas_call(lambda *refs: with_product(rings, rows, *refs), out_shape=...]
    pallas_call x1, Pallas kernels: 6.48 us -> 4.98 us  [metric_factor(): pl.pallas_call(metric_head, out_shape=(shape(2 * width, 2 * width), shape...]
    pallas_call x1, Pallas kernels: 5.37 us -> 4.06 us  [metric_factor(): pl.pallas_call(metric_tail, out_shape=shape(2 * width, 2 * width), in_spe...]
    pallas_call x1 -> x2, Pallas kernels: 6.63 us -> 5.32 us  [the longest x1 5.25 us: second_metric(): pl.pallas_call(second_factor, out_shape=(shape(width, width),) * 4, in_sp...]
  transfers between devices with their start and end apart: 30 -> 38, of which waited for: 17 -> 14; matrix products, arithmetic and copies ran while one was open for 0% -> 0% of each run, Pallas kernels for 17% -> 15%
where the time goes in v5:
time: 96.9 us; the launch traced here: 96.6 us
  starting transfers between devices  37.8 us (39%)
  Pallas kernels  34.3 us (35%)
  waiting for transfers between devices  21.9 us (23%)
  local copies, waits for them, and re-layouts  1.68 us (2%)
    ppermute x38, starting transfers between devices, swap(): return lax.ppermute(x, 'blk', [(i, i ^ m) for i in range(n)])  37.8 us
    ppermute x38, waiting for transfers between devices, swap(): return lax.ppermute(x, 'blk', [(i, i ^ m) for i in range(n)])  21.9 us
    pallas_call x1, Pallas kernels, cubed(): pl.pallas_call(lambda *refs: with_product(rings, rows, *refs), out_shape=...  9.96 us
    pallas_call x1, Pallas kernels, cubed(): pl.pallas_call(lambda *refs: last_step(rings, rows, *refs), out_shape=(sh...  9.12 us
    pallas_call x1, Pallas kernels, second_metric(): pl.pallas_call(second_factor, out_shape=(shape(width, width),) * 4, in_sp...  5.25 us
    pallas_call x1, Pallas kernels, metric_factor(): pl.pallas_call(metric_head, out_shape=(shape(2 * width, 2 * width), shape...  4.98 us
    pallas_call x1, Pallas kernels, metric_factor(): pl.pallas_call(metric_tail, out_shape=shape(2 * width, 2 * width), in_spe...  4.06 us
  transfers between devices with their start and end apart: 38, of which 14 were waited for; matrix products, arithmetic and copies ran while one was open for 0% of the time, Pallas kernels for 15%

profile of v5, /device:TPU:0, one launch (start us, length us, event | category | flops | bytes accessed | tf_op | source)
XLA Modules:
  0.0 96.6 jit_solution(15439386895587703684)
XLA Ops:
  0.6 0.7 copy-done.1
  1.4 0.8 copy-done.2
  2.3 5.1 %collective-permute-start.5 = (f32[128,128]{1,0:T(8,128)S(1)}, f32[128,128]{1,0:T(8,128)S(1)}, u32[]{:S(2)}, u32[]{:S(2)}) collective-permute-start(f32[128,128]{1,0:T(8,128)S(1)} %own.1.refs_0_), channel_id=1, source_target_pairs={{0,24},{1,25},{2,26},{3,27},{4,28},{5,29},{6,30},{7,31},{8,16},{9,... | collective-permute-start | bytes 196616 | tf_op jit(solution)/shard_map/ppermute | solution.py:200
  7.4 0.6 collective-permute-start.3
  8.0 2.6 %collective-permute-start.2 = (f32[128,128]{1,0:T(8,128)S(1)}, f32[128,128]{1,0:T(8,128)S(1)}, u32[]{:S(2)}, u32[]{:S(2)}) collective-permute-start(f32[128,128]{1,0:T(8,128)S(1)} %own.1.refs_0_), channel_id=1, source_target_pairs={{0,6},{1,7},{2,4},{3,5},{4,2},{5,3},{6,0},{7,1},{8,14},{9,15},{10,... | collective-permute-start | bytes 196616 | tf_op jit(solution)/shard_map/ppermute | solution.py:200
  10.6 2.4 %collective-permute-done.4.refs_1_ = f32[128,128]{1,0:T(8,128)S(1)} collective-permute-done((f32[128,128]{1,0:T(8,128)S(1)}, f32[128,128]{1,0:T(8,128)S(1)}, u32[]{:S(2)}, u32[]{:S(2)}) %collective-permute-start.4) | collective-permute-done | bytes 65568 | tf_op jit(solution)/shard_map/ppermute | solution.py:200
  13.0 2.5 %collective-permute-start.8 = (f32[384,128]{1,0:T(8,128)S(1)}, f32[384,128]{1,0:T(8,128)S(1)}, u32[]{:S(2)}, u32[]{:S(2)}) collective-permute-start(f32[384,128]{1,0:T(8,128)S(1)} %shard_map.68.refs_4_), channel_id=1, source_target_pairs={{0,6},{1,7},{2,4},{3,5},{4,2},{5,3},{6,0},{7,1},{8,14},{9,15},{10,... | collective-permute-start | bytes 589832 | tf_op jit(solution)/shard_map/ppermute | solution.py:200
  15.5 0.5 collective-permute-start.7
  16.0 0.5 collective-permute-start.6
  16.6 1.5 %collective-permute-start.1 = (f32[128,128]{1,0:T(8,128)S(1)}, f32[128,128]{1,0:T(8,128)S(1)}, u32[]{:S(2)}, u32[]{:S(2)}) collective-permute-start(f32[128,128]{1,0:T(8,128)S(1)} %own.1.refs_0_), channel_id=1, source_target_pairs={{0,4},{1,5},{2,6},{3,7},{4,0},{5,1},{6,2},{7,3},{8,12},{9,13},{10,... | collective-permute-start | bytes 196616 | tf_op jit(solution)/shard_map/ppermute | solution.py:200
  18.1 1.5 %collective-permute-start = (f32[128,128]{1,0:T(8,128)S(1)}, f32[128,128]{1,0:T(8,128)S(1)}, u32[]{:S(2)}, u32[]{:S(2)}) collective-permute-start(f32[128,128]{1,0:T(8,128)S(1)} %own.1.refs_0_), channel_id=1, source_target_pairs={{0,2},{1,3},{2,0},{3,1},{4,6},{5,7},{6,4},{7,5},{8,10},{9,11},{10,... | collective-permute-start | bytes 196616 | tf_op jit(solution)/shard_map/ppermute | solution.py:200
  19.6 6.5 %collective-permute-done.1.refs_2_ = f32[128,128]{1,0:T(8,128)S(1)} collective-permute-done((f32[128,128]{1,0:T(8,128)S(1)}, f32[128,128]{1,0:T(8,128)S(1)}, u32[]{:S(2)}, u32[]{:S(2)}) %collective-permute-start.1) | collective-permute-done | bytes 65568 | tf_op jit(solution)/shard_map/ppermute | solution.py:200
  26.1 0.2 collective-permute-done.refs_1_
  26.4 0.5 collective-permute-start.10
  27.0 0.4 collective-permute-start.12
  27.7 0.5 collective-permute-done.10.refs_9_
  28.2 0.3 collective-permute-done.13.refs_12_
  28.5 0.3 collective-permute-done.12.refs_11_
  28.8 0.3 collective-permute-done.11.refs_10_
  29.0 0.8 first_product.1
  29.9 1.6 %collective-permute-start.19 = (f32[136,128]{1,0:T(8,128)S(1)}, f32[136,128]{1,0:T(8,128)S(1)}, u32[]{:S(2)}, u32[]{:S(2)}) collective-permute-start(f32[136,128]{1,0:T(8,128)S(1)} %get-tuple-element.19.refs_0_), channel_id=1, source_target_pairs={{0,24},{1,25},{2,26},{3,27},{4,28},{5,29},{6,30},{7,31},{8,16},{9,... | collective-permute-start | bytes 208904 | tf_op jit(solution)/shard_map/ppermute | solution.py:200
  31.4 2.9 %collective-permute-start.17 = (f32[136,128]{1,0:T(8,128)S(1)}, f32[136,128]{1,0:T(8,128)S(1)}, u32[]{:S(2)}, u32[]{:S(2)}) collective-permute-start(f32[136,128]{1,0:T(8,128)S(1)} %get-tuple-element.19.refs_0_), channel_id=1, source_target_pairs={{0,8},{1,9},{2,10},{3,11},{4,12},{5,13},{6,14},{7,15},{8,0},{9,1},... | collective-permute-start | bytes 208904 | tf_op jit(solution)/shard_map/ppermute | solution.py:200
  34.3 1.5 %collective-permute-start.16 = (f32[136,128]{1,0:T(8,128)S(1)}, f32[136,128]{1,0:T(8,128)S(1)}, u32[]{:S(2)}, u32[]{:S(2)}) collective-permute-start(f32[136,128]{1,0:T(8,128)S(1)} %get-tuple-element.19.refs_0_), channel_id=1, source_target_pairs={{0,6},{1,7},{2,4},{3,5},{4,2},{5,3},{6,0},{7,1},{8,14},{9,15},{10,... | collective-permute-start | bytes 208904 | tf_op jit(solution)/shard_map/ppermute | solution.py:200
  35.9 1.4 %collective-permute-start.15 = (f32[136,128]{1,0:T(8,128)S(1)}, f32[136,128]{1,0:T(8,128)S(1)}, u32[]{:S(2)}, u32[]{:S(2)}) collective-permute-start(f32[136,128]{1,0:T(8,128)S(1)} %get-tuple-element.19.refs_0_), channel_id=1, source_target_pairs={{0,4},{1,5},{2,6},{3,7},{4,0},{5,1},{6,2},{7,3},{8,12},{9,13},{10,... | collective-permute-start | bytes 208904 | tf_op jit(solution)/shard_map/ppermute | solution.py:200
  37.3 1.0 %collective-permute-start.14 = (f32[136,128]{1,0:T(8,128)S(1)}, f32[136,128]{1,0:T(8,128)S(1)}, u32[]{:S(2)}, u32[]{:S(2)}) collective-permute-start(f32[136,128]{1,0:T(8,128)S(1)} %get-tuple-element.19.refs_0_), channel_id=1, source_target_pairs={{0,2},{1,3},{2,0},{3,1},{4,6},{5,7},{6,4},{7,5},{8,10},{9,11},{10,... | collective-permute-start | bytes 208904 | tf_op jit(solution)/shard_map/ppermute | solution.py:200
  38.3 0.6 collective-permute-done.18.refs_1_
  39.0 1.6 %collective-permute-start.22 = (f32[408,128]{1,0:T(8,128)S(1)}, f32[408,128]{1,0:T(8,128)S(1)}, u32[]{:S(2)}, u32[]{:S(2)}) collective-permute-start(f32[408,128]{1,0:T(8,128)S(1)} %shard_map.70.refs_5_), channel_id=1, source_target_pairs={{0,6},{1,7},{2,4},{3,5},{4,2},{5,3},{6,0},{7,1},{8,14},{9,15},{10,... | collective-permute-start | bytes 626696 | tf_op jit(solution)/shard_map/ppermute | solution.py:200
  40.6 1.4 %collective-permute-start.21 = (f32[408,128]{1,0:T(8,128)S(1)}, f32[408,128]{1,0:T(8,128)S(1)}, u32[]{:S(2)}, u32[]{:S(2)}) collective-permute-start(f32[408,128]{1,0:T(8,128)S(1)} %shard_map.70.refs_5_), channel_id=1, source_target_pairs={{0,4},{1,5},{2,6},{3,7},{4,0},{5,1},{6,2},{7,3},{8,12},{9,13},{10,... | collective-permute-start | bytes 626696 | tf_op jit(solution)/shard_map/ppermute | solution.py:200
  42.0 0.5 collective-permute-start.20
  42.5 5.0 %metric_head.1 = (f32[256,256]{1,0:T(8,128)S(1)}, f32[128,128]{1,0:T(8,128)S(1)}) custom-call(f32[2048,256]{1,0:T(8,128)S(1)} %get-tuple-element.16.y_ref.refs_2_), custom_call_target="tpu_custom_call" | custom-call | flops 7000000000 | tf_op jit(solution)/shard_map/metric_head/pallas_call | solution.py:450
  47.6 0.5 collective-permute-start.23
  48.3 3.2 %collective-permute-done.21.refs_7_ = f32[408,128]{1,0:T(8,128)S(1)} collective-permute-done((f32[408,128]{1,0:T(8,128)S(1)}, f32[408,128]{1,0:T(8,128)S(1)}, u32[]{:S(2)}, u32[]{:S(2)}) %collective-permute-start.21) | collective-permute-done | bytes 208928 | tf_op jit(solution)/shard_map/ppermute | solution.py:200
  51.5 0.5 collective-permute-start.25
  52.0 4.1 %metric_tail.1.refs_3_ = f32[256,256]{1,0:T(8,128)S(1)} custom-call(f32[256,256]{1,0:T(8,128)S(1)} %get-tuple-element.17.metric_ref, f32[128,128]{1,0:T(8,128)S(1)} %get-tuple-element.18.upper_ref), custom_call_target="tpu_custom_call" | custom-call | flops 7000000000 | tf_op jit(solution)/shard_map/metric_tail/pallas_call | solution.py:459
  56.1 10.0 %first_step.1 = (f32[2048,256]{1,0:T(8,128)S(1)}, f32[2048,128]{1,0:T(8,128)S(1)}, f32[128,128]{1,0:T(8,128)S(1)}, f32[1,128]{1,0:T(1,128)S(1)}, f32[64,128]{1,0:T(8,128)S(1)}) custom-call(s32[1]{0:T(128)} %bitcast.refs_0_, f32[64,2048]{1,0:T(8,128)S(1)} %bitcast.6, f32[2048,256]{1,0:T(8,128)S(1)} %get-tuple-element.16.y_ref.refs_2_, ...), custom_call_target="tpu_custom_call" | custom-call | tf_op jit(solution)/shard_map/first_step/pallas_call | solution.py:501
  66.1 1.6 %collective-permute-start.30 = (f32[64,128]{1,0:T(8,128)S(1)}, f32[64,128]{1,0:T(8,128)S(1)}, u32[]{:S(2)}, u32[]{:S(2)}) collective-permute-start(f32[64,128]{1,0:T(8,128)S(1)} %get-tuple-element.28.refs_0_), channel_id=1, source_target_pairs={{0,24},{1,25},{2,26},{3,27},{4,28},{5,29},{6,30},{7,31},{8,16},{9,... | collective-permute-start | bytes 98312 | tf_op jit(solution)/shard_map/ppermute | solution.py:200
  67.7 2.9 %collective-permute-start.28 = (f32[64,128]{1,0:T(8,128)S(1)}, f32[64,128]{1,0:T(8,128)S(1)}, u32[]{:S(2)}, u32[]{:S(2)}) collective-permute-start(f32[64,128]{1,0:T(8,128)S(1)} %get-tuple-element.28.refs_0_), channel_id=1, source_target_pairs={{0,8},{1,9},{2,10},{3,11},{4,12},{5,13},{6,14},{7,15},{8,0},{9,1},... | collective-permute-start | bytes 98312 | tf_op jit(solution)/shard_map/ppermute | solution.py:200
  70.5 1.3 %collective-permute-done.30.refs_3_ = f32[64,128]{1,0:T(8,128)S(1)} collective-permute-done((f32[64,128]{1,0:T(8,128)S(1)}, f32[64,128]{1,0:T(8,128)S(1)}, u32[]{:S(2)}, u32[]{:S(2)}) %collective-permute-start.30) | collective-permute-done | bytes 32800 | tf_op jit(solution)/shard_map/ppermute | solution.py:200
  71.9 0.8 collective-permute-done.29.refs_2_
  72.7 0.2 collective-permute-done.28.refs_1_
  72.9 1.6 %collective-permute-start.33 = (f32[256,128]{1,0:T(8,128)S(1)}, f32[256,128]{1,0:T(8,128)S(1)}, u32[]{:S(2)}, u32[]{:S(2)}) collective-permute-start(f32[256,128]{1,0:T(8,128)S(1)} %shard_map.71.refs_10_), channel_id=1, source_target_pairs={{0,6},{1,7},{2,4},{3,5},{4,2},{5,3},{6,0},{7,1},{8,14},{9,15},{10,... | collective-permute-start | bytes 393224 | tf_op jit(solution)/shard_map/ppermute | solution.py:200
  74.5 1.4 %collective-permute-start.32 = (f32[256,128]{1,0:T(8,128)S(1)}, f32[256,128]{1,0:T(8,128)S(1)}, u32[]{:S(2)}, u32[]{:S(2)}) collective-permute-start(f32[256,128]{1,0:T(8,128)S(1)} %shard_map.71.refs_10_), channel_id=1, source_target_pairs={{0,4},{1,5},{2,6},{3,7},{4,0},{5,1},{6,2},{7,3},{8,12},{9,13},{10,... | collective-permute-start | bytes 393224 | tf_op jit(solution)/shard_map/ppermute | solution.py:200
  75.9 0.6 collective-permute-start.31
  76.5 3.7 %collective-permute-done.33.refs_13_ = f32[256,128]{1,0:T(8,128)S(1)} collective-permute-done((f32[256,128]{1,0:T(8,128)S(1)}, f32[256,128]{1,0:T(8,128)S(1)}, u32[]{:S(2)}, u32[]{:S(2)}) %collective-permute-start.33) | collective-permute-done | bytes 131104 | tf_op jit(solution)/shard_map/ppermute | solution.py:200
  80.2 1.5 %collective-permute-done.32.refs_12_ = f32[256,128]{1,0:T(8,128)S(1)} collective-permute-done((f32[256,128]{1,0:T(8,128)S(1)}, f32[256,128]{1,0:T(8,128)S(1)}, u32[]{:S(2)}, u32[]{:S(2)}) %collective-permute-start.32) | collective-permute-done | bytes 131104 | tf_op jit(solution)/shard_map/ppermute | solution.py:200
  81.7 0.5 collective-permute-start.35
  82.2 5.2 %second_factor.1 = (f32[128,128]{1,0:T(8,128)S(1)}, f32[128,128]{1,0:T(8,128)S(1)}, f32[128,128]{1,0:T(8,128)S(1)}, f32[128,128]{1,0:T(8,128)S(1)}) custom-call(f32[2048,256]{1,0:T(8,128)S(1)} %get-tuple-element.20.y2_ref.refs_1_, f32[128,128]{1,0:T(8,128)S(1)} %get-tuple-element.23.small_ref.refs_5_), custom_call_target="tpu_custom_call" | custom-call | flops 8999999488 | tf_op jit(solution)/shard_map/second_factor/pallas_call | solution.py:472
  87.5 9.1 %last_step.1 = (f32[64,128]{1,0:T(8,128)}, f32[64,128]{1,0:T(8,128)}, f32[2,128]{1,0:T(2,128)}) custom-call(s32[1]{0:T(128)} %bitcast.refs_0_, f32[2048,256]{1,0:T(8,128)S(1)} %get-tuple-element.20.y2_ref.refs_1_, f32[2048,128]{1,0:T(8,128)S(1)} %get-tuple-element.21.refs_2_, f32[1,128]{1,0:T(1,128)S(1)} %get-tuple-element.22.refs_3_, f32[1,64]{1,0:T(1,128)S(1)} %bitcast.8, ...), custom_call_target="tpu_custom_call" | custom-call | tf_op jit(solution)/shard_map/last_step/pallas_call | solution.py:522
  (49 shorter events, 0.8 us)
Async XLA Ops:
  0.6 0.8 copy-start.1
  1.4 0.8 copy-start.2
  2.2 25.3 %copy-start.3 = (f32[64,1,2048]{2,1,0:T(1,128)S(1)}, f32[64,1,2048]{2,1,0:T(1,128)}, u32[]{:S(2)}) copy-start(f32[64,1,2048]{2,1,0:T(1,128)} %param.4) | copy-start | bytes 1572868
  2.2 26.8 %copy-start = (f32[64]{0:T(128)S(1)}, f32[64]{0:T(128)}, u32[]{:S(2)}) copy-start(f32[64]{0:T(128)} %param.7) | copy-start | bytes 772
  2.3 8.4 %collective-permute-start.5 = (f32[128,128]{1,0:T(8,128)S(1)}, f32[128,128]{1,0:T(8,128)S(1)}, u32[]{:S(2)}, u32[]{:S(2)}) collective-permute-start(f32[128,128]{1,0:T(8,128)S(1)} %own.1.refs_0_), channel_id=1, source_target_pairs={{0,24},{1,25},{2,26},{3,27},{4,28},{5,29},{6,30},{7,31},{8,16},{9,... | collective-permute-start | bytes 196616 | tf_op jit(solution)/shard_map/ppermute | solution.py:200
  7.4 5.6 %collective-permute-start.4 = (f32[128,128]{1,0:T(8,128)S(1)}, f32[128,128]{1,0:T(8,128)S(1)}, u32[]{:S(2)}, u32[]{:S(2)}) collective-permute-start(f32[128,128]{1,0:T(8,128)S(1)} %own.1.refs_0_), channel_id=1, source_target_pairs={{0,16},{1,17},{2,18},{3,19},{4,20},{5,21},{6,22},{7,23},{8,24},{9,... | collective-permute-start | bytes 196616 | tf_op jit(solution)/shard_map/ppermute | solution.py:200
  7.4 5.6 %collective-permute-start.3 = (f32[128,128]{1,0:T(8,128)S(1)}, f32[128,128]{1,0:T(8,128)S(1)}, u32[]{:S(2)}, u32[]{:S(2)}) collective-permute-start(f32[128,128]{1,0:T(8,128)S(1)} %own.1.refs_0_), channel_id=1, source_target_pairs={{0,8},{1,9},{2,10},{3,11},{4,12},{5,13},{6,14},{7,15},{8,0},{9,1},... | collective-permute-start | bytes 196616 | tf_op jit(solution)/shard_map/ppermute | solution.py:200
  8.0 10.1 %collective-permute-start.2 = (f32[128,128]{1,0:T(8,128)S(1)}, f32[128,128]{1,0:T(8,128)S(1)}, u32[]{:S(2)}, u32[]{:S(2)}) collective-permute-start(f32[128,128]{1,0:T(8,128)S(1)} %own.1.refs_0_), channel_id=1, source_target_pairs={{0,6},{1,7},{2,4},{3,5},{4,2},{5,3},{6,0},{7,1},{8,14},{9,15},{10,... | collective-permute-start | bytes 196616 | tf_op jit(solution)/shard_map/ppermute | solution.py:200
  13.0 13.9 %collective-permute-start.8 = (f32[384,128]{1,0:T(8,128)S(1)}, f32[384,128]{1,0:T(8,128)S(1)}, u32[]{:S(2)}, u32[]{:S(2)}) collective-permute-start(f32[384,128]{1,0:T(8,128)S(1)} %shard_map.68.refs_4_), channel_id=1, source_target_pairs={{0,6},{1,7},{2,4},{3,5},{4,2},{5,3},{6,0},{7,1},{8,14},{9,15},{10,... | collective-permute-start | bytes 589832 | tf_op jit(solution)/shard_map/ppermute | solution.py:200
  15.5 11.4 %collective-permute-start.7 = (f32[384,128]{1,0:T(8,128)S(1)}, f32[384,128]{1,0:T(8,128)S(1)}, u32[]{:S(2)}, u32[]{:S(2)}) collective-permute-start(f32[384,128]{1,0:T(8,128)S(1)} %shard_map.68.refs_4_), channel_id=1, source_target_pairs={{0,4},{1,5},{2,6},{3,7},{4,0},{5,1},{6,2},{7,3},{8,12},{9,13},{10,... | collective-permute-start | bytes 589832 | tf_op jit(solution)/shard_map/ppermute | solution.py:200
  16.0 11.4 %collective-permute-start.6 = (f32[384,128]{1,0:T(8,128)S(1)}, f32[384,128]{1,0:T(8,128)S(1)}, u32[]{:S(2)}, u32[]{:S(2)}) collective-permute-start(f32[384,128]{1,0:T(8,128)S(1)} %shard_map.68.refs_4_), channel_id=1, source_target_pairs={{0,2},{1,3},{2,0},{3,1},{4,6},{5,7},{6,4},{7,5},{8,10},{9,11},{10,... | collective-permute-start | bytes 589832 | tf_op jit(solution)/shard_map/ppermute | solution.py:200
  16.6 9.5 %collective-permute-start.1 = (f32[128,128]{1,0:T(8,128)S(1)}, f32[128,128]{1,0:T(8,128)S(1)}, u32[]{:S(2)}, u32[]{:S(2)}) collective-permute-start(f32[128,128]{1,0:T(8,128)S(1)} %own.1.refs_0_), channel_id=1, source_target_pairs={{0,4},{1,5},{2,6},{3,7},{4,0},{5,1},{6,2},{7,3},{8,12},{9,13},{10,... | collective-permute-start | bytes 196616 | tf_op jit(solution)/shard_map/ppermute | solution.py:200
  18.1 8.2 %collective-permute-start = (f32[128,128]{1,0:T(8,128)S(1)}, f32[128,128]{1,0:T(8,128)S(1)}, u32[]{:S(2)}, u32[]{:S(2)}) collective-permute-start(f32[128,128]{1,0:T(8,128)S(1)} %own.1.refs_0_), channel_id=1, source_target_pairs={{0,2},{1,3},{2,0},{3,1},{4,6},{5,7},{6,4},{7,5},{8,10},{9,11},{10,... | collective-permute-start | bytes 196616 | tf_op jit(solution)/shard_map/ppermute | solution.py:200
  26.3 1.9 %collective-permute-start.9 = (f32[512,128]{1,0:T(8,128)S(1)}, f32[512,128]{1,0:T(8,128)S(1)}, u32[]{:S(2)}, u32[]{:S(2)}) collective-permute-start(f32[512,128]{1,0:T(8,128)S(1)} %shard_map.67.refs_3_), channel_id=1, source_target_pairs={{0,1},{1,0},{2,3},{3,2},{4,5},{5,4},{6,7},{7,6},{8,9},{9,8},{10,11... | collective-permute-start | bytes 786440 | tf_op jit(solution)/shard_map/ppermute | solution.py:200
  26.4 1.8 %collective-permute-start.10 = (f32[384,128]{1,0:T(8,128)S(1)}, f32[384,128]{1,0:T(8,128)S(1)}, u32[]{:S(2)}, u32[]{:S(2)}) collective-permute-start(f32[384,128]{1,0:T(8,128)S(1)} %shard_map.68.refs_4_), channel_id=1, source_target_pairs={{0,1},{1,0},{2,3},{3,2},{4,5},{5,4},{6,7},{7,6},{8,9},{9,8},{10,11... | collective-permute-start | bytes 589832 | tf_op jit(solution)/shard_map/ppermute | solution.py:200
  26.9 1.6 %collective-permute-start.13 = (f32[384,128]{1,0:T(8,128)S(1)}, f32[384,128]{1,0:T(8,128)S(1)}, u32[]{:S(2)}, u32[]{:S(2)}) collective-permute-start(f32[384,128]{1,0:T(8,128)S(1)} %collective-permute-done.8.refs_7_), channel_id=1, source_target_pairs={{0,1},{1,0},{2,3},{3,2},{4,5},{5,4},{6,7},{7,6},{8,9},{9,8},{10,11... | collective-permute-start | bytes 589832 | tf_op jit(solution)/shard_map/ppermute | solution.py:200
  27.0 1.8 %collective-permute-start.12 = (f32[384,128]{1,0:T(8,128)S(1)}, f32[384,128]{1,0:T(8,128)S(1)}, u32[]{:S(2)}, u32[]{:S(2)}) collective-permute-start(f32[384,128]{1,0:T(8,128)S(1)} %collective-permute-done.7.refs_6_), channel_id=1, source_target_pairs={{0,1},{1,0},{2,3},{3,2},{4,5},{5,4},{6,7},{7,6},{8,9},{9,8},{10,11... | collective-permute-start | bytes 589832 | tf_op jit(solution)/shard_map/ppermute | solution.py:200
  27.4 1.6 %collective-permute-start.11 = (f32[384,128]{1,0:T(8,128)S(1)}, f32[384,128]{1,0:T(8,128)S(1)}, u32[]{:S(2)}, u32[]{:S(2)}) collective-permute-start(f32[384,128]{1,0:T(8,128)S(1)} %collective-permute-done.6.refs_5_), channel_id=1, source_target_pairs={{0,1},{1,0},{2,3},{3,2},{4,5},{5,4},{6,7},{7,6},{8,9},{9,8},{10,11... | collective-permute-start | bytes 589832 | tf_op jit(solution)/shard_map/ppermute | solution.py:200
  29.9 7.4 %collective-permute-start.19 = (f32[136,128]{1,0:T(8,128)S(1)}, f32[136,128]{1,0:T(8,128)S(1)}, u32[]{:S(2)}, u32[]{:S(2)}) collective-permute-start(f32[136,128]{1,0:T(8,128)S(1)} %get-tuple-element.19.refs_0_), channel_id=1, source_target_pairs={{0,24},{1,25},{2,26},{3,27},{4,28},{5,29},{6,30},{7,31},{8,16},{9,... | collective-permute-start | bytes 208904 | tf_op jit(solution)/shard_map/ppermute | solution.py:200
  31.4 7.5 %collective-permute-start.18 = (f32[136,128]{1,0:T(8,128)S(1)}, f32[136,128]{1,0:T(8,128)S(1)}, u32[]{:S(2)}, u32[]{:S(2)}) collective-permute-start(f32[136,128]{1,0:T(8,128)S(1)} %get-tuple-element.19.refs_0_), channel_id=1, source_target_pairs={{0,16},{1,17},{2,18},{3,19},{4,20},{5,21},{6,22},{7,23},{8,24},{9,... | collective-permute-start | bytes 208904 | tf_op jit(solution)/shard_map/ppermute | solution.py:200
  31.4 7.5 %collective-permute-start.17 = (f32[136,128]{1,0:T(8,128)S(1)}, f32[136,128]{1,0:T(8,128)S(1)}, u32[]{:S(2)}, u32[]{:S(2)}) collective-permute-start(f32[136,128]{1,0:T(8,128)S(1)} %get-tuple-element.19.refs_0_), channel_id=1, source_target_pairs={{0,8},{1,9},{2,10},{3,11},{4,12},{5,13},{6,14},{7,15},{8,0},{9,1},... | collective-permute-start | bytes 208904 | tf_op jit(solution)/shard_map/ppermute | solution.py:200
  34.3 7.7 %collective-permute-start.16 = (f32[136,128]{1,0:T(8,128)S(1)}, f32[136,128]{1,0:T(8,128)S(1)}, u32[]{:S(2)}, u32[]{:S(2)}) collective-permute-start(f32[136,128]{1,0:T(8,128)S(1)} %get-tuple-element.19.refs_0_), channel_id=1, source_target_pairs={{0,6},{1,7},{2,4},{3,5},{4,2},{5,3},{6,0},{7,1},{8,14},{9,15},{10,... | collective-permute-start | bytes 208904 | tf_op jit(solution)/shard_map/ppermute | solution.py:200
  35.9 11.6 %collective-permute-start.15 = (f32[136,128]{1,0:T(8,128)S(1)}, f32[136,128]{1,0:T(8,128)S(1)}, u32[]{:S(2)}, u32[]{:S(2)}) collective-permute-start(f32[136,128]{1,0:T(8,128)S(1)} %get-tuple-element.19.refs_0_), channel_id=1, source_target_pairs={{0,4},{1,5},{2,6},{3,7},{4,0},{5,1},{6,2},{7,3},{8,12},{9,13},{10,... | collective-permute-start | bytes 208904 | tf_op jit(solution)/shard_map/ppermute | solution.py:200
  37.3 10.3 %collective-permute-start.14 = (f32[136,128]{1,0:T(8,128)S(1)}, f32[136,128]{1,0:T(8,128)S(1)}, u32[]{:S(2)}, u32[]{:S(2)}) collective-permute-start(f32[136,128]{1,0:T(8,128)S(1)} %get-tuple-element.19.refs_0_), channel_id=1, source_target_pairs={{0,2},{1,3},{2,0},{3,1},{4,6},{5,7},{6,4},{7,5},{8,10},{9,11},{10,... | collective-permute-start | bytes 208904 | tf_op jit(solution)/shard_map/ppermute | solution.py:200
  39.0 9.2 %collective-permute-start.22 = (f32[408,128]{1,0:T(8,128)S(1)}, f32[408,128]{1,0:T(8,128)S(1)}, u32[]{:S(2)}, u32[]{:S(2)}) collective-permute-start(f32[408,128]{1,0:T(8,128)S(1)} %shard_map.70.refs_5_), channel_id=1, source_target_pairs={{0,6},{1,7},{2,4},{3,5},{4,2},{5,3},{6,0},{7,1},{8,14},{9,15},{10,... | collective-permute-start | bytes 626696 | tf_op jit(solution)/shard_map/ppermute | solution.py:200
  40.6 10.9 %collective-permute-start.21 = (f32[408,128]{1,0:T(8,128)S(1)}, f32[408,128]{1,0:T(8,128)S(1)}, u32[]{:S(2)}, u32[]{:S(2)}) collective-permute-start(f32[408,128]{1,0:T(8,128)S(1)} %shard_map.70.refs_5_), channel_id=1, source_target_pairs={{0,4},{1,5},{2,6},{3,7},{4,0},{5,1},{6,2},{7,3},{8,12},{9,13},{10,... | collective-permute-start | bytes 626696 | tf_op jit(solution)/shard_map/ppermute | solution.py:200
  42.0 9.5 %collective-permute-start.20 = (f32[408,128]{1,0:T(8,128)S(1)}, f32[408,128]{1,0:T(8,128)S(1)}, u32[]{:S(2)}, u32[]{:S(2)}) collective-permute-start(f32[408,128]{1,0:T(8,128)S(1)} %shard_map.70.refs_5_), channel_id=1, source_target_pairs={{0,2},{1,3},{2,0},{3,1},{4,6},{5,7},{6,4},{7,5},{8,10},{9,11},{10,... | collective-permute-start | bytes 626696 | tf_op jit(solution)/shard_map/ppermute | solution.py:200
  47.5 8.6 %collective-permute-start.24 = (f32[408,128]{1,0:T(8,128)S(1)}, f32[408,128]{1,0:T(8,128)S(1)}, u32[]{:S(2)}, u32[]{:S(2)}) collective-permute-start(f32[408,128]{1,0:T(8,128)S(1)} %shard_map.70.refs_5_), channel_id=1, source_target_pairs={{0,1},{1,0},{2,3},{3,2},{4,5},{5,4},{6,7},{7,6},{8,9},{9,8},{10,11... | collective-permute-start | bytes 626696 | tf_op jit(solution)/shard_map/ppermute | solution.py:200
  47.6 8.5 %collective-permute-start.23 = (f32[544,128]{1,0:T(8,128)S(1)}, f32[544,128]{1,0:T(8,128)S(1)}, u32[]{:S(2)}, u32[]{:S(2)}) collective-permute-start(f32[544,128]{1,0:T(8,128)S(1)} %shard_map.69.refs_4_), channel_id=1, source_target_pairs={{0,1},{1,0},{2,3},{3,2},{4,5},{5,4},{6,7},{7,6},{8,9},{9,8},{10,11... | collective-permute-start | bytes 835592 | tf_op jit(solution)/shard_map/ppermute | solution.py:200
  48.2 7.9 %collective-permute-start.27 = (f32[408,128]{1,0:T(8,128)S(1)}, f32[408,128]{1,0:T(8,128)S(1)}, u32[]{:S(2)}, u32[]{:S(2)}) collective-permute-start(f32[408,128]{1,0:T(8,128)S(1)} %collective-permute-done.22.refs_8_), channel_id=1, source_target_pairs={{0,1},{1,0},{2,3},{3,2},{4,5},{5,4},{6,7},{7,6},{8,9},{9,8},{10,11... | collective-permute-start | bytes 626696 | tf_op jit(solution)/shard_map/ppermute | solution.py:200
  51.5 4.6 %collective-permute-start.26 = (f32[408,128]{1,0:T(8,128)S(1)}, f32[408,128]{1,0:T(8,128)S(1)}, u32[]{:S(2)}, u32[]{:S(2)}) collective-permute-start(f32[408,128]{1,0:T(8,128)S(1)} %collective-permute-done.21.refs_7_), channel_id=1, source_target_pairs={{0,1},{1,0},{2,3},{3,2},{4,5},{5,4},{6,7},{7,6},{8,9},{9,8},{10,11... | collective-permute-start | bytes 626696 | tf_op jit(solution)/shard_map/ppermute | solution.py:200
  51.5 4.6 %collective-permute-start.25 = (f32[408,128]{1,0:T(8,128)S(1)}, f32[408,128]{1,0:T(8,128)S(1)}, u32[]{:S(2)}, u32[]{:S(2)}) collective-permute-start(f32[408,128]{1,0:T(8,128)S(1)} %collective-permute-done.20.refs_6_), channel_id=1, source_target_pairs={{0,1},{1,0},{2,3},{3,2},{4,5},{5,4},{6,7},{7,6},{8,9},{9,8},{10,11... | collective-permute-start | bytes 626696 | tf_op jit(solution)/shard_map/ppermute | solution.py:200
  66.1 5.8 %collective-permute-start.30 = (f32[64,128]{1,0:T(8,128)S(1)}, f32[64,128]{1,0:T(8,128)S(1)}, u32[]{:S(2)}, u32[]{:S(2)}) collective-permute-start(f32[64,128]{1,0:T(8,128)S(1)} %get-tuple-element.28.refs_0_), channel_id=1, source_target_pairs={{0,24},{1,25},{2,26},{3,27},{4,28},{5,29},{6,30},{7,31},{8,16},{9,... | collective-permute-start | bytes 98312 | tf_op jit(solution)/shard_map/ppermute | solution.py:200
  67.6 5.0 %collective-permute-start.29 = (f32[64,128]{1,0:T(8,128)S(1)}, f32[64,128]{1,0:T(8,128)S(1)}, u32[]{:S(2)}, u32[]{:S(2)}) collective-permute-start(f32[64,128]{1,0:T(8,128)S(1)} %get-tuple-element.28.refs_0_), channel_id=1, source_target_pairs={{0,16},{1,17},{2,18},{3,19},{4,20},{5,21},{6,22},{7,23},{8,24},{9,... | collective-permute-start | bytes 98312 | tf_op jit(solution)/shard_map/ppermute | solution.py:200
  67.7 5.2 %collective-permute-start.28 = (f32[64,128]{1,0:T(8,128)S(1)}, f32[64,128]{1,0:T(8,128)S(1)}, u32[]{:S(2)}, u32[]{:S(2)}) collective-permute-start(f32[64,128]{1,0:T(8,128)S(1)} %get-tuple-element.28.refs_0_), channel_id=1, source_target_pairs={{0,8},{1,9},{2,10},{3,11},{4,12},{5,13},{6,14},{7,15},{8,0},{9,1},... | collective-permute-start | bytes 98312 | tf_op jit(solution)/shard_map/ppermute | solution.py:200
  72.9 7.3 %collective-permute-start.33 = (f32[256,128]{1,0:T(8,128)S(1)}, f32[256,128]{1,0:T(8,128)S(1)}, u32[]{:S(2)}, u32[]{:S(2)}) collective-permute-start(f32[256,128]{1,0:T(8,128)S(1)} %shard_map.71.refs_10_), channel_id=1, source_target_pairs={{0,6},{1,7},{2,4},{3,5},{4,2},{5,3},{6,0},{7,1},{8,14},{9,15},{10,... | collective-permute-start | bytes 393224 | tf_op jit(solution)/shard_map/ppermute | solution.py:200
  74.5 7.2 %collective-permute-start.32 = (f32[256,128]{1,0:T(8,128)S(1)}, f32[256,128]{1,0:T(8,128)S(1)}, u32[]{:S(2)}, u32[]{:S(2)}) collective-permute-start(f32[256,128]{1,0:T(8,128)S(1)} %shard_map.71.refs_10_), channel_id=1, source_target_pairs={{0,4},{1,5},{2,6},{3,7},{4,0},{5,1},{6,2},{7,3},{8,12},{9,13},{10,... | collective-permute-start | bytes 393224 | tf_op jit(solution)/shard_map/ppermute | solution.py:200
  75.9 5.8 %collective-permute-start.31 = (f32[256,128]{1,0:T(8,128)S(1)}, f32[256,128]{1,0:T(8,128)S(1)}, u32[]{:S(2)}, u32[]{:S(2)}) collective-permute-start(f32[256,128]{1,0:T(8,128)S(1)} %shard_map.71.refs_10_), channel_id=1, source_target_pairs={{0,2},{1,3},{2,0},{3,1},{4,6},{5,7},{6,4},{7,5},{8,10},{9,11},{10,... | collective-permute-start | bytes 393224 | tf_op jit(solution)/shard_map/ppermute | solution.py:200
  76.4 11.0 %collective-permute-start.34 = (f32[256,128]{1,0:T(8,128)S(1)}, f32[256,128]{1,0:T(8,128)S(1)}, u32[]{:S(2)}, u32[]{:S(2)}) collective-permute-start(f32[256,128]{1,0:T(8,128)S(1)} %shard_map.71.refs_10_), channel_id=1, source_target_pairs={{0,1},{1,0},{2,3},{3,2},{4,5},{5,4},{6,7},{7,6},{8,9},{9,8},{10,11... | collective-permute-start | bytes 393224 | tf_op jit(solution)/shard_map/ppermute | solution.py:200
  80.2 7.3 %collective-permute-start.37 = (f32[256,128]{1,0:T(8,128)S(1)}, f32[256,128]{1,0:T(8,128)S(1)}, u32[]{:S(2)}, u32[]{:S(2)}) collective-permute-start(f32[256,128]{1,0:T(8,128)S(1)} %collective-permute-done.33.refs_13_), channel_id=1, source_target_pairs={{0,1},{1,0},{2,3},{3,2},{4,5},{5,4},{6,7},{7,6},{8,9},{9,8},{10,11... | collective-permute-start | bytes 393224 | tf_op jit(solution)/shard_map/ppermute | solution.py:200
  81.7 5.8 %collective-permute-start.36 = (f32[256,128]{1,0:T(8,128)S(1)}, f32[256,128]{1,0:T(8,128)S(1)}, u32[]{:S(2)}, u32[]{:S(2)}) collective-permute-start(f32[256,128]{1,0:T(8,128)S(1)} %collective-permute-done.32.refs_12_), channel_id=1, source_target_pairs={{0,1},{1,0},{2,3},{3,2},{4,5},{5,4},{6,7},{7,6},{8,9},{9,8},{10,11... | collective-permute-start | bytes 393224 | tf_op jit(solution)/shard_map/ppermute | solution.py:200
  81.7 5.8 %collective-permute-start.35 = (f32[256,128]{1,0:T(8,128)S(1)}, f32[256,128]{1,0:T(8,128)S(1)}, u32[]{:S(2)}, u32[]{:S(2)}) collective-permute-start(f32[256,128]{1,0:T(8,128)S(1)} %collective-permute-done.31.refs_11_), channel_id=1, source_target_pairs={{0,1},{1,0},{2,3},{3,2},{4,5},{5,4},{6,7},{7,6},{8,9},{9,8},{10,11... | collective-permute-start | bytes 393224 | tf_op jit(solution)/shard_map/ppermute | solution.py:200

commit v6 on v5

--- a/solution.py
+++ b/solution.py
@@ -10,7 +10,7 @@
 F32 = jnp.float32
 BF16 = jnp.bfloat16
 highest = lax.Precision.HIGHEST
-CHUNK = 512
+CHUNK = 2048
 
 
 def params(mebibytes=56):
@@ -21,6 +21,17 @@
     return lax.dot_general(
         a, b, (((ca,), (cb,)), ((), ())), precision=highest, preferred_element_type=F32
     )
+
+
+def sweep(total, add, zero, chunk=CHUNK):
+    chunk = min(chunk, total)
+    if chunk == total:
+        return add(pl.ds(0, total), zero)
+
+    def part(i, acc):
+        return add(pl.ds(pl.multiple_of(i * chunk, chunk), chunk), acc)
+
+    return lax.fori_loop(0, total // chunk, part, zero)
 
 
 def halves(x):
@@ -158,31 +169,6 @@
         at += part.shape[0]
 
 
-def join_blocks(a_ref, b_ref, out_ref, sems):
-    rows = a_ref.shape[0]
-    copies = [
-        pltpu.make_async_copy(a_ref, out_ref.at[:rows, :], sems.at[0]),
-        pltpu.make_async_copy(b_ref, out_ref.at[rows:, :], sems.at[1]),
-    ]
-    for copy in copies:
-        copy.start()
-    for copy in copies:
-        copy.wait()
-
-
-def joined(a, b):
-    return pl.pallas_call(
-        join_blocks,
-        out_shape=shape(2 * a.shape[0], a.shape[1]),
-        in_specs=[pl.BlockSpec(memory_space=pltpu.HBM)] * 2,
-        out_specs=VMEM,
-        scratch_shapes=[pltpu.SemaphoreType.DMA((2,))],
-        compiler_params=params(2),
-        cost_estimate=cost(1),
-        name="own",
-    )(a, b)
-
-
 def packed(parts):
     rows = sum(part.shape[0] for part in parts)
     return pl.pallas_call(
@@ -235,13 +221,12 @@
     ky_ref[2 * rows : 2 * rows + 1, :rows] = diag_ref[...]
 
 
-def metric_head(y_ref, metric_ref, upper_ref):
+def metric_kernel(y_ref, out_ref):
     total, double = y_ref.shape
     width = double // 2
-    chunk = min(CHUNK, total)
-
-    def add(i, acc):
-        top, rest = halves(y_ref[pl.ds(pl.multiple_of(i * chunk, chunk), chunk), :])
+
+    def add(at, acc):
+        top, rest = halves(y_ref[at, :])
         product = lax.dot_general(
             top,
             jnp.concatenate([top, rest], 1),
@@ -250,17 +235,11 @@
         )
         return acc + product
 
-    sums = lax.fori_loop(0, total // chunk, add, jnp.zeros((double, 2 * double), F32))
+    sums = sweep(total, add, jnp.zeros((double, 2 * double), F32))
     metric = sums[:, :double] + (sums[:, double:] + sums[:, double:].T)
-    metric_ref[...] = metric
-    upper_ref[...] = inverse_factor(metric[:width, :width])
-
-
-def metric_tail(metric_ref, upper_ref, out_ref):
-    width = upper_ref.shape[0]
-    upper = upper_ref[...]
-    cross = mm(upper, metric_ref[:width, width:])
-    lower = inverse_factor(metric_ref[width:, width:] - mm(cross, cross, 0, 0))
+    upper = inverse_factor(metric[:width, :width])
+    cross = mm(upper, metric[:width, width:])
+    lower = inverse_factor(metric[width:, width:] - mm(cross, cross, 0, 0))
     out_ref[:width, :width] = upper
     out_ref[:width, width:] = jnp.zeros((width, width), F32)
     out_ref[width:, :width] = -mm(lower, mm(cross, upper, 0, 0))
@@ -279,13 +258,11 @@
     total, double = y_ref.shape
     width = double // 2
     rows = diag_ref.shape[0]
-    chunk = min(CHUNK, total)
-
-    def add(i, acc):
-        at = pl.ds(pl.multiple_of(i * chunk, chunk), chunk)
+
+    def add(at, acc):
         return acc + mm3(y_ref[at, :], ky_ref[at, :], 0, 0)
 
-    g = lax.fori_loop(0, total // chunk, add, jnp.zeros((double, double), F32))
+    g = sweep(total, add, jnp.zeros((double, double), F32), 1024)
     factor = factor_ref[...]
     tie = g[:width, width:].T
     side = jnp.concatenate([g[:width, :width], tie], 0)
@@ -300,8 +277,7 @@
     mixing = stacked(mixing)
     small_ref[...] = values
 
-    def update(i, acc):
-        at = pl.ds(pl.multiple_of(i * chunk, chunk), chunk)
+    def update(at, acc):
         pair = with_stacked(y_ref[at, :], both)
         image = with_stacked(ky_ref[at, :], mixing)
         y2_ref[at, :width] = pair[:, :width]
@@ -310,7 +286,7 @@
         y2_ref[at, width:] = residual
         return acc + jnp.sum(residual * residual, axis=0, keepdims=True)
 
-    squares = lax.fori_loop(0, total // chunk, update, jnp.zeros((1, width), F32))
+    squares = sweep(total, update, jnp.zeros((1, width), F32))
     norm_ref[...] = jnp.sqrt(squares)
     for b in range(total // rows):
         at = pl.ds(b * rows, rows)
@@ -342,13 +318,11 @@
 def second_factor(y2_ref, small_ref, tie_ref, factor_ref, known_ref, square_ref):
     total, double = y2_ref.shape
     width = double // 2
-    chunk = min(CHUNK, total)
-
-    def add(i, acc):
-        at = pl.ds(pl.multiple_of(i * chunk, chunk), chunk)
+
+    def add(at, acc):
         return acc + mm3(y2_ref[at, width:], y2_ref[at, :], 0, 0)
 
-    gram = lax.fori_loop(0, total // chunk, add, jnp.zeros((width, double), F32))
+    gram = sweep(total, add, jnp.zeros((width, double), F32))
     tie = gram[:, :width]
     values = small_ref[...]
     factor = inverse_factor(gram[:, width:] - mm(tie, tie, 1, 1))
@@ -362,13 +336,11 @@
     ritz_ref, search_ref, norm_ref = outs
     total, double = y2_ref.shape
     width = double // 2
-    chunk = min(CHUNK, total)
-
-    def add(i, acc):
-        at = pl.ds(pl.multiple_of(i * chunk, chunk), chunk)
+
+    def add(at, acc):
         return acc + mm3(image_ref[at, width:], y2_ref[at, :], 0, 0)
 
-    g = lax.fori_loop(0, total // chunk, add, jnp.zeros((width, double), F32))
+    g = sweep(total, add, jnp.zeros((width, double), F32))
     values, tie, factor, done, square = [ref[...] for ref in known]
     z = mm3(factor, g[:, :width]) - done
     small = inverse_factor(square + mm3(z, z, 0, 0))
@@ -380,12 +352,11 @@
     values2 = mm3(mixing, held[double:], 0, 0)
     weights = stacked(jnp.concatenate([mixing, -mm3(mixing, values2)], 0))
 
-    def update(i, acc):
-        at = pl.ds(pl.multiple_of(i * chunk, chunk), chunk)
+    def update(at, acc):
         residual = with_stacked(jnp.concatenate([image_ref[at, :], y2_ref[at, :]], 1), weights)
         return acc + jnp.sum(residual * residual, axis=0, keepdims=True)
 
-    squares = lax.fori_loop(0, total // chunk, update, jnp.zeros((1, width), F32))
+    squares = sweep(total, update, jnp.zeros((1, width), F32))
     norm_ref[:1, :] = first_ref[...]
     norm_ref[1:, :] = jnp.sqrt(squares)
     own = own_y2()
@@ -446,25 +417,16 @@
 
 
 def metric_factor(y, mebibytes):
-    width = y.shape[1] // 2
-    metric, upper = pl.pallas_call(
-        metric_head,
-        out_shape=(shape(2 * width, 2 * width), shape(width, width)),
+    double = y.shape[1]
+    return pl.pallas_call(
+        metric_kernel,
+        out_shape=shape(double, double),
         in_specs=[VMEM],
-        out_specs=(VMEM, VMEM),
-        compiler_params=params(mebibytes),
-        cost_estimate=cost(7),
-        name="metric_head",
-    )(y)
-    return pl.pallas_call(
-        metric_tail,
-        out_shape=shape(2 * width, 2 * width),
-        in_specs=[VMEM, VMEM],
         out_specs=VMEM,
         compiler_params=params(mebibytes),
-        cost_estimate=cost(7),
-        name="metric_tail",
-    )(metric, upper)
+        cost_estimate=cost(9),
+        name="metric",
+    )(y)
 
 
 def second_metric(y2, values, mebibytes):
@@ -487,7 +449,8 @@
     lanes = max(n, 128)
     me = lax.axis_index("blk").astype(jnp.int32).reshape(1)
     along = diag.reshape(1, rows)
-    sent = gather(joined(ritz, search), n, True)
+    own = lax.pad(ritz, 0.0, ((0, rows, 0), (0, 0, 0))) + lax.pad(search, 0.0, ((rows, 0, 0), (0, 0, 0)))
+    sent = gather(own, n, True)
     y, ky_own = pl.pallas_call(
         lambda *refs: first_product(rings, rows, *refs),
         out_shape=(shape(total, 2 * width), shape(2 * rows + 8, width)),

time: 96.9 us -> 105 us (1.084)
  waiting for transfers between devices: 21.9 us -> 33.3 us
  Pallas kernels: 34.3 us -> 31.2 us
  local copies, waits for them, and re-layouts: 1.68 us -> 0.17 us
    ppermute x38, waiting for transfers between devices: 21.9 us -> 33.3 us  [swap(): return lax.ppermute(x, 'blk', [(i, i ^ m) for i in range(n)])]
    unnamed x9 -> x5, local copies, waits for them, and re-layouts: 1.68 us -> 0.17 us
    pallas_call x1, Pallas kernels: 9.96 us -> 8.88 us  [cubed(): pl.pallas_call(lambda *refs: with_product(rings, rows, *refs), out_shape=...]
    pallas_call x3 -> x1, Pallas kernels: 9.11 us -> 8.27 us  [metric_factor(): pl.pallas_call(metric_kernel, out_shape=shape(double, double), in_specs=[...]
  transfers between devices with their start and end apart: 38 -> 38, of which waited for: 14 -> 16; matrix products, arithmetic and copies ran while one was open for 0% -> 0% of each run, Pallas kernels for 15% -> 13%
where the time goes in v6:
time: 105 us; the launch traced here: 104 us
  starting transfers between devices  38.1 us (36%)
  waiting for transfers between devices  33.3 us (32%)
  Pallas kernels  31.2 us (30%)
    ppermute x38, starting transfers between devices, swap(): return lax.ppermute(x, 'blk', [(i, i ^ m) for i in range(n)])  38.1 us
    ppermute x38, waiting for transfers between devices, swap(): return lax.ppermute(x, 'blk', [(i, i ^ m) for i in range(n)])  33.3 us
    pallas_call x1, Pallas kernels, cubed(): pl.pallas_call(lambda *refs: with_product(rings, rows, *refs), out_shape=...  8.88 us
    pallas_call x1, Pallas kernels, metric_factor(): pl.pallas_call(metric_kernel, out_shape=shape(double, double), in_specs=[...  8.27 us
    pallas_call x1, Pallas kernels, cubed(): pl.pallas_call(lambda *refs: last_step(rings, rows, *refs), out_shape=(sh...  8.18 us
    pallas_call x1, Pallas kernels, second_metric(): pl.pallas_call(second_factor, out_shape=(shape(width, width),) * 4, in_sp...  4.99 us
  transfers between devices with their start and end apart: 38, of which 16 were waited for; matrix products, arithmetic and copies ran while one was open for 0% of the time, Pallas kernels for 13%

profile of v6, /device:TPU:0, one launch (start us, length us, event | category | flops | bytes accessed | tf_op | source)
XLA Modules:
  0.0 104.5 jit_solution(10681743910134681667)
XLA Ops:
  0.6 0.8 pad_add_fusion.refs_0_
  1.5 5.1 %collective-permute-start.5 = (f32[128,128]{1,0:T(8,128)S(1)}, f32[128,128]{1,0:T(8,128)S(1)}, u32[]{:S(2)}, u32[]{:S(2)}) collective-permute-start(f32[128,128]{1,0:T(8,128)S(1)} %pad_add_fusion.refs_0_), channel_id=1, source_target_pairs={{0,24},{1,25},{2,26},{3,27},{4,28},{5,29},{6,30},{7,31},{8,16},{9,... | collective-permute-start | bytes 196616 | tf_op jit(solution)/shard_map/ppermute | solution.py:186
  6.6 0.6 collective-permute-start.3
  7.3 2.6 %collective-permute-start.2 = (f32[128,128]{1,0:T(8,128)S(1)}, f32[128,128]{1,0:T(8,128)S(1)}, u32[]{:S(2)}, u32[]{:S(2)}) collective-permute-start(f32[128,128]{1,0:T(8,128)S(1)} %pad_add_fusion.refs_0_), channel_id=1, source_target_pairs={{0,6},{1,7},{2,4},{3,5},{4,2},{5,3},{6,0},{7,1},{8,14},{9,15},{10,... | collective-permute-start | bytes 196616 | tf_op jit(solution)/shard_map/ppermute | solution.py:186
  9.8 2.4 %collective-permute-done.4.refs_1_ = f32[128,128]{1,0:T(8,128)S(1)} collective-permute-done((f32[128,128]{1,0:T(8,128)S(1)}, f32[128,128]{1,0:T(8,128)S(1)}, u32[]{:S(2)}, u32[]{:S(2)}) %collective-permute-start.4) | collective-permute-done | bytes 65568 | tf_op jit(solution)/shard_map/ppermute | solution.py:186
  12.2 2.5 %collective-permute-start.8 = (f32[384,128]{1,0:T(8,128)S(1)}, f32[384,128]{1,0:T(8,128)S(1)}, u32[]{:S(2)}, u32[]{:S(2)}) collective-permute-start(f32[384,128]{1,0:T(8,128)S(1)} %shard_map.68.refs_4_), channel_id=1, source_target_pairs={{0,6},{1,7},{2,4},{3,5},{4,2},{5,3},{6,0},{7,1},{8,14},{9,15},{10,... | collective-permute-start | bytes 589832 | tf_op jit(solution)/shard_map/ppermute | solution.py:186
  14.7 0.5 collective-permute-start.7
  15.3 0.5 collective-permute-start.6
  15.8 1.5 %collective-permute-start.1 = (f32[128,128]{1,0:T(8,128)S(1)}, f32[128,128]{1,0:T(8,128)S(1)}, u32[]{:S(2)}, u32[]{:S(2)}) collective-permute-start(f32[128,128]{1,0:T(8,128)S(1)} %pad_add_fusion.refs_0_), channel_id=1, source_target_pairs={{0,4},{1,5},{2,6},{3,7},{4,0},{5,1},{6,2},{7,3},{8,12},{9,13},{10,... | collective-permute-start | bytes 196616 | tf_op jit(solution)/shard_map/ppermute | solution.py:186
  17.3 1.5 %collective-permute-start = (f32[128,128]{1,0:T(8,128)S(1)}, f32[128,128]{1,0:T(8,128)S(1)}, u32[]{:S(2)}, u32[]{:S(2)}) collective-permute-start(f32[128,128]{1,0:T(8,128)S(1)} %pad_add_fusion.refs_0_), channel_id=1, source_target_pairs={{0,2},{1,3},{2,0},{3,1},{4,6},{5,7},{6,4},{7,5},{8,10},{9,11},{10,... | collective-permute-start | bytes 196616 | tf_op jit(solution)/shard_map/ppermute | solution.py:186
  18.8 6.5 %collective-permute-done.1.refs_2_ = f32[128,128]{1,0:T(8,128)S(1)} collective-permute-done((f32[128,128]{1,0:T(8,128)S(1)}, f32[128,128]{1,0:T(8,128)S(1)}, u32[]{:S(2)}, u32[]{:S(2)}) %collective-permute-start.1) | collective-permute-done | bytes 65568 | tf_op jit(solution)/shard_map/ppermute | solution.py:186
  25.3 0.2 collective-permute-done.refs_1_
  25.6 0.5 collective-permute-start.10
  26.2 0.4 collective-permute-start.12
  26.9 0.5 collective-permute-done.10.refs_9_
  27.4 0.3 collective-permute-done.13.refs_12_
  27.7 0.3 collective-permute-done.12.refs_11_
  28.0 0.3 collective-permute-done.11.refs_10_
  28.3 0.8 first_product.1
  29.1 1.6 %collective-permute-start.19 = (f32[136,128]{1,0:T(8,128)S(1)}, f32[136,128]{1,0:T(8,128)S(1)}, u32[]{:S(2)}, u32[]{:S(2)}) collective-permute-start(f32[136,128]{1,0:T(8,128)S(1)} %get-tuple-element.15.refs_0_), channel_id=1, source_target_pairs={{0,24},{1,25},{2,26},{3,27},{4,28},{5,29},{6,30},{7,31},{8,16},{9,... | collective-permute-start | bytes 208904 | tf_op jit(solution)/shard_map/ppermute | solution.py:186
  30.6 2.9 %collective-permute-start.17 = (f32[136,128]{1,0:T(8,128)S(1)}, f32[136,128]{1,0:T(8,128)S(1)}, u32[]{:S(2)}, u32[]{:S(2)}) collective-permute-start(f32[136,128]{1,0:T(8,128)S(1)} %get-tuple-element.15.refs_0_), channel_id=1, source_target_pairs={{0,8},{1,9},{2,10},{3,11},{4,12},{5,13},{6,14},{7,15},{8,0},{9,1},... | collective-permute-start | bytes 208904 | tf_op jit(solution)/shard_map/ppermute | solution.py:186
  33.5 2.5 %collective-permute-done.19.refs_2_ = f32[136,128]{1,0:T(8,128)S(1)} collective-permute-done((f32[136,128]{1,0:T(8,128)S(1)}, f32[136,128]{1,0:T(8,128)S(1)}, u32[]{:S(2)}, u32[]{:S(2)}) %collective-permute-start.19) | collective-permute-done | bytes 69664 | tf_op jit(solution)/shard_map/ppermute | solution.py:186
  36.0 2.1 %collective-permute-done.18.refs_1_ = f32[136,128]{1,0:T(8,128)S(1)} collective-permute-done((f32[136,128]{1,0:T(8,128)S(1)}, f32[136,128]{1,0:T(8,128)S(1)}, u32[]{:S(2)}, u32[]{:S(2)}) %collective-permute-start.18) | collective-permute-done | bytes 69664 | tf_op jit(solution)/shard_map/ppermute | solution.py:186
  38.2 1.6 %collective-permute-start.22 = (f32[408,128]{1,0:T(8,128)S(1)}, f32[408,128]{1,0:T(8,128)S(1)}, u32[]{:S(2)}, u32[]{:S(2)}) collective-permute-start(f32[408,128]{1,0:T(8,128)S(1)} %shard_map.70.refs_5_), channel_id=1, source_target_pairs={{0,6},{1,7},{2,4},{3,5},{4,2},{5,3},{6,0},{7,1},{8,14},{9,15},{10,... | collective-permute-start | bytes 626696 | tf_op jit(solution)/shard_map/ppermute | solution.py:186
  39.8 1.4 %collective-permute-start.21 = (f32[408,128]{1,0:T(8,128)S(1)}, f32[408,128]{1,0:T(8,128)S(1)}, u32[]{:S(2)}, u32[]{:S(2)}) collective-permute-start(f32[408,128]{1,0:T(8,128)S(1)} %shard_map.70.refs_5_), channel_id=1, source_target_pairs={{0,4},{1,5},{2,6},{3,7},{4,0},{5,1},{6,2},{7,3},{8,12},{9,13},{10,... | collective-permute-start | bytes 626696 | tf_op jit(solution)/shard_map/ppermute | solution.py:186
  41.2 0.5 collective-permute-start.20
  41.7 1.5 %collective-permute-start.16 = (f32[136,128]{1,0:T(8,128)S(1)}, f32[136,128]{1,0:T(8,128)S(1)}, u32[]{:S(2)}, u32[]{:S(2)}) collective-permute-start(f32[136,128]{1,0:T(8,128)S(1)} %get-tuple-element.15.refs_0_), channel_id=1, source_target_pairs={{0,6},{1,7},{2,4},{3,5},{4,2},{5,3},{6,0},{7,1},{8,14},{9,15},{10,... | collective-permute-start | bytes 208904 | tf_op jit(solution)/shard_map/ppermute | solution.py:186
  43.3 1.4 %collective-permute-start.15 = (f32[136,128]{1,0:T(8,128)S(1)}, f32[136,128]{1,0:T(8,128)S(1)}, u32[]{:S(2)}, u32[]{:S(2)}) collective-permute-start(f32[136,128]{1,0:T(8,128)S(1)} %get-tuple-element.15.refs_0_), channel_id=1, source_target_pairs={{0,4},{1,5},{2,6},{3,7},{4,0},{5,1},{6,2},{7,3},{8,12},{9,13},{10,... | collective-permute-start | bytes 208904 | tf_op jit(solution)/shard_map/ppermute | solution.py:186
  44.7 7.7 %collective-permute-done.16.refs_3_ = f32[136,128]{1,0:T(8,128)S(1)} collective-permute-done((f32[136,128]{1,0:T(8,128)S(1)}, f32[136,128]{1,0:T(8,128)S(1)}, u32[]{:S(2)}, u32[]{:S(2)}) %collective-permute-start.16) | collective-permute-done | bytes 69664 | tf_op jit(solution)/shard_map/ppermute | solution.py:186
  52.3 1.5 %collective-permute-start.14 = (f32[136,128]{1,0:T(8,128)S(1)}, f32[136,128]{1,0:T(8,128)S(1)}, u32[]{:S(2)}, u32[]{:S(2)}) collective-permute-start(f32[136,128]{1,0:T(8,128)S(1)} %get-tuple-element.15.refs_0_), channel_id=1, source_target_pairs={{0,2},{1,3},{2,0},{3,1},{4,6},{5,7},{6,4},{7,5},{8,10},{9,11},{10,... | collective-permute-start | bytes 208904 | tf_op jit(solution)/shard_map/ppermute | solution.py:186
  53.8 2.8 %collective-permute-done.14.refs_1_ = f32[136,128]{1,0:T(8,128)S(1)} collective-permute-done((f32[136,128]{1,0:T(8,128)S(1)}, f32[136,128]{1,0:T(8,128)S(1)}, u32[]{:S(2)}, u32[]{:S(2)}) %collective-permute-start.14) | collective-permute-done | bytes 69664 | tf_op jit(solution)/shard_map/ppermute | solution.py:186
  56.8 0.5 collective-permute-start.27
  57.3 0.4 collective-permute-start.25
  57.8 8.3 %metric.1.refs_3_ = f32[256,256]{1,0:T(8,128)S(1)} custom-call(f32[2048,256]{1,0:T(8,128)S(1)} %get-tuple-element.14.y_ref.refs_2_), custom_call_target="tpu_custom_call" | custom-call | flops 8999999488 | tf_op jit(solution)/shard_map/metric/pallas_call | solution.py:421
  66.1 8.9 %first_step.1 = (f32[2048,256]{1,0:T(8,128)S(1)}, f32[2048,128]{1,0:T(8,128)S(1)}, f32[128,128]{1,0:T(8,128)S(1)}, f32[1,128]{1,0:T(1,128)S(1)}, f32[64,128]{1,0:T(8,128)S(1)}) custom-call(s32[1]{0:T(128)} %bitcast.refs_0_, f32[64,2048]{1,0:T(8,128)S(1)} %bitcast.6, f32[2048,256]{1,0:T(8,128)S(1)} %get-tuple-element.14.y_ref.refs_2_, ...), custom_call_target="tpu_custom_call" | custom-call | tf_op jit(solution)/shard_map/first_step/pallas_call | solution.py:464
  75.0 1.5 %collective-permute-start.30 = (f32[64,128]{1,0:T(8,128)S(1)}, f32[64,128]{1,0:T(8,128)S(1)}, u32[]{:S(2)}, u32[]{:S(2)}) collective-permute-start(f32[64,128]{1,0:T(8,128)S(1)} %get-tuple-element.24.refs_0_), channel_id=1, source_target_pairs={{0,24},{1,25},{2,26},{3,27},{4,28},{5,29},{6,30},{7,31},{8,16},{9,... | collective-permute-start | bytes 98312 | tf_op jit(solution)/shard_map/ppermute | solution.py:186
  76.5 2.9 %collective-permute-start.28 = (f32[64,128]{1,0:T(8,128)S(1)}, f32[64,128]{1,0:T(8,128)S(1)}, u32[]{:S(2)}, u32[]{:S(2)}) collective-permute-start(f32[64,128]{1,0:T(8,128)S(1)} %get-tuple-element.24.refs_0_), channel_id=1, source_target_pairs={{0,8},{1,9},{2,10},{3,11},{4,12},{5,13},{6,14},{7,15},{8,0},{9,1},... | collective-permute-start | bytes 98312 | tf_op jit(solution)/shard_map/ppermute | solution.py:186
  79.4 1.3 %collective-permute-done.30.refs_3_ = f32[64,128]{1,0:T(8,128)S(1)} collective-permute-done((f32[64,128]{1,0:T(8,128)S(1)}, f32[64,128]{1,0:T(8,128)S(1)}, u32[]{:S(2)}, u32[]{:S(2)}) %collective-permute-start.30) | collective-permute-done | bytes 32800 | tf_op jit(solution)/shard_map/ppermute | solution.py:186
  80.8 0.9 collective-permute-done.29.refs_2_
  81.6 0.2 collective-permute-done.28.refs_1_
  81.8 1.6 %collective-permute-start.33 = (f32[256,128]{1,0:T(8,128)S(1)}, f32[256,128]{1,0:T(8,128)S(1)}, u32[]{:S(2)}, u32[]{:S(2)}) collective-permute-start(f32[256,128]{1,0:T(8,128)S(1)} %shard_map.71.refs_10_), channel_id=1, source_target_pairs={{0,6},{1,7},{2,4},{3,5},{4,2},{5,3},{6,0},{7,1},{8,14},{9,15},{10,... | collective-permute-start | bytes 393224 | tf_op jit(solution)/shard_map/ppermute | solution.py:186
  83.4 1.4 %collective-permute-start.32 = (f32[256,128]{1,0:T(8,128)S(1)}, f32[256,128]{1,0:T(8,128)S(1)}, u32[]{:S(2)}, u32[]{:S(2)}) collective-permute-start(f32[256,128]{1,0:T(8,128)S(1)} %shard_map.71.refs_10_), channel_id=1, source_target_pairs={{0,4},{1,5},{2,6},{3,7},{4,0},{5,1},{6,2},{7,3},{8,12},{9,13},{10,... | collective-permute-start | bytes 393224 | tf_op jit(solution)/shard_map/ppermute | solution.py:186
  84.9 0.5 collective-permute-start.31
  85.4 3.8 %collective-permute-done.33.refs_13_ = f32[256,128]{1,0:T(8,128)S(1)} collective-permute-done((f32[256,128]{1,0:T(8,128)S(1)}, f32[256,128]{1,0:T(8,128)S(1)}, u32[]{:S(2)}, u32[]{:S(2)}) %collective-permute-start.33) | collective-permute-done | bytes 131104 | tf_op jit(solution)/shard_map/ppermute | solution.py:186
  89.2 1.5 %collective-permute-done.32.refs_12_ = f32[256,128]{1,0:T(8,128)S(1)} collective-permute-done((f32[256,128]{1,0:T(8,128)S(1)}, f32[256,128]{1,0:T(8,128)S(1)}, u32[]{:S(2)}, u32[]{:S(2)}) %collective-permute-start.32) | collective-permute-done | bytes 131104 | tf_op jit(solution)/shard_map/ppermute | solution.py:186
  90.7 0.5 collective-permute-start.35
  91.2 5.0 %second_factor.1 = (f32[128,128]{1,0:T(8,128)S(1)}, f32[128,128]{1,0:T(8,128)S(1)}, f32[128,128]{1,0:T(8,128)S(1)}, f32[128,128]{1,0:T(8,128)S(1)}) custom-call(f32[2048,256]{1,0:T(8,128)S(1)} %get-tuple-element.16.y2_ref.refs_1_, f32[128,128]{1,0:T(8,128)S(1)} %get-tuple-element.19.small_ref.refs_5_), custom_call_target="tpu_custom_call" | custom-call | flops 8999999488 | tf_op jit(solution)/shard_map/second_factor/pallas_call | solution.py:434
  96.3 8.2 %last_step.1 = (f32[64,128]{1,0:T(8,128)}, f32[64,128]{1,0:T(8,128)}, f32[2,128]{1,0:T(2,128)}) custom-call(s32[1]{0:T(128)} %bitcast.refs_0_, f32[2048,256]{1,0:T(8,128)S(1)} %get-tuple-element.16.y2_ref.refs_1_, f32[2048,128]{1,0:T(8,128)S(1)} %get-tuple-element.17.refs_2_, f32[1,128]{1,0:T(1,128)S(1)} %get-tuple-element.18.refs_3_, f32[1,64]{1,0:T(1,128)S(1)} %bitcast.8, ...), custom_call_target="tpu_custom_call" | custom-call | tf_op jit(solution)/shard_map/last_step/pallas_call | solution.py:485
  (44 shorter events, 0.7 us)
Async XLA Ops:
  0.6 26.1 %copy-start.1 = (f32[64,1,2048]{2,1,0:T(1,128)S(1)}, f32[64,1,2048]{2,1,0:T(1,128)}, u32[]{:S(2)}) copy-start(f32[64,1,2048]{2,1,0:T(1,128)} %param.4) | copy-start | bytes 1572868
  1.5 26.8 %copy-start = (f32[64]{0:T(128)S(1)}, f32[64]{0:T(128)}, u32[]{:S(2)}) copy-start(f32[64]{0:T(128)} %param.7) | copy-start | bytes 772
  1.5 8.4 %collective-permute-start.5 = (f32[128,128]{1,0:T(8,128)S(1)}, f32[128,128]{1,0:T(8,128)S(1)}, u32[]{:S(2)}, u32[]{:S(2)}) collective-permute-start(f32[128,128]{1,0:T(8,128)S(1)} %pad_add_fusion.refs_0_), channel_id=1, source_target_pairs={{0,24},{1,25},{2,26},{3,27},{4,28},{5,29},{6,30},{7,31},{8,16},{9,... | collective-permute-start | bytes 196616 | tf_op jit(solution)/shard_map/ppermute | solution.py:186
  6.6 5.6 %collective-permute-start.4 = (f32[128,128]{1,0:T(8,128)S(1)}, f32[128,128]{1,0:T(8,128)S(1)}, u32[]{:S(2)}, u32[]{:S(2)}) collective-permute-start(f32[128,128]{1,0:T(8,128)S(1)} %pad_add_fusion.refs_0_), channel_id=1, source_target_pairs={{0,16},{1,17},{2,18},{3,19},{4,20},{5,21},{6,22},{7,23},{8,24},{9,... | collective-permute-start | bytes 196616 | tf_op jit(solution)/shard_map/ppermute | solution.py:186
  6.6 5.6 %collective-permute-start.3 = (f32[128,128]{1,0:T(8,128)S(1)}, f32[128,128]{1,0:T(8,128)S(1)}, u32[]{:S(2)}, u32[]{:S(2)}) collective-permute-start(f32[128,128]{1,0:T(8,128)S(1)} %pad_add_fusion.refs_0_), channel_id=1, source_target_pairs={{0,8},{1,9},{2,10},{3,11},{4,12},{5,13},{6,14},{7,15},{8,0},{9,1},... | collective-permute-start | bytes 196616 | tf_op jit(solution)/shard_map/ppermute | solution.py:186
  7.3 10.1 %collective-permute-start.2 = (f32[128,128]{1,0:T(8,128)S(1)}, f32[128,128]{1,0:T(8,128)S(1)}, u32[]{:S(2)}, u32[]{:S(2)}) collective-permute-start(f32[128,128]{1,0:T(8,128)S(1)} %pad_add_fusion.refs_0_), channel_id=1, source_target_pairs={{0,6},{1,7},{2,4},{3,5},{4,2},{5,3},{6,0},{7,1},{8,14},{9,15},{10,... | collective-permute-start | bytes 196616 | tf_op jit(solution)/shard_map/ppermute | solution.py:186
  12.2 13.9 %collective-permute-start.8 = (f32[384,128]{1,0:T(8,128)S(1)}, f32[384,128]{1,0:T(8,128)S(1)}, u32[]{:S(2)}, u32[]{:S(2)}) collective-permute-start(f32[384,128]{1,0:T(8,128)S(1)} %shard_map.68.refs_4_), channel_id=1, source_target_pairs={{0,6},{1,7},{2,4},{3,5},{4,2},{5,3},{6,0},{7,1},{8,14},{9,15},{10,... | collective-permute-start | bytes 589832 | tf_op jit(solution)/shard_map/ppermute | solution.py:186
  14.7 11.4 %collective-permute-start.7 = (f32[384,128]{1,0:T(8,128)S(1)}, f32[384,128]{1,0:T(8,128)S(1)}, u32[]{:S(2)}, u32[]{:S(2)}) collective-permute-start(f32[384,128]{1,0:T(8,128)S(1)} %shard_map.68.refs_4_), channel_id=1, source_target_pairs={{0,4},{1,5},{2,6},{3,7},{4,0},{5,1},{6,2},{7,3},{8,12},{9,13},{10,... | collective-permute-start | bytes 589832 | tf_op jit(solution)/shard_map/ppermute | solution.py:186
  15.3 11.4 %collective-permute-start.6 = (f32[384,128]{1,0:T(8,128)S(1)}, f32[384,128]{1,0:T(8,128)S(1)}, u32[]{:S(2)}, u32[]{:S(2)}) collective-permute-start(f32[384,128]{1,0:T(8,128)S(1)} %shard_map.68.refs_4_), channel_id=1, source_target_pairs={{0,2},{1,3},{2,0},{3,1},{4,6},{5,7},{6,4},{7,5},{8,10},{9,11},{10,... | collective-permute-start | bytes 589832 | tf_op jit(solution)/shard_map/ppermute | solution.py:186
  15.8 9.5 %collective-permute-start.1 = (f32[128,128]{1,0:T(8,128)S(1)}, f32[128,128]{1,0:T(8,128)S(1)}, u32[]{:S(2)}, u32[]{:S(2)}) collective-permute-start(f32[128,128]{1,0:T(8,128)S(1)} %pad_add_fusion.refs_0_), channel_id=1, source_target_pairs={{0,4},{1,5},{2,6},{3,7},{4,0},{5,1},{6,2},{7,3},{8,12},{9,13},{10,... | collective-permute-start | bytes 196616 | tf_op jit(solution)/shard_map/ppermute | solution.py:186
  17.3 8.2 %collective-permute-start = (f32[128,128]{1,0:T(8,128)S(1)}, f32[128,128]{1,0:T(8,128)S(1)}, u32[]{:S(2)}, u32[]{:S(2)}) collective-permute-start(f32[128,128]{1,0:T(8,128)S(1)} %pad_add_fusion.refs_0_), channel_id=1, source_target_pairs={{0,2},{1,3},{2,0},{3,1},{4,6},{5,7},{6,4},{7,5},{8,10},{9,11},{10,... | collective-permute-start | bytes 196616 | tf_op jit(solution)/shard_map/ppermute | solution.py:186
  25.5 1.9 %collective-permute-start.9 = (f32[512,128]{1,0:T(8,128)S(1)}, f32[512,128]{1,0:T(8,128)S(1)}, u32[]{:S(2)}, u32[]{:S(2)}) collective-permute-start(f32[512,128]{1,0:T(8,128)S(1)} %shard_map.67.refs_3_), channel_id=1, source_target_pairs={{0,1},{1,0},{2,3},{3,2},{4,5},{5,4},{6,7},{7,6},{8,9},{9,8},{10,11... | collective-permute-start | bytes 786440 | tf_op jit(solution)/shard_map/ppermute | solution.py:186
  25.6 1.8 %collective-permute-start.10 = (f32[384,128]{1,0:T(8,128)S(1)}, f32[384,128]{1,0:T(8,128)S(1)}, u32[]{:S(2)}, u32[]{:S(2)}) collective-permute-start(f32[384,128]{1,0:T(8,128)S(1)} %shard_map.68.refs_4_), channel_id=1, source_target_pairs={{0,1},{1,0},{2,3},{3,2},{4,5},{5,4},{6,7},{7,6},{8,9},{9,8},{10,11... | collective-permute-start | bytes 589832 | tf_op jit(solution)/shard_map/ppermute | solution.py:186
  26.1 1.6 %collective-permute-start.13 = (f32[384,128]{1,0:T(8,128)S(1)}, f32[384,128]{1,0:T(8,128)S(1)}, u32[]{:S(2)}, u32[]{:S(2)}) collective-permute-start(f32[384,128]{1,0:T(8,128)S(1)} %collective-permute-done.8.refs_7_), channel_id=1, source_target_pairs={{0,1},{1,0},{2,3},{3,2},{4,5},{5,4},{6,7},{7,6},{8,9},{9,8},{10,11... | collective-permute-start | bytes 589832 | tf_op jit(solution)/shard_map/ppermute | solution.py:186
  26.2 1.8 %collective-permute-start.12 = (f32[384,128]{1,0:T(8,128)S(1)}, f32[384,128]{1,0:T(8,128)S(1)}, u32[]{:S(2)}, u32[]{:S(2)}) collective-permute-start(f32[384,128]{1,0:T(8,128)S(1)} %collective-permute-done.7.refs_6_), channel_id=1, source_target_pairs={{0,1},{1,0},{2,3},{3,2},{4,5},{5,4},{6,7},{7,6},{8,9},{9,8},{10,11... | collective-permute-start | bytes 589832 | tf_op jit(solution)/shard_map/ppermute | solution.py:186
  26.6 1.6 %collective-permute-start.11 = (f32[384,128]{1,0:T(8,128)S(1)}, f32[384,128]{1,0:T(8,128)S(1)}, u32[]{:S(2)}, u32[]{:S(2)}) collective-permute-start(f32[384,128]{1,0:T(8,128)S(1)} %collective-permute-done.6.refs_5_), channel_id=1, source_target_pairs={{0,1},{1,0},{2,3},{3,2},{4,5},{5,4},{6,7},{7,6},{8,9},{9,8},{10,11... | collective-permute-start | bytes 589832 | tf_op jit(solution)/shard_map/ppermute | solution.py:186
  29.1 7.0 %collective-permute-start.19 = (f32[136,128]{1,0:T(8,128)S(1)}, f32[136,128]{1,0:T(8,128)S(1)}, u32[]{:S(2)}, u32[]{:S(2)}) collective-permute-start(f32[136,128]{1,0:T(8,128)S(1)} %get-tuple-element.15.refs_0_), channel_id=1, source_target_pairs={{0,24},{1,25},{2,26},{3,27},{4,28},{5,29},{6,30},{7,31},{8,16},{9,... | collective-permute-start | bytes 208904 | tf_op jit(solution)/shard_map/ppermute | solution.py:186
  30.6 7.5 %collective-permute-start.18 = (f32[136,128]{1,0:T(8,128)S(1)}, f32[136,128]{1,0:T(8,128)S(1)}, u32[]{:S(2)}, u32[]{:S(2)}) collective-permute-start(f32[136,128]{1,0:T(8,128)S(1)} %get-tuple-element.15.refs_0_), channel_id=1, source_target_pairs={{0,16},{1,17},{2,18},{3,19},{4,20},{5,21},{6,22},{7,23},{8,24},{9,... | collective-permute-start | bytes 208904 | tf_op jit(solution)/shard_map/ppermute | solution.py:186
  30.6 7.5 %collective-permute-start.17 = (f32[136,128]{1,0:T(8,128)S(1)}, f32[136,128]{1,0:T(8,128)S(1)}, u32[]{:S(2)}, u32[]{:S(2)}) collective-permute-start(f32[136,128]{1,0:T(8,128)S(1)} %get-tuple-element.15.refs_0_), channel_id=1, source_target_pairs={{0,8},{1,9},{2,10},{3,11},{4,12},{5,13},{6,14},{7,15},{8,0},{9,1},... | collective-permute-start | bytes 208904 | tf_op jit(solution)/shard_map/ppermute | solution.py:186
  38.2 18.6 %collective-permute-start.22 = (f32[408,128]{1,0:T(8,128)S(1)}, f32[408,128]{1,0:T(8,128)S(1)}, u32[]{:S(2)}, u32[]{:S(2)}) collective-permute-start(f32[408,128]{1,0:T(8,128)S(1)} %shard_map.70.refs_5_), channel_id=1, source_target_pairs={{0,6},{1,7},{2,4},{3,5},{4,2},{5,3},{6,0},{7,1},{8,14},{9,15},{10,... | collective-permute-start | bytes 626696 | tf_op jit(solution)/shard_map/ppermute | solution.py:186
  39.8 17.5 %collective-permute-start.21 = (f32[408,128]{1,0:T(8,128)S(1)}, f32[408,128]{1,0:T(8,128)S(1)}, u32[]{:S(2)}, u32[]{:S(2)}) collective-permute-start(f32[408,128]{1,0:T(8,128)S(1)} %shard_map.70.refs_5_), channel_id=1, source_target_pairs={{0,4},{1,5},{2,6},{3,7},{4,0},{5,1},{6,2},{7,3},{8,12},{9,13},{10,... | collective-permute-start | bytes 626696 | tf_op jit(solution)/shard_map/ppermute | solution.py:186
  41.2 16.1 %collective-permute-start.20 = (f32[408,128]{1,0:T(8,128)S(1)}, f32[408,128]{1,0:T(8,128)S(1)}, u32[]{:S(2)}, u32[]{:S(2)}) collective-permute-start(f32[408,128]{1,0:T(8,128)S(1)} %shard_map.70.refs_5_), channel_id=1, source_target_pairs={{0,2},{1,3},{2,0},{3,1},{4,6},{5,7},{6,4},{7,5},{8,10},{9,11},{10,... | collective-permute-start | bytes 626696 | tf_op jit(solution)/shard_map/ppermute | solution.py:186
  41.7 10.6 %collective-permute-start.16 = (f32[136,128]{1,0:T(8,128)S(1)}, f32[136,128]{1,0:T(8,128)S(1)}, u32[]{:S(2)}, u32[]{:S(2)}) collective-permute-start(f32[136,128]{1,0:T(8,128)S(1)} %get-tuple-element.15.refs_0_), channel_id=1, source_target_pairs={{0,6},{1,7},{2,4},{3,5},{4,2},{5,3},{6,0},{7,1},{8,14},{9,15},{10,... | collective-permute-start | bytes 208904 | tf_op jit(solution)/shard_map/ppermute | solution.py:186
  43.3 10.6 %collective-permute-start.15 = (f32[136,128]{1,0:T(8,128)S(1)}, f32[136,128]{1,0:T(8,128)S(1)}, u32[]{:S(2)}, u32[]{:S(2)}) collective-permute-start(f32[136,128]{1,0:T(8,128)S(1)} %get-tuple-element.15.refs_0_), channel_id=1, source_target_pairs={{0,4},{1,5},{2,6},{3,7},{4,0},{5,1},{6,2},{7,3},{8,12},{9,13},{10,... | collective-permute-start | bytes 208904 | tf_op jit(solution)/shard_map/ppermute | solution.py:186
  52.3 4.3 %collective-permute-start.14 = (f32[136,128]{1,0:T(8,128)S(1)}, f32[136,128]{1,0:T(8,128)S(1)}, u32[]{:S(2)}, u32[]{:S(2)}) collective-permute-start(f32[136,128]{1,0:T(8,128)S(1)} %get-tuple-element.15.refs_0_), channel_id=1, source_target_pairs={{0,2},{1,3},{2,0},{3,1},{4,6},{5,7},{6,4},{7,5},{8,10},{9,11},{10,... | collective-permute-start | bytes 208904 | tf_op jit(solution)/shard_map/ppermute | solution.py:186
  53.8 12.2 %collective-permute-start.24 = (f32[408,128]{1,0:T(8,128)S(1)}, f32[408,128]{1,0:T(8,128)S(1)}, u32[]{:S(2)}, u32[]{:S(2)}) collective-permute-start(f32[408,128]{1,0:T(8,128)S(1)} %shard_map.70.refs_5_), channel_id=1, source_target_pairs={{0,1},{1,0},{2,3},{3,2},{4,5},{5,4},{6,7},{7,6},{8,9},{9,8},{10,11... | collective-permute-start | bytes 626696 | tf_op jit(solution)/shard_map/ppermute | solution.py:186
  56.7 9.4 %collective-permute-start.23 = (f32[544,128]{1,0:T(8,128)S(1)}, f32[544,128]{1,0:T(8,128)S(1)}, u32[]{:S(2)}, u32[]{:S(2)}) collective-permute-start(f32[544,128]{1,0:T(8,128)S(1)} %shard_map.69.refs_4_), channel_id=1, source_target_pairs={{0,1},{1,0},{2,3},{3,2},{4,5},{5,4},{6,7},{7,6},{8,9},{9,8},{10,11... | collective-permute-start | bytes 835592 | tf_op jit(solution)/shard_map/ppermute | solution.py:186
  56.8 9.3 %collective-permute-start.27 = (f32[408,128]{1,0:T(8,128)S(1)}, f32[408,128]{1,0:T(8,128)S(1)}, u32[]{:S(2)}, u32[]{:S(2)}) collective-permute-start(f32[408,128]{1,0:T(8,128)S(1)} %collective-permute-done.22.refs_8_), channel_id=1, source_target_pairs={{0,1},{1,0},{2,3},{3,2},{4,5},{5,4},{6,7},{7,6},{8,9},{9,8},{10,11... | collective-permute-start | bytes 626696 | tf_op jit(solution)/shard_map/ppermute | solution.py:186
  57.3 8.8 %collective-permute-start.26 = (f32[408,128]{1,0:T(8,128)S(1)}, f32[408,128]{1,0:T(8,128)S(1)}, u32[]{:S(2)}, u32[]{:S(2)}) collective-permute-start(f32[408,128]{1,0:T(8,128)S(1)} %collective-permute-done.21.refs_7_), channel_id=1, source_target_pairs={{0,1},{1,0},{2,3},{3,2},{4,5},{5,4},{6,7},{7,6},{8,9},{9,8},{10,11... | collective-permute-start | bytes 626696 | tf_op jit(solution)/shard_map/ppermute | solution.py:186
  57.3 8.7 %collective-permute-start.25 = (f32[408,128]{1,0:T(8,128)S(1)}, f32[408,128]{1,0:T(8,128)S(1)}, u32[]{:S(2)}, u32[]{:S(2)}) collective-permute-start(f32[408,128]{1,0:T(8,128)S(1)} %collective-permute-done.20.refs_6_), channel_id=1, source_target_pairs={{0,1},{1,0},{2,3},{3,2},{4,5},{5,4},{6,7},{7,6},{8,9},{9,8},{10,11... | collective-permute-start | bytes 626696 | tf_op jit(solution)/shard_map/ppermute | solution.py:186
  75.0 5.8 %collective-permute-start.30 = (f32[64,128]{1,0:T(8,128)S(1)}, f32[64,128]{1,0:T(8,128)S(1)}, u32[]{:S(2)}, u32[]{:S(2)}) collective-permute-start(f32[64,128]{1,0:T(8,128)S(1)} %get-tuple-element.24.refs_0_), channel_id=1, source_target_pairs={{0,24},{1,25},{2,26},{3,27},{4,28},{5,29},{6,30},{7,31},{8,16},{9,... | collective-permute-start | bytes 98312 | tf_op jit(solution)/shard_map/ppermute | solution.py:186
  76.5 5.1 %collective-permute-start.29 = (f32[64,128]{1,0:T(8,128)S(1)}, f32[64,128]{1,0:T(8,128)S(1)}, u32[]{:S(2)}, u32[]{:S(2)}) collective-permute-start(f32[64,128]{1,0:T(8,128)S(1)} %get-tuple-element.24.refs_0_), channel_id=1, source_target_pairs={{0,16},{1,17},{2,18},{3,19},{4,20},{5,21},{6,22},{7,23},{8,24},{9,... | collective-permute-start | bytes 98312 | tf_op jit(solution)/shard_map/ppermute | solution.py:186
  76.5 5.3 %collective-permute-start.28 = (f32[64,128]{1,0:T(8,128)S(1)}, f32[64,128]{1,0:T(8,128)S(1)}, u32[]{:S(2)}, u32[]{:S(2)}) collective-permute-start(f32[64,128]{1,0:T(8,128)S(1)} %get-tuple-element.24.refs_0_), channel_id=1, source_target_pairs={{0,8},{1,9},{2,10},{3,11},{4,12},{5,13},{6,14},{7,15},{8,0},{9,1},... | collective-permute-start | bytes 98312 | tf_op jit(solution)/shard_map/ppermute | solution.py:186
  81.8 7.3 %collective-permute-start.33 = (f32[256,128]{1,0:T(8,128)S(1)}, f32[256,128]{1,0:T(8,128)S(1)}, u32[]{:S(2)}, u32[]{:S(2)}) collective-permute-start(f32[256,128]{1,0:T(8,128)S(1)} %shard_map.71.refs_10_), channel_id=1, source_target_pairs={{0,6},{1,7},{2,4},{3,5},{4,2},{5,3},{6,0},{7,1},{8,14},{9,15},{10,... | collective-permute-start | bytes 393224 | tf_op jit(solution)/shard_map/ppermute | solution.py:186
  83.4 7.3 %collective-permute-start.32 = (f32[256,128]{1,0:T(8,128)S(1)}, f32[256,128]{1,0:T(8,128)S(1)}, u32[]{:S(2)}, u32[]{:S(2)}) collective-permute-start(f32[256,128]{1,0:T(8,128)S(1)} %shard_map.71.refs_10_), channel_id=1, source_target_pairs={{0,4},{1,5},{2,6},{3,7},{4,0},{5,1},{6,2},{7,3},{8,12},{9,13},{10,... | collective-permute-start | bytes 393224 | tf_op jit(solution)/shard_map/ppermute | solution.py:186
  84.9 5.9 %collective-permute-start.31 = (f32[256,128]{1,0:T(8,128)S(1)}, f32[256,128]{1,0:T(8,128)S(1)}, u32[]{:S(2)}, u32[]{:S(2)}) collective-permute-start(f32[256,128]{1,0:T(8,128)S(1)} %shard_map.71.refs_10_), channel_id=1, source_target_pairs={{0,2},{1,3},{2,0},{3,1},{4,6},{5,7},{6,4},{7,5},{8,10},{9,11},{10,... | collective-permute-start | bytes 393224 | tf_op jit(solution)/shard_map/ppermute | solution.py:186
  85.4 10.8 %collective-permute-start.34 = (f32[256,128]{1,0:T(8,128)S(1)}, f32[256,128]{1,0:T(8,128)S(1)}, u32[]{:S(2)}, u32[]{:S(2)}) collective-permute-start(f32[256,128]{1,0:T(8,128)S(1)} %shard_map.71.refs_10_), channel_id=1, source_target_pairs={{0,1},{1,0},{2,3},{3,2},{4,5},{5,4},{6,7},{7,6},{8,9},{9,8},{10,11... | collective-permute-start | bytes 393224 | tf_op jit(solution)/shard_map/ppermute | solution.py:186
  89.2 7.1 %collective-permute-start.37 = (f32[256,128]{1,0:T(8,128)S(1)}, f32[256,128]{1,0:T(8,128)S(1)}, u32[]{:S(2)}, u32[]{:S(2)}) collective-permute-start(f32[256,128]{1,0:T(8,128)S(1)} %collective-permute-done.33.refs_13_), channel_id=1, source_target_pairs={{0,1},{1,0},{2,3},{3,2},{4,5},{5,4},{6,7},{7,6},{8,9},{9,8},{10,11... | collective-permute-start | bytes 393224 | tf_op jit(solution)/shard_map/ppermute | solution.py:186
  90.7 5.5 %collective-permute-start.36 = (f32[256,128]{1,0:T(8,128)S(1)}, f32[256,128]{1,0:T(8,128)S(1)}, u32[]{:S(2)}, u32[]{:S(2)}) collective-permute-start(f32[256,128]{1,0:T(8,128)S(1)} %collective-permute-done.32.refs_12_), channel_id=1, source_target_pairs={{0,1},{1,0},{2,3},{3,2},{4,5},{5,4},{6,7},{7,6},{8,9},{9,8},{10,11... | collective-permute-start | bytes 393224 | tf_op jit(solution)/shard_map/ppermute | solution.py:186
  90.7 5.5 %collective-permute-start.35 = (f32[256,128]{1,0:T(8,128)S(1)}, f32[256,128]{1,0:T(8,128)S(1)}, u32[]{:S(2)}, u32[]{:S(2)}) collective-permute-start(f32[256,128]{1,0:T(8,128)S(1)} %collective-permute-done.31.refs_11_), channel_id=1, source_target_pairs={{0,1},{1,0},{2,3},{3,2},{4,5},{5,4},{6,7},{7,6},{8,9},{9,8},{10,11... | collective-permute-start | bytes 393224 | tf_op jit(solution)/shard_map/ppermute | solution.py:186

commit v7 on v6

--- a/solution.py
+++ b/solution.py
@@ -11,6 +11,7 @@
 BF16 = jnp.bfloat16
 highest = lax.Precision.HIGHEST
 CHUNK = 2048
+EARLY = ((1, 2, 3), (1, 2, 3), (1, 2, 3))
 
 
 def params(mebibytes=56):
@@ -97,7 +98,7 @@
     ]
 
 
-def inverse_factor(matrix, panel=32):
+def inverse_factor(matrix, panel=128):
     n, step = matrix.shape[0], 8
     lane = lax.broadcasted_iota(jnp.int32, (8, n), 1)
     sub = lax.broadcasted_iota(jnp.int32, (8, n), 0)
@@ -152,12 +153,12 @@
 
 def layout_of(rings, early):
     column = [8 * z for z in range(rings)]
-    if early:
-        first = [[0, 2, 4, 6], column[1:]]
-        column = column[1:]
+    if len(early) == 3:
+        first, sent = [[0, 2, 4, 6], column[1:]], {k: column[1:] for k in early}
     else:
-        first = [column]
-    chips = first + [[d ^ m for d in column] for m in (2, 4, 6)]
+        first = [column] + [[2 * k] for k in early]
+        sent = {k: column[1:] if k in early else column for k in (1, 2, 3)}
+    chips = first + [[d ^ (2 * k) for d in sent[k]] for k in (1, 2, 3)]
     return chips + [[d ^ 1 for d in piece] for piece in chips]
 
 
@@ -185,15 +186,18 @@
     def swap(x, m):
         return lax.ppermute(x, "blk", [(i, i ^ m) for i in range(n)])
 
-    column = [swap(block, 8 * z) for z in range(1, n // 8)]
-    if early:
-        near = packed([block] + [swap(block, 2 * k) for k in (1, 2, 3)])
-        column = packed(column)
-        chips = [near, column]
+    far = [swap(block, 8 * z) for z in range(1, n // 8)]
+    near = [swap(block, 2 * k) for k in early]
+    if len(early) == 3:
+        rest = packed(far)
+        chips = [packed([block] + near), rest]
+        sent = {k: rest for k in early}
     else:
-        column = packed([block] + column)
-        chips = [column]
-    chips += [swap(column, 2 * k) for k in (1, 2, 3)]
+        full = packed([block] + far)
+        rest = packed(far) if early else None
+        chips = [full] + near
+        sent = {k: rest if k in early else full for k in (1, 2, 3)}
+    chips += [swap(sent[k], 2 * k) for k in (1, 2, 3)]
     return chips + [swap(x, 1) for x in chips]
 
 
@@ -213,7 +217,7 @@
         y_ref[at, :width] = piece[base : base + rows, :]
         y_ref[at, width:] = piece[base + rows : base + 2 * rows, :]
 
-    assemble(me_ref[0], pieces, rings, True, place)
+    assemble(me_ref[0], pieces, rings, EARLY[0], place)
     result = mm3(kernel_ref[...], y_ref[...])
     ky_ref[:rows, :] = result[:, :width]
     ky_ref[rows : 2 * rows, :] = result[:, width:]
@@ -307,7 +311,7 @@
         table[pl.ds(device, 1), :] = piece[base + 2 * rows : base + 2 * rows + 1, :]
 
     table[...] = jnp.zeros_like(table)
-    assemble(me_ref[0], pieces, rings, True, place)
+    assemble(me_ref[0], pieces, rings, EARLY[1], place)
     diag_ref[...] = table[...].T
     first_step(
         y_ref, ky_ref, factor_ref, diag_ref.at[:rows, :], y2_ref, kx_ref, small_ref, norm_ref
@@ -315,17 +319,21 @@
     kw_ref[...] = mm3(kernel_ref[...], y2_ref[:, width:])
 
 
-def second_factor(y2_ref, small_ref, tie_ref, factor_ref, known_ref, square_ref):
+def second_gram(y2_ref, gram_ref):
     total, double = y2_ref.shape
     width = double // 2
 
     def add(at, acc):
         return acc + mm3(y2_ref[at, width:], y2_ref[at, :], 0, 0)
 
-    gram = sweep(total, add, jnp.zeros((width, double), F32))
-    tie = gram[:, :width]
+    gram_ref[...] = sweep(total, add, jnp.zeros((width, double), F32))
+
+
+def second_factor(gram_ref, small_ref, tie_ref, factor_ref, known_ref, square_ref):
+    width = small_ref.shape[0]
+    tie = gram_ref[:, :width]
     values = small_ref[...]
-    factor = inverse_factor(gram[:, width:] - mm(tie, tie, 1, 1))
+    factor = inverse_factor(gram_ref[:, width:] - mm(tie, tie, 1, 1))
     tie_ref[...] = tie
     factor_ref[...] = factor
     known_ref[...] = mm(factor, mm(tie, values))
@@ -375,7 +383,7 @@
         at = pl.ds(pl.multiple_of(device * rows, rows), rows)
         image_ref[at, width:] = piece[slot * rows : (slot + 1) * rows, :]
 
-    assemble(me, pieces, rings, False, place)
+    assemble(me, pieces, rings, EARLY[2], place)
     image_ref[:, :width] = kx_ref[...]
     mine = pl.ds(pl.multiple_of(me * rows, rows), rows)
     second_step(
@@ -431,6 +439,15 @@
 
 def second_metric(y2, values, mebibytes):
     width = y2.shape[1] // 2
+    gram = pl.pallas_call(
+        second_gram,
+        out_shape=shape(width, 2 * width),
+        in_specs=[VMEM],
+        out_specs=VMEM,
+        compiler_params=params(mebibytes),
+        cost_estimate=cost(1),
+        name="second_gram",
+    )(y2)
     return pl.pallas_call(
         second_factor,
         out_shape=(shape(width, width),) * 4,
@@ -439,7 +456,7 @@
         compiler_params=params(mebibytes),
         cost_estimate=cost(9),
         name="second_factor",
-    )(y2, values)
+    )(gram, values)
 
 
 def cubed(n, kernel, ritz, search, diag):
@@ -450,7 +467,7 @@
     me = lax.axis_index("blk").astype(jnp.int32).reshape(1)
     along = diag.reshape(1, rows)
     own = lax.pad(ritz, 0.0, ((0, rows, 0), (0, 0, 0))) + lax.pad(search, 0.0, ((rows, 0, 0), (0, 0, 0)))
-    sent = gather(own, n, True)
+    sent = gather(own, n, EARLY[0])
     y, ky_own = pl.pallas_call(
         lambda *refs: first_product(rings, rows, *refs),
         out_shape=(shape(total, 2 * width), shape(2 * rows + 8, width)),
@@ -459,7 +476,7 @@
         compiler_params=params(16),
         name="first_product",
     )(me, kernel, along, *sent)
-    images = gather(ky_own, n, True)
+    images = gather(ky_own, n, EARLY[1])
     factor = metric_factor(y, 12)
     y2, kx, values, norm1, kw_own = pl.pallas_call(
         lambda *refs: with_product(rings, rows, *refs),
@@ -480,7 +497,7 @@
         compiler_params=params(24),
         name="first_step",
     )(me, kernel, y, factor, *images)
-    images2 = gather(kw_own, n, False)
+    images2 = gather(kw_own, n, EARLY[2])
     known = second_metric(y2, values, 12)
     return pl.pallas_call(
         lambda *refs: last_step(rings, rows, *refs),

time: 105 us -> 103 us (0.981)
  waiting for transfers between devices: 33.3 us -> 28.3 us
  starting transfers between devices: 38.1 us -> 41.7 us
    ppermute x38 -> x42, waiting for transfers between devices: 33.3 us -> 28.3 us  [swap(): return lax.ppermute(x, 'blk', [(i, i ^ m) for i in range(n)])]
    ppermute x38 -> x42, starting transfers between devices: 38.1 us -> 41.7 us  [swap(): return lax.ppermute(x, 'blk', [(i, i ^ m) for i in range(n)])]
    pallas_call x1, Pallas kernels: 4.99 us -> 3.94 us  [second_metric(): pl.pallas_call(second_factor, out_shape=(shape(width, width),) * 4, in_sp...]
  transfers between devices with their start and end apart: 38 -> 42, of which waited for: 16 -> 14; matrix products, arithmetic and copies ran while one was open for 0% -> 0% of each run, Pallas kernels for 13% -> 13%
where the time goes in v7:
time: 103 us; the launch traced here: 102 us
  starting transfers between devices  41.7 us (40%)
  Pallas kernels  30.5 us (30%)
  waiting for transfers between devices  28.3 us (27%)
    ppermute x42, starting transfers between devices, swap(): return lax.ppermute(x, 'blk', [(i, i ^ m) for i in range(n)])  41.7 us
    ppermute x42, waiting for transfers between devices, swap(): return lax.ppermute(x, 'blk', [(i, i ^ m) for i in range(n)])  28.3 us
    pallas_call x1, Pallas kernels, cubed(): pl.pallas_call(lambda *refs: with_product(rings, rows, *refs), out_shape=...  8.78 us
    pallas_call x1, Pallas kernels, metric_factor(): pl.pallas_call(metric_kernel, out_shape=shape(double, double), in_specs=[...  8.26 us
    pallas_call x1, Pallas kernels, cubed(): pl.pallas_call(lambda *refs: last_step(rings, rows, *refs), out_shape=(sh...  7.97 us
    pallas_call x1, Pallas kernels, second_metric(): pl.pallas_call(second_factor, out_shape=(shape(width, width),) * 4, in_sp...  3.94 us
  transfers between devices with their start and end apart: 42, of which 14 were waited for; matrix products, arithmetic and copies ran while one was open for 0% of the time, Pallas kernels for 13%

profile of v7, /device:TPU:0, one launch (start us, length us, event | category | flops | bytes accessed | tf_op | source)
XLA Modules:
  0.0 102.5 jit_solution(510344913203434717)
XLA Ops:
  0.6 0.8 pad_add_fusion.refs_0_
  1.5 5.1 %collective-permute-start.5 = (f32[128,128]{1,0:T(8,128)S(1)}, f32[128,128]{1,0:T(8,128)S(1)}, u32[]{:S(2)}, u32[]{:S(2)}) collective-permute-start(f32[128,128]{1,0:T(8,128)S(1)} %pad_add_fusion.refs_0_), channel_id=1, source_target_pairs={{0,24},{1,25},{2,26},{3,27},{4,28},{5,29},{6,30},{7,31},{8,16},{9,... | collective-permute-start | bytes 196616 | tf_op jit(solution)/shard_map/ppermute | solution.py:187
  6.6 0.6 collective-permute-start.3
  7.3 2.6 %collective-permute-start.2 = (f32[128,128]{1,0:T(8,128)S(1)}, f32[128,128]{1,0:T(8,128)S(1)}, u32[]{:S(2)}, u32[]{:S(2)}) collective-permute-start(f32[128,128]{1,0:T(8,128)S(1)} %pad_add_fusion.refs_0_), channel_id=1, source_target_pairs={{0,6},{1,7},{2,4},{3,5},{4,2},{5,3},{6,0},{7,1},{8,14},{9,15},{10,... | collective-permute-start | bytes 196616 | tf_op jit(solution)/shard_map/ppermute | solution.py:187
  9.8 2.4 %collective-permute-done.4.refs_1_ = f32[128,128]{1,0:T(8,128)S(1)} collective-permute-done((f32[128,128]{1,0:T(8,128)S(1)}, f32[128,128]{1,0:T(8,128)S(1)}, u32[]{:S(2)}, u32[]{:S(2)}) %collective-permute-start.4) | collective-permute-done | bytes 65568 | tf_op jit(solution)/shard_map/ppermute | solution.py:187
  12.2 2.5 %collective-permute-start.8 = (f32[384,128]{1,0:T(8,128)S(1)}, f32[384,128]{1,0:T(8,128)S(1)}, u32[]{:S(2)}, u32[]{:S(2)}) collective-permute-start(f32[384,128]{1,0:T(8,128)S(1)} %shard_map.68.refs_4_), channel_id=1, source_target_pairs={{0,6},{1,7},{2,4},{3,5},{4,2},{5,3},{6,0},{7,1},{8,14},{9,15},{10,... | collective-permute-start | bytes 589832 | tf_op jit(solution)/shard_map/ppermute | solution.py:187
  14.7 0.5 collective-permute-start.7
  15.3 0.5 collective-permute-start.6
  15.8 1.5 %collective-permute-start.1 = (f32[128,128]{1,0:T(8,128)S(1)}, f32[128,128]{1,0:T(8,128)S(1)}, u32[]{:S(2)}, u32[]{:S(2)}) collective-permute-start(f32[128,128]{1,0:T(8,128)S(1)} %pad_add_fusion.refs_0_), channel_id=1, source_target_pairs={{0,4},{1,5},{2,6},{3,7},{4,0},{5,1},{6,2},{7,3},{8,12},{9,13},{10,... | collective-permute-start | bytes 196616 | tf_op jit(solution)/shard_map/ppermute | solution.py:187
  17.3 1.5 %collective-permute-start = (f32[128,128]{1,0:T(8,128)S(1)}, f32[128,128]{1,0:T(8,128)S(1)}, u32[]{:S(2)}, u32[]{:S(2)}) collective-permute-start(f32[128,128]{1,0:T(8,128)S(1)} %pad_add_fusion.refs_0_), channel_id=1, source_target_pairs={{0,2},{1,3},{2,0},{3,1},{4,6},{5,7},{6,4},{7,5},{8,10},{9,11},{10,... | collective-permute-start | bytes 196616 | tf_op jit(solution)/shard_map/ppermute | solution.py:187
  18.8 6.5 %collective-permute-done.1.refs_2_ = f32[128,128]{1,0:T(8,128)S(1)} collective-permute-done((f32[128,128]{1,0:T(8,128)S(1)}, f32[128,128]{1,0:T(8,128)S(1)}, u32[]{:S(2)}, u32[]{:S(2)}) %collective-permute-start.1) | collective-permute-done | bytes 65568 | tf_op jit(solution)/shard_map/ppermute | solution.py:187
  25.6 0.5 collective-permute-start.10
  26.2 0.4 collective-permute-start.12
  26.9 0.5 collective-permute-done.10.refs_9_
  27.7 0.3 collective-permute-done.12.refs_11_
  28.0 0.3 collective-permute-done.11.refs_10_
  28.3 0.8 first_product.1
  29.1 1.6 %collective-permute-start.19 = (f32[136,128]{1,0:T(8,128)S(1)}, f32[136,128]{1,0:T(8,128)S(1)}, u32[]{:S(2)}, u32[]{:S(2)}) collective-permute-start(f32[136,128]{1,0:T(8,128)S(1)} %get-tuple-element.15.refs_0_), channel_id=1, source_target_pairs={{0,24},{1,25},{2,26},{3,27},{4,28},{5,29},{6,30},{7,31},{8,16},{9,... | collective-permute-start | bytes 208904 | tf_op jit(solution)/shard_map/ppermute | solution.py:187
  30.6 2.9 %collective-permute-start.17 = (f32[136,128]{1,0:T(8,128)S(1)}, f32[136,128]{1,0:T(8,128)S(1)}, u32[]{:S(2)}, u32[]{:S(2)}) collective-permute-start(f32[136,128]{1,0:T(8,128)S(1)} %get-tuple-element.15.refs_0_), channel_id=1, source_target_pairs={{0,8},{1,9},{2,10},{3,11},{4,12},{5,13},{6,14},{7,15},{8,0},{9,1},... | collective-permute-start | bytes 208904 | tf_op jit(solution)/shard_map/ppermute | solution.py:187
  33.5 2.5 %collective-permute-done.19.refs_2_ = f32[136,128]{1,0:T(8,128)S(1)} collective-permute-done((f32[136,128]{1,0:T(8,128)S(1)}, f32[136,128]{1,0:T(8,128)S(1)}, u32[]{:S(2)}, u32[]{:S(2)}) %collective-permute-start.19) | collective-permute-done | bytes 69664 | tf_op jit(solution)/shard_map/ppermute | solution.py:187
  36.0 2.1 %collective-permute-done.18.refs_1_ = f32[136,128]{1,0:T(8,128)S(1)} collective-permute-done((f32[136,128]{1,0:T(8,128)S(1)}, f32[136,128]{1,0:T(8,128)S(1)}, u32[]{:S(2)}, u32[]{:S(2)}) %collective-permute-start.18) | collective-permute-done | bytes 69664 | tf_op jit(solution)/shard_map/ppermute | solution.py:187
  38.2 1.6 %collective-permute-start.22 = (f32[408,128]{1,0:T(8,128)S(1)}, f32[408,128]{1,0:T(8,128)S(1)}, u32[]{:S(2)}, u32[]{:S(2)}) collective-permute-start(f32[408,128]{1,0:T(8,128)S(1)} %shard_map.70.refs_5_), channel_id=1, source_target_pairs={{0,6},{1,7},{2,4},{3,5},{4,2},{5,3},{6,0},{7,1},{8,14},{9,15},{10,... | collective-permute-start | bytes 626696 | tf_op jit(solution)/shard_map/ppermute | solution.py:187
  39.8 1.4 %collective-permute-start.21 = (f32[408,128]{1,0:T(8,128)S(1)}, f32[408,128]{1,0:T(8,128)S(1)}, u32[]{:S(2)}, u32[]{:S(2)}) collective-permute-start(f32[408,128]{1,0:T(8,128)S(1)} %shard_map.70.refs_5_), channel_id=1, source_target_pairs={{0,4},{1,5},{2,6},{3,7},{4,0},{5,1},{6,2},{7,3},{8,12},{9,13},{10,... | collective-permute-start | bytes 626696 | tf_op jit(solution)/shard_map/ppermute | solution.py:187
  41.2 0.5 collective-permute-start.20
  41.7 1.5 %collective-permute-start.16 = (f32[136,128]{1,0:T(8,128)S(1)}, f32[136,128]{1,0:T(8,128)S(1)}, u32[]{:S(2)}, u32[]{:S(2)}) collective-permute-start(f32[136,128]{1,0:T(8,128)S(1)} %get-tuple-element.15.refs_0_), channel_id=1, source_target_pairs={{0,6},{1,7},{2,4},{3,5},{4,2},{5,3},{6,0},{7,1},{8,14},{9,15},{10,... | collective-permute-start | bytes 208904 | tf_op jit(solution)/shard_map/ppermute | solution.py:187
  43.3 1.4 %collective-permute-start.15 = (f32[136,128]{1,0:T(8,128)S(1)}, f32[136,128]{1,0:T(8,128)S(1)}, u32[]{:S(2)}, u32[]{:S(2)}) collective-permute-start(f32[136,128]{1,0:T(8,128)S(1)} %get-tuple-element.15.refs_0_), channel_id=1, source_target_pairs={{0,4},{1,5},{2,6},{3,7},{4,0},{5,1},{6,2},{7,3},{8,12},{9,13},{10,... | collective-permute-start | bytes 208904 | tf_op jit(solution)/shard_map/ppermute | solution.py:187
  44.7 7.7 %collective-permute-done.16.refs_3_ = f32[136,128]{1,0:T(8,128)S(1)} collective-permute-done((f32[136,128]{1,0:T(8,128)S(1)}, f32[136,128]{1,0:T(8,128)S(1)}, u32[]{:S(2)}, u32[]{:S(2)}) %collective-permute-start.16) | collective-permute-done | bytes 69664 | tf_op jit(solution)/shard_map/ppermute | solution.py:187
  52.3 1.5 %collective-permute-start.14 = (f32[136,128]{1,0:T(8,128)S(1)}, f32[136,128]{1,0:T(8,128)S(1)}, u32[]{:S(2)}, u32[]{:S(2)}) collective-permute-start(f32[136,128]{1,0:T(8,128)S(1)} %get-tuple-element.15.refs_0_), channel_id=1, source_target_pairs={{0,2},{1,3},{2,0},{3,1},{4,6},{5,7},{6,4},{7,5},{8,10},{9,11},{10,... | collective-permute-start | bytes 208904 | tf_op jit(solution)/shard_map/ppermute | solution.py:187
  53.8 2.8 %collective-permute-done.14.refs_1_ = f32[136,128]{1,0:T(8,128)S(1)} collective-permute-done((f32[136,128]{1,0:T(8,128)S(1)}, f32[136,128]{1,0:T(8,128)S(1)}, u32[]{:S(2)}, u32[]{:S(2)}) %collective-permute-start.14) | collective-permute-done | bytes 69664 | tf_op jit(solution)/shard_map/ppermute | solution.py:187
  56.8 0.5 collective-permute-start.27
  57.3 0.4 collective-permute-start.25
  57.8 8.3 %metric.1.refs_3_ = f32[256,256]{1,0:T(8,128)S(1)} custom-call(f32[2048,256]{1,0:T(8,128)S(1)} %get-tuple-element.14.y_ref.refs_2_), custom_call_target="tpu_custom_call" | custom-call | flops 8999999488 | tf_op jit(solution)/shard_map/metric/pallas_call | solution.py:429
  66.1 8.8 %first_step.1 = (f32[2048,256]{1,0:T(8,128)S(1)}, f32[2048,128]{1,0:T(8,128)S(1)}, f32[128,128]{1,0:T(8,128)S(1)}, f32[1,128]{1,0:T(1,128)S(1)}, f32[64,128]{1,0:T(8,128)S(1)}) custom-call(s32[1]{0:T(128)} %bitcast.refs_0_, f32[64,2048]{1,0:T(8,128)S(1)} %bitcast.6, f32[2048,256]{1,0:T(8,128)S(1)} %get-tuple-element.14.y_ref.refs_2_, ...), custom_call_target="tpu_custom_call" | custom-call | tf_op jit(solution)/shard_map/first_step/pallas_call | solution.py:481
  74.9 1.5 %collective-permute-start.33 = (f32[64,128]{1,0:T(8,128)S(1)}, f32[64,128]{1,0:T(8,128)S(1)}, u32[]{:S(2)}, u32[]{:S(2)}) collective-permute-start(f32[64,128]{1,0:T(8,128)S(1)} %get-tuple-element.24.refs_0_), channel_id=1, source_target_pairs={{0,24},{1,25},{2,26},{3,27},{4,28},{5,29},{6,30},{7,31},{8,16},{9,... | collective-permute-start | bytes 98312 | tf_op jit(solution)/shard_map/ppermute | solution.py:187
  76.4 2.9 %collective-permute-start.31 = (f32[64,128]{1,0:T(8,128)S(1)}, f32[64,128]{1,0:T(8,128)S(1)}, u32[]{:S(2)}, u32[]{:S(2)}) collective-permute-start(f32[64,128]{1,0:T(8,128)S(1)} %get-tuple-element.24.refs_0_), channel_id=1, source_target_pairs={{0,8},{1,9},{2,10},{3,11},{4,12},{5,13},{6,14},{7,15},{8,0},{9,1},... | collective-permute-start | bytes 98312 | tf_op jit(solution)/shard_map/ppermute | solution.py:187
  79.3 1.5 %collective-permute-start.30 = (f32[64,128]{1,0:T(8,128)S(1)}, f32[64,128]{1,0:T(8,128)S(1)}, u32[]{:S(2)}, u32[]{:S(2)}) collective-permute-start(f32[64,128]{1,0:T(8,128)S(1)} %get-tuple-element.24.refs_0_), channel_id=1, source_target_pairs={{0,6},{1,7},{2,4},{3,5},{4,2},{5,3},{6,0},{7,1},{8,14},{9,15},{10,... | collective-permute-start | bytes 98312 | tf_op jit(solution)/shard_map/ppermute | solution.py:187
  80.9 1.4 %collective-permute-start.29 = (f32[64,128]{1,0:T(8,128)S(1)}, f32[64,128]{1,0:T(8,128)S(1)}, u32[]{:S(2)}, u32[]{:S(2)}) collective-permute-start(f32[64,128]{1,0:T(8,128)S(1)} %get-tuple-element.24.refs_0_), channel_id=1, source_target_pairs={{0,4},{1,5},{2,6},{3,7},{4,0},{5,1},{6,2},{7,3},{8,12},{9,13},{10,... | collective-permute-start | bytes 98312 | tf_op jit(solution)/shard_map/ppermute | solution.py:187
  82.3 0.5 collective-permute-start.28
  82.8 1.6 %collective-permute-start.36 = (f32[192,128]{1,0:T(8,128)S(1)}, f32[192,128]{1,0:T(8,128)S(1)}, u32[]{:S(2)}, u32[]{:S(2)}) collective-permute-start(f32[192,128]{1,0:T(8,128)S(1)} %shard_map.72.refs_11_), channel_id=1, source_target_pairs={{0,6},{1,7},{2,4},{3,5},{4,2},{5,3},{6,0},{7,1},{8,14},{9,15},{10,... | collective-permute-start | bytes 294920 | tf_op jit(solution)/shard_map/ppermute | solution.py:187
  84.4 1.4 %collective-permute-start.35 = (f32[192,128]{1,0:T(8,128)S(1)}, f32[192,128]{1,0:T(8,128)S(1)}, u32[]{:S(2)}, u32[]{:S(2)}) collective-permute-start(f32[192,128]{1,0:T(8,128)S(1)} %shard_map.72.refs_11_), channel_id=1, source_target_pairs={{0,4},{1,5},{2,6},{3,7},{4,0},{5,1},{6,2},{7,3},{8,12},{9,13},{10,... | collective-permute-start | bytes 294920 | tf_op jit(solution)/shard_map/ppermute | solution.py:187
  85.9 0.5 collective-permute-start.34
  86.4 0.7 second_gram.1.gram_ref
  87.2 0.5 collective-permute-start.37
  87.8 1.0 collective-permute-done.36.refs_14_
  88.7 1.0 collective-permute-done.35.refs_13_
  89.7 0.8 collective-permute-done.34.refs_12_
  90.5 3.9 %second_factor.1 = (f32[128,128]{1,0:T(8,128)S(1)}, f32[128,128]{1,0:T(8,128)S(1)}, f32[128,128]{1,0:T(8,128)S(1)}, f32[128,128]{1,0:T(8,128)S(1)}) custom-call(f32[128,256]{1,0:T(8,128)S(1)} %second_gram.1.gram_ref, f32[128,128]{1,0:T(8,128)S(1)} %get-tuple-element.19.small_ref.refs_5_), custom_call_target="tpu_custom_call" | custom-call | flops 8999999488 | tf_op jit(solution)/shard_map/second_factor/pallas_call | solution.py:451
  94.5 8.0 %last_step.1 = (f32[64,128]{1,0:T(8,128)}, f32[64,128]{1,0:T(8,128)}, f32[2,128]{1,0:T(2,128)}) custom-call(s32[1]{0:T(128)} %bitcast.refs_0_, f32[2048,256]{1,0:T(8,128)S(1)} %get-tuple-element.16.y2_ref.refs_1_, f32[2048,128]{1,0:T(8,128)S(1)} %get-tuple-element.17.refs_2_, f32[1,128]{1,0:T(1,128)S(1)} %get-tuple-element.18.refs_3_, f32[1,64]{1,0:T(1,128)S(1)} %bitcast.8, ...), custom_call_target="tpu_custom_call" | custom-call | tf_op jit(solution)/shard_map/last_step/pallas_call | solution.py:502
  (54 shorter events, 1.3 us)
Async XLA Ops:
  0.6 26.1 %copy-start.1 = (f32[64,1,2048]{2,1,0:T(1,128)S(1)}, f32[64,1,2048]{2,1,0:T(1,128)}, u32[]{:S(2)}) copy-start(f32[64,1,2048]{2,1,0:T(1,128)} %param.4) | copy-start | bytes 1572868
  1.5 26.8 %copy-start = (f32[64]{0:T(128)S(1)}, f32[64]{0:T(128)}, u32[]{:S(2)}) copy-start(f32[64]{0:T(128)} %param.7) | copy-start | bytes 772
  1.5 8.4 %collective-permute-start.5 = (f32[128,128]{1,0:T(8,128)S(1)}, f32[128,128]{1,0:T(8,128)S(1)}, u32[]{:S(2)}, u32[]{:S(2)}) collective-permute-start(f32[128,128]{1,0:T(8,128)S(1)} %pad_add_fusion.refs_0_), channel_id=1, source_target_pairs={{0,24},{1,25},{2,26},{3,27},{4,28},{5,29},{6,30},{7,31},{8,16},{9,... | collective-permute-start | bytes 196616 | tf_op jit(solution)/shard_map/ppermute | solution.py:187
  6.6 5.6 %collective-permute-start.4 = (f32[128,128]{1,0:T(8,128)S(1)}, f32[128,128]{1,0:T(8,128)S(1)}, u32[]{:S(2)}, u32[]{:S(2)}) collective-permute-start(f32[128,128]{1,0:T(8,128)S(1)} %pad_add_fusion.refs_0_), channel_id=1, source_target_pairs={{0,16},{1,17},{2,18},{3,19},{4,20},{5,21},{6,22},{7,23},{8,24},{9,... | collective-permute-start | bytes 196616 | tf_op jit(solution)/shard_map/ppermute | solution.py:187
  6.6 5.6 %collective-permute-start.3 = (f32[128,128]{1,0:T(8,128)S(1)}, f32[128,128]{1,0:T(8,128)S(1)}, u32[]{:S(2)}, u32[]{:S(2)}) collective-permute-start(f32[128,128]{1,0:T(8,128)S(1)} %pad_add_fusion.refs_0_), channel_id=1, source_target_pairs={{0,8},{1,9},{2,10},{3,11},{4,12},{5,13},{6,14},{7,15},{8,0},{9,1},... | collective-permute-start | bytes 196616 | tf_op jit(solution)/shard_map/ppermute | solution.py:187
  7.3 10.1 %collective-permute-start.2 = (f32[128,128]{1,0:T(8,128)S(1)}, f32[128,128]{1,0:T(8,128)S(1)}, u32[]{:S(2)}, u32[]{:S(2)}) collective-permute-start(f32[128,128]{1,0:T(8,128)S(1)} %pad_add_fusion.refs_0_), channel_id=1, source_target_pairs={{0,6},{1,7},{2,4},{3,5},{4,2},{5,3},{6,0},{7,1},{8,14},{9,15},{10,... | collective-permute-start | bytes 196616 | tf_op jit(solution)/shard_map/ppermute | solution.py:187
  12.2 13.9 %collective-permute-start.8 = (f32[384,128]{1,0:T(8,128)S(1)}, f32[384,128]{1,0:T(8,128)S(1)}, u32[]{:S(2)}, u32[]{:S(2)}) collective-permute-start(f32[384,128]{1,0:T(8,128)S(1)} %shard_map.68.refs_4_), channel_id=1, source_target_pairs={{0,6},{1,7},{2,4},{3,5},{4,2},{5,3},{6,0},{7,1},{8,14},{9,15},{10,... | collective-permute-start | bytes 589832 | tf_op jit(solution)/shard_map/ppermute | solution.py:187
  14.7 11.4 %collective-permute-start.7 = (f32[384,128]{1,0:T(8,128)S(1)}, f32[384,128]{1,0:T(8,128)S(1)}, u32[]{:S(2)}, u32[]{:S(2)}) collective-permute-start(f32[384,128]{1,0:T(8,128)S(1)} %shard_map.68.refs_4_), channel_id=1, source_target_pairs={{0,4},{1,5},{2,6},{3,7},{4,0},{5,1},{6,2},{7,3},{8,12},{9,13},{10,... | collective-permute-start | bytes 589832 | tf_op jit(solution)/shard_map/ppermute | solution.py:187
  15.3 11.4 %collective-permute-start.6 = (f32[384,128]{1,0:T(8,128)S(1)}, f32[384,128]{1,0:T(8,128)S(1)}, u32[]{:S(2)}, u32[]{:S(2)}) collective-permute-start(f32[384,128]{1,0:T(8,128)S(1)} %shard_map.68.refs_4_), channel_id=1, source_target_pairs={{0,2},{1,3},{2,0},{3,1},{4,6},{5,7},{6,4},{7,5},{8,10},{9,11},{10,... | collective-permute-start | bytes 589832 | tf_op jit(solution)/shard_map/ppermute | solution.py:187
  15.8 9.5 %collective-permute-start.1 = (f32[128,128]{1,0:T(8,128)S(1)}, f32[128,128]{1,0:T(8,128)S(1)}, u32[]{:S(2)}, u32[]{:S(2)}) collective-permute-start(f32[128,128]{1,0:T(8,128)S(1)} %pad_add_fusion.refs_0_), channel_id=1, source_target_pairs={{0,4},{1,5},{2,6},{3,7},{4,0},{5,1},{6,2},{7,3},{8,12},{9,13},{10,... | collective-permute-start | bytes 196616 | tf_op jit(solution)/shard_map/ppermute | solution.py:187
  17.3 8.2 %collective-permute-start = (f32[128,128]{1,0:T(8,128)S(1)}, f32[128,128]{1,0:T(8,128)S(1)}, u32[]{:S(2)}, u32[]{:S(2)}) collective-permute-start(f32[128,128]{1,0:T(8,128)S(1)} %pad_add_fusion.refs_0_), channel_id=1, source_target_pairs={{0,2},{1,3},{2,0},{3,1},{4,6},{5,7},{6,4},{7,5},{8,10},{9,11},{10,... | collective-permute-start | bytes 196616 | tf_op jit(solution)/shard_map/ppermute | solution.py:187
  25.5 1.9 %collective-permute-start.9 = (f32[512,128]{1,0:T(8,128)S(1)}, f32[512,128]{1,0:T(8,128)S(1)}, u32[]{:S(2)}, u32[]{:S(2)}) collective-permute-start(f32[512,128]{1,0:T(8,128)S(1)} %shard_map.67.refs_3_), channel_id=1, source_target_pairs={{0,1},{1,0},{2,3},{3,2},{4,5},{5,4},{6,7},{7,6},{8,9},{9,8},{10,11... | collective-permute-start | bytes 786440 | tf_op jit(solution)/shard_map/ppermute | solution.py:187
  25.6 1.8 %collective-permute-start.10 = (f32[384,128]{1,0:T(8,128)S(1)}, f32[384,128]{1,0:T(8,128)S(1)}, u32[]{:S(2)}, u32[]{:S(2)}) collective-permute-start(f32[384,128]{1,0:T(8,128)S(1)} %shard_map.68.refs_4_), channel_id=1, source_target_pairs={{0,1},{1,0},{2,3},{3,2},{4,5},{5,4},{6,7},{7,6},{8,9},{9,8},{10,11... | collective-permute-start | bytes 589832 | tf_op jit(solution)/shard_map/ppermute | solution.py:187
  26.1 1.6 %collective-permute-start.13 = (f32[384,128]{1,0:T(8,128)S(1)}, f32[384,128]{1,0:T(8,128)S(1)}, u32[]{:S(2)}, u32[]{:S(2)}) collective-permute-start(f32[384,128]{1,0:T(8,128)S(1)} %collective-permute-done.8.refs_7_), channel_id=1, source_target_pairs={{0,1},{1,0},{2,3},{3,2},{4,5},{5,4},{6,7},{7,6},{8,9},{9,8},{10,11... | collective-permute-start | bytes 589832 | tf_op jit(solution)/shard_map/ppermute | solution.py:187
  26.2 1.8 %collective-permute-start.12 = (f32[384,128]{1,0:T(8,128)S(1)}, f32[384,128]{1,0:T(8,128)S(1)}, u32[]{:S(2)}, u32[]{:S(2)}) collective-permute-start(f32[384,128]{1,0:T(8,128)S(1)} %collective-permute-done.7.refs_6_), channel_id=1, source_target_pairs={{0,1},{1,0},{2,3},{3,2},{4,5},{5,4},{6,7},{7,6},{8,9},{9,8},{10,11... | collective-permute-start | bytes 589832 | tf_op jit(solution)/shard_map/ppermute | solution.py:187
  26.6 1.6 %collective-permute-start.11 = (f32[384,128]{1,0:T(8,128)S(1)}, f32[384,128]{1,0:T(8,128)S(1)}, u32[]{:S(2)}, u32[]{:S(2)}) collective-permute-start(f32[384,128]{1,0:T(8,128)S(1)} %collective-permute-done.6.refs_5_), channel_id=1, source_target_pairs={{0,1},{1,0},{2,3},{3,2},{4,5},{5,4},{6,7},{7,6},{8,9},{9,8},{10,11... | collective-permute-start | bytes 589832 | tf_op jit(solution)/shard_map/ppermute | solution.py:187
  29.1 7.0 %collective-permute-start.19 = (f32[136,128]{1,0:T(8,128)S(1)}, f32[136,128]{1,0:T(8,128)S(1)}, u32[]{:S(2)}, u32[]{:S(2)}) collective-permute-start(f32[136,128]{1,0:T(8,128)S(1)} %get-tuple-element.15.refs_0_), channel_id=1, source_target_pairs={{0,24},{1,25},{2,26},{3,27},{4,28},{5,29},{6,30},{7,31},{8,16},{9,... | collective-permute-start | bytes 208904 | tf_op jit(solution)/shard_map/ppermute | solution.py:187
  30.6 7.5 %collective-permute-start.18 = (f32[136,128]{1,0:T(8,128)S(1)}, f32[136,128]{1,0:T(8,128)S(1)}, u32[]{:S(2)}, u32[]{:S(2)}) collective-permute-start(f32[136,128]{1,0:T(8,128)S(1)} %get-tuple-element.15.refs_0_), channel_id=1, source_target_pairs={{0,16},{1,17},{2,18},{3,19},{4,20},{5,21},{6,22},{7,23},{8,24},{9,... | collective-permute-start | bytes 208904 | tf_op jit(solution)/shard_map/ppermute | solution.py:187
  30.6 7.5 %collective-permute-start.17 = (f32[136,128]{1,0:T(8,128)S(1)}, f32[136,128]{1,0:T(8,128)S(1)}, u32[]{:S(2)}, u32[]{:S(2)}) collective-permute-start(f32[136,128]{1,0:T(8,128)S(1)} %get-tuple-element.15.refs_0_), channel_id=1, source_target_pairs={{0,8},{1,9},{2,10},{3,11},{4,12},{5,13},{6,14},{7,15},{8,0},{9,1},... | collective-permute-start | bytes 208904 | tf_op jit(solution)/shard_map/ppermute | solution.py:187
  38.2 18.6 %collective-permute-start.22 = (f32[408,128]{1,0:T(8,128)S(1)}, f32[408,128]{1,0:T(8,128)S(1)}, u32[]{:S(2)}, u32[]{:S(2)}) collective-permute-start(f32[408,128]{1,0:T(8,128)S(1)} %shard_map.70.refs_5_), channel_id=1, source_target_pairs={{0,6},{1,7},{2,4},{3,5},{4,2},{5,3},{6,0},{7,1},{8,14},{9,15},{10,... | collective-permute-start | bytes 626696 | tf_op jit(solution)/shard_map/ppermute | solution.py:187
  39.8 17.5 %collective-permute-start.21 = (f32[408,128]{1,0:T(8,128)S(1)}, f32[408,128]{1,0:T(8,128)S(1)}, u32[]{:S(2)}, u32[]{:S(2)}) collective-permute-start(f32[408,128]{1,0:T(8,128)S(1)} %shard_map.70.refs_5_), channel_id=1, source_target_pairs={{0,4},{1,5},{2,6},{3,7},{4,0},{5,1},{6,2},{7,3},{8,12},{9,13},{10,... | collective-permute-start | bytes 626696 | tf_op jit(solution)/shard_map/ppermute | solution.py:187
  41.2 16.1 %collective-permute-start.20 = (f32[408,128]{1,0:T(8,128)S(1)}, f32[408,128]{1,0:T(8,128)S(1)}, u32[]{:S(2)}, u32[]{:S(2)}) collective-permute-start(f32[408,128]{1,0:T(8,128)S(1)} %shard_map.70.refs_5_), channel_id=1, source_target_pairs={{0,2},{1,3},{2,0},{3,1},{4,6},{5,7},{6,4},{7,5},{8,10},{9,11},{10,... | collective-permute-start | bytes 626696 | tf_op jit(solution)/shard_map/ppermute | solution.py:187
  41.7 10.6 %collective-permute-start.16 = (f32[136,128]{1,0:T(8,128)S(1)}, f32[136,128]{1,0:T(8,128)S(1)}, u32[]{:S(2)}, u32[]{:S(2)}) collective-permute-start(f32[136,128]{1,0:T(8,128)S(1)} %get-tuple-element.15.refs_0_), channel_id=1, source_target_pairs={{0,6},{1,7},{2,4},{3,5},{4,2},{5,3},{6,0},{7,1},{8,14},{9,15},{10,... | collective-permute-start | bytes 208904 | tf_op jit(solution)/shard_map/ppermute | solution.py:187
  43.3 10.6 %collective-permute-start.15 = (f32[136,128]{1,0:T(8,128)S(1)}, f32[136,128]{1,0:T(8,128)S(1)}, u32[]{:S(2)}, u32[]{:S(2)}) collective-permute-start(f32[136,128]{1,0:T(8,128)S(1)} %get-tuple-element.15.refs_0_), channel_id=1, source_target_pairs={{0,4},{1,5},{2,6},{3,7},{4,0},{5,1},{6,2},{7,3},{8,12},{9,13},{10,... | collective-permute-start | bytes 208904 | tf_op jit(solution)/shard_map/ppermute | solution.py:187
  52.3 4.3 %collective-permute-start.14 = (f32[136,128]{1,0:T(8,128)S(1)}, f32[136,128]{1,0:T(8,128)S(1)}, u32[]{:S(2)}, u32[]{:S(2)}) collective-permute-start(f32[136,128]{1,0:T(8,128)S(1)} %get-tuple-element.15.refs_0_), channel_id=1, source_target_pairs={{0,2},{1,3},{2,0},{3,1},{4,6},{5,7},{6,4},{7,5},{8,10},{9,11},{10,... | collective-permute-start | bytes 208904 | tf_op jit(solution)/shard_map/ppermute | solution.py:187
  53.8 12.2 %collective-permute-start.24 = (f32[408,128]{1,0:T(8,128)S(1)}, f32[408,128]{1,0:T(8,128)S(1)}, u32[]{:S(2)}, u32[]{:S(2)}) collective-permute-start(f32[408,128]{1,0:T(8,128)S(1)} %shard_map.70.refs_5_), channel_id=1, source_target_pairs={{0,1},{1,0},{2,3},{3,2},{4,5},{5,4},{6,7},{7,6},{8,9},{9,8},{10,11... | collective-permute-start | bytes 626696 | tf_op jit(solution)/shard_map/ppermute | solution.py:187
  56.7 9.4 %collective-permute-start.23 = (f32[544,128]{1,0:T(8,128)S(1)}, f32[544,128]{1,0:T(8,128)S(1)}, u32[]{:S(2)}, u32[]{:S(2)}) collective-permute-start(f32[544,128]{1,0:T(8,128)S(1)} %shard_map.69.refs_4_), channel_id=1, source_target_pairs={{0,1},{1,0},{2,3},{3,2},{4,5},{5,4},{6,7},{7,6},{8,9},{9,8},{10,11... | collective-permute-start | bytes 835592 | tf_op jit(solution)/shard_map/ppermute | solution.py:187
  56.8 9.3 %collective-permute-start.27 = (f32[408,128]{1,0:T(8,128)S(1)}, f32[408,128]{1,0:T(8,128)S(1)}, u32[]{:S(2)}, u32[]{:S(2)}) collective-permute-start(f32[408,128]{1,0:T(8,128)S(1)} %collective-permute-done.22.refs_8_), channel_id=1, source_target_pairs={{0,1},{1,0},{2,3},{3,2},{4,5},{5,4},{6,7},{7,6},{8,9},{9,8},{10,11... | collective-permute-start | bytes 626696 | tf_op jit(solution)/shard_map/ppermute | solution.py:187
  57.3 8.8 %collective-permute-start.26 = (f32[408,128]{1,0:T(8,128)S(1)}, f32[408,128]{1,0:T(8,128)S(1)}, u32[]{:S(2)}, u32[]{:S(2)}) collective-permute-start(f32[408,128]{1,0:T(8,128)S(1)} %collective-permute-done.21.refs_7_), channel_id=1, source_target_pairs={{0,1},{1,0},{2,3},{3,2},{4,5},{5,4},{6,7},{7,6},{8,9},{9,8},{10,11... | collective-permute-start | bytes 626696 | tf_op jit(solution)/shard_map/ppermute | solution.py:187
  57.3 8.7 %collective-permute-start.25 = (f32[408,128]{1,0:T(8,128)S(1)}, f32[408,128]{1,0:T(8,128)S(1)}, u32[]{:S(2)}, u32[]{:S(2)}) collective-permute-start(f32[408,128]{1,0:T(8,128)S(1)} %collective-permute-done.20.refs_6_), channel_id=1, source_target_pairs={{0,1},{1,0},{2,3},{3,2},{4,5},{5,4},{6,7},{7,6},{8,9},{9,8},{10,11... | collective-permute-start | bytes 626696 | tf_op jit(solution)/shard_map/ppermute | solution.py:187
  74.9 7.4 %collective-permute-start.33 = (f32[64,128]{1,0:T(8,128)S(1)}, f32[64,128]{1,0:T(8,128)S(1)}, u32[]{:S(2)}, u32[]{:S(2)}) collective-permute-start(f32[64,128]{1,0:T(8,128)S(1)} %get-tuple-element.24.refs_0_), channel_id=1, source_target_pairs={{0,24},{1,25},{2,26},{3,27},{4,28},{5,29},{6,30},{7,31},{8,16},{9,... | collective-permute-start | bytes 98312 | tf_op jit(solution)/shard_map/ppermute | solution.py:187
  76.4 6.4 %collective-permute-start.32 = (f32[64,128]{1,0:T(8,128)S(1)}, f32[64,128]{1,0:T(8,128)S(1)}, u32[]{:S(2)}, u32[]{:S(2)}) collective-permute-start(f32[64,128]{1,0:T(8,128)S(1)} %get-tuple-element.24.refs_0_), channel_id=1, source_target_pairs={{0,16},{1,17},{2,18},{3,19},{4,20},{5,21},{6,22},{7,23},{8,24},{9,... | collective-permute-start | bytes 98312 | tf_op jit(solution)/shard_map/ppermute | solution.py:187
  76.4 6.4 %collective-permute-start.31 = (f32[64,128]{1,0:T(8,128)S(1)}, f32[64,128]{1,0:T(8,128)S(1)}, u32[]{:S(2)}, u32[]{:S(2)}) collective-permute-start(f32[64,128]{1,0:T(8,128)S(1)} %get-tuple-element.24.refs_0_), channel_id=1, source_target_pairs={{0,8},{1,9},{2,10},{3,11},{4,12},{5,13},{6,14},{7,15},{8,0},{9,1},... | collective-permute-start | bytes 98312 | tf_op jit(solution)/shard_map/ppermute | solution.py:187
  79.3 6.5 %collective-permute-start.30 = (f32[64,128]{1,0:T(8,128)S(1)}, f32[64,128]{1,0:T(8,128)S(1)}, u32[]{:S(2)}, u32[]{:S(2)}) collective-permute-start(f32[64,128]{1,0:T(8,128)S(1)} %get-tuple-element.24.refs_0_), channel_id=1, source_target_pairs={{0,6},{1,7},{2,4},{3,5},{4,2},{5,3},{6,0},{7,1},{8,14},{9,15},{10,... | collective-permute-start | bytes 98312 | tf_op jit(solution)/shard_map/ppermute | solution.py:187
  80.9 6.2 %collective-permute-start.29 = (f32[64,128]{1,0:T(8,128)S(1)}, f32[64,128]{1,0:T(8,128)S(1)}, u32[]{:S(2)}, u32[]{:S(2)}) collective-permute-start(f32[64,128]{1,0:T(8,128)S(1)} %get-tuple-element.24.refs_0_), channel_id=1, source_target_pairs={{0,4},{1,5},{2,6},{3,7},{4,0},{5,1},{6,2},{7,3},{8,12},{9,13},{10,... | collective-permute-start | bytes 98312 | tf_op jit(solution)/shard_map/ppermute | solution.py:187
  82.3 4.9 %collective-permute-start.28 = (f32[64,128]{1,0:T(8,128)S(1)}, f32[64,128]{1,0:T(8,128)S(1)}, u32[]{:S(2)}, u32[]{:S(2)}) collective-permute-start(f32[64,128]{1,0:T(8,128)S(1)} %get-tuple-element.24.refs_0_), channel_id=1, source_target_pairs={{0,2},{1,3},{2,0},{3,1},{4,6},{5,7},{6,4},{7,5},{8,10},{9,11},{10,... | collective-permute-start | bytes 98312 | tf_op jit(solution)/shard_map/ppermute | solution.py:187
  82.8 5.9 %collective-permute-start.36 = (f32[192,128]{1,0:T(8,128)S(1)}, f32[192,128]{1,0:T(8,128)S(1)}, u32[]{:S(2)}, u32[]{:S(2)}) collective-permute-start(f32[192,128]{1,0:T(8,128)S(1)} %shard_map.72.refs_11_), channel_id=1, source_target_pairs={{0,6},{1,7},{2,4},{3,5},{4,2},{5,3},{6,0},{7,1},{8,14},{9,15},{10,... | collective-permute-start | bytes 294920 | tf_op jit(solution)/shard_map/ppermute | solution.py:187
  84.4 5.3 %collective-permute-start.35 = (f32[192,128]{1,0:T(8,128)S(1)}, f32[192,128]{1,0:T(8,128)S(1)}, u32[]{:S(2)}, u32[]{:S(2)}) collective-permute-start(f32[192,128]{1,0:T(8,128)S(1)} %shard_map.72.refs_11_), channel_id=1, source_target_pairs={{0,4},{1,5},{2,6},{3,7},{4,0},{5,1},{6,2},{7,3},{8,12},{9,13},{10,... | collective-permute-start | bytes 294920 | tf_op jit(solution)/shard_map/ppermute | solution.py:187
  85.9 4.6 %collective-permute-start.34 = (f32[192,128]{1,0:T(8,128)S(1)}, f32[192,128]{1,0:T(8,128)S(1)}, u32[]{:S(2)}, u32[]{:S(2)}) collective-permute-start(f32[192,128]{1,0:T(8,128)S(1)} %shard_map.72.refs_11_), channel_id=1, source_target_pairs={{0,2},{1,3},{2,0},{3,1},{4,6},{5,7},{6,4},{7,5},{8,10},{9,11},{10,... | collective-permute-start | bytes 294920 | tf_op jit(solution)/shard_map/ppermute | solution.py:187
  87.1 7.3 %collective-permute-start.38 = (f32[192,128]{1,0:T(8,128)S(1)}, f32[192,128]{1,0:T(8,128)S(1)}, u32[]{:S(2)}, u32[]{:S(2)}) collective-permute-start(f32[192,128]{1,0:T(8,128)S(1)} %shard_map.72.refs_11_), channel_id=1, source_target_pairs={{0,1},{1,0},{2,3},{3,2},{4,5},{5,4},{6,7},{7,6},{8,9},{9,8},{10,11... | collective-permute-start | bytes 294920 | tf_op jit(solution)/shard_map/ppermute | solution.py:187
  87.2 7.2 %collective-permute-start.37 = (f32[256,128]{1,0:T(8,128)S(1)}, f32[256,128]{1,0:T(8,128)S(1)}, u32[]{:S(2)}, u32[]{:S(2)}) collective-permute-start(f32[256,128]{1,0:T(8,128)S(1)} %shard_map.71.refs_10_), channel_id=1, source_target_pairs={{0,1},{1,0},{2,3},{3,2},{4,5},{5,4},{6,7},{7,6},{8,9},{9,8},{10,11... | collective-permute-start | bytes 393224 | tf_op jit(solution)/shard_map/ppermute | solution.py:187
  88.7 5.7 %collective-permute-start.41 = (f32[192,128]{1,0:T(8,128)S(1)}, f32[192,128]{1,0:T(8,128)S(1)}, u32[]{:S(2)}, u32[]{:S(2)}) collective-permute-start(f32[192,128]{1,0:T(8,128)S(1)} %collective-permute-done.36.refs_14_), channel_id=1, source_target_pairs={{0,1},{1,0},{2,3},{3,2},{4,5},{5,4},{6,7},{7,6},{8,9},{9,8},{10,11... | collective-permute-start | bytes 294920 | tf_op jit(solution)/shard_map/ppermute | solution.py:187
  89.7 4.8 %collective-permute-start.40 = (f32[192,128]{1,0:T(8,128)S(1)}, f32[192,128]{1,0:T(8,128)S(1)}, u32[]{:S(2)}, u32[]{:S(2)}) collective-permute-start(f32[192,128]{1,0:T(8,128)S(1)} %collective-permute-done.35.refs_13_), channel_id=1, source_target_pairs={{0,1},{1,0},{2,3},{3,2},{4,5},{5,4},{6,7},{7,6},{8,9},{9,8},{10,11... | collective-permute-start | bytes 294920 | tf_op jit(solution)/shard_map/ppermute | solution.py:187
  90.5 4.0 %collective-permute-start.39 = (f32[192,128]{1,0:T(8,128)S(1)}, f32[192,128]{1,0:T(8,128)S(1)}, u32[]{:S(2)}, u32[]{:S(2)}) collective-permute-start(f32[192,128]{1,0:T(8,128)S(1)} %collective-permute-done.34.refs_12_), channel_id=1, source_target_pairs={{0,1},{1,0},{2,3},{3,2},{4,5},{5,4},{6,7},{7,6},{8,9},{9,8},{10,11... | collective-permute-start | bytes 294920 | tf_op jit(solution)/shard_map/ppermute | solution.py:187

commit v8 on v7

--- a/solution.py
+++ b/solution.py
@@ -358,10 +358,11 @@
     held = mm3(jnp.concatenate([raw, mm3(whole, raw)], 0), small, 1, 1)
     mixing = held[:double]
     values2 = mm3(mixing, held[double:], 0, 0)
-    weights = stacked(jnp.concatenate([mixing, -mm3(mixing, values2)], 0))
+    turned = stacked(mm3(mixing, values2))
+    weights = stacked(mixing)
 
     def update(at, acc):
-        residual = with_stacked(jnp.concatenate([image_ref[at, :], y2_ref[at, :]], 1), weights)
+        residual = with_stacked(image_ref[at, :], weights) - with_stacked(y2_ref[at, :], turned)
         return acc + jnp.sum(residual * residual, axis=0, keepdims=True)
 
     squares = sweep(total, update, jnp.zeros((1, width), F32))
@@ -369,7 +370,7 @@
     norm_ref[1:, :] = jnp.sqrt(squares)
     own = own_y2()
     ritz_ref[...] = mm3(own, mixing)
-    residual = with_stacked(jnp.concatenate([own_image(), own], 1), weights)
+    residual = with_stacked(own_image(), weights) - with_stacked(own, turned)
     search_ref[...] = divided(residual, own_diag(), values2)
 
 

time: 103 us -> 103 us (level)
  no operation moved by 1% of the time
where the time goes in v8:
time: 103 us
  starting transfers between devices  41.7 us (40%)
  Pallas kernels  30.6 us (30%)
  waiting for transfers between devices  28.3 us (27%)
    ppermute x42, starting transfers between devices, swap(): return lax.ppermute(x, 'blk', [(i, i ^ m) for i in range(n)])  41.7 us
    ppermute x42, waiting for transfers between devices, swap(): return lax.ppermute(x, 'blk', [(i, i ^ m) for i in range(n)])  28.3 us
    pallas_call x1, Pallas kernels, cubed(): pl.pallas_call(lambda *refs: with_product(rings, rows, *refs), out_shape=...  8.78 us
    pallas_call x1, Pallas kernels, metric_factor(): pl.pallas_call(metric_kernel, out_shape=shape(double, double), in_specs=[...  8.26 us
    pallas_call x1, Pallas kernels, cubed(): pl.pallas_call(lambda *refs: last_step(rings, rows, *refs), out_shape=(sh...  8.05 us
    pallas_call x1, Pallas kernels, second_metric(): pl.pallas_call(second_factor, out_shape=(shape(width, width),) * 4, in_sp...  3.94 us
  transfers between devices with their start and end apart: 42, of which 14 were waited for; matrix products, arithmetic and copies ran while one was open for 0% of the time, Pallas kernels for 13%

profile of v8, /device:TPU:0, one launch (start us, length us, event | category | flops | bytes accessed | tf_op | source)
XLA Modules:
  0.0 102.5 jit_solution(5280527182091314850)
XLA Ops:
  0.6 0.8 pad_add_fusion.refs_0_
  1.5 5.1 %collective-permute-start.5 = (f32[128,128]{1,0:T(8,128)S(1)}, f32[128,128]{1,0:T(8,128)S(1)}, u32[]{:S(2)}, u32[]{:S(2)}) collective-permute-start(f32[128,128]{1,0:T(8,128)S(1)} %pad_add_fusion.refs_0_), channel_id=1, source_target_pairs={{0,24},{1,25},{2,26},{3,27},{4,28},{5,29},{6,30},{7,31},{8,16},{9,... | collective-permute-start | bytes 196616 | tf_op jit(solution)/shard_map/ppermute | solution.py:187
  6.6 0.6 collective-permute-start.3
  7.3 2.6 %collective-permute-start.2 = (f32[128,128]{1,0:T(8,128)S(1)}, f32[128,128]{1,0:T(8,128)S(1)}, u32[]{:S(2)}, u32[]{:S(2)}) collective-permute-start(f32[128,128]{1,0:T(8,128)S(1)} %pad_add_fusion.refs_0_), channel_id=1, source_target_pairs={{0,6},{1,7},{2,4},{3,5},{4,2},{5,3},{6,0},{7,1},{8,14},{9,15},{10,... | collective-permute-start | bytes 196616 | tf_op jit(solution)/shard_map/ppermute | solution.py:187
  9.8 2.4 %collective-permute-done.4.refs_1_ = f32[128,128]{1,0:T(8,128)S(1)} collective-permute-done((f32[128,128]{1,0:T(8,128)S(1)}, f32[128,128]{1,0:T(8,128)S(1)}, u32[]{:S(2)}, u32[]{:S(2)}) %collective-permute-start.4) | collective-permute-done | bytes 65568 | tf_op jit(solution)/shard_map/ppermute | solution.py:187
  12.2 2.5 %collective-permute-start.8 = (f32[384,128]{1,0:T(8,128)S(1)}, f32[384,128]{1,0:T(8,128)S(1)}, u32[]{:S(2)}, u32[]{:S(2)}) collective-permute-start(f32[384,128]{1,0:T(8,128)S(1)} %shard_map.68.refs_4_), channel_id=1, source_target_pairs={{0,6},{1,7},{2,4},{3,5},{4,2},{5,3},{6,0},{7,1},{8,14},{9,15},{10,... | collective-permute-start | bytes 589832 | tf_op jit(solution)/shard_map/ppermute | solution.py:187
  14.7 0.5 collective-permute-start.7
  15.3 0.5 collective-permute-start.6
  15.8 1.5 %collective-permute-start.1 = (f32[128,128]{1,0:T(8,128)S(1)}, f32[128,128]{1,0:T(8,128)S(1)}, u32[]{:S(2)}, u32[]{:S(2)}) collective-permute-start(f32[128,128]{1,0:T(8,128)S(1)} %pad_add_fusion.refs_0_), channel_id=1, source_target_pairs={{0,4},{1,5},{2,6},{3,7},{4,0},{5,1},{6,2},{7,3},{8,12},{9,13},{10,... | collective-permute-start | bytes 196616 | tf_op jit(solution)/shard_map/ppermute | solution.py:187
  17.3 1.5 %collective-permute-start = (f32[128,128]{1,0:T(8,128)S(1)}, f32[128,128]{1,0:T(8,128)S(1)}, u32[]{:S(2)}, u32[]{:S(2)}) collective-permute-start(f32[128,128]{1,0:T(8,128)S(1)} %pad_add_fusion.refs_0_), channel_id=1, source_target_pairs={{0,2},{1,3},{2,0},{3,1},{4,6},{5,7},{6,4},{7,5},{8,10},{9,11},{10,... | collective-permute-start | bytes 196616 | tf_op jit(solution)/shard_map/ppermute | solution.py:187
  18.8 6.5 %collective-permute-done.1.refs_2_ = f32[128,128]{1,0:T(8,128)S(1)} collective-permute-done((f32[128,128]{1,0:T(8,128)S(1)}, f32[128,128]{1,0:T(8,128)S(1)}, u32[]{:S(2)}, u32[]{:S(2)}) %collective-permute-start.1) | collective-permute-done | bytes 65568 | tf_op jit(solution)/shard_map/ppermute | solution.py:187
  25.6 0.5 collective-permute-start.10
  26.2 0.4 collective-permute-start.12
  26.9 0.5 collective-permute-done.10.refs_9_
  27.7 0.3 collective-permute-done.12.refs_11_
  28.0 0.3 collective-permute-done.11.refs_10_
  28.3 0.8 first_product.1
  29.1 1.6 %collective-permute-start.19 = (f32[136,128]{1,0:T(8,128)S(1)}, f32[136,128]{1,0:T(8,128)S(1)}, u32[]{:S(2)}, u32[]{:S(2)}) collective-permute-start(f32[136,128]{1,0:T(8,128)S(1)} %get-tuple-element.15.refs_0_), channel_id=1, source_target_pairs={{0,24},{1,25},{2,26},{3,27},{4,28},{5,29},{6,30},{7,31},{8,16},{9,... | collective-permute-start | bytes 208904 | tf_op jit(solution)/shard_map/ppermute | solution.py:187
  30.6 2.9 %collective-permute-start.17 = (f32[136,128]{1,0:T(8,128)S(1)}, f32[136,128]{1,0:T(8,128)S(1)}, u32[]{:S(2)}, u32[]{:S(2)}) collective-permute-start(f32[136,128]{1,0:T(8,128)S(1)} %get-tuple-element.15.refs_0_), channel_id=1, source_target_pairs={{0,8},{1,9},{2,10},{3,11},{4,12},{5,13},{6,14},{7,15},{8,0},{9,1},... | collective-permute-start | bytes 208904 | tf_op jit(solution)/shard_map/ppermute | solution.py:187
  33.5 2.5 %collective-permute-done.19.refs_2_ = f32[136,128]{1,0:T(8,128)S(1)} collective-permute-done((f32[136,128]{1,0:T(8,128)S(1)}, f32[136,128]{1,0:T(8,128)S(1)}, u32[]{:S(2)}, u32[]{:S(2)}) %collective-permute-start.19) | collective-permute-done | bytes 69664 | tf_op jit(solution)/shard_map/ppermute | solution.py:187
  36.0 2.1 %collective-permute-done.18.refs_1_ = f32[136,128]{1,0:T(8,128)S(1)} collective-permute-done((f32[136,128]{1,0:T(8,128)S(1)}, f32[136,128]{1,0:T(8,128)S(1)}, u32[]{:S(2)}, u32[]{:S(2)}) %collective-permute-start.18) | collective-permute-done | bytes 69664 | tf_op jit(solution)/shard_map/ppermute | solution.py:187
  38.2 1.6 %collective-permute-start.22 = (f32[408,128]{1,0:T(8,128)S(1)}, f32[408,128]{1,0:T(8,128)S(1)}, u32[]{:S(2)}, u32[]{:S(2)}) collective-permute-start(f32[408,128]{1,0:T(8,128)S(1)} %shard_map.70.refs_5_), channel_id=1, source_target_pairs={{0,6},{1,7},{2,4},{3,5},{4,2},{5,3},{6,0},{7,1},{8,14},{9,15},{10,... | collective-permute-start | bytes 626696 | tf_op jit(solution)/shard_map/ppermute | solution.py:187
  39.8 1.4 %collective-permute-start.21 = (f32[408,128]{1,0:T(8,128)S(1)}, f32[408,128]{1,0:T(8,128)S(1)}, u32[]{:S(2)}, u32[]{:S(2)}) collective-permute-start(f32[408,128]{1,0:T(8,128)S(1)} %shard_map.70.refs_5_), channel_id=1, source_target_pairs={{0,4},{1,5},{2,6},{3,7},{4,0},{5,1},{6,2},{7,3},{8,12},{9,13},{10,... | collective-permute-start | bytes 626696 | tf_op jit(solution)/shard_map/ppermute | solution.py:187
  41.2 0.5 collective-permute-start.20
  41.7 1.5 %collective-permute-start.16 = (f32[136,128]{1,0:T(8,128)S(1)}, f32[136,128]{1,0:T(8,128)S(1)}, u32[]{:S(2)}, u32[]{:S(2)}) collective-permute-start(f32[136,128]{1,0:T(8,128)S(1)} %get-tuple-element.15.refs_0_), channel_id=1, source_target_pairs={{0,6},{1,7},{2,4},{3,5},{4,2},{5,3},{6,0},{7,1},{8,14},{9,15},{10,... | collective-permute-start | bytes 208904 | tf_op jit(solution)/shard_map/ppermute | solution.py:187
  43.3 1.4 %collective-permute-start.15 = (f32[136,128]{1,0:T(8,128)S(1)}, f32[136,128]{1,0:T(8,128)S(1)}, u32[]{:S(2)}, u32[]{:S(2)}) collective-permute-start(f32[136,128]{1,0:T(8,128)S(1)} %get-tuple-element.15.refs_0_), channel_id=1, source_target_pairs={{0,4},{1,5},{2,6},{3,7},{4,0},{5,1},{6,2},{7,3},{8,12},{9,13},{10,... | collective-permute-start | bytes 208904 | tf_op jit(solution)/shard_map/ppermute | solution.py:187
  44.7 7.7 %collective-permute-done.16.refs_3_ = f32[136,128]{1,0:T(8,128)S(1)} collective-permute-done((f32[136,128]{1,0:T(8,128)S(1)}, f32[136,128]{1,0:T(8,128)S(1)}, u32[]{:S(2)}, u32[]{:S(2)}) %collective-permute-start.16) | collective-permute-done | bytes 69664 | tf_op jit(solution)/shard_map/ppermute | solution.py:187
  52.3 1.5 %collective-permute-start.14 = (f32[136,128]{1,0:T(8,128)S(1)}, f32[136,128]{1,0:T(8,128)S(1)}, u32[]{:S(2)}, u32[]{:S(2)}) collective-permute-start(f32[136,128]{1,0:T(8,128)S(1)} %get-tuple-element.15.refs_0_), channel_id=1, source_target_pairs={{0,2},{1,3},{2,0},{3,1},{4,6},{5,7},{6,4},{7,5},{8,10},{9,11},{10,... | collective-permute-start | bytes 208904 | tf_op jit(solution)/shard_map/ppermute | solution.py:187
  53.8 2.8 %collective-permute-done.14.refs_1_ = f32[136,128]{1,0:T(8,128)S(1)} collective-permute-done((f32[136,128]{1,0:T(8,128)S(1)}, f32[136,128]{1,0:T(8,128)S(1)}, u32[]{:S(2)}, u32[]{:S(2)}) %collective-permute-start.14) | collective-permute-done | bytes 69664 | tf_op jit(solution)/shard_map/ppermute | solution.py:187
  56.8 0.5 collective-permute-start.27
  57.3 0.4 collective-permute-start.25
  57.8 8.3 %metric.1.refs_3_ = f32[256,256]{1,0:T(8,128)S(1)} custom-call(f32[2048,256]{1,0:T(8,128)S(1)} %get-tuple-element.14.y_ref.refs_2_), custom_call_target="tpu_custom_call" | custom-call | flops 8999999488 | tf_op jit(solution)/shard_map/metric/pallas_call | solution.py:430
  66.1 8.8 %first_step.1 = (f32[2048,256]{1,0:T(8,128)S(1)}, f32[2048,128]{1,0:T(8,128)S(1)}, f32[128,128]{1,0:T(8,128)S(1)}, f32[1,128]{1,0:T(1,128)S(1)}, f32[64,128]{1,0:T(8,128)S(1)}) custom-call(s32[1]{0:T(128)} %bitcast.refs_0_, f32[64,2048]{1,0:T(8,128)S(1)} %bitcast.6, f32[2048,256]{1,0:T(8,128)S(1)} %get-tuple-element.14.y_ref.refs_2_, ...), custom_call_target="tpu_custom_call" | custom-call | tf_op jit(solution)/shard_map/first_step/pallas_call | solution.py:482
  74.9 1.5 %collective-permute-start.33 = (f32[64,128]{1,0:T(8,128)S(1)}, f32[64,128]{1,0:T(8,128)S(1)}, u32[]{:S(2)}, u32[]{:S(2)}) collective-permute-start(f32[64,128]{1,0:T(8,128)S(1)} %get-tuple-element.24.refs_0_), channel_id=1, source_target_pairs={{0,24},{1,25},{2,26},{3,27},{4,28},{5,29},{6,30},{7,31},{8,16},{9,... | collective-permute-start | bytes 98312 | tf_op jit(solution)/shard_map/ppermute | solution.py:187
  76.4 2.9 %collective-permute-start.31 = (f32[64,128]{1,0:T(8,128)S(1)}, f32[64,128]{1,0:T(8,128)S(1)}, u32[]{:S(2)}, u32[]{:S(2)}) collective-permute-start(f32[64,128]{1,0:T(8,128)S(1)} %get-tuple-element.24.refs_0_), channel_id=1, source_target_pairs={{0,8},{1,9},{2,10},{3,11},{4,12},{5,13},{6,14},{7,15},{8,0},{9,1},... | collective-permute-start | bytes 98312 | tf_op jit(solution)/shard_map/ppermute | solution.py:187
  79.3 1.5 %collective-permute-start.30 = (f32[64,128]{1,0:T(8,128)S(1)}, f32[64,128]{1,0:T(8,128)S(1)}, u32[]{:S(2)}, u32[]{:S(2)}) collective-permute-start(f32[64,128]{1,0:T(8,128)S(1)} %get-tuple-element.24.refs_0_), channel_id=1, source_target_pairs={{0,6},{1,7},{2,4},{3,5},{4,2},{5,3},{6,0},{7,1},{8,14},{9,15},{10,... | collective-permute-start | bytes 98312 | tf_op jit(solution)/shard_map/ppermute | solution.py:187
  80.9 1.4 %collective-permute-start.29 = (f32[64,128]{1,0:T(8,128)S(1)}, f32[64,128]{1,0:T(8,128)S(1)}, u32[]{:S(2)}, u32[]{:S(2)}) collective-permute-start(f32[64,128]{1,0:T(8,128)S(1)} %get-tuple-element.24.refs_0_), channel_id=1, source_target_pairs={{0,4},{1,5},{2,6},{3,7},{4,0},{5,1},{6,2},{7,3},{8,12},{9,13},{10,... | collective-permute-start | bytes 98312 | tf_op jit(solution)/shard_map/ppermute | solution.py:187
  82.3 0.5 collective-permute-start.28
  82.8 1.6 %collective-permute-start.36 = (f32[192,128]{1,0:T(8,128)S(1)}, f32[192,128]{1,0:T(8,128)S(1)}, u32[]{:S(2)}, u32[]{:S(2)}) collective-permute-start(f32[192,128]{1,0:T(8,128)S(1)} %shard_map.72.refs_11_), channel_id=1, source_target_pairs={{0,6},{1,7},{2,4},{3,5},{4,2},{5,3},{6,0},{7,1},{8,14},{9,15},{10,... | collective-permute-start | bytes 294920 | tf_op jit(solution)/shard_map/ppermute | solution.py:187
  84.4 1.4 %collective-permute-start.35 = (f32[192,128]{1,0:T(8,128)S(1)}, f32[192,128]{1,0:T(8,128)S(1)}, u32[]{:S(2)}, u32[]{:S(2)}) collective-permute-start(f32[192,128]{1,0:T(8,128)S(1)} %shard_map.72.refs_11_), channel_id=1, source_target_pairs={{0,4},{1,5},{2,6},{3,7},{4,0},{5,1},{6,2},{7,3},{8,12},{9,13},{10,... | collective-permute-start | bytes 294920 | tf_op jit(solution)/shard_map/ppermute | solution.py:187
  85.9 0.5 collective-permute-start.34
  86.4 0.7 second_gram.1.gram_ref
  87.2 0.5 collective-permute-start.37
  87.8 1.0 collective-permute-done.36.refs_14_
  88.7 1.0 collective-permute-done.35.refs_13_
  89.7 0.8 collective-permute-done.34.refs_12_
  90.5 3.9 %second_factor.1 = (f32[128,128]{1,0:T(8,128)S(1)}, f32[128,128]{1,0:T(8,128)S(1)}, f32[128,128]{1,0:T(8,128)S(1)}, f32[128,128]{1,0:T(8,128)S(1)}) custom-call(f32[128,256]{1,0:T(8,128)S(1)} %second_gram.1.gram_ref, f32[128,128]{1,0:T(8,128)S(1)} %get-tuple-element.19.small_ref.refs_5_), custom_call_target="tpu_custom_call" | custom-call | flops 8999999488 | tf_op jit(solution)/shard_map/second_factor/pallas_call | solution.py:452
  94.5 8.1 %last_step.1 = (f32[64,128]{1,0:T(8,128)}, f32[64,128]{1,0:T(8,128)}, f32[2,128]{1,0:T(2,128)}) custom-call(s32[1]{0:T(128)} %bitcast.refs_0_, f32[2048,256]{1,0:T(8,128)S(1)} %get-tuple-element.16.y2_ref.refs_1_, f32[2048,128]{1,0:T(8,128)S(1)} %get-tuple-element.17.refs_2_, f32[1,128]{1,0:T(1,128)S(1)} %get-tuple-element.18.refs_3_, f32[1,64]{1,0:T(1,128)S(1)} %bitcast.8, ...), custom_call_target="tpu_custom_call" | custom-call | tf_op jit(solution)/shard_map/last_step/pallas_call | solution.py:503
  (54 shorter events, 1.3 us)
Async XLA Ops:
  0.6 26.1 %copy-start.1 = (f32[64,1,2048]{2,1,0:T(1,128)S(1)}, f32[64,1,2048]{2,1,0:T(1,128)}, u32[]{:S(2)}) copy-start(f32[64,1,2048]{2,1,0:T(1,128)} %param.4) | copy-start | bytes 1572868
  1.5 26.8 %copy-start = (f32[64]{0:T(128)S(1)}, f32[64]{0:T(128)}, u32[]{:S(2)}) copy-start(f32[64]{0:T(128)} %param.7) | copy-start | bytes 772
  1.5 8.4 %collective-permute-start.5 = (f32[128,128]{1,0:T(8,128)S(1)}, f32[128,128]{1,0:T(8,128)S(1)}, u32[]{:S(2)}, u32[]{:S(2)}) collective-permute-start(f32[128,128]{1,0:T(8,128)S(1)} %pad_add_fusion.refs_0_), channel_id=1, source_target_pairs={{0,24},{1,25},{2,26},{3,27},{4,28},{5,29},{6,30},{7,31},{8,16},{9,... | collective-permute-start | bytes 196616 | tf_op jit(solution)/shard_map/ppermute | solution.py:187
  6.6 5.6 %collective-permute-start.4 = (f32[128,128]{1,0:T(8,128)S(1)}, f32[128,128]{1,0:T(8,128)S(1)}, u32[]{:S(2)}, u32[]{:S(2)}) collective-permute-start(f32[128,128]{1,0:T(8,128)S(1)} %pad_add_fusion.refs_0_), channel_id=1, source_target_pairs={{0,16},{1,17},{2,18},{3,19},{4,20},{5,21},{6,22},{7,23},{8,24},{9,... | collective-permute-start | bytes 196616 | tf_op jit(solution)/shard_map/ppermute | solution.py:187
  6.6 5.6 %collective-permute-start.3 = (f32[128,128]{1,0:T(8,128)S(1)}, f32[128,128]{1,0:T(8,128)S(1)}, u32[]{:S(2)}, u32[]{:S(2)}) collective-permute-start(f32[128,128]{1,0:T(8,128)S(1)} %pad_add_fusion.refs_0_), channel_id=1, source_target_pairs={{0,8},{1,9},{2,10},{3,11},{4,12},{5,13},{6,14},{7,15},{8,0},{9,1},... | collective-permute-start | bytes 196616 | tf_op jit(solution)/shard_map/ppermute | solution.py:187
  7.3 10.1 %collective-permute-start.2 = (f32[128,128]{1,0:T(8,128)S(1)}, f32[128,128]{1,0:T(8,128)S(1)}, u32[]{:S(2)}, u32[]{:S(2)}) collective-permute-start(f32[128,128]{1,0:T(8,128)S(1)} %pad_add_fusion.refs_0_), channel_id=1, source_target_pairs={{0,6},{1,7},{2,4},{3,5},{4,2},{5,3},{6,0},{7,1},{8,14},{9,15},{10,... | collective-permute-start | bytes 196616 | tf_op jit(solution)/shard_map/ppermute | solution.py:187
  12.2 13.9 %collective-permute-start.8 = (f32[384,128]{1,0:T(8,128)S(1)}, f32[384,128]{1,0:T(8,128)S(1)}, u32[]{:S(2)}, u32[]{:S(2)}) collective-permute-start(f32[384,128]{1,0:T(8,128)S(1)} %shard_map.68.refs_4_), channel_id=1, source_target_pairs={{0,6},{1,7},{2,4},{3,5},{4,2},{5,3},{6,0},{7,1},{8,14},{9,15},{10,... | collective-permute-start | bytes 589832 | tf_op jit(solution)/shard_map/ppermute | solution.py:187
  14.7 11.4 %collective-permute-start.7 = (f32[384,128]{1,0:T(8,128)S(1)}, f32[384,128]{1,0:T(8,128)S(1)}, u32[]{:S(2)}, u32[]{:S(2)}) collective-permute-start(f32[384,128]{1,0:T(8,128)S(1)} %shard_map.68.refs_4_), channel_id=1, source_target_pairs={{0,4},{1,5},{2,6},{3,7},{4,0},{5,1},{6,2},{7,3},{8,12},{9,13},{10,... | collective-permute-start | bytes 589832 | tf_op jit(solution)/shard_map/ppermute | solution.py:187
  15.3 11.4 %collective-permute-start.6 = (f32[384,128]{1,0:T(8,128)S(1)}, f32[384,128]{1,0:T(8,128)S(1)}, u32[]{:S(2)}, u32[]{:S(2)}) collective-permute-start(f32[384,128]{1,0:T(8,128)S(1)} %shard_map.68.refs_4_), channel_id=1, source_target_pairs={{0,2},{1,3},{2,0},{3,1},{4,6},{5,7},{6,4},{7,5},{8,10},{9,11},{10,... | collective-permute-start | bytes 589832 | tf_op jit(solution)/shard_map/ppermute | solution.py:187
  15.8 9.5 %collective-permute-start.1 = (f32[128,128]{1,0:T(8,128)S(1)}, f32[128,128]{1,0:T(8,128)S(1)}, u32[]{:S(2)}, u32[]{:S(2)}) collective-permute-start(f32[128,128]{1,0:T(8,128)S(1)} %pad_add_fusion.refs_0_), channel_id=1, source_target_pairs={{0,4},{1,5},{2,6},{3,7},{4,0},{5,1},{6,2},{7,3},{8,12},{9,13},{10,... | collective-permute-start | bytes 196616 | tf_op jit(solution)/shard_map/ppermute | solution.py:187
  17.3 8.2 %collective-permute-start = (f32[128,128]{1,0:T(8,128)S(1)}, f32[128,128]{1,0:T(8,128)S(1)}, u32[]{:S(2)}, u32[]{:S(2)}) collective-permute-start(f32[128,128]{1,0:T(8,128)S(1)} %pad_add_fusion.refs_0_), channel_id=1, source_target_pairs={{0,2},{1,3},{2,0},{3,1},{4,6},{5,7},{6,4},{7,5},{8,10},{9,11},{10,... | collective-permute-start | bytes 196616 | tf_op jit(solution)/shard_map/ppermute | solution.py:187
  25.5 1.9 %collective-permute-start.9 = (f32[512,128]{1,0:T(8,128)S(1)}, f32[512,128]{1,0:T(8,128)S(1)}, u32[]{:S(2)}, u32[]{:S(2)}) collective-permute-start(f32[512,128]{1,0:T(8,128)S(1)} %shard_map.67.refs_3_), channel_id=1, source_target_pairs={{0,1},{1,0},{2,3},{3,2},{4,5},{5,4},{6,7},{7,6},{8,9},{9,8},{10,11... | collective-permute-start | bytes 786440 | tf_op jit(solution)/shard_map/ppermute | solution.py:187
  25.6 1.8 %collective-permute-start.10 = (f32[384,128]{1,0:T(8,128)S(1)}, f32[384,128]{1,0:T(8,128)S(1)}, u32[]{:S(2)}, u32[]{:S(2)}) collective-permute-start(f32[384,128]{1,0:T(8,128)S(1)} %shard_map.68.refs_4_), channel_id=1, source_target_pairs={{0,1},{1,0},{2,3},{3,2},{4,5},{5,4},{6,7},{7,6},{8,9},{9,8},{10,11... | collective-permute-start | bytes 589832 | tf_op jit(solution)/shard_map/ppermute | solution.py:187
  26.1 1.6 %collective-permute-start.13 = (f32[384,128]{1,0:T(8,128)S(1)}, f32[384,128]{1,0:T(8,128)S(1)}, u32[]{:S(2)}, u32[]{:S(2)}) collective-permute-start(f32[384,128]{1,0:T(8,128)S(1)} %collective-permute-done.8.refs_7_), channel_id=1, source_target_pairs={{0,1},{1,0},{2,3},{3,2},{4,5},{5,4},{6,7},{7,6},{8,9},{9,8},{10,11... | collective-permute-start | bytes 589832 | tf_op jit(solution)/shard_map/ppermute | solution.py:187
  26.2 1.8 %collective-permute-start.12 = (f32[384,128]{1,0:T(8,128)S(1)}, f32[384,128]{1,0:T(8,128)S(1)}, u32[]{:S(2)}, u32[]{:S(2)}) collective-permute-start(f32[384,128]{1,0:T(8,128)S(1)} %collective-permute-done.7.refs_6_), channel_id=1, source_target_pairs={{0,1},{1,0},{2,3},{3,2},{4,5},{5,4},{6,7},{7,6},{8,9},{9,8},{10,11... | collective-permute-start | bytes 589832 | tf_op jit(solution)/shard_map/ppermute | solution.py:187
  26.6 1.6 %collective-permute-start.11 = (f32[384,128]{1,0:T(8,128)S(1)}, f32[384,128]{1,0:T(8,128)S(1)}, u32[]{:S(2)}, u32[]{:S(2)}) collective-permute-start(f32[384,128]{1,0:T(8,128)S(1)} %collective-permute-done.6.refs_5_), channel_id=1, source_target_pairs={{0,1},{1,0},{2,3},{3,2},{4,5},{5,4},{6,7},{7,6},{8,9},{9,8},{10,11... | collective-permute-start | bytes 589832 | tf_op jit(solution)/shard_map/ppermute | solution.py:187
  29.1 7.0 %collective-permute-start.19 = (f32[136,128]{1,0:T(8,128)S(1)}, f32[136,128]{1,0:T(8,128)S(1)}, u32[]{:S(2)}, u32[]{:S(2)}) collective-permute-start(f32[136,128]{1,0:T(8,128)S(1)} %get-tuple-element.15.refs_0_), channel_id=1, source_target_pairs={{0,24},{1,25},{2,26},{3,27},{4,28},{5,29},{6,30},{7,31},{8,16},{9,... | collective-permute-start | bytes 208904 | tf_op jit(solution)/shard_map/ppermute | solution.py:187
  30.6 7.5 %collective-permute-start.18 = (f32[136,128]{1,0:T(8,128)S(1)}, f32[136,128]{1,0:T(8,128)S(1)}, u32[]{:S(2)}, u32[]{:S(2)}) collective-permute-start(f32[136,128]{1,0:T(8,128)S(1)} %get-tuple-element.15.refs_0_), channel_id=1, source_target_pairs={{0,16},{1,17},{2,18},{3,19},{4,20},{5,21},{6,22},{7,23},{8,24},{9,... | collective-permute-start | bytes 208904 | tf_op jit(solution)/shard_map/ppermute | solution.py:187
  30.6 7.5 %collective-permute-start.17 = (f32[136,128]{1,0:T(8,128)S(1)}, f32[136,128]{1,0:T(8,128)S(1)}, u32[]{:S(2)}, u32[]{:S(2)}) collective-permute-start(f32[136,128]{1,0:T(8,128)S(1)} %get-tuple-element.15.refs_0_), channel_id=1, source_target_pairs={{0,8},{1,9},{2,10},{3,11},{4,12},{5,13},{6,14},{7,15},{8,0},{9,1},... | collective-permute-start | bytes 208904 | tf_op jit(solution)/shard_map/ppermute | solution.py:187
  38.2 18.6 %collective-permute-start.22 = (f32[408,128]{1,0:T(8,128)S(1)}, f32[408,128]{1,0:T(8,128)S(1)}, u32[]{:S(2)}, u32[]{:S(2)}) collective-permute-start(f32[408,128]{1,0:T(8,128)S(1)} %shard_map.70.refs_5_), channel_id=1, source_target_pairs={{0,6},{1,7},{2,4},{3,5},{4,2},{5,3},{6,0},{7,1},{8,14},{9,15},{10,... | collective-permute-start | bytes 626696 | tf_op jit(solution)/shard_map/ppermute | solution.py:187
  39.8 17.5 %collective-permute-start.21 = (f32[408,128]{1,0:T(8,128)S(1)}, f32[408,128]{1,0:T(8,128)S(1)}, u32[]{:S(2)}, u32[]{:S(2)}) collective-permute-start(f32[408,128]{1,0:T(8,128)S(1)} %shard_map.70.refs_5_), channel_id=1, source_target_pairs={{0,4},{1,5},{2,6},{3,7},{4,0},{5,1},{6,2},{7,3},{8,12},{9,13},{10,... | collective-permute-start | bytes 626696 | tf_op jit(solution)/shard_map/ppermute | solution.py:187
  41.2 16.1 %collective-permute-start.20 = (f32[408,128]{1,0:T(8,128)S(1)}, f32[408,128]{1,0:T(8,128)S(1)}, u32[]{:S(2)}, u32[]{:S(2)}) collective-permute-start(f32[408,128]{1,0:T(8,128)S(1)} %shard_map.70.refs_5_), channel_id=1, source_target_pairs={{0,2},{1,3},{2,0},{3,1},{4,6},{5,7},{6,4},{7,5},{8,10},{9,11},{10,... | collective-permute-start | bytes 626696 | tf_op jit(solution)/shard_map/ppermute | solution.py:187
  41.7 10.6 %collective-permute-start.16 = (f32[136,128]{1,0:T(8,128)S(1)}, f32[136,128]{1,0:T(8,128)S(1)}, u32[]{:S(2)}, u32[]{:S(2)}) collective-permute-start(f32[136,128]{1,0:T(8,128)S(1)} %get-tuple-element.15.refs_0_), channel_id=1, source_target_pairs={{0,6},{1,7},{2,4},{3,5},{4,2},{5,3},{6,0},{7,1},{8,14},{9,15},{10,... | collective-permute-start | bytes 208904 | tf_op jit(solution)/shard_map/ppermute | solution.py:187
  43.3 10.6 %collective-permute-start.15 = (f32[136,128]{1,0:T(8,128)S(1)}, f32[136,128]{1,0:T(8,128)S(1)}, u32[]{:S(2)}, u32[]{:S(2)}) collective-permute-start(f32[136,128]{1,0:T(8,128)S(1)} %get-tuple-element.15.refs_0_), channel_id=1, source_target_pairs={{0,4},{1,5},{2,6},{3,7},{4,0},{5,1},{6,2},{7,3},{8,12},{9,13},{10,... | collective-permute-start | bytes 208904 | tf_op jit(solution)/shard_map/ppermute | solution.py:187
  52.3 4.3 %collective-permute-start.14 = (f32[136,128]{1,0:T(8,128)S(1)}, f32[136,128]{1,0:T(8,128)S(1)}, u32[]{:S(2)}, u32[]{:S(2)}) collective-permute-start(f32[136,128]{1,0:T(8,128)S(1)} %get-tuple-element.15.refs_0_), channel_id=1, source_target_pairs={{0,2},{1,3},{2,0},{3,1},{4,6},{5,7},{6,4},{7,5},{8,10},{9,11},{10,... | collective-permute-start | bytes 208904 | tf_op jit(solution)/shard_map/ppermute | solution.py:187
  53.8 12.2 %collective-permute-start.24 = (f32[408,128]{1,0:T(8,128)S(1)}, f32[408,128]{1,0:T(8,128)S(1)}, u32[]{:S(2)}, u32[]{:S(2)}) collective-permute-start(f32[408,128]{1,0:T(8,128)S(1)} %shard_map.70.refs_5_), channel_id=1, source_target_pairs={{0,1},{1,0},{2,3},{3,2},{4,5},{5,4},{6,7},{7,6},{8,9},{9,8},{10,11... | collective-permute-start | bytes 626696 | tf_op jit(solution)/shard_map/ppermute | solution.py:187
  56.7 9.4 %collective-permute-start.23 = (f32[544,128]{1,0:T(8,128)S(1)}, f32[544,128]{1,0:T(8,128)S(1)}, u32[]{:S(2)}, u32[]{:S(2)}) collective-permute-start(f32[544,128]{1,0:T(8,128)S(1)} %shard_map.69.refs_4_), channel_id=1, source_target_pairs={{0,1},{1,0},{2,3},{3,2},{4,5},{5,4},{6,7},{7,6},{8,9},{9,8},{10,11... | collective-permute-start | bytes 835592 | tf_op jit(solution)/shard_map/ppermute | solution.py:187
  56.8 9.3 %collective-permute-start.27 = (f32[408,128]{1,0:T(8,128)S(1)}, f32[408,128]{1,0:T(8,128)S(1)}, u32[]{:S(2)}, u32[]{:S(2)}) collective-permute-start(f32[408,128]{1,0:T(8,128)S(1)} %collective-permute-done.22.refs_8_), channel_id=1, source_target_pairs={{0,1},{1,0},{2,3},{3,2},{4,5},{5,4},{6,7},{7,6},{8,9},{9,8},{10,11... | collective-permute-start | bytes 626696 | tf_op jit(solution)/shard_map/ppermute | solution.py:187
  57.3 8.8 %collective-permute-start.26 = (f32[408,128]{1,0:T(8,128)S(1)}, f32[408,128]{1,0:T(8,128)S(1)}, u32[]{:S(2)}, u32[]{:S(2)}) collective-permute-start(f32[408,128]{1,0:T(8,128)S(1)} %collective-permute-done.21.refs_7_), channel_id=1, source_target_pairs={{0,1},{1,0},{2,3},{3,2},{4,5},{5,4},{6,7},{7,6},{8,9},{9,8},{10,11... | collective-permute-start | bytes 626696 | tf_op jit(solution)/shard_map/ppermute | solution.py:187
  57.3 8.7 %collective-permute-start.25 = (f32[408,128]{1,0:T(8,128)S(1)}, f32[408,128]{1,0:T(8,128)S(1)}, u32[]{:S(2)}, u32[]{:S(2)}) collective-permute-start(f32[408,128]{1,0:T(8,128)S(1)} %collective-permute-done.20.refs_6_), channel_id=1, source_target_pairs={{0,1},{1,0},{2,3},{3,2},{4,5},{5,4},{6,7},{7,6},{8,9},{9,8},{10,11... | collective-permute-start | bytes 626696 | tf_op jit(solution)/shard_map/ppermute | solution.py:187
  74.9 7.4 %collective-permute-start.33 = (f32[64,128]{1,0:T(8,128)S(1)}, f32[64,128]{1,0:T(8,128)S(1)}, u32[]{:S(2)}, u32[]{:S(2)}) collective-permute-start(f32[64,128]{1,0:T(8,128)S(1)} %get-tuple-element.24.refs_0_), channel_id=1, source_target_pairs={{0,24},{1,25},{2,26},{3,27},{4,28},{5,29},{6,30},{7,31},{8,16},{9,... | collective-permute-start | bytes 98312 | tf_op jit(solution)/shard_map/ppermute | solution.py:187
  76.4 6.4 %collective-permute-start.32 = (f32[64,128]{1,0:T(8,128)S(1)}, f32[64,128]{1,0:T(8,128)S(1)}, u32[]{:S(2)}, u32[]{:S(2)}) collective-permute-start(f32[64,128]{1,0:T(8,128)S(1)} %get-tuple-element.24.refs_0_), channel_id=1, source_target_pairs={{0,16},{1,17},{2,18},{3,19},{4,20},{5,21},{6,22},{7,23},{8,24},{9,... | collective-permute-start | bytes 98312 | tf_op jit(solution)/shard_map/ppermute | solution.py:187
  76.4 6.4 %collective-permute-start.31 = (f32[64,128]{1,0:T(8,128)S(1)}, f32[64,128]{1,0:T(8,128)S(1)}, u32[]{:S(2)}, u32[]{:S(2)}) collective-permute-start(f32[64,128]{1,0:T(8,128)S(1)} %get-tuple-element.24.refs_0_), channel_id=1, source_target_pairs={{0,8},{1,9},{2,10},{3,11},{4,12},{5,13},{6,14},{7,15},{8,0},{9,1},... | collective-permute-start | bytes 98312 | tf_op jit(solution)/shard_map/ppermute | solution.py:187
  79.3 6.5 %collective-permute-start.30 = (f32[64,128]{1,0:T(8,128)S(1)}, f32[64,128]{1,0:T(8,128)S(1)}, u32[]{:S(2)}, u32[]{:S(2)}) collective-permute-start(f32[64,128]{1,0:T(8,128)S(1)} %get-tuple-element.24.refs_0_), channel_id=1, source_target_pairs={{0,6},{1,7},{2,4},{3,5},{4,2},{5,3},{6,0},{7,1},{8,14},{9,15},{10,... | collective-permute-start | bytes 98312 | tf_op jit(solution)/shard_map/ppermute | solution.py:187
  80.9 6.2 %collective-permute-start.29 = (f32[64,128]{1,0:T(8,128)S(1)}, f32[64,128]{1,0:T(8,128)S(1)}, u32[]{:S(2)}, u32[]{:S(2)}) collective-permute-start(f32[64,128]{1,0:T(8,128)S(1)} %get-tuple-element.24.refs_0_), channel_id=1, source_target_pairs={{0,4},{1,5},{2,6},{3,7},{4,0},{5,1},{6,2},{7,3},{8,12},{9,13},{10,... | collective-permute-start | bytes 98312 | tf_op jit(solution)/shard_map/ppermute | solution.py:187
  82.3 4.9 %collective-permute-start.28 = (f32[64,128]{1,0:T(8,128)S(1)}, f32[64,128]{1,0:T(8,128)S(1)}, u32[]{:S(2)}, u32[]{:S(2)}) collective-permute-start(f32[64,128]{1,0:T(8,128)S(1)} %get-tuple-element.24.refs_0_), channel_id=1, source_target_pairs={{0,2},{1,3},{2,0},{3,1},{4,6},{5,7},{6,4},{7,5},{8,10},{9,11},{10,... | collective-permute-start | bytes 98312 | tf_op jit(solution)/shard_map/ppermute | solution.py:187
  82.8 5.9 %collective-permute-start.36 = (f32[192,128]{1,0:T(8,128)S(1)}, f32[192,128]{1,0:T(8,128)S(1)}, u32[]{:S(2)}, u32[]{:S(2)}) collective-permute-start(f32[192,128]{1,0:T(8,128)S(1)} %shard_map.72.refs_11_), channel_id=1, source_target_pairs={{0,6},{1,7},{2,4},{3,5},{4,2},{5,3},{6,0},{7,1},{8,14},{9,15},{10,... | collective-permute-start | bytes 294920 | tf_op jit(solution)/shard_map/ppermute | solution.py:187
  84.4 5.3 %collective-permute-start.35 = (f32[192,128]{1,0:T(8,128)S(1)}, f32[192,128]{1,0:T(8,128)S(1)}, u32[]{:S(2)}, u32[]{:S(2)}) collective-permute-start(f32[192,128]{1,0:T(8,128)S(1)} %shard_map.72.refs_11_), channel_id=1, source_target_pairs={{0,4},{1,5},{2,6},{3,7},{4,0},{5,1},{6,2},{7,3},{8,12},{9,13},{10,... | collective-permute-start | bytes 294920 | tf_op jit(solution)/shard_map/ppermute | solution.py:187
  85.9 4.6 %collective-permute-start.34 = (f32[192,128]{1,0:T(8,128)S(1)}, f32[192,128]{1,0:T(8,128)S(1)}, u32[]{:S(2)}, u32[]{:S(2)}) collective-permute-start(f32[192,128]{1,0:T(8,128)S(1)} %shard_map.72.refs_11_), channel_id=1, source_target_pairs={{0,2},{1,3},{2,0},{3,1},{4,6},{5,7},{6,4},{7,5},{8,10},{9,11},{10,... | collective-permute-start | bytes 294920 | tf_op jit(solution)/shard_map/ppermute | solution.py:187
  87.1 7.3 %collective-permute-start.38 = (f32[192,128]{1,0:T(8,128)S(1)}, f32[192,128]{1,0:T(8,128)S(1)}, u32[]{:S(2)}, u32[]{:S(2)}) collective-permute-start(f32[192,128]{1,0:T(8,128)S(1)} %shard_map.72.refs_11_), channel_id=1, source_target_pairs={{0,1},{1,0},{2,3},{3,2},{4,5},{5,4},{6,7},{7,6},{8,9},{9,8},{10,11... | collective-permute-start | bytes 294920 | tf_op jit(solution)/shard_map/ppermute | solution.py:187
  87.2 7.2 %collective-permute-start.37 = (f32[256,128]{1,0:T(8,128)S(1)}, f32[256,128]{1,0:T(8,128)S(1)}, u32[]{:S(2)}, u32[]{:S(2)}) collective-permute-start(f32[256,128]{1,0:T(8,128)S(1)} %shard_map.71.refs_10_), channel_id=1, source_target_pairs={{0,1},{1,0},{2,3},{3,2},{4,5},{5,4},{6,7},{7,6},{8,9},{9,8},{10,11... | collective-permute-start | bytes 393224 | tf_op jit(solution)/shard_map/ppermute | solution.py:187
  88.7 5.7 %collective-permute-start.41 = (f32[192,128]{1,0:T(8,128)S(1)}, f32[192,128]{1,0:T(8,128)S(1)}, u32[]{:S(2)}, u32[]{:S(2)}) collective-permute-start(f32[192,128]{1,0:T(8,128)S(1)} %collective-permute-done.36.refs_14_), channel_id=1, source_target_pairs={{0,1},{1,0},{2,3},{3,2},{4,5},{5,4},{6,7},{7,6},{8,9},{9,8},{10,11... | collective-permute-start | bytes 294920 | tf_op jit(solution)/shard_map/ppermute | solution.py:187
  89.7 4.8 %collective-permute-start.40 = (f32[192,128]{1,0:T(8,128)S(1)}, f32[192,128]{1,0:T(8,128)S(1)}, u32[]{:S(2)}, u32[]{:S(2)}) collective-permute-start(f32[192,128]{1,0:T(8,128)S(1)} %collective-permute-done.35.refs_13_), channel_id=1, source_target_pairs={{0,1},{1,0},{2,3},{3,2},{4,5},{5,4},{6,7},{7,6},{8,9},{9,8},{10,11... | collective-permute-start | bytes 294920 | tf_op jit(solution)/shard_map/ppermute | solution.py:187
  90.5 4.0 %collective-permute-start.39 = (f32[192,128]{1,0:T(8,128)S(1)}, f32[192,128]{1,0:T(8,128)S(1)}, u32[]{:S(2)}, u32[]{:S(2)}) collective-permute-start(f32[192,128]{1,0:T(8,128)S(1)} %collective-permute-done.34.refs_12_), channel_id=1, source_target_pairs={{0,1},{1,0},{2,3},{3,2},{4,5},{5,4},{6,7},{7,6},{8,9},{9,8},{10,11... | collective-permute-start | bytes 294920 | tf_op jit(solution)/shard_map/ppermute | solution.py:187
